TPU v7x, 128 devices: a whole 4x4x4 slice. The times are simulated.
128 devices in a mesh: tm: 8 (over x_lo, z), rows: 16 (over y, x_hi, core).
Axes of the slice: x: 4 (x_hi: 2, x_lo: 2; x = x_hi * 2 + x_lo), y: 4, z: 4, core: 2. Of those that a mesh axis runs over, the one named last changes fastest.
Arguments:
- features: bfloat16 [8, 256, 64, 256], P('tm', 'rows'), may hold values from -6 to 6
- block_shift: int32 [3, 4, 8, 32, 32], P(None, None, 'tm', 'rows'), may hold values from -5 to 5
- quarter_pel: int32 [3, 4, 8, 32, 32], P(None, None, 'tm', 'rows'), may hold values from 0 to 3
- update_mask: int32 [3, 8], P(None, 'tm'), may hold values 0 or 1
- uniting_weight: bfloat16 [3, 3, 64, 192], replicated, may hold values from -0.15625 to 0.15625
- mixing_weight: bfloat16 [3, 3, 64, 64], replicated, may hold values from -0.25 to 0.25
Outputs:
- refined: bfloat16 [8, 256, 64, 256], P('tm', 'rows')
All inputs are finite; a program needn't handle non-finite values. No bound on the sum of `update_mask` on one device may be relied on, other than what follows from the above.
Results may differ from a plain program's by a relative error of at most 0.0057.
Values may be sent and summed in bfloat16 or wider, within the bound.
No kernel may reach another device: no remote copies, remote signals or barrier semaphores. Data moves between devices by JAX's collectives and lax.ppermute only.
A program may use at most 128 MiB of HBM per device.

v0:
```python
import jax
import jax.numpy as jnp
from jax import lax
from jax.sharding import PartitionSpec as P

LEVELS = 3
SPAN = 5


def passed_along(block, axis, distance):
    devices = range(lax.axis_size(axis))
    route = [((i - distance) % len(devices), i) for i in devices]
    return lax.ppermute(block, axis, route)


def with_halo(cells, sides, width):
    for axis, dim in sides:
        count = lax.axis_size(axis)
        ends = count - 1
        head = lax.slice_in_dim(cells, 0, width, axis=dim)
        tail = lax.slice_in_dim(cells, cells.shape[dim] - width, cells.shape[dim], axis=dim)
        cells = jnp.concatenate(
            [
                lax.ppermute(tail, axis, [(i, (i + 1) % count) for i in range(ends)]),
                cells,
                lax.ppermute(head, axis, [((i + 1) % count, i) for i in range(ends)]),
            ],
            axis=dim,
        )
    return cells


def warp_band(extended, shifts, quarters):
    margin = SPAN + 1
    span_rows = extended.shape[0]
    local_rows = span_rows - 2 * margin
    channels = extended.shape[1]
    columns = extended.shape[2]
    wide_cols = columns + 2 * margin
    window_rows = 8 + 2 * margin
    padded = jnp.pad(extended, ((0, 0), (0, 0), (margin, margin)))
    source_cols = jnp.arange(wide_cols, dtype=jnp.int32)[:, None]
    target_cols = jnp.arange(columns, dtype=jnp.int32)[None, :]
    source_rows = jnp.arange(window_rows, dtype=jnp.int32)[None, :, None]
    target_rows = jnp.arange(8, dtype=jnp.int32)[:, None, None]
    outputs = []
    for block_row in range(local_rows // 8):
        shift_rows = jnp.repeat(shifts[0][block_row], 8)
        shift_cols = jnp.repeat(shifts[1][block_row], 8)
        part_rows = jnp.repeat(quarters[0][block_row], 8).astype(jnp.float32) * 0.25
        part_cols = jnp.repeat(quarters[1][block_row], 8).astype(jnp.float32) * 0.25
        col_base = target_cols + shift_cols[None, :] + margin
        col_matrix = (
            jnp.where(source_cols == col_base, 1.0 - part_cols[None, :], 0.0)
            + jnp.where(source_cols == col_base + 1, part_cols[None, :], 0.0)
        ).astype(jnp.bfloat16)
        row_base = target_rows + shift_rows[None, None, :] + margin
        row_tensor = jnp.where(
            source_rows == row_base, 1.0 - part_rows[None, None, :], 0.0
        ) + jnp.where(source_rows == row_base + 1, part_rows[None, None, :], 0.0)
        window = padded[8 * block_row : 8 * block_row + window_rows].reshape(
            window_rows * channels, wide_cols
        )
        column_pass = jnp.dot(window, col_matrix, preferred_element_type=jnp.float32).reshape(
            window_rows, channels, columns
        )
        outputs.append(
            jnp.einsum("iux,ucx->icx", row_tensor, column_pass, precision=lax.Precision.HIGHEST)
        )
    return jnp.concatenate(outputs, axis=0).astype(jnp.bfloat16)


def convolve(pieces, weight):
    count_parts, length, channels, columns = pieces.shape
    outputs = weight.shape[2]
    blocks = weight.reshape(3, 3, outputs, count_parts, channels)
    padded = jnp.pad(pieces, ((0, 0), (0, 0), (0, 0), (1, 1)))
    interior = length - 2
    summed = jnp.zeros((interior, outputs, columns), jnp.float32)
    for tap_row in range(3):
        for tap_col in range(3):
            window = padded[:, tap_row : tap_row + interior, :, tap_col : tap_col + columns]
            summed = summed + jnp.einsum(
                "opc,phcw->how",
                blocks[tap_row, tap_col],
                window,
                preferred_element_type=jnp.float32,
            )
    return summed


def move_earlier_wide(panel_band, ahead_by):
    return passed_along(panel_band, "tm", ahead_by)


def move_later_wide(panel_band, behind):
    return passed_along(panel_band, "tm", behind)


def shards(features, block_shift, quarter_pel, update_mask, uniting_weight, mixing_weight):
    current = features[0]
    frames = lax.axis_size("tm")
    margin = SPAN + 1
    local_rows = current.shape[0]
    for level_index in range(LEVELS - 1, -1, -1):
        distance = 2**level_index
        ahead_by = distance % frames
        behind = (frames - ahead_by) % frames
        own_shift = block_shift[level_index, :, 0]
        own_quarter = quarter_pel[level_index, :, 0]
        extended = with_halo(current, (("rows", 0),), SPAN + 1)
        earlier = move_earlier_wide(extended, ahead_by)
        following = move_later_wide(extended, behind)
        warped = jnp.stack(
            [
                warp_band(earlier, own_shift[0:2], own_quarter[0:2]),
                warp_band(following, own_shift[2:4], own_quarter[2:4]),
            ]
        )
        warped_ext = with_halo(warped, (("rows", 1),), 1)
        own_ext = extended[margin - 1 : margin + local_rows + 1]
        pieces = jnp.concatenate([warped_ext, own_ext[None]], axis=0)
        uniting_sum = convolve(pieces, uniting_weight)
        activation = (uniting_sum * jax.nn.sigmoid(uniting_sum)).astype(jnp.bfloat16)
        activation_ext = with_halo(activation, (("rows", 0),), 1)
        mixing_sum = convolve(activation_ext[None], mixing_weight)
        current = (
            current.astype(jnp.float32)
            + update_mask[level_index, 0].astype(jnp.float32) * mixing_sum
        ).astype(jnp.bfloat16)
    return current[None]


def solution(mesh):
    placed = (
        P("tm", "rows", None, None),
        P(None, None, "tm", "rows", None),
        P(None, None, "tm", "rows", None),
        P(None, "tm"),
        P(),
        P(),
    )
    return jax.shard_map(
        shards, mesh=mesh, in_specs=placed, out_specs=P("tm", "rows", None, None), check_vma=False
    )
```

profile of v0, /device:TPU:7, one launch (start us, length us, event | category | flops | bytes accessed | tf_op | source)
XLA Modules:
  0.0 356.1 jit_solution(7297735439839969080)
XLA Ops:
  1.1 4.6 %collective-permute-start = (bf16[6,64,256]{2,1,0:T(8,128)(2,1)S(1)}, bf16[6,64,256]{2,1,0:T(8,128)(2,1)S(1)}, u32[]{:S(2)}, u32[]{:S(2)}) collective-permute-start(bf16[6,64,256]{2,1,0:T(8,128)(2,1)S(1)} %get-tuple-element.21), channel_id=1, source_target_pairs={{0,1},{1,2},{2,3},{3,4},{4,5},{5,6},{6,7},{7,8},{8,9},{9,10},{10,1... | collective-permute-start | bytes 589832 | tf_op jit(solution)/shard_map/ppermute | solution.py:24
  5.7 1.9 collective-permute-start.1
  41.4 15.5 %collective-permute-done.2 = bf16[28,64,256]{2,1,0:T(8,128)(2,1)S(1)} collective-permute-done((bf16[28,64,256]{2,1,0:T(8,128)(2,1)S(1)}, bf16[28,64,256]{2,1,0:T(8,128)(2,1)S(1)}, u32[]{:S(2)}, u32[]{:S(2)}) %collective-permute-start.2) | collective-permute-done | bytes 917536 | tf_op jit(solution)/shard_map/ppermute | solution.py:13
  58.2 2.3 copy.135
  61.7 2.2 copy.136
  65.3 2.2 copy.134
  68.1 2.3 copy.133
  70.4 5.1 %fusion.146 = bf16[1,8,64,256]{2,1,3,0:T(8,128)(2,1)S(1)} fusion(f32[20,64,256]{1,0,2:T(8,128)} %copy.135, f32[256]{0:T(256)S(1)} %copy-done.93, s32[8,256]{0,1:T(8,128)S(1)} %get-tuple-element.112, f32[256]{0:T(256)S(1)} %copy-done.123, s32[8,256]{0,1:T(8,128)S(1)} %get-tuple-element.111), kind=kOutput, calls=%fused_computation.188 | convolution fusion | flops 31793152 | bytes 1591296 | tf_op jit(solution)/shard_map/iux,ucx->icx/dot_general | solution.py:68
  75.6 3.9 %fusion.147 = bf16[1,8,64,256]{2,1,3,0:T(8,128)(2,1)S(1)} fusion(f32[20,64,256]{1,0,2:T(8,128)S(1)} %copy-done.4, f32[256]{0:T(256)S(1)} %copy-done.95, s32[8,256]{0,1:T(8,128)S(1)} %copy-done.22, f32[256]{0:T(256)S(1)} %copy-done.124, s32[8,256]{0,1:T(8,128)S(1)} %copy-done.21), kind=kOutput, calls=%fused_computation.189 | convolution fusion | flops 31793152 | bytes 1591296 | tf_op jit(solution)/shard_map/iux,ucx->icx/dot_general | solution.py:68
  79.6 3.9 %fusion.145 = bf16[1,8,64,256]{2,1,3,0:T(8,128)(2,1)S(1)} fusion(f32[20,64,256]{1,0,2:T(8,128)S(1)} %copy-done.5, f32[256]{0:T(256)S(1)} %copy-done.97, s32[8,256]{0,1:T(8,128)S(1)} %copy-done.24, f32[256]{0:T(256)S(1)} %copy-done.125, s32[8,256]{0,1:T(8,128)S(1)} %copy-done.23), kind=kOutput, calls=%fused_computation.187 | convolution fusion | flops 31793152 | bytes 1591296 | tf_op jit(solution)/shard_map/iux,ucx->icx/dot_general | solution.py:68
  83.6 3.9 %fusion.144 = bf16[1,8,64,256]{2,1,3,0:T(8,128)(2,1)S(1)} fusion(f32[20,64,256]{1,0,2:T(8,128)S(1)} %copy-done.8, f32[256]{0:T(256)S(1)} %copy-done.99, s32[8,256]{0,1:T(8,128)S(1)} %copy-done.30, f32[256]{0:T(256)S(1)} %copy-done.126, s32[8,256]{0,1:T(8,128)S(1)} %copy-done.29), kind=kOutput, calls=%fused_computation.186 | convolution fusion | flops 31793152 | bytes 1591296 | tf_op jit(solution)/shard_map/iux,ucx->icx/dot_general | solution.py:68
  89.2 5.7 %collective-permute-start.3 = (bf16[2,1,64,256]{2,1,3,0:T(2,128)(2,1)}, bf16[2,1,64,256]{2,1,3,0:T(2,128)(2,1)}, u32[]{:S(2)}, u32[]{:S(2)}) collective-permute-start(bf16[2,1,64,256]{2,1,3,0:T(2,128)(2,1)} %get-tuple-element.9), channel_id=1, source_target_pairs={{0,1},{1,2},{2,3},{3,4},{4,5},{5,6},{6,7},{7,8},{8,9},{9,10},{10,1... | collective-permute-start | bytes 196616 | tf_op jit(solution)/shard_map/ppermute | solution.py:24
  94.9 2.1 collective-permute-start.4
  97.9 1.7 copy.138
  100.7 4.6 %collective-permute-done.4 = bf16[2,1,64,256]{2,1,3,0:T(2,128)(2,1)S(1)} collective-permute-done((bf16[2,1,64,256]{2,1,3,0:T(2,128)(2,1)}, bf16[2,1,64,256]{2,1,3,0:T(2,128)(2,1)S(1)}, u32[]{:S(2)}, u32[]{:S(2)}) %collective-permute-start.4) | collective-permute-done | bytes 65568 | tf_op jit(solution)/shard_map/ppermute | solution.py:26
  112.6 1.9 collective-permute-start.5
  114.5 2.4 collective-permute-start.6
  118.5 3.6 %collective-permute-done.6 = bf16[1,64,256]{2,1,0:T(8,128)(2,1)S(1)} collective-permute-done((bf16[1,64,256]{2,1,0:T(8,128)(2,1)S(1)}, bf16[1,64,256]{2,1,0:T(8,128)(2,1)S(1)}, u32[]{:S(2)}, u32[]{:S(2)}) %collective-permute-start.6) | collective-permute-done | bytes 32800 | tf_op jit(solution)/shard_map/ppermute | solution.py:26
  126.3 2.0 collective-permute-start.7
  128.2 2.4 collective-permute-start.8
  131.2 6.4 %collective-permute-done.8 = bf16[6,64,256]{2,1,0:T(8,128)(2,1)S(1)} collective-permute-done((bf16[6,64,256]{2,1,0:T(8,128)(2,1)S(1)}, bf16[6,64,256]{2,1,0:T(8,128)(2,1)S(1)}, u32[]{:S(2)}, u32[]{:S(2)}) %collective-permute-start.8) | collective-permute-done | bytes 196640 | tf_op jit(solution)/shard_map/ppermute | solution.py:26
  138.7 3.6 %collective-permute-start.9 = (bf16[28,64,256]{2,1,0:T(8,128)(2,1)}, bf16[28,64,256]{2,1,0:T(8,128)(2,1)S(1)}, u32[]{:S(2)}, u32[]{:S(2)}) collective-permute-start(bf16[28,64,256]{2,1,0:T(8,128)(2,1)} %pad_maximum_fusion.4), channel_id=1, source_target_pairs={{96,0},{112,16},{0,32},{16,48},{32,64},{48,80},{64,96},{80,112},{9... | collective-permute-start | bytes 2752520 | tf_op jit(solution)/shard_map/ppermute | solution.py:13
  147.9 31.1 %collective-permute-done.9 = bf16[28,64,256]{2,1,0:T(8,128)(2,1)S(1)} collective-permute-done((bf16[28,64,256]{2,1,0:T(8,128)(2,1)}, bf16[28,64,256]{2,1,0:T(8,128)(2,1)S(1)}, u32[]{:S(2)}, u32[]{:S(2)}) %collective-permute-start.9) | collective-permute-done | bytes 917536 | tf_op jit(solution)/shard_map/ppermute | solution.py:13
  179.7 2.3 copy.154
  182.6 2.3 copy.155
  184.9 1.7 fusion.54
  186.6 2.2 copy.156
  188.9 1.7 fusion.52
  190.6 2.2 copy.157
  192.9 5.1 %fusion.148 = bf16[1,8,64,256]{2,1,3,0:T(8,128)(2,1)S(1)} fusion(f32[20,64,256]{1,0,2:T(8,128)} %copy.154, f32[256]{0:T(256)S(1)} %copy-done.81, s32[8,256]{0,1:T(8,128)S(1)} %copy-done.18, f32[256]{0:T(256)S(1)} %copy-done.117, s32[8,256]{0,1:T(8,128)S(1)} %copy-done.17), kind=kOutput, calls=%fused_computation.190 | convolution fusion | flops 31793152 | bytes 1591296 | tf_op jit(solution)/shard_map/iux,ucx->icx/dot_general | solution.py:68
  198.1 3.9 %fusion.149 = bf16[1,8,64,256]{2,1,3,0:T(8,128)(2,1)S(1)} fusion(f32[20,64,256]{1,0,2:T(8,128)S(1)} %copy-done.2, f32[256]{0:T(256)S(1)} %copy-done.83, s32[8,256]{0,1:T(8,128)S(1)} %copy-done.16, f32[256]{0:T(256)S(1)} %copy-done.118, s32[8,256]{0,1:T(8,128)S(1)} %get-tuple-element.91), kind=kOutput, calls=%fused_computation.191 | convolution fusion | flops 31793152 | bytes 1591296 | tf_op jit(solution)/shard_map/iux,ucx->icx/dot_general | solution.py:68
  202.1 3.9 %fusion.150 = bf16[1,8,64,256]{2,1,3,0:T(8,128)(2,1)S(1)} fusion(f32[20,64,256]{1,0,2:T(8,128)S(1)} %copy-done.6, f32[256]{0:T(256)S(1)} %copy-done.85, s32[8,256]{0,1:T(8,128)S(1)} %copy-done.28, f32[256]{0:T(256)S(1)} %copy-done.119, s32[8,256]{0,1:T(8,128)S(1)} %copy-done.27), kind=kOutput, calls=%fused_computation.192 | convolution fusion | flops 31793152 | bytes 1591296 | tf_op jit(solution)/shard_map/iux,ucx->icx/dot_general | solution.py:68
  206.1 3.9 %fusion.151 = bf16[1,8,64,256]{2,1,3,0:T(8,128)(2,1)S(1)} fusion(f32[20,64,256]{1,0,2:T(8,128)S(1)} %copy-done.9, f32[256]{0:T(256)S(1)} %copy-done.89, s32[8,256]{0,1:T(8,128)S(1)} %copy-done.26, f32[256]{0:T(256)S(1)} %copy-done.120, s32[8,256]{0,1:T(8,128)S(1)} %copy-done.25), kind=kOutput, calls=%fused_computation.193 | convolution fusion | flops 31793152 | bytes 1591296 | tf_op jit(solution)/shard_map/iux,ucx->icx/dot_general | solution.py:68
  211.7 5.7 %collective-permute-start.11 = (bf16[2,1,64,256]{2,1,3,0:T(2,128)(2,1)}, bf16[2,1,64,256]{2,1,3,0:T(2,128)(2,1)}, u32[]{:S(2)}, u32[]{:S(2)}) collective-permute-start(bf16[2,1,64,256]{2,1,3,0:T(2,128)(2,1)} %get-tuple-element.7), channel_id=1, source_target_pairs={{0,1},{1,2},{2,3},{3,4},{4,5},{5,6},{6,7},{7,8},{8,9},{9,10},{10,1... | collective-permute-start | bytes 196616 | tf_op jit(solution)/shard_map/ppermute | solution.py:24
  217.5 2.1 collective-permute-start.12
  220.7 2.5 copy.159
  224.3 3.6 %collective-permute-done.12 = bf16[2,1,64,256]{2,1,3,0:T(2,128)(2,1)} collective-permute-done((bf16[2,1,64,256]{2,1,3,0:T(2,128)(2,1)}, bf16[2,1,64,256]{2,1,3,0:T(2,128)(2,1)}, u32[]{:S(2)}, u32[]{:S(2)}) %collective-permute-start.12) | collective-permute-done | bytes 65568 | tf_op jit(solution)/shard_map/ppermute | solution.py:26
  236.3 2.6 collective-permute-start.13
  239.0 1.9 collective-permute-start.14
  242.4 4.2 %collective-permute-done.14 = bf16[1,64,256]{2,1,0:T(8,128)(2,1)S(1)} collective-permute-done((bf16[1,64,256]{2,1,0:T(8,128)(2,1)S(1)}, bf16[1,64,256]{2,1,0:T(8,128)(2,1)S(1)}, u32[]{:S(2)}, u32[]{:S(2)}) %collective-permute-start.14) | collective-permute-done | bytes 32800 | tf_op jit(solution)/shard_map/ppermute | solution.py:26
  250.0 1.9 collective-permute-start.15
  251.9 2.4 collective-permute-start.16
  254.9 6.4 %collective-permute-done.16 = bf16[6,64,256]{2,1,0:T(8,128)(2,1)S(1)} collective-permute-done((bf16[6,64,256]{2,1,0:T(8,128)(2,1)S(1)}, bf16[6,64,256]{2,1,0:T(8,128)(2,1)S(1)}, u32[]{:S(2)}, u32[]{:S(2)}) %collective-permute-start.16) | collective-permute-done | bytes 196640 | tf_op jit(solution)/shard_map/ppermute | solution.py:26
  264.7 3.3 collective-permute-start.18
  269.4 14.0 %collective-permute-done.17 = bf16[28,64,256]{2,1,0:T(8,128)(2,1)S(1)} collective-permute-done((bf16[28,64,256]{2,1,0:T(8,128)(2,1)}, bf16[28,64,256]{2,1,0:T(8,128)(2,1)S(1)}, u32[]{:S(2)}, u32[]{:S(2)}) %collective-permute-start.17) | collective-permute-done | bytes 917536 | tf_op jit(solution)/shard_map/ppermute | solution.py:13
  284.0 2.3 copy.165
  287.0 2.2 copy.166
  289.2 1.6 fusion.46
  290.9 2.3 copy.167
  293.2 1.7 fusion.44
  294.9 2.2 copy.168
  297.2 5.1 %fusion.152 = bf16[1,8,64,256]{2,1,3,0:T(8,128)(2,1)S(1)} fusion(f32[20,64,256]{1,0,2:T(8,128)} %copy.165, f32[256]{0:T(256)S(1)} %copy-done.87, s32[8,256]{0,1:T(8,128)S(1)} %copy-done.20, f32[256]{0:T(256)S(1)} %copy-done.121, s32[8,256]{0,1:T(8,128)S(1)} %copy-done.19), kind=kOutput, calls=%fused_computation.194 | convolution fusion | flops 31793152 | bytes 1591296 | tf_op jit(solution)/shard_map/iux,ucx->icx/dot_general | solution.py:68
  302.4 3.9 %fusion.153 = bf16[1,8,64,256]{2,1,3,0:T(8,128)(2,1)S(1)} fusion(f32[20,64,256]{1,0,2:T(8,128)S(1)} %copy-done.3, f32[256]{0:T(256)S(1)} %copy-done.91, s32[8,256]{0,1:T(8,128)S(1)} %copy-done.33, f32[256]{0:T(256)S(1)} %copy-done.122, s32[8,256]{0,1:T(8,128)S(1)} %copy-done.32), kind=kOutput, calls=%fused_computation.195 | convolution fusion | flops 31793152 | bytes 1591296 | tf_op jit(solution)/shard_map/iux,ucx->icx/dot_general | solution.py:68
  306.4 3.9 %fusion.154 = bf16[1,8,64,256]{2,1,3,0:T(8,128)(2,1)S(1)} fusion(f32[20,64,256]{1,0,2:T(8,128)S(1)} %copy-done.7, f32[256]{0:T(256)S(1)} %copy-done.101, s32[8,256]{0,1:T(8,128)S(1)} %get-tuple-element.80, f32[256]{0:T(256)S(1)} %copy-done.127, s32[8,256]{0,1:T(8,128)S(1)} %get-tuple-element.79), kind=kOutput, calls=%fused_computation.196 | convolution fusion | flops 31793152 | bytes 1591296 | tf_op jit(solution)/shard_map/iux,ucx->icx/dot_general | solution.py:68
  310.4 3.9 %fusion.155 = bf16[1,8,64,256]{2,1,3,0:T(8,128)(2,1)S(1)} fusion(f32[20,64,256]{1,0,2:T(8,128)S(1)} %copy-done.10, f32[256]{0:T(256)S(1)} %copy-done.103, s32[8,256]{0,1:T(8,128)S(1)} %copy-done.31, f32[256]{0:T(256)S(1)} %copy-done.128, s32[8,256]{0,1:T(8,128)S(1)} %get-tuple-element.83), kind=kOutput, calls=%fused_computation.197 | convolution fusion | flops 31793152 | bytes 1591296 | tf_op jit(solution)/shard_map/iux,ucx->icx/dot_general | solution.py:68
  316.0 6.8 %collective-permute-start.19 = (bf16[2,1,64,256]{2,1,3,0:T(2,128)(2,1)}, bf16[2,1,64,256]{2,1,3,0:T(2,128)(2,1)}, u32[]{:S(2)}, u32[]{:S(2)}) collective-permute-start(bf16[2,1,64,256]{2,1,3,0:T(2,128)(2,1)} %get-tuple-element.5), channel_id=1, source_target_pairs={{0,1},{1,2},{2,3},{3,4},{4,5},{5,6},{6,7},{7,8},{8,9},{9,10},{10,1... | collective-permute-start | bytes 196616 | tf_op jit(solution)/shard_map/ppermute | solution.py:24
  322.8 2.2 collective-permute-start.20
  325.0 1.9 slice_bitcast_fusion
  326.9 2.5 copy.170
  330.5 2.6 collective-permute-done.20
  333.2 1.7 pad_maximum_fusion.2
  340.8 3.4 collective-permute-start.21
  344.2 1.9 collective-permute-start.22
  346.7 5.1 %collective-permute-done.22 = bf16[1,64,256]{2,1,0:T(8,128)(2,1)S(1)} collective-permute-done((bf16[1,64,256]{2,1,0:T(8,128)(2,1)S(1)}, bf16[1,64,256]{2,1,0:T(8,128)(2,1)S(1)}, u32[]{:S(2)}, u32[]{:S(2)}) %collective-permute-start.22) | collective-permute-done | bytes 32800 | tf_op jit(solution)/shard_map/ppermute | solution.py:26
  (513 shorter events, 98.7 us)
Async XLA Ops:
  0.0 35.8 %copy-start = (bf16[1,16,64,256]{3,2,1,0:T(8,128)(2,1)S(1)}, bf16[1,16,64,256]{3,2,1,0:T(8,128)(2,1)}, u32[]{:S(2)}) copy-start(bf16[1,16,64,256]{3,2,1,0:T(8,128)(2,1)} %param.6) | copy-start | bytes 1572868
  1.1 34.7 %collective-permute-start = (bf16[6,64,256]{2,1,0:T(8,128)(2,1)S(1)}, bf16[6,64,256]{2,1,0:T(8,128)(2,1)S(1)}, u32[]{:S(2)}, u32[]{:S(2)}) collective-permute-start(bf16[6,64,256]{2,1,0:T(8,128)(2,1)S(1)} %get-tuple-element.21), channel_id=1, source_target_pairs={{0,1},{1,2},{2,3},{3,4},{4,5},{5,6},{6,7},{7,8},{8,9},{9,10},{10,1... | collective-permute-start | bytes 589832 | tf_op jit(solution)/shard_map/ppermute | solution.py:24
  5.7 30.1 %collective-permute-start.1 = (bf16[6,64,256]{2,1,0:T(8,128)(2,1)S(1)}, bf16[6,64,256]{2,1,0:T(8,128)(2,1)S(1)}, u32[]{:S(2)}, u32[]{:S(2)}) collective-permute-start(bf16[6,64,256]{2,1,0:T(8,128)(2,1)S(1)} %get-tuple-element.22), channel_id=1, source_target_pairs={{1,0},{2,1},{3,2},{4,3},{5,4},{6,5},{7,6},{8,7},{9,8},{10,9},{11,1... | collective-permute-start | bytes 589832 | tf_op jit(solution)/shard_map/ppermute | solution.py:26
  15.0 22.0 %copy-start.15 = (bf16[3,3,64,192]{3,2,1,0:T(8,128)(2,1)S(1)}, bf16[3,3,64,192]{3,2,1,0:T(8,128)(2,1)}, u32[]{:S(2)}) copy-start(bf16[3,3,64,192]{3,2,1,0:T(8,128)(2,1)} %param.10) | copy-start | bytes 663556
  25.4 8.2 %copy-start.36 = (f32[256]{0:T(256)}, f32[256]{0:T(256)S(1)}, u32[]{:S(2)}) copy-start(f32[256]{0:T(256)S(1)} %mul.465) | copy-start | bytes 3076
  27.6 13.1 %copy-start.38 = (f32[256]{0:T(256)}, f32[256]{0:T(256)S(1)}, u32[]{:S(2)}) copy-start(f32[256]{0:T(256)S(1)} %mul.471) | copy-start | bytes 3076
  29.8 10.8 %copy-start.40 = (f32[256]{0:T(256)}, f32[256]{0:T(256)S(1)}, u32[]{:S(2)}) copy-start(f32[256]{0:T(256)S(1)} %mul.477) | copy-start | bytes 3076
  32.1 9.3 %copy-start.42 = (f32[256]{0:T(256)}, f32[256]{0:T(256)S(1)}, u32[]{:S(2)}) copy-start(f32[256]{0:T(256)S(1)} %mul.483) | copy-start | bytes 3076
  32.8 8.6 %copy-start.88 = (f32[256]{0:T(256)}, f32[256]{0:T(256)S(1)}, u32[]{:S(2)}) copy-start(f32[256]{0:T(256)S(1)} %mul.486) | copy-start | bytes 3076
  33.7 7.7 %copy-start.34 = (f32[256]{0:T(256)}, f32[256]{0:T(256)S(1)}, u32[]{:S(2)}) copy-start(f32[256]{0:T(256)S(1)} %mul.492) | copy-start | bytes 3076
  36.0 20.9 %collective-permute-start.2 = (bf16[28,64,256]{2,1,0:T(8,128)(2,1)S(1)}, bf16[28,64,256]{2,1,0:T(8,128)(2,1)S(1)}, u32[]{:S(2)}, u32[]{:S(2)}) collective-permute-start(bf16[28,64,256]{2,1,0:T(8,128)(2,1)S(1)} %pad_maximum_fusion.3), channel_id=1, source_target_pairs={{64,0},{80,16},{96,32},{112,48},{0,64},{16,80},{32,96},{48,112},{6... | collective-permute-start | bytes 2752520 | tf_op jit(solution)/shard_map/ppermute | solution.py:13
  70.4 5.1 %copy-start.22 = (s32[8,256]{0,1:T(8,128)S(1)}, s32[8,256]{0,1:T(8,128)}, u32[]{:S(2)}) copy-start(s32[8,256]{0,1:T(8,128)} %get-tuple-element.116) | copy-start | bytes 24580
  70.4 5.1 %copy-start.95 = (f32[256]{0:T(256)S(1)}, f32[256]{0:T(256)}, u32[]{:S(2)}) copy-start(f32[256]{0:T(256)} %copy-done.94) | copy-start | bytes 3076
  70.4 5.1 %copy-start.124 = (f32[256]{0:T(256)S(1)}, f32[256]{0:T(256)}, u32[]{:S(2)}) copy-start(f32[256]{0:T(256)} %broadcast_subtract_fusion.16) | copy-start | bytes 3076
  89.2 10.4 %collective-permute-start.3 = (bf16[2,1,64,256]{2,1,3,0:T(2,128)(2,1)}, bf16[2,1,64,256]{2,1,3,0:T(2,128)(2,1)}, u32[]{:S(2)}, u32[]{:S(2)}) collective-permute-start(bf16[2,1,64,256]{2,1,3,0:T(2,128)(2,1)} %get-tuple-element.9), channel_id=1, source_target_pairs={{0,1},{1,2},{2,3},{3,4},{4,5},{5,6},{6,7},{7,8},{8,9},{9,10},{10,1... | collective-permute-start | bytes 196616 | tf_op jit(solution)/shard_map/ppermute | solution.py:24
  94.9 10.3 %collective-permute-start.4 = (bf16[2,1,64,256]{2,1,3,0:T(2,128)(2,1)}, bf16[2,1,64,256]{2,1,3,0:T(2,128)(2,1)S(1)}, u32[]{:S(2)}, u32[]{:S(2)}) collective-permute-start(bf16[2,1,64,256]{2,1,3,0:T(2,128)(2,1)} %get-tuple-element.10), channel_id=1, source_target_pairs={{1,0},{2,1},{3,2},{4,3},{5,4},{6,5},{7,6},{8,7},{9,8},{10,9},{11,1... | collective-permute-start | bytes 196616 | tf_op jit(solution)/shard_map/ppermute | solution.py:26
  111.4 5.5 %copy-start.50 = (s32[3,1]{0,1:T(1,128)S(1)}, s32[3,1]{0,1:T(1,128)}, u32[]{:S(2)}) copy-start(s32[3,1]{0,1:T(1,128)} %param.9) | copy-start | bytes 40
  111.4 6.8 %copy-start.116 = (f32[32]{0:T(128)S(1)}, f32[32]{0:T(128)}, u32[]{:S(2)}) copy-start(f32[32]{0:T(128)} %get-tuple-element.42) | copy-start | bytes 388
  111.4 6.9 %copy-start.115 = (f32[32]{0:T(128)S(1)}, f32[32]{0:T(128)}, u32[]{:S(2)}) copy-start(f32[32]{0:T(128)} %get-tuple-element.46) | copy-start | bytes 388
  111.4 10.8 %copy-start.14 = (bf16[3,3,64,64]{3,2,1,0:T(8,128)(2,1)S(1)}, bf16[3,3,64,64]{3,2,1,0:T(8,128)(2,1)}, u32[]{:S(2)}) copy-start(bf16[3,3,64,64]{3,2,1,0:T(8,128)(2,1)} %param.11) | copy-start | bytes 221188
  112.6 5.9 %collective-permute-start.5 = (bf16[1,64,256]{2,1,0:T(8,128)(2,1)S(1)}, bf16[1,64,256]{2,1,0:T(8,128)(2,1)S(1)}, u32[]{:S(2)}, u32[]{:S(2)}) collective-permute-start(bf16[1,64,256]{2,1,0:T(8,128)(2,1)S(1)} %get-tuple-element.19), channel_id=1, source_target_pairs={{0,1},{1,2},{2,3},{3,4},{4,5},{5,6},{6,7},{7,8},{8,9},{9,10},{10,1... | collective-permute-start | bytes 98312 | tf_op jit(solution)/shard_map/ppermute | solution.py:24
  114.5 7.6 %collective-permute-start.6 = (bf16[1,64,256]{2,1,0:T(8,128)(2,1)S(1)}, bf16[1,64,256]{2,1,0:T(8,128)(2,1)S(1)}, u32[]{:S(2)}, u32[]{:S(2)}) collective-permute-start(bf16[1,64,256]{2,1,0:T(8,128)(2,1)S(1)} %get-tuple-element.20), channel_id=1, source_target_pairs={{1,0},{2,1},{3,2},{4,3},{5,4},{6,5},{7,6},{8,7},{9,8},{10,9},{11,1... | collective-permute-start | bytes 98312 | tf_op jit(solution)/shard_map/ppermute | solution.py:26
  118.3 12.3 %copy-start.86 = (f32[256]{0:T(256)}, f32[256]{0:T(256)S(1)}, u32[]{:S(2)}) copy-start(f32[256]{0:T(256)S(1)} %mul.495) | copy-start | bytes 3076
  118.5 23.8 %copy-start.44 = (f32[256]{0:T(256)}, f32[256]{0:T(256)S(1)}, u32[]{:S(2)}) copy-start(f32[256]{0:T(256)S(1)} %mul.498) | copy-start | bytes 3076
  126.2 16.7 %copy-start.112 = (s32[32]{0:T(128)S(1)}, s32[32]{0:T(128)}, u32[]{:S(2)}) copy-start(s32[32]{0:T(128)} %get-tuple-element.31) | copy-start | bytes 388
  126.2 16.9 %copy-start.111 = (s32[32]{0:T(128)S(1)}, s32[32]{0:T(128)}, u32[]{:S(2)}) copy-start(s32[32]{0:T(128)} %get-tuple-element.29) | copy-start | bytes 388
  126.2 17.0 %copy-start.110 = (s32[32]{0:T(128)S(1)}, s32[32]{0:T(128)}, u32[]{:S(2)}) copy-start(s32[32]{0:T(128)} %get-tuple-element.23) | copy-start | bytes 388
  126.2 17.2 %copy-start.114 = (f32[32]{0:T(128)S(1)}, f32[32]{0:T(128)}, u32[]{:S(2)}) copy-start(f32[32]{0:T(128)} %get-tuple-element.45) | copy-start | bytes 388
  126.2 17.4 %copy-start.113 = (f32[32]{0:T(128)S(1)}, f32[32]{0:T(128)}, u32[]{:S(2)}) copy-start(f32[32]{0:T(128)} %get-tuple-element.44) | copy-start | bytes 388
  126.2 52.8 %copy-start.37 = (f32[256]{0:T(256)S(1)}, f32[256]{0:T(256)}, u32[]{:S(2)}) copy-start(f32[256]{0:T(256)} %copy-done.36) | copy-start | bytes 3076
  126.2 52.8 %copy-start.59 = (s32[256]{0:T(256)S(1)}, s32[256]{0:T(256)}, u32[]{:S(2)}) copy-start(s32[256]{0:T(256)} %get-tuple-element.89) | copy-start | bytes 3076
  126.2 52.8 %copy-start.60 = (s32[256]{0:T(256)S(1)}, s32[256]{0:T(256)}, u32[]{:S(2)}) copy-start(s32[256]{0:T(256)} %get-tuple-element.90) | copy-start | bytes 3076
  126.2 52.8 %copy-start.73 = (f32[256]{0:T(256)S(1)}, f32[256]{0:T(256)}, u32[]{:S(2)}) copy-start(f32[256]{0:T(256)} %broadcast_subtract_fusion.15) | copy-start | bytes 3076
  126.3 4.9 %collective-permute-start.7 = (bf16[6,64,256]{2,1,0:T(8,128)(2,1)S(1)}, bf16[6,64,256]{2,1,0:T(8,128)(2,1)S(1)}, u32[]{:S(2)}, u32[]{:S(2)}) collective-permute-start(bf16[6,64,256]{2,1,0:T(8,128)(2,1)S(1)} %get-tuple-element.17), channel_id=1, source_target_pairs={{0,1},{1,2},{2,3},{3,4},{4,5},{5,6},{6,7},{7,8},{8,9},{9,10},{10,1... | collective-permute-start | bytes 589832 | tf_op jit(solution)/shard_map/ppermute | solution.py:24
  128.2 9.4 %collective-permute-start.8 = (bf16[6,64,256]{2,1,0:T(8,128)(2,1)S(1)}, bf16[6,64,256]{2,1,0:T(8,128)(2,1)S(1)}, u32[]{:S(2)}, u32[]{:S(2)}) collective-permute-start(bf16[6,64,256]{2,1,0:T(8,128)(2,1)S(1)} %get-tuple-element.18), channel_id=1, source_target_pairs={{1,0},{2,1},{3,2},{4,3},{5,4},{6,5},{7,6},{8,7},{9,8},{10,9},{11,1... | collective-permute-start | bytes 589832 | tf_op jit(solution)/shard_map/ppermute | solution.py:26
  138.7 40.3 %collective-permute-start.9 = (bf16[28,64,256]{2,1,0:T(8,128)(2,1)}, bf16[28,64,256]{2,1,0:T(8,128)(2,1)S(1)}, u32[]{:S(2)}, u32[]{:S(2)}) collective-permute-start(bf16[28,64,256]{2,1,0:T(8,128)(2,1)} %pad_maximum_fusion.4), channel_id=1, source_target_pairs={{96,0},{112,16},{0,32},{16,48},{32,64},{48,80},{64,96},{80,112},{9... | collective-permute-start | bytes 2752520 | tf_op jit(solution)/shard_map/ppermute | solution.py:13
  143.5 38.4 %copy-start.90 = (f32[256]{0:T(256)}, f32[256]{0:T(256)S(1)}, u32[]{:S(2)}) copy-start(f32[256]{0:T(256)S(1)} %mul.501) | copy-start | bytes 3076
  145.9 39.0 %collective-permute-start.10 = (bf16[28,64,256]{2,1,0:T(8,128)(2,1)}, bf16[28,64,256]{2,1,0:T(8,128)(2,1)}, u32[]{:S(2)}, u32[]{:S(2)}) collective-permute-start(bf16[28,64,256]{2,1,0:T(8,128)(2,1)} %pad_maximum_fusion.4), channel_id=1, source_target_pairs={{32,0},{48,16},{64,32},{80,48},{96,64},{112,80},{0,96},{16,112},{3... | collective-permute-start | bytes 2752520 | tf_op jit(solution)/shard_map/ppermute | solution.py:13
  211.7 11.5 %collective-permute-start.11 = (bf16[2,1,64,256]{2,1,3,0:T(2,128)(2,1)}, bf16[2,1,64,256]{2,1,3,0:T(2,128)(2,1)}, u32[]{:S(2)}, u32[]{:S(2)}) collective-permute-start(bf16[2,1,64,256]{2,1,3,0:T(2,128)(2,1)} %get-tuple-element.7), channel_id=1, source_target_pairs={{0,1},{1,2},{2,3},{3,4},{4,5},{5,6},{6,7},{7,8},{8,9},{9,10},{10,1... | collective-permute-start | bytes 196616 | tf_op jit(solution)/shard_map/ppermute | solution.py:24
  217.5 10.4 %collective-permute-start.12 = (bf16[2,1,64,256]{2,1,3,0:T(2,128)(2,1)}, bf16[2,1,64,256]{2,1,3,0:T(2,128)(2,1)}, u32[]{:S(2)}, u32[]{:S(2)}) collective-permute-start(bf16[2,1,64,256]{2,1,3,0:T(2,128)(2,1)} %get-tuple-element.8), channel_id=1, source_target_pairs={{1,0},{2,1},{3,2},{4,3},{5,4},{6,5},{7,6},{8,7},{9,8},{10,9},{11,1... | collective-permute-start | bytes 196616 | tf_op jit(solution)/shard_map/ppermute | solution.py:26
  235.1 5.8 %copy-start.46 = (f32[256]{0:T(256)S(1)}, f32[256]{0:T(256)}, u32[]{:S(2)}) copy-start(f32[256]{0:T(256)} %mul.504) | copy-start | bytes 3076
  235.2 6.9 %copy-start.108 = (f32[32]{0:T(128)S(1)}, f32[32]{0:T(128)}, u32[]{:S(2)}) copy-start(f32[32]{0:T(128)} %get-tuple-element.43) | copy-start | bytes 388
  235.2 7.1 %copy-start.109 = (f32[32]{0:T(128)S(1)}, f32[32]{0:T(128)}, u32[]{:S(2)}) copy-start(f32[32]{0:T(128)} %get-tuple-element.70) | copy-start | bytes 388
  236.3 6.1 %collective-permute-start.13 = (bf16[1,64,256]{2,1,0:T(8,128)(2,1)S(1)}, bf16[1,64,256]{2,1,0:T(8,128)(2,1)S(1)}, u32[]{:S(2)}, u32[]{:S(2)}) collective-permute-start(bf16[1,64,256]{2,1,0:T(8,128)(2,1)S(1)} %get-tuple-element.15), channel_id=1, source_target_pairs={{0,1},{1,2},{2,3},{3,4},{4,5},{5,6},{6,7},{7,8},{8,9},{9,10},{10,1... | collective-permute-start | bytes 98312 | tf_op jit(solution)/shard_map/ppermute | solution.py:24
  239.0 7.6 %collective-permute-start.14 = (bf16[1,64,256]{2,1,0:T(8,128)(2,1)S(1)}, bf16[1,64,256]{2,1,0:T(8,128)(2,1)S(1)}, u32[]{:S(2)}, u32[]{:S(2)}) collective-permute-start(bf16[1,64,256]{2,1,0:T(8,128)(2,1)S(1)} %get-tuple-element.16), channel_id=1, source_target_pairs={{1,0},{2,1},{3,2},{4,3},{5,4},{6,5},{7,6},{8,7},{9,8},{10,9},{11,1... | collective-permute-start | bytes 98312 | tf_op jit(solution)/shard_map/ppermute | solution.py:26
  242.2 12.1 %copy-start.100 = (f32[256]{0:T(256)}, f32[256]{0:T(256)S(1)}, u32[]{:S(2)}) copy-start(f32[256]{0:T(256)S(1)} %mul.507) | copy-start | bytes 3076
  242.4 20.7 %copy-start.48 = (f32[256]{0:T(256)}, f32[256]{0:T(256)S(1)}, u32[]{:S(2)}) copy-start(f32[256]{0:T(256)S(1)} %mul.510) | copy-start | bytes 3076
  249.8 13.2 %copy-start.106 = (s32[32]{0:T(128)S(1)}, s32[32]{0:T(128)}, u32[]{:S(2)}) copy-start(s32[32]{0:T(128)} %get-tuple-element.26) | copy-start | bytes 388
  249.9 13.4 %copy-start.104 = (s32[32]{0:T(128)S(1)}, s32[32]{0:T(128)}, u32[]{:S(2)}) copy-start(s32[32]{0:T(128)} %get-tuple-element.24) | copy-start | bytes 388
  249.9 13.6 %copy-start.105 = (s32[32]{0:T(128)S(1)}, s32[32]{0:T(128)}, u32[]{:S(2)}) copy-start(s32[32]{0:T(128)} %get-tuple-element.61) | copy-start | bytes 388
  249.9 13.7 %copy-start.107 = (f32[32]{0:T(128)S(1)}, f32[32]{0:T(128)}, u32[]{:S(2)}) copy-start(f32[32]{0:T(128)} %get-tuple-element.66) | copy-start | bytes 388
  249.9 33.5 %copy-start.35 = (f32[256]{0:T(256)S(1)}, f32[256]{0:T(256)}, u32[]{:S(2)}) copy-start(f32[256]{0:T(256)} %copy-done.34) | copy-start | bytes 3076
  249.9 33.5 %copy-start.51 = (s32[256]{0:T(256)S(1)}, s32[256]{0:T(256)}, u32[]{:S(2)}) copy-start(s32[256]{0:T(256)} %get-tuple-element.73) | copy-start | bytes 3076
  249.9 33.5 %copy-start.52 = (s32[256]{0:T(256)S(1)}, s32[256]{0:T(256)}, u32[]{:S(2)}) copy-start(s32[256]{0:T(256)} %get-tuple-element.74) | copy-start | bytes 3076
  249.9 33.5 %copy-start.72 = (f32[256]{0:T(256)S(1)}, f32[256]{0:T(256)}, u32[]{:S(2)}) copy-start(f32[256]{0:T(256)} %broadcast_subtract_fusion.7) | copy-start | bytes 3076
  250.0 4.9 %collective-permute-start.15 = (bf16[6,64,256]{2,1,0:T(8,128)(2,1)S(1)}, bf16[6,64,256]{2,1,0:T(8,128)(2,1)S(1)}, u32[]{:S(2)}, u32[]{:S(2)}) collective-permute-start(bf16[6,64,256]{2,1,0:T(8,128)(2,1)S(1)} %get-tuple-element.13), channel_id=1, source_target_pairs={{0,1},{1,2},{2,3},{3,4},{4,5},{5,6},{6,7},{7,8},{8,9},{9,10},{10,1... | collective-permute-start | bytes 589832 | tf_op jit(solution)/shard_map/ppermute | solution.py:24
  251.9 9.4 %collective-permute-start.16 = (bf16[6,64,256]{2,1,0:T(8,128)(2,1)S(1)}, bf16[6,64,256]{2,1,0:T(8,128)(2,1)S(1)}, u32[]{:S(2)}, u32[]{:S(2)}) collective-permute-start(bf16[6,64,256]{2,1,0:T(8,128)(2,1)S(1)} %get-tuple-element.14), channel_id=1, source_target_pairs={{1,0},{2,1},{3,2},{4,3},{5,4},{6,5},{7,6},{8,7},{9,8},{10,9},{11,1... | collective-permute-start | bytes 589832 | tf_op jit(solution)/shard_map/ppermute | solution.py:26
  262.3 21.1 %collective-permute-start.17 = (bf16[28,64,256]{2,1,0:T(8,128)(2,1)}, bf16[28,64,256]{2,1,0:T(8,128)(2,1)S(1)}, u32[]{:S(2)}, u32[]{:S(2)}) collective-permute-start(bf16[28,64,256]{2,1,0:T(8,128)(2,1)} %pad_maximum_fusion.5), channel_id=1, source_target_pairs={{112,0},{0,16},{16,32},{32,48},{48,64},{64,80},{80,96},{96,112},{1... | collective-permute-start | bytes 2752520 | tf_op jit(solution)/shard_map/ppermute | solution.py:13
  263.8 22.5 %copy-start.102 = (f32[256]{0:T(256)}, f32[256]{0:T(256)S(1)}, u32[]{:S(2)}) copy-start(f32[256]{0:T(256)S(1)} %mul.513) | copy-start | bytes 3076
  264.7 24.5 %collective-permute-start.18 = (bf16[28,64,256]{2,1,0:T(8,128)(2,1)}, bf16[28,64,256]{2,1,0:T(8,128)(2,1)}, u32[]{:S(2)}, u32[]{:S(2)}) collective-permute-start(bf16[28,64,256]{2,1,0:T(8,128)(2,1)} %pad_maximum_fusion.5), channel_id=1, source_target_pairs={{16,0},{32,16},{48,32},{64,48},{80,64},{96,80},{112,96},{0,112},{1... | collective-permute-start | bytes 2752520 | tf_op jit(solution)/shard_map/ppermute | solution.py:13
  316.0 13.4 %collective-permute-start.19 = (bf16[2,1,64,256]{2,1,3,0:T(2,128)(2,1)}, bf16[2,1,64,256]{2,1,3,0:T(2,128)(2,1)}, u32[]{:S(2)}, u32[]{:S(2)}) collective-permute-start(bf16[2,1,64,256]{2,1,3,0:T(2,128)(2,1)} %get-tuple-element.5), channel_id=1, source_target_pairs={{0,1},{1,2},{2,3},{3,4},{4,5},{5,6},{6,7},{7,8},{8,9},{9,10},{10,1... | collective-permute-start | bytes 196616 | tf_op jit(solution)/shard_map/ppermute | solution.py:24
  322.8 10.3 %collective-permute-start.20 = (bf16[2,1,64,256]{2,1,3,0:T(2,128)(2,1)}, bf16[2,1,64,256]{2,1,3,0:T(2,128)(2,1)S(1)}, u32[]{:S(2)}, u32[]{:S(2)}) collective-permute-start(bf16[2,1,64,256]{2,1,3,0:T(2,128)(2,1)} %get-tuple-element.6), channel_id=1, source_target_pairs={{1,0},{2,1},{3,2},{4,3},{5,4},{6,5},{7,6},{8,7},{9,8},{10,9},{11,1... | collective-permute-start | bytes 196616 | tf_op jit(solution)/shard_map/ppermute | solution.py:26
  340.8 6.0 %collective-permute-start.21 = (bf16[1,64,256]{2,1,0:T(8,128)(2,1)S(1)}, bf16[1,64,256]{2,1,0:T(8,128)(2,1)S(1)}, u32[]{:S(2)}, u32[]{:S(2)}) collective-permute-start(bf16[1,64,256]{2,1,0:T(8,128)(2,1)S(1)} %get-tuple-element.11), channel_id=1, source_target_pairs={{0,1},{1,2},{2,3},{3,4},{4,5},{5,6},{6,7},{7,8},{8,9},{9,10},{10,1... | collective-permute-start | bytes 98312 | tf_op jit(solution)/shard_map/ppermute | solution.py:24
  344.2 7.6 %collective-permute-start.22 = (bf16[1,64,256]{2,1,0:T(8,128)(2,1)S(1)}, bf16[1,64,256]{2,1,0:T(8,128)(2,1)S(1)}, u32[]{:S(2)}, u32[]{:S(2)}) collective-permute-start(bf16[1,64,256]{2,1,0:T(8,128)(2,1)S(1)} %get-tuple-element.12), channel_id=1, source_target_pairs={{1,0},{2,1},{3,2},{4,3},{5,4},{6,5},{7,6},{8,7},{9,8},{10,9},{11,1... | collective-permute-start | bytes 98312 | tf_op jit(solution)/shard_map/ppermute | solution.py:26
  (88 other events, 263.4 us)
where the time goes:
time: 360 us; the launch traced here: 356 us
  waiting for transfers between devices  97.1 us (27%)
  matrix products  91.2 us (25%)
  starting transfers between devices  62.6 us (17%)
  local copies, waits for them, and re-layouts  60.9 us (17%)
  other arithmetic  39.6 us (11%)
  between operations  4.68 us (1%)
    ppermute x5, waiting for transfers between devices, passed_along(): return lax.ppermute(block, axis, route)  60.6 us
    dot_general x12, matrix products, warp_band(): jnp.einsum('iux,ucx->icx', row_tensor, column_pass, precision=lax.Precisi...  50.6 us
    ppermute x9, waiting for transfers between devices, with_halo(): lax.ppermute(head, axis, [((i + 1) % count, i) for i in range(ends)])  36.5 us
    ppermute x9, starting transfers between devices, with_halo(): lax.ppermute(tail, axis, [(i, (i + 1) % count) for i in range(ends)])  34.7 us
    dot_general x54, matrix products, convolve(): jnp.einsum('opc,phcw->how', blocks[tap_row, tap_col], window, preferred_e...  27.4 us
    dot_general x12, local copies, waits for them, and re-layouts, warp_band(): jnp.dot(window, col_matrix, preferred_element_type=jnp.float32)  27.2 us
    ppermute x9, starting transfers between devices, with_halo(): lax.ppermute(head, axis, [((i + 1) % count, i) for i in range(ends)])  19.3 us
    dot_general x12, matrix products, warp_band(): jnp.dot(window, col_matrix, preferred_element_type=jnp.float32)  13.2 us
  transfers between devices with their start and end apart: 23, of which 11 were waited for; matrix products, arithmetic and copies ran while one was open for 19% of the time, Pallas kernels for 0%

commit v1 on v0

v1 whole, which is shorter than its diff:
```python
import functools

import jax
import jax.numpy as jnp
from jax import lax
from jax.experimental import pallas as pl
from jax.experimental.pallas import tpu as pltpu
from jax.sharding import PartitionSpec as P

LEVELS = 3
CH = 64
WIDTH = 256
HALF = 8
F32 = jnp.float32
BF16 = jnp.bfloat16


def pick_rows(v, bits, w0, w1, outs):
    b8, b4, b2, b1 = bits
    n8, n4, n2, n1 = outs + 8, outs + 4, outs + 2, outs + 1
    x8 = [jnp.where(b8, v[j + 8], v[j]) if j < outs + 3 else v[j] for j in range(n8)]
    x4 = [jnp.where(b4, x8[j + 4], x8[j]) for j in range(n4)]
    x2 = [jnp.where(b2, x4[j + 2], x4[j]) for j in range(n2)]
    x1 = [jnp.where(b1, x2[j + 1], x2[j]) for j in range(n1)]
    return [w0 * x1[i] + w1 * x1[i + 1] for i in range(outs)]


def level_kernel(sources, flags, vals, wu, wm, *refs):
    pieces = [refs[4 * i : 4 * i + 4] for i in range(sources)]
    own_top, own_a, own_b, own_bot, out_a, out_b, out_first, out_last = refs[
        4 * sources : 4 * sources + 8
    ]
    src, table, cols, passed, joined, act = refs[4 * sources + 8 :]

    for i in range(sources):
        for p in range(4):
            src[i, 8 * p : 8 * p + 8] = pieces[i][p][...]
    own_at = 2 * CH
    joined[0:2, own_at : own_at + CH] = own_top[...]
    joined[2:10, own_at : own_at + CH] = own_a[...]
    joined[10:18, own_at : own_at + CH] = own_b[...]
    joined[18:20, own_at : own_at + CH] = own_bot[...]

    block_of = lax.broadcasted_iota(jnp.int32, (32, WIDTH), 1) // 8
    spread = (block_of == lax.broadcasted_iota(jnp.int32, (32, WIDTH), 0)).astype(F32)
    table[...] = jnp.dot(
        vals[...].astype(F32).astype(BF16), spread.astype(BF16), preferred_element_type=F32
    )

    has_above = flags[0] > 0
    has_below = flags[1] > 0

    def warp_block(which, block, first_source, count, outs, put):
        base = (which * 4 + block) * 8
        entry = table[pl.ds(pl.multiple_of(base, 8), 8), :]
        dy = entry[0:1].astype(jnp.int32)
        dx = entry[1:2].astype(jnp.int32)
        fy = entry[2:3] * 0.25
        fx = entry[3:4] * 0.25
        off = lax.broadcasted_iota(jnp.int32, (WIDTH, WIDTH), 0) - (
            lax.broadcasted_iota(jnp.int32, (WIDTH, WIDTH), 1) + dx
        )
        cols[...] = jnp.where(
            off == 0, 1.0 - fx, jnp.where(off == 1, fx, 0.0)
        ).astype(BF16)
        source = which if sources == 2 else 0
        window = src[source, pl.ds(first_source, count)].reshape(count * CH, WIDTH)
        passed[0:count] = jnp.dot(
            window, cols[...], preferred_element_type=F32
        ).reshape(count, CH, WIDTH)
        s = dy + 5
        lanes = (16, WIDTH)
        bits = [jnp.broadcast_to((s & b) != 0, lanes) for b in (8, 4, 2, 1)]
        w1 = jnp.broadcast_to(fy, lanes)
        w0 = 1.0 - w1
        for c in range(CH // 16):
            v = [passed[u, 16 * c : 16 * c + 16, :] for u in range(count)]
            for i, row in enumerate(pick_rows(v, bits, w0, w1, outs)):
                put(i, 16 * c, row)

    @pl.loop(0, 4)
    def _(n):
        which, block = n // 2, n % 2

        def put(i, c, row):
            at = pl.multiple_of(which * CH + c, 16)
            joined[2 + 8 * block + i, pl.ds(at, 16), :] = row.astype(BF16)

        warp_block(which, block + 1, 3 + 8 * block, 19, 8, put)

    @pl.loop(0, 4)
    def _(n):
        which, side = n // 2, n % 2
        keep = jnp.where(side == 0, has_above, has_below).astype(F32)

        def put(i, c, row):
            at = pl.multiple_of(which * CH + c, 16)
            joined[18 * side + i, pl.ds(at, 16), :] = (row * keep).astype(BF16)

        warp_block(which, 3 * side, 1 + 18 * side, 13, 2, put)

    lane = lax.broadcasted_iota(jnp.int32, (CH, WIDTH), 1)
    not_first = lane > 0
    not_last = lane < WIDTH - 1

    def gather_taps(s):
        left = jnp.where(not_first, pltpu.roll(s[0:CH], 1, 1), 0.0)
        right = jnp.where(not_last, pltpu.roll(s[2 * CH :], WIDTH - 1, 1), 0.0)
        return s[CH : 2 * CH] + left + right

    @pl.loop(0, 18)
    def _(a):
        window = joined[pl.ds(a, 3)].reshape(9 * CH, WIDTH)
        total = gather_taps(jnp.dot(wu[...], window, preferred_element_type=F32))
        half = 0.5 * total
        value = half + half * jnp.tanh(half)
        keep = jnp.where(
            a == 0, has_above, jnp.where(a == 17, has_below, True)
        ).astype(F32)
        act[a] = (value * keep).astype(BF16)

    scale = flags[2].astype(F32)

    def finish(y):
        window = act[pl.ds(y, 3)].reshape(3 * CH, WIDTH)
        total = gather_taps(jnp.dot(wm[...], window, preferred_element_type=F32))
        own = joined[y + 2, own_at : own_at + CH, :].astype(F32)
        return (own + scale * total).astype(BF16)

    @pl.loop(0, HALF)
    def _(y):
        out_a[y] = finish(y)

    @pl.loop(0, HALF)
    def _(y):
        out_b[y] = finish(y + HALF)

    out_first[...] = out_a[0:2]
    out_last[...] = out_b[6:8]


def run_level(flags, vals, wu, wm, sources, own, interpret=False):
    half = jax.ShapeDtypeStruct((HALF, CH, WIDTH), BF16)
    edge = jax.ShapeDtypeStruct((2, CH, WIDTH), BF16)
    operands = [p for s in sources for p in s] + list(own)
    vmem = pl.BlockSpec(memory_space=pltpu.VMEM)
    return pl.pallas_call(
        functools.partial(level_kernel, len(sources)),
        out_shape=(half, half, edge, edge),
        in_specs=[pl.BlockSpec(memory_space=pltpu.SMEM)] + [vmem] * (3 + len(operands)),
        out_specs=(vmem,) * 4,
        scratch_shapes=[
            pltpu.VMEM((len(sources), 32, CH, WIDTH), BF16),
            pltpu.VMEM((64, WIDTH), F32),
            pltpu.VMEM((WIDTH, WIDTH), BF16),
            pltpu.VMEM((19, CH, WIDTH), F32),
            pltpu.VMEM((20, 3 * CH, WIDTH), BF16),
            pltpu.VMEM((18, CH, WIDTH), BF16),
        ],
        cost_estimate=pl.CostEstimate(
            flops=3_000_000_000, bytes_accessed=4_000_000, transcendentals=300_000
        ),
        interpret=interpret,
    )(flags, vals, wu, wm, *operands)


def moved(x, axis, distance, wrap):
    count = lax.axis_size(axis)
    route = [
        (i, (i + distance) % count) for i in range(count) if wrap or 0 <= i + distance < count
    ]
    return lax.ppermute(x, axis, route)


def level_values(packed, level):
    t = packed[:, level]
    t = t.reshape(2, 2, 2, 4, 32)
    t = jnp.transpose(t, (1, 3, 0, 2, 4)).reshape(2, 4, 4, 32)
    return jnp.pad(t, ((0, 0), (0, 0), (0, 4), (0, 0))).reshape(64, 32)


def tap_weights(w):
    o, j = w.shape[2], w.shape[3]
    return jnp.transpose(w, (1, 2, 0, 3)).reshape(3 * o, 3 * j)


def shards(features, block_shift, quarter_pel, update_mask, uniting_weight, mixing_weight):
    band = features[0]
    a, b = band[:HALF], band[HALF:]
    first, last = band[:2], band[-2:]
    row = lax.axis_index("rows")
    rows = lax.axis_size("rows")
    own = jnp.stack([block_shift[:, :, 0], quarter_pel[:, :, 0]])
    above = moved(own[:, :, :, 1:2], "rows", 1, False)
    below = moved(own[:, :, :, 0:1], "rows", -1, False)
    packed = jnp.concatenate([above, own, below], axis=3)
    wu, wm = tap_weights(uniting_weight), tap_weights(mixing_weight)
    frames = lax.axis_size("tm")
    for level in range(LEVELS - 1, -1, -1):
        distance = 2**level
        steps = [distance] if 2 * distance == frames else [distance, -distance]
        own_top = moved(last, "rows", 1, False)
        own_bot = moved(first, "rows", -1, False)
        sources = []
        for step in steps:
            ra = moved(a, "tm", step, True)
            rb = moved(b, "tm", step, True)
            sources.append((ra, rb))
        sources = [
            (moved(rb, "rows", 1, False), ra, rb, moved(ra, "rows", -1, False))
            for ra, rb in sources
        ]
        flags = jnp.stack(
            [
                (row > 0).astype(jnp.int32),
                (row < rows - 1).astype(jnp.int32),
                update_mask[level, 0],
            ]
        )
        a, b, first, last = run_level(
            flags, level_values(packed, level), wu, wm, sources, (own_top, a, b, own_bot)
        )
    return jnp.concatenate([a, b])[None]


def solution(mesh):
    placed = (
        P("tm", "rows", None, None),
        P(None, None, "tm", "rows", None),
        P(None, None, "tm", "rows", None),
        P(None, "tm"),
        P(),
        P(),
    )
    return jax.shard_map(
        shards, mesh=mesh, in_specs=placed, out_specs=P("tm", "rows", None, None), check_vma=False
    )
```

time: 360 us -> 184 us (0.51)
  matrix products: 91.2 us -> 0 us
  waiting for transfers between devices: 97.1 us -> 37.1 us
  local copies, waits for them, and re-layouts: 60.9 us -> 9.14 us
  Pallas kernels: 0 us -> 48.2 us
  other arithmetic: 39.6 us -> 6.55 us
  starting transfers between devices: 62.6 us -> 81 us
  between operations: 4.68 us -> 0.66 us
    dot_general x78 -> x0, matrix products: 91.2 us -> none  [the longest x12 50.6 us: warp_band(): jnp.einsum('iux,ucx->icx', row_tensor, column_pass, precision=lax.Precisi...]
    ppermute x23 -> x28, waiting for transfers between devices: 97.1 us -> 37.1 us  [moved(): return lax.ppermute(x, axis, route)]
    pallas_call x0 -> x3, Pallas kernels: none -> 48.2 us  [run_level(): pl.pallas_call(functools.partial(level_kernel, len(sources)), out_shape=(...]
    dot_general x12 -> x0, local copies, waits for them, and re-layouts: 27.2 us -> none  [warp_band(): jnp.dot(window, col_matrix, preferred_element_type=jnp.float32)]
    ppermute x23 -> x28, starting transfers between devices: 62.6 us -> 81 us  [moved(): return lax.ppermute(x, axis, route)]
    add x24 -> x0, other arithmetic: 15.3 us -> none  [the longest x12 8.16 us: warp_band(): row_base = target_rows + shift_rows[None, None, :] + margin]
    sub x24 -> x0, other arithmetic: 13.1 us -> none  [the longest x12 6.82 us: warp_band(): 1.0 - part_rows[None, None, :]]
    another operation x15 -> x0, local copies, waits for them, and re-layouts: 7.73 us -> none  [the longest x3 6.66 us: shards(): jnp.stack([warp_band(earlier, own_shift[0:2], own_quarter[0:2]), warp_ban...]
  transfers between devices with their start and end apart: 23 -> 28, of which waited for: 11 -> 8; matrix products, arithmetic and copies ran while one was open for 19% -> 6% of each run, Pallas kernels for 0% -> 0%
where the time goes in v1:
time: 184 us; the launch traced here: 183 us
  starting transfers between devices  81 us (44%)
  Pallas kernels  48.2 us (26%)
  waiting for transfers between devices  37.1 us (20%)
  local copies, waits for them, and re-layouts  9.14 us (5%)
  other arithmetic  6.55 us (4%)
    ppermute x28, starting transfers between devices, moved(): return lax.ppermute(x, axis, route)  81 us
    pallas_call x3, Pallas kernels, run_level(): pl.pallas_call(functools.partial(level_kernel, len(sources)), out_shape=(...  48.2 us
    ppermute x28, waiting for transfers between devices, moved(): return lax.ppermute(x, axis, route)  37.1 us
    another operation x3, other arithmetic, shards(): jnp.stack([(row > 0).astype(jnp.int32), (row < rows - 1).astype(jnp.int32...  3.83 us
  transfers between devices with their start and end apart: 28, of which 8 were waited for; matrix products, arithmetic and copies ran while one was open for 6% of the time, Pallas kernels for 0%

profile of v1, /device:TPU:7, one launch (start us, length us, event | category | flops | bytes accessed | tf_op | source)
XLA Modules:
  0.0 182.7 jit_solution(5072712363057619038)
XLA Ops:
  0.0 0.8 fusion
  0.8 4.6 %collective-permute-start = (s32[2,3,4,1,32]{4,3,2,1,0:T(1,128)S(1)}, s32[2,3,4,1,32]{4,3,2,1,0:T(1,128)S(1)}, u32[]{:S(2)}, u32[]{:S(2)}) collective-permute-start(s32[2,3,4,1,32]{4,3,2,1,0:T(1,128)S(1)} %get-tuple-element.32), channel_id=1, source_target_pairs={{0,1},{1,2},{2,3},{3,4},{4,5},{5,6},{6,7},{7,8},{8,9},{9,10},{10,1... | collective-permute-start | bytes 9224 | tf_op jit(solution)/shard_map/ppermute | solution.py:172
  5.4 1.9 %collective-permute-start.1 = (s32[2,3,4,1,32]{4,3,2,1,0:T(1,128)S(1)}, s32[2,3,4,1,32]{4,3,2,1,0:T(1,128)S(1)}, u32[]{:S(2)}, u32[]{:S(2)}) collective-permute-start(s32[2,3,4,1,32]{4,3,2,1,0:T(1,128)S(1)} %get-tuple-element.33), channel_id=1, source_target_pairs={{1,0},{2,1},{3,2},{4,3},{5,4},{6,5},{7,6},{8,7},{9,8},{10,9},{11,1... | collective-permute-start | bytes 9224 | tf_op jit(solution)/shard_map/ppermute | solution.py:172
  7.4 1.1 slice_bitcast_fusion
  8.5 0.1 collective-permute-start.2
  8.6 1.5 collective-permute-start.4
  10.0 0.9 slice_bitcast_fusion.2
  10.9 6.6 %collective-permute-start.6 = (bf16[2,64,256]{2,1,0:T(8,128)(2,1)S(1)}, bf16[2,64,256]{2,1,0:T(8,128)(2,1)S(1)}, u32[]{:S(2)}, u32[]{:S(2)}) collective-permute-start(bf16[2,64,256]{2,1,0:T(8,128)(2,1)S(1)} %get-tuple-element.26), channel_id=1, source_target_pairs={{0,1},{1,2},{2,3},{3,4},{4,5},{5,6},{6,7},{7,8},{8,9},{9,10},{10,1... | collective-permute-start | bytes 196616 | tf_op jit(solution)/shard_map/ppermute | solution.py:172
  17.5 0.7 fusion.2
  18.2 1.3 pad_add_fusion.5.flags
  19.5 0.3 copy.13
  19.8 1.0 reshape.30.wu
  20.8 0.1 copy.14
  20.9 0.8 reshape.31.wm
  21.7 1.9 %collective-permute-start.7 = (bf16[2,64,256]{2,1,0:T(8,128)(2,1)S(1)}, bf16[2,64,256]{2,1,0:T(8,128)(2,1)S(1)}, u32[]{:S(2)}, u32[]{:S(2)}) collective-permute-start(bf16[2,64,256]{2,1,0:T(8,128)(2,1)S(1)} %get-tuple-element.25), channel_id=1, source_target_pairs={{1,0},{2,1},{3,2},{4,3},{5,4},{6,5},{7,6},{8,7},{9,8},{10,9},{11,1... | collective-permute-start | bytes 196616 | tf_op jit(solution)/shard_map/ppermute | solution.py:172
  23.7 6.0 %collective-permute-start.3 = (bf16[8,64,256]{2,1,0:T(8,128)(2,1)S(1)}, bf16[8,64,256]{2,1,0:T(8,128)(2,1)S(1)}, u32[]{:S(2)}, u32[]{:S(2)}) collective-permute-start(bf16[8,64,256]{2,1,0:T(8,128)(2,1)S(1)} %collective-permute-done.2.refs_2_), channel_id=1, source_target_pairs={{0,1},{1,2},{2,3},{3,4},{4,5},{5,6},{6,7},{7,8},{8,9},{9,10},{10,1... | collective-permute-start | bytes 786440 | tf_op jit(solution)/shard_map/ppermute | solution.py:172
  29.8 1.9 %collective-permute-start.5 = (bf16[8,64,256]{2,1,0:T(8,128)(2,1)S(1)}, bf16[8,64,256]{2,1,0:T(8,128)(2,1)S(1)}, u32[]{:S(2)}, u32[]{:S(2)}) collective-permute-start(bf16[8,64,256]{2,1,0:T(8,128)(2,1)S(1)} %collective-permute-done.4.refs_1_), channel_id=1, source_target_pairs={{1,0},{2,1},{3,2},{4,3},{5,4},{6,5},{7,6},{8,7},{9,8},{10,9},{11,1... | collective-permute-start | bytes 786440 | tf_op jit(solution)/shard_map/ppermute | solution.py:172
  31.8 0.6 pad.12
  32.4 1.9 %collective-permute-done.3.refs_0_ = bf16[8,64,256]{2,1,0:T(8,128)(2,1)S(1)} collective-permute-done((bf16[8,64,256]{2,1,0:T(8,128)(2,1)S(1)}, bf16[8,64,256]{2,1,0:T(8,128)(2,1)S(1)}, u32[]{:S(2)}, u32[]{:S(2)}) %collective-permute-start.3) | collective-permute-done | bytes 262176 | tf_op jit(solution)/shard_map/ppermute | solution.py:172
  34.3 5.6 %collective-permute-done.5.refs_3_ = bf16[8,64,256]{2,1,0:T(8,128)(2,1)S(1)} collective-permute-done((bf16[8,64,256]{2,1,0:T(8,128)(2,1)S(1)}, bf16[8,64,256]{2,1,0:T(8,128)(2,1)S(1)}, u32[]{:S(2)}, u32[]{:S(2)}) %collective-permute-start.5) | collective-permute-done | bytes 262176 | tf_op jit(solution)/shard_map/ppermute | solution.py:172
  39.9 0.7 copy-done.26
  40.5 15.8 %shard_map.64 = (bf16[8,64,256]{2,1,0:T(8,128)(2,1)}, bf16[8,64,256]{2,1,0:T(8,128)(2,1)}, bf16[2,64,256]{2,1,0:T(8,128)(2,1)}, bf16[2,64,256]{2,1,0:T(8,128)(2,1)}) custom-call(s32[3]{0:T(128)} %pad_add_fusion.5.flags, s32[64,32]{1,0:T(8,128)} %bitcast.48, bf16[192,576]{1,0:T(8,128)(2,1)} %reshape.30.wu, bf16[192,192]{1,0:T(8,128)(2,1)} %reshape.31.wm, ...), custom_call_target="tpu_custom_call" | custom-call | flops 3000000000 | bytes 4000000 | tf_op jit(solution)/shard_map/pallas_call | solution.py:147
  56.4 3.6 %collective-permute-start.10 = (bf16[8,64,256]{2,1,0:T(8,128)(2,1)}, bf16[8,64,256]{2,1,0:T(8,128)(2,1)S(1)}, u32[]{:S(2)}, u32[]{:S(2)}) collective-permute-start(bf16[8,64,256]{2,1,0:T(8,128)(2,1)} %get-tuple-element.16.refs_9_), channel_id=1, source_target_pairs={{0,32},{16,48},{32,64},{48,80},{64,96},{80,112},{96,0},{112,16},{1... | collective-permute-start | bytes 786440 | tf_op jit(solution)/shard_map/ppermute | solution.py:172
  60.0 0.3 collective-permute-start.12
  60.3 2.1 %collective-permute-start.14 = (bf16[8,64,256]{2,1,0:T(8,128)(2,1)}, bf16[8,64,256]{2,1,0:T(8,128)(2,1)S(1)}, u32[]{:S(2)}, u32[]{:S(2)}) collective-permute-start(bf16[8,64,256]{2,1,0:T(8,128)(2,1)} %get-tuple-element.16.refs_9_), channel_id=1, source_target_pairs={{0,96},{16,112},{32,0},{48,16},{64,32},{80,48},{96,64},{112,80},{1... | collective-permute-start | bytes 786440 | tf_op jit(solution)/shard_map/ppermute | solution.py:172
  62.3 0.9 collective-permute-start.8
  63.2 12.3 %collective-permute-done.10.refs_1_ = bf16[8,64,256]{2,1,0:T(8,128)(2,1)S(1)} collective-permute-done((bf16[8,64,256]{2,1,0:T(8,128)(2,1)}, bf16[8,64,256]{2,1,0:T(8,128)(2,1)S(1)}, u32[]{:S(2)}, u32[]{:S(2)}) %collective-permute-start.10) | collective-permute-done | bytes 262176 | tf_op jit(solution)/shard_map/ppermute | solution.py:172
  75.6 1.9 %collective-permute-start.11 = (bf16[8,64,256]{2,1,0:T(8,128)(2,1)S(1)}, bf16[8,64,256]{2,1,0:T(8,128)(2,1)S(1)}, u32[]{:S(2)}, u32[]{:S(2)}) collective-permute-start(bf16[8,64,256]{2,1,0:T(8,128)(2,1)S(1)} %collective-permute-done.10.refs_1_), channel_id=1, source_target_pairs={{1,0},{2,1},{3,2},{4,3},{5,4},{6,5},{7,6},{8,7},{9,8},{10,9},{11,1... | collective-permute-start | bytes 786440 | tf_op jit(solution)/shard_map/ppermute | solution.py:172
  77.5 6.0 %collective-permute-start.13 = (bf16[8,64,256]{2,1,0:T(8,128)(2,1)S(1)}, bf16[8,64,256]{2,1,0:T(8,128)(2,1)S(1)}, u32[]{:S(2)}, u32[]{:S(2)}) collective-permute-start(bf16[8,64,256]{2,1,0:T(8,128)(2,1)S(1)} %collective-permute-done.12.refs_6_), channel_id=1, source_target_pairs={{0,1},{1,2},{2,3},{3,4},{4,5},{5,6},{6,7},{7,8},{8,9},{9,10},{10,1... | collective-permute-start | bytes 786440 | tf_op jit(solution)/shard_map/ppermute | solution.py:172
  83.6 1.9 %collective-permute-start.15 = (bf16[8,64,256]{2,1,0:T(8,128)(2,1)S(1)}, bf16[8,64,256]{2,1,0:T(8,128)(2,1)S(1)}, u32[]{:S(2)}, u32[]{:S(2)}) collective-permute-start(bf16[8,64,256]{2,1,0:T(8,128)(2,1)S(1)} %collective-permute-done.14.refs_5_), channel_id=1, source_target_pairs={{1,0},{2,1},{3,2},{4,3},{5,4},{6,5},{7,6},{8,7},{9,8},{10,9},{11,1... | collective-permute-start | bytes 786440 | tf_op jit(solution)/shard_map/ppermute | solution.py:172
  85.5 6.0 %collective-permute-start.9 = (bf16[8,64,256]{2,1,0:T(8,128)(2,1)S(1)}, bf16[8,64,256]{2,1,0:T(8,128)(2,1)S(1)}, u32[]{:S(2)}, u32[]{:S(2)}) collective-permute-start(bf16[8,64,256]{2,1,0:T(8,128)(2,1)S(1)} %collective-permute-done.8.refs_2_), channel_id=1, source_target_pairs={{0,1},{1,2},{2,3},{3,4},{4,5},{5,6},{6,7},{7,8},{8,9},{9,10},{10,1... | collective-permute-start | bytes 786440 | tf_op jit(solution)/shard_map/ppermute | solution.py:172
  91.6 1.9 %collective-permute-start.16 = (bf16[2,64,256]{2,1,0:T(8,128)(2,1)}, bf16[2,64,256]{2,1,0:T(8,128)(2,1)S(1)}, u32[]{:S(2)}, u32[]{:S(2)}) collective-permute-start(bf16[2,64,256]{2,1,0:T(8,128)(2,1)} %get-tuple-element.17), channel_id=1, source_target_pairs={{0,1},{1,2},{2,3},{3,4},{4,5},{5,6},{6,7},{7,8},{8,9},{9,10},{10,1... | collective-permute-start | bytes 196616 | tf_op jit(solution)/shard_map/ppermute | solution.py:172
  93.5 2.2 %collective-permute-done.16.refs_8_ = bf16[2,64,256]{2,1,0:T(8,128)(2,1)S(1)} collective-permute-done((bf16[2,64,256]{2,1,0:T(8,128)(2,1)}, bf16[2,64,256]{2,1,0:T(8,128)(2,1)S(1)}, u32[]{:S(2)}, u32[]{:S(2)}) %collective-permute-start.16) | collective-permute-done | bytes 65568 | tf_op jit(solution)/shard_map/ppermute | solution.py:172
  95.7 1.9 %collective-permute-start.17 = (bf16[2,64,256]{2,1,0:T(8,128)(2,1)}, bf16[2,64,256]{2,1,0:T(8,128)(2,1)S(1)}, u32[]{:S(2)}, u32[]{:S(2)}) collective-permute-start(bf16[2,64,256]{2,1,0:T(8,128)(2,1)} %get-tuple-element.18), channel_id=1, source_target_pairs={{1,0},{2,1},{3,2},{4,3},{5,4},{6,5},{7,6},{8,7},{9,8},{10,9},{11,1... | collective-permute-start | bytes 196616 | tf_op jit(solution)/shard_map/ppermute | solution.py:172
  97.6 1.3 pad_add_fusion.4.flags
  98.9 0.6 pad.11
  99.5 5.0 %collective-permute-done.17.refs_11_ = bf16[2,64,256]{2,1,0:T(8,128)(2,1)S(1)} collective-permute-done((bf16[2,64,256]{2,1,0:T(8,128)(2,1)}, bf16[2,64,256]{2,1,0:T(8,128)(2,1)S(1)}, u32[]{:S(2)}, u32[]{:S(2)}) %collective-permute-start.17) | collective-permute-done | bytes 65568 | tf_op jit(solution)/shard_map/ppermute | solution.py:172
  104.6 0.5 copy-done.32
  105.1 0.1 copy-done.19
  105.2 0.1 copy-done.21
  105.3 0.1 copy-done.23
  105.4 0.1 copy-done.25
  105.5 16.2 %shard_map.65 = (bf16[8,64,256]{2,1,0:T(8,128)(2,1)}, bf16[8,64,256]{2,1,0:T(8,128)(2,1)}, bf16[2,64,256]{2,1,0:T(8,128)(2,1)}, bf16[2,64,256]{2,1,0:T(8,128)(2,1)}) custom-call(s32[3]{0:T(128)} %pad_add_fusion.4.flags, s32[64,32]{1,0:T(8,128)} %bitcast.47, bf16[192,576]{1,0:T(8,128)(2,1)} %reshape.30.wu, bf16[192,192]{1,0:T(8,128)(2,1)} %reshape.31.wm, ...), custom_call_target="tpu_custom_call" | custom-call | flops 3000000000 | bytes 4000000 | tf_op jit(solution)/shard_map/pallas_call | solution.py:147
  121.7 0.7 collective-permute-start.18
  122.4 2.5 %collective-permute-start.20 = (bf16[8,64,256]{2,1,0:T(8,128)(2,1)}, bf16[8,64,256]{2,1,0:T(8,128)(2,1)S(1)}, u32[]{:S(2)}, u32[]{:S(2)}) collective-permute-start(bf16[8,64,256]{2,1,0:T(8,128)(2,1)} %get-tuple-element.20.refs_9_), channel_id=1, source_target_pairs={{0,16},{16,32},{32,48},{48,64},{64,80},{80,96},{96,112},{112,0},{1... | collective-permute-start | bytes 786440 | tf_op jit(solution)/shard_map/ppermute | solution.py:172
  125.0 1.8 collective-permute-start.22
  126.8 1.4 collective-permute-start.24
  128.2 3.1 %collective-permute-done.18.refs_2_ = bf16[8,64,256]{2,1,0:T(8,128)(2,1)S(1)} collective-permute-done((bf16[8,64,256]{2,1,0:T(8,128)(2,1)}, bf16[8,64,256]{2,1,0:T(8,128)(2,1)S(1)}, u32[]{:S(2)}, u32[]{:S(2)}) %collective-permute-start.18) | collective-permute-done | bytes 262176 | tf_op jit(solution)/shard_map/ppermute | solution.py:172
  131.3 5.6 %collective-permute-start.19 = (bf16[8,64,256]{2,1,0:T(8,128)(2,1)S(1)}, bf16[8,64,256]{2,1,0:T(8,128)(2,1)S(1)}, u32[]{:S(2)}, u32[]{:S(2)}) collective-permute-start(bf16[8,64,256]{2,1,0:T(8,128)(2,1)S(1)} %collective-permute-done.18.refs_2_), channel_id=1, source_target_pairs={{0,1},{1,2},{2,3},{3,4},{4,5},{5,6},{6,7},{7,8},{8,9},{9,10},{10,1... | collective-permute-start | bytes 786440 | tf_op jit(solution)/shard_map/ppermute | solution.py:172
  136.9 1.9 %collective-permute-start.21 = (bf16[8,64,256]{2,1,0:T(8,128)(2,1)S(1)}, bf16[8,64,256]{2,1,0:T(8,128)(2,1)S(1)}, u32[]{:S(2)}, u32[]{:S(2)}) collective-permute-start(bf16[8,64,256]{2,1,0:T(8,128)(2,1)S(1)} %collective-permute-done.20.refs_1_), channel_id=1, source_target_pairs={{1,0},{2,1},{3,2},{4,3},{5,4},{6,5},{7,6},{8,7},{9,8},{10,9},{11,1... | collective-permute-start | bytes 786440 | tf_op jit(solution)/shard_map/ppermute | solution.py:172
  138.8 6.0 %collective-permute-start.23 = (bf16[8,64,256]{2,1,0:T(8,128)(2,1)S(1)}, bf16[8,64,256]{2,1,0:T(8,128)(2,1)S(1)}, u32[]{:S(2)}, u32[]{:S(2)}) collective-permute-start(bf16[8,64,256]{2,1,0:T(8,128)(2,1)S(1)} %collective-permute-done.22.refs_6_), channel_id=1, source_target_pairs={{0,1},{1,2},{2,3},{3,4},{4,5},{5,6},{6,7},{7,8},{8,9},{9,10},{10,1... | collective-permute-start | bytes 786440 | tf_op jit(solution)/shard_map/ppermute | solution.py:172
  144.9 1.9 %collective-permute-start.25 = (bf16[8,64,256]{2,1,0:T(8,128)(2,1)S(1)}, bf16[8,64,256]{2,1,0:T(8,128)(2,1)S(1)}, u32[]{:S(2)}, u32[]{:S(2)}) collective-permute-start(bf16[8,64,256]{2,1,0:T(8,128)(2,1)S(1)} %collective-permute-done.24.refs_5_), channel_id=1, source_target_pairs={{1,0},{2,1},{3,2},{4,3},{5,4},{6,5},{7,6},{8,7},{9,8},{10,9},{11,1... | collective-permute-start | bytes 786440 | tf_op jit(solution)/shard_map/ppermute | solution.py:172
  146.8 6.0 %collective-permute-start.26 = (bf16[2,64,256]{2,1,0:T(8,128)(2,1)}, bf16[2,64,256]{2,1,0:T(8,128)(2,1)S(1)}, u32[]{:S(2)}, u32[]{:S(2)}) collective-permute-start(bf16[2,64,256]{2,1,0:T(8,128)(2,1)} %get-tuple-element.21), channel_id=1, source_target_pairs={{0,1},{1,2},{2,3},{3,4},{4,5},{5,6},{6,7},{7,8},{8,9},{9,10},{10,1... | collective-permute-start | bytes 196616 | tf_op jit(solution)/shard_map/ppermute | solution.py:172
  152.9 1.9 %collective-permute-done.26.refs_8_ = bf16[2,64,256]{2,1,0:T(8,128)(2,1)S(1)} collective-permute-done((bf16[2,64,256]{2,1,0:T(8,128)(2,1)}, bf16[2,64,256]{2,1,0:T(8,128)(2,1)S(1)}, u32[]{:S(2)}, u32[]{:S(2)}) %collective-permute-start.26) | collective-permute-done | bytes 65568 | tf_op jit(solution)/shard_map/ppermute | solution.py:172
  154.8 1.9 %collective-permute-start.27 = (bf16[2,64,256]{2,1,0:T(8,128)(2,1)}, bf16[2,64,256]{2,1,0:T(8,128)(2,1)S(1)}, u32[]{:S(2)}, u32[]{:S(2)}) collective-permute-start(bf16[2,64,256]{2,1,0:T(8,128)(2,1)} %get-tuple-element.22), channel_id=1, source_target_pairs={{1,0},{2,1},{3,2},{4,3},{5,4},{6,5},{7,6},{8,7},{9,8},{10,9},{11,1... | collective-permute-start | bytes 196616 | tf_op jit(solution)/shard_map/ppermute | solution.py:172
  156.7 1.3 pad_add_fusion.2.flags
  158.0 0.6 pad.10
  158.6 5.0 %collective-permute-done.27.refs_11_ = bf16[2,64,256]{2,1,0:T(8,128)(2,1)S(1)} collective-permute-done((bf16[2,64,256]{2,1,0:T(8,128)(2,1)}, bf16[2,64,256]{2,1,0:T(8,128)(2,1)S(1)}, u32[]{:S(2)}, u32[]{:S(2)}) %collective-permute-start.27) | collective-permute-done | bytes 65568 | tf_op jit(solution)/shard_map/ppermute | solution.py:172
  163.8 0.5 copy-done.31
  164.3 0.1 copy-done.16
  164.4 0.1 copy-done.18
  164.4 0.1 copy-done.20
  164.6 16.2 %shard_map.66 = (bf16[8,64,256]{2,1,0:T(8,128)(2,1)}, bf16[8,64,256]{2,1,0:T(8,128)(2,1)}, bf16[2,64,256]{2,1,0:T(8,128)(2,1)}, bf16[2,64,256]{2,1,0:T(8,128)(2,1)}) custom-call(s32[3]{0:T(128)} %pad_add_fusion.2.flags, s32[64,32]{1,0:T(8,128)} %bitcast.46, bf16[192,576]{1,0:T(8,128)(2,1)} %reshape.30.wu, bf16[192,192]{1,0:T(8,128)(2,1)} %reshape.31.wm, ...), custom_call_target="tpu_custom_call" | custom-call | flops 3000000000 | bytes 4000000 | tf_op jit(solution)/shard_map/pallas_call | solution.py:147
  180.8 1.9 %maximum_bitcast_fusion = bf16[1,16,64,256]{3,2,1,0:T(8,128)(2,1)} fusion(bf16[8,64,256]{2,1,0:T(8,128)(2,1)} %get-tuple-element.24, bf16[8,64,256]{2,1,0:T(8,128)(2,1)} %get-tuple-element.23), kind=kLoop, calls=%fused_computation | loop fusion | flops 262144 | bytes 1048576 | tf_op jit(solution)/shard_map/broadcast_in_dim | solution.py:223
  (81 shorter events, 0.3 us)
Async XLA Ops:
  0.8 20.9 %collective-permute-start = (s32[2,3,4,1,32]{4,3,2,1,0:T(1,128)S(1)}, s32[2,3,4,1,32]{4,3,2,1,0:T(1,128)S(1)}, u32[]{:S(2)}, u32[]{:S(2)}) collective-permute-start(s32[2,3,4,1,32]{4,3,2,1,0:T(1,128)S(1)} %get-tuple-element.32), channel_id=1, source_target_pairs={{0,1},{1,2},{2,3},{3,4},{4,5},{5,6},{6,7},{7,8},{8,9},{9,10},{10,1... | collective-permute-start | bytes 9224 | tf_op jit(solution)/shard_map/ppermute | solution.py:172
  5.4 26.3 %collective-permute-start.1 = (s32[2,3,4,1,32]{4,3,2,1,0:T(1,128)S(1)}, s32[2,3,4,1,32]{4,3,2,1,0:T(1,128)S(1)}, u32[]{:S(2)}, u32[]{:S(2)}) collective-permute-start(s32[2,3,4,1,32]{4,3,2,1,0:T(1,128)S(1)} %get-tuple-element.33), channel_id=1, source_target_pairs={{1,0},{2,1},{3,2},{4,3},{5,4},{6,5},{7,6},{8,7},{9,8},{10,9},{11,1... | collective-permute-start | bytes 9224 | tf_op jit(solution)/shard_map/ppermute | solution.py:172
  7.4 10.2 %copy-start.6 = (s32[3,1]{0,1:T(1,128)S(1)}, s32[3,1]{0,1:T(1,128)}, u32[]{:S(2)}) copy-start(s32[3,1]{0,1:T(1,128)} %param.9) | copy-start | bytes 40
  8.4 11.3 %copy-start.1 = (bf16[8,64,256]{2,1,0:T(8,128)(2,1)}, bf16[8,64,256]{2,1,0:T(8,128)(2,1)S(1)}, u32[]{:S(2)}) copy-start(bf16[8,64,256]{2,1,0:T(8,128)(2,1)S(1)} %get-tuple-element.27.refs_5_) | copy-start | bytes 786436
  8.5 11.3 %copy-start.2 = (bf16[8,64,256]{2,1,0:T(8,128)(2,1)}, bf16[8,64,256]{2,1,0:T(8,128)(2,1)S(1)}, u32[]{:S(2)}) copy-start(bf16[8,64,256]{2,1,0:T(8,128)(2,1)S(1)} %get-tuple-element.28.refs_6_) | copy-start | bytes 786436
  8.5 11.0 %copy-start = (bf16[3,3,64,192]{3,2,1,0:T(8,128)(2,1)S(1)}, bf16[3,3,64,192]{3,2,1,0:T(8,128)(2,1)}, u32[]{:S(2)}) copy-start(bf16[3,3,64,192]{3,2,1,0:T(8,128)(2,1)} %param.10) | copy-start | bytes 663556
  8.5 15.2 %collective-permute-start.2 = (bf16[8,64,256]{2,1,0:T(8,128)(2,1)S(1)}, bf16[8,64,256]{2,1,0:T(8,128)(2,1)S(1)}, u32[]{:S(2)}, u32[]{:S(2)}) collective-permute-start(bf16[8,64,256]{2,1,0:T(8,128)(2,1)S(1)} %get-tuple-element.28.refs_6_), channel_id=1, source_target_pairs={{0,64},{16,80},{32,96},{48,112},{64,0},{80,16},{96,32},{112,48},{1... | collective-permute-start | bytes 786440 | tf_op jit(solution)/shard_map/ppermute | solution.py:172
  8.6 21.2 %collective-permute-start.4 = (bf16[8,64,256]{2,1,0:T(8,128)(2,1)S(1)}, bf16[8,64,256]{2,1,0:T(8,128)(2,1)S(1)}, u32[]{:S(2)}, u32[]{:S(2)}) collective-permute-start(bf16[8,64,256]{2,1,0:T(8,128)(2,1)S(1)} %get-tuple-element.27.refs_5_), channel_id=1, source_target_pairs={{0,64},{16,80},{32,96},{48,112},{64,0},{80,16},{96,32},{112,48},{1... | collective-permute-start | bytes 786440 | tf_op jit(solution)/shard_map/ppermute | solution.py:172
  10.9 21.5 %collective-permute-start.6 = (bf16[2,64,256]{2,1,0:T(8,128)(2,1)S(1)}, bf16[2,64,256]{2,1,0:T(8,128)(2,1)S(1)}, u32[]{:S(2)}, u32[]{:S(2)}) collective-permute-start(bf16[2,64,256]{2,1,0:T(8,128)(2,1)S(1)} %get-tuple-element.26), channel_id=1, source_target_pairs={{0,1},{1,2},{2,3},{3,4},{4,5},{5,6},{6,7},{7,8},{8,9},{9,10},{10,1... | collective-permute-start | bytes 196616 | tf_op jit(solution)/shard_map/ppermute | solution.py:172
  19.8 1.0 copy-start.3
  20.9 10.8 %copy-start.4 = (s32[3,4,1,2,32]{4,3,2,1,0:T(2,128)S(1)}, s32[3,4,1,2,32]{4,3,2,1,0:T(2,128)}, u32[]{:S(2)}) copy-start(s32[3,4,1,2,32]{4,3,2,1,0:T(2,128)} %param.7) | copy-start | bytes 9220
  20.9 10.8 %copy-start.5 = (s32[3,4,1,2,32]{4,3,2,1,0:T(2,128)S(1)}, s32[3,4,1,2,32]{4,3,2,1,0:T(2,128)}, u32[]{:S(2)}) copy-start(s32[3,4,1,2,32]{4,3,2,1,0:T(2,128)} %param.8) | copy-start | bytes 9220
  21.7 10.7 %collective-permute-start.7 = (bf16[2,64,256]{2,1,0:T(8,128)(2,1)S(1)}, bf16[2,64,256]{2,1,0:T(8,128)(2,1)S(1)}, u32[]{:S(2)}, u32[]{:S(2)}) collective-permute-start(bf16[2,64,256]{2,1,0:T(8,128)(2,1)S(1)} %get-tuple-element.25), channel_id=1, source_target_pairs={{1,0},{2,1},{3,2},{4,3},{5,4},{6,5},{7,6},{8,7},{9,8},{10,9},{11,1... | collective-permute-start | bytes 196616 | tf_op jit(solution)/shard_map/ppermute | solution.py:172
  23.7 16.2 %copy-start.7 = (bf16[8,64,256]{2,1,0:T(8,128)(2,1)}, bf16[8,64,256]{2,1,0:T(8,128)(2,1)S(1)}, u32[]{:S(2)}) copy-start(bf16[8,64,256]{2,1,0:T(8,128)(2,1)S(1)} %collective-permute-done.2.refs_2_) | copy-start | bytes 786436
  23.7 10.6 %collective-permute-start.3 = (bf16[8,64,256]{2,1,0:T(8,128)(2,1)S(1)}, bf16[8,64,256]{2,1,0:T(8,128)(2,1)S(1)}, u32[]{:S(2)}, u32[]{:S(2)}) collective-permute-start(bf16[8,64,256]{2,1,0:T(8,128)(2,1)S(1)} %collective-permute-done.2.refs_2_), channel_id=1, source_target_pairs={{0,1},{1,2},{2,3},{3,4},{4,5},{5,6},{6,7},{7,8},{8,9},{9,10},{10,1... | collective-permute-start | bytes 786440 | tf_op jit(solution)/shard_map/ppermute | solution.py:172
  29.7 10.1 %copy-start.8 = (bf16[8,64,256]{2,1,0:T(8,128)(2,1)}, bf16[8,64,256]{2,1,0:T(8,128)(2,1)S(1)}, u32[]{:S(2)}) copy-start(bf16[8,64,256]{2,1,0:T(8,128)(2,1)S(1)} %collective-permute-done.4.refs_1_) | copy-start | bytes 786436
  29.8 10.1 %collective-permute-start.5 = (bf16[8,64,256]{2,1,0:T(8,128)(2,1)S(1)}, bf16[8,64,256]{2,1,0:T(8,128)(2,1)S(1)}, u32[]{:S(2)}, u32[]{:S(2)}) collective-permute-start(bf16[8,64,256]{2,1,0:T(8,128)(2,1)S(1)} %collective-permute-done.4.refs_1_), channel_id=1, source_target_pairs={{1,0},{2,1},{3,2},{4,3},{5,4},{6,5},{7,6},{8,7},{9,8},{10,9},{11,1... | collective-permute-start | bytes 786440 | tf_op jit(solution)/shard_map/ppermute | solution.py:172
  32.4 7.4 %copy-start.27 = (bf16[2,64,256]{2,1,0:T(8,128)(2,1)}, bf16[2,64,256]{2,1,0:T(8,128)(2,1)S(1)}, u32[]{:S(2)}) copy-start(bf16[2,64,256]{2,1,0:T(8,128)(2,1)S(1)} %collective-permute-done.6.refs_4_) | copy-start | bytes 196612
  32.4 7.4 %copy-start.28 = (bf16[2,64,256]{2,1,0:T(8,128)(2,1)}, bf16[2,64,256]{2,1,0:T(8,128)(2,1)S(1)}, u32[]{:S(2)}) copy-start(bf16[2,64,256]{2,1,0:T(8,128)(2,1)S(1)} %collective-permute-done.7.refs_7_) | copy-start | bytes 196612
  34.3 5.6 %copy-start.24 = (bf16[8,64,256]{2,1,0:T(8,128)(2,1)}, bf16[8,64,256]{2,1,0:T(8,128)(2,1)S(1)}, u32[]{:S(2)}) copy-start(bf16[8,64,256]{2,1,0:T(8,128)(2,1)S(1)} %collective-permute-done.3.refs_0_) | copy-start | bytes 786436
  39.9 0.7 copy-start.26
  56.4 19.2 %collective-permute-start.10 = (bf16[8,64,256]{2,1,0:T(8,128)(2,1)}, bf16[8,64,256]{2,1,0:T(8,128)(2,1)S(1)}, u32[]{:S(2)}, u32[]{:S(2)}) collective-permute-start(bf16[8,64,256]{2,1,0:T(8,128)(2,1)} %get-tuple-element.16.refs_9_), channel_id=1, source_target_pairs={{0,32},{16,48},{32,64},{48,80},{64,96},{80,112},{96,0},{112,16},{1... | collective-permute-start | bytes 786440 | tf_op jit(solution)/shard_map/ppermute | solution.py:172
  60.0 17.5 %collective-permute-start.12 = (bf16[8,64,256]{2,1,0:T(8,128)(2,1)}, bf16[8,64,256]{2,1,0:T(8,128)(2,1)S(1)}, u32[]{:S(2)}, u32[]{:S(2)}) collective-permute-start(bf16[8,64,256]{2,1,0:T(8,128)(2,1)} %get-tuple-element.15.refs_10_), channel_id=1, source_target_pairs={{0,96},{16,112},{32,0},{48,16},{64,32},{80,48},{96,64},{112,80},{1... | collective-permute-start | bytes 786440 | tf_op jit(solution)/shard_map/ppermute | solution.py:172
  60.3 23.3 %collective-permute-start.14 = (bf16[8,64,256]{2,1,0:T(8,128)(2,1)}, bf16[8,64,256]{2,1,0:T(8,128)(2,1)S(1)}, u32[]{:S(2)}, u32[]{:S(2)}) collective-permute-start(bf16[8,64,256]{2,1,0:T(8,128)(2,1)} %get-tuple-element.16.refs_9_), channel_id=1, source_target_pairs={{0,96},{16,112},{32,0},{48,16},{64,32},{80,48},{96,64},{112,80},{1... | collective-permute-start | bytes 786440 | tf_op jit(solution)/shard_map/ppermute | solution.py:172
  62.3 23.2 %collective-permute-start.8 = (bf16[8,64,256]{2,1,0:T(8,128)(2,1)}, bf16[8,64,256]{2,1,0:T(8,128)(2,1)S(1)}, u32[]{:S(2)}, u32[]{:S(2)}) collective-permute-start(bf16[8,64,256]{2,1,0:T(8,128)(2,1)} %get-tuple-element.15.refs_10_), channel_id=1, source_target_pairs={{0,32},{16,48},{32,64},{48,80},{64,96},{80,112},{96,0},{112,16},{1... | collective-permute-start | bytes 786440 | tf_op jit(solution)/shard_map/ppermute | solution.py:172
  75.6 29.0 %copy-start.12 = (bf16[8,64,256]{2,1,0:T(8,128)(2,1)}, bf16[8,64,256]{2,1,0:T(8,128)(2,1)S(1)}, u32[]{:S(2)}) copy-start(bf16[8,64,256]{2,1,0:T(8,128)(2,1)S(1)} %collective-permute-done.10.refs_1_) | copy-start | bytes 786436
  75.6 29.0 %collective-permute-start.11 = (bf16[8,64,256]{2,1,0:T(8,128)(2,1)S(1)}, bf16[8,64,256]{2,1,0:T(8,128)(2,1)S(1)}, u32[]{:S(2)}, u32[]{:S(2)}) collective-permute-start(bf16[8,64,256]{2,1,0:T(8,128)(2,1)S(1)} %collective-permute-done.10.refs_1_), channel_id=1, source_target_pairs={{1,0},{2,1},{3,2},{4,3},{5,4},{6,5},{7,6},{8,7},{9,8},{10,9},{11,1... | collective-permute-start | bytes 786440 | tf_op jit(solution)/shard_map/ppermute | solution.py:172
  77.5 27.1 %copy-start.14 = (bf16[8,64,256]{2,1,0:T(8,128)(2,1)}, bf16[8,64,256]{2,1,0:T(8,128)(2,1)S(1)}, u32[]{:S(2)}) copy-start(bf16[8,64,256]{2,1,0:T(8,128)(2,1)S(1)} %collective-permute-done.12.refs_6_) | copy-start | bytes 786436
  77.5 27.0 %collective-permute-start.13 = (bf16[8,64,256]{2,1,0:T(8,128)(2,1)S(1)}, bf16[8,64,256]{2,1,0:T(8,128)(2,1)S(1)}, u32[]{:S(2)}, u32[]{:S(2)}) collective-permute-start(bf16[8,64,256]{2,1,0:T(8,128)(2,1)S(1)} %collective-permute-done.12.refs_6_), channel_id=1, source_target_pairs={{0,1},{1,2},{2,3},{3,4},{4,5},{5,6},{6,7},{7,8},{8,9},{9,10},{10,1... | collective-permute-start | bytes 786440 | tf_op jit(solution)/shard_map/ppermute | solution.py:172
  83.6 21.0 %copy-start.15 = (bf16[8,64,256]{2,1,0:T(8,128)(2,1)}, bf16[8,64,256]{2,1,0:T(8,128)(2,1)S(1)}, u32[]{:S(2)}) copy-start(bf16[8,64,256]{2,1,0:T(8,128)(2,1)S(1)} %collective-permute-done.14.refs_5_) | copy-start | bytes 786436
  83.6 21.0 %collective-permute-start.15 = (bf16[8,64,256]{2,1,0:T(8,128)(2,1)S(1)}, bf16[8,64,256]{2,1,0:T(8,128)(2,1)S(1)}, u32[]{:S(2)}, u32[]{:S(2)}) collective-permute-start(bf16[8,64,256]{2,1,0:T(8,128)(2,1)S(1)} %collective-permute-done.14.refs_5_), channel_id=1, source_target_pairs={{1,0},{2,1},{3,2},{4,3},{5,4},{6,5},{7,6},{8,7},{9,8},{10,9},{11,1... | collective-permute-start | bytes 786440 | tf_op jit(solution)/shard_map/ppermute | solution.py:172
  85.5 19.1 %copy-start.17 = (bf16[8,64,256]{2,1,0:T(8,128)(2,1)}, bf16[8,64,256]{2,1,0:T(8,128)(2,1)S(1)}, u32[]{:S(2)}) copy-start(bf16[8,64,256]{2,1,0:T(8,128)(2,1)S(1)} %collective-permute-done.8.refs_2_) | copy-start | bytes 786436
  85.5 19.0 %collective-permute-start.9 = (bf16[8,64,256]{2,1,0:T(8,128)(2,1)S(1)}, bf16[8,64,256]{2,1,0:T(8,128)(2,1)S(1)}, u32[]{:S(2)}, u32[]{:S(2)}) collective-permute-start(bf16[8,64,256]{2,1,0:T(8,128)(2,1)S(1)} %collective-permute-done.8.refs_2_), channel_id=1, source_target_pairs={{0,1},{1,2},{2,3},{3,4},{4,5},{5,6},{6,7},{7,8},{8,9},{9,10},{10,1... | collective-permute-start | bytes 786440 | tf_op jit(solution)/shard_map/ppermute | solution.py:172
  91.6 4.1 %collective-permute-start.16 = (bf16[2,64,256]{2,1,0:T(8,128)(2,1)}, bf16[2,64,256]{2,1,0:T(8,128)(2,1)S(1)}, u32[]{:S(2)}, u32[]{:S(2)}) collective-permute-start(bf16[2,64,256]{2,1,0:T(8,128)(2,1)} %get-tuple-element.17), channel_id=1, source_target_pairs={{0,1},{1,2},{2,3},{3,4},{4,5},{5,6},{6,7},{7,8},{8,9},{9,10},{10,1... | collective-permute-start | bytes 196616 | tf_op jit(solution)/shard_map/ppermute | solution.py:172
  95.7 8.9 %copy-start.30 = (bf16[2,64,256]{2,1,0:T(8,128)(2,1)}, bf16[2,64,256]{2,1,0:T(8,128)(2,1)S(1)}, u32[]{:S(2)}) copy-start(bf16[2,64,256]{2,1,0:T(8,128)(2,1)S(1)} %collective-permute-done.16.refs_8_) | copy-start | bytes 196612
  95.7 8.8 %collective-permute-start.17 = (bf16[2,64,256]{2,1,0:T(8,128)(2,1)}, bf16[2,64,256]{2,1,0:T(8,128)(2,1)S(1)}, u32[]{:S(2)}, u32[]{:S(2)}) collective-permute-start(bf16[2,64,256]{2,1,0:T(8,128)(2,1)} %get-tuple-element.18), channel_id=1, source_target_pairs={{1,0},{2,1},{3,2},{4,3},{5,4},{6,5},{7,6},{8,7},{9,8},{10,9},{11,1... | collective-permute-start | bytes 196616 | tf_op jit(solution)/shard_map/ppermute | solution.py:172
  104.5 0.6 copy-start.32
  104.5 0.7 copy-start.19
  104.5 0.8 copy-start.21
  104.6 0.9 copy-start.23
  104.6 0.9 copy-start.25
  121.7 9.6 %collective-permute-start.18 = (bf16[8,64,256]{2,1,0:T(8,128)(2,1)}, bf16[8,64,256]{2,1,0:T(8,128)(2,1)S(1)}, u32[]{:S(2)}, u32[]{:S(2)}) collective-permute-start(bf16[8,64,256]{2,1,0:T(8,128)(2,1)} %get-tuple-element.19.refs_10_), channel_id=1, source_target_pairs={{0,16},{16,32},{32,48},{48,64},{64,80},{80,96},{96,112},{112,0},{1... | collective-permute-start | bytes 786440 | tf_op jit(solution)/shard_map/ppermute | solution.py:172
  122.4 14.4 %collective-permute-start.20 = (bf16[8,64,256]{2,1,0:T(8,128)(2,1)}, bf16[8,64,256]{2,1,0:T(8,128)(2,1)S(1)}, u32[]{:S(2)}, u32[]{:S(2)}) collective-permute-start(bf16[8,64,256]{2,1,0:T(8,128)(2,1)} %get-tuple-element.20.refs_9_), channel_id=1, source_target_pairs={{0,16},{16,32},{32,48},{48,64},{64,80},{80,96},{96,112},{112,0},{1... | collective-permute-start | bytes 786440 | tf_op jit(solution)/shard_map/ppermute | solution.py:172
  125.0 13.8 %collective-permute-start.22 = (bf16[8,64,256]{2,1,0:T(8,128)(2,1)}, bf16[8,64,256]{2,1,0:T(8,128)(2,1)S(1)}, u32[]{:S(2)}, u32[]{:S(2)}) collective-permute-start(bf16[8,64,256]{2,1,0:T(8,128)(2,1)} %get-tuple-element.19.refs_10_), channel_id=1, source_target_pairs={{0,112},{16,0},{32,16},{48,32},{64,48},{80,64},{96,80},{112,96},{1... | collective-permute-start | bytes 786440 | tf_op jit(solution)/shard_map/ppermute | solution.py:172
  126.8 18.1 %collective-permute-start.24 = (bf16[8,64,256]{2,1,0:T(8,128)(2,1)}, bf16[8,64,256]{2,1,0:T(8,128)(2,1)S(1)}, u32[]{:S(2)}, u32[]{:S(2)}) collective-permute-start(bf16[8,64,256]{2,1,0:T(8,128)(2,1)} %get-tuple-element.20.refs_9_), channel_id=1, source_target_pairs={{0,112},{16,0},{32,16},{48,32},{64,48},{80,64},{96,80},{112,96},{1... | collective-permute-start | bytes 786440 | tf_op jit(solution)/shard_map/ppermute | solution.py:172
  131.3 32.4 %copy-start.9 = (bf16[8,64,256]{2,1,0:T(8,128)(2,1)}, bf16[8,64,256]{2,1,0:T(8,128)(2,1)S(1)}, u32[]{:S(2)}) copy-start(bf16[8,64,256]{2,1,0:T(8,128)(2,1)S(1)} %collective-permute-done.18.refs_2_) | copy-start | bytes 786436
  131.3 32.4 %collective-permute-start.19 = (bf16[8,64,256]{2,1,0:T(8,128)(2,1)S(1)}, bf16[8,64,256]{2,1,0:T(8,128)(2,1)S(1)}, u32[]{:S(2)}, u32[]{:S(2)}) collective-permute-start(bf16[8,64,256]{2,1,0:T(8,128)(2,1)S(1)} %collective-permute-done.18.refs_2_), channel_id=1, source_target_pairs={{0,1},{1,2},{2,3},{3,4},{4,5},{5,6},{6,7},{7,8},{8,9},{9,10},{10,1... | collective-permute-start | bytes 786440 | tf_op jit(solution)/shard_map/ppermute | solution.py:172
  136.9 26.8 %copy-start.10 = (bf16[8,64,256]{2,1,0:T(8,128)(2,1)}, bf16[8,64,256]{2,1,0:T(8,128)(2,1)S(1)}, u32[]{:S(2)}) copy-start(bf16[8,64,256]{2,1,0:T(8,128)(2,1)S(1)} %collective-permute-done.20.refs_1_) | copy-start | bytes 786436
  136.9 26.8 %collective-permute-start.21 = (bf16[8,64,256]{2,1,0:T(8,128)(2,1)S(1)}, bf16[8,64,256]{2,1,0:T(8,128)(2,1)S(1)}, u32[]{:S(2)}, u32[]{:S(2)}) collective-permute-start(bf16[8,64,256]{2,1,0:T(8,128)(2,1)S(1)} %collective-permute-done.20.refs_1_), channel_id=1, source_target_pairs={{1,0},{2,1},{3,2},{4,3},{5,4},{6,5},{7,6},{8,7},{9,8},{10,9},{11,1... | collective-permute-start | bytes 786440 | tf_op jit(solution)/shard_map/ppermute | solution.py:172
  138.8 24.9 %copy-start.11 = (bf16[8,64,256]{2,1,0:T(8,128)(2,1)}, bf16[8,64,256]{2,1,0:T(8,128)(2,1)S(1)}, u32[]{:S(2)}) copy-start(bf16[8,64,256]{2,1,0:T(8,128)(2,1)S(1)} %collective-permute-done.22.refs_6_) | copy-start | bytes 786436
  138.8 24.8 %collective-permute-start.23 = (bf16[8,64,256]{2,1,0:T(8,128)(2,1)S(1)}, bf16[8,64,256]{2,1,0:T(8,128)(2,1)S(1)}, u32[]{:S(2)}, u32[]{:S(2)}) collective-permute-start(bf16[8,64,256]{2,1,0:T(8,128)(2,1)S(1)} %collective-permute-done.22.refs_6_), channel_id=1, source_target_pairs={{0,1},{1,2},{2,3},{3,4},{4,5},{5,6},{6,7},{7,8},{8,9},{9,10},{10,1... | collective-permute-start | bytes 786440 | tf_op jit(solution)/shard_map/ppermute | solution.py:172
  144.9 18.8 %copy-start.13 = (bf16[8,64,256]{2,1,0:T(8,128)(2,1)}, bf16[8,64,256]{2,1,0:T(8,128)(2,1)S(1)}, u32[]{:S(2)}) copy-start(bf16[8,64,256]{2,1,0:T(8,128)(2,1)S(1)} %collective-permute-done.24.refs_5_) | copy-start | bytes 786436
  144.9 18.8 %collective-permute-start.25 = (bf16[8,64,256]{2,1,0:T(8,128)(2,1)S(1)}, bf16[8,64,256]{2,1,0:T(8,128)(2,1)S(1)}, u32[]{:S(2)}, u32[]{:S(2)}) collective-permute-start(bf16[8,64,256]{2,1,0:T(8,128)(2,1)S(1)} %collective-permute-done.24.refs_5_), channel_id=1, source_target_pairs={{1,0},{2,1},{3,2},{4,3},{5,4},{6,5},{7,6},{8,7},{9,8},{10,9},{11,1... | collective-permute-start | bytes 786440 | tf_op jit(solution)/shard_map/ppermute | solution.py:172
  146.8 8.0 %collective-permute-start.26 = (bf16[2,64,256]{2,1,0:T(8,128)(2,1)}, bf16[2,64,256]{2,1,0:T(8,128)(2,1)S(1)}, u32[]{:S(2)}, u32[]{:S(2)}) collective-permute-start(bf16[2,64,256]{2,1,0:T(8,128)(2,1)} %get-tuple-element.21), channel_id=1, source_target_pairs={{0,1},{1,2},{2,3},{3,4},{4,5},{5,6},{6,7},{7,8},{8,9},{9,10},{10,1... | collective-permute-start | bytes 196616 | tf_op jit(solution)/shard_map/ppermute | solution.py:172
  154.8 8.9 %copy-start.29 = (bf16[2,64,256]{2,1,0:T(8,128)(2,1)}, bf16[2,64,256]{2,1,0:T(8,128)(2,1)S(1)}, u32[]{:S(2)}) copy-start(bf16[2,64,256]{2,1,0:T(8,128)(2,1)S(1)} %collective-permute-done.26.refs_8_) | copy-start | bytes 196612
  154.8 8.8 %collective-permute-start.27 = (bf16[2,64,256]{2,1,0:T(8,128)(2,1)}, bf16[2,64,256]{2,1,0:T(8,128)(2,1)S(1)}, u32[]{:S(2)}, u32[]{:S(2)}) collective-permute-start(bf16[2,64,256]{2,1,0:T(8,128)(2,1)} %get-tuple-element.22), channel_id=1, source_target_pairs={{1,0},{2,1},{3,2},{4,3},{5,4},{6,5},{7,6},{8,7},{9,8},{10,9},{11,1... | collective-permute-start | bytes 196616 | tf_op jit(solution)/shard_map/ppermute | solution.py:172
  163.6 0.6 copy-start.31
  163.6 0.7 copy-start.16
  163.6 0.8 copy-start.18
  163.7 0.9 copy-start.20
  163.7 0.9 copy-start.22

commit v2 on v1

--- a/solution.py
+++ b/solution.py
@@ -25,21 +25,25 @@
     return [w0 * x1[i] + w1 * x1[i + 1] for i in range(outs)]
 
 
-def level_kernel(sources, flags, vals, wu, wm, *refs):
+def level_kernel(sources, final, flags, vals, wu, wm, *refs):
     pieces = [refs[4 * i : 4 * i + 4] for i in range(sources)]
-    own_top, own_a, own_b, own_bot, out_a, out_b, out_first, out_last = refs[
-        4 * sources : 4 * sources + 8
-    ]
-    src, table, cols, passed, joined, act = refs[4 * sources + 8 :]
+    own_outer, own_edge, own_inner, own_near = refs[4 * sources : 4 * sources + 4]
+    outs = refs[4 * sources + 4 : -6]
+    src, table, cols, passed, joined, act = refs[-6:]
+    turned = flags[0]
+
+    def at(place, size):
+        return place + turned * (size - 2 * place)
 
     for i in range(sources):
         for p in range(4):
-            src[i, 8 * p : 8 * p + 8] = pieces[i][p][...]
+            src[i, pl.ds(at(8 * p, 24), 8)] = pieces[i][p][...]
     own_at = 2 * CH
-    joined[0:2, own_at : own_at + CH] = own_top[...]
-    joined[2:10, own_at : own_at + CH] = own_a[...]
-    joined[10:18, own_at : own_at + CH] = own_b[...]
-    joined[18:20, own_at : own_at + CH] = own_bot[...]
+    own_ch = slice(own_at, own_at + CH)
+    joined[pl.ds(at(0, 18), 2), own_ch] = own_outer[...]
+    joined[pl.ds(at(2, 12), 8), own_ch] = own_edge[...]
+    joined[pl.ds(at(10, 12), 8), own_ch] = own_inner[...]
+    joined[pl.ds(at(18, 18), 2), own_ch] = own_near[...]
 
     block_of = lax.broadcasted_iota(jnp.int32, (32, WIDTH), 1) // 8
     spread = (block_of == lax.broadcasted_iota(jnp.int32, (32, WIDTH), 0)).astype(F32)
@@ -47,8 +51,8 @@
         vals[...].astype(F32).astype(BF16), spread.astype(BF16), preferred_element_type=F32
     )
 
-    has_above = flags[0] > 0
-    has_below = flags[1] > 0
+    has_above = flags[1] > 0
+    has_below = flags[2] > 0
 
     def warp_block(which, block, first_source, count, outs, put):
         base = (which * 4 + block) * 8
@@ -63,7 +67,7 @@
         cols[...] = jnp.where(
             off == 0, 1.0 - fx, jnp.where(off == 1, fx, 0.0)
         ).astype(BF16)
-        source = which if sources == 2 else 0
+        source = which ^ flags[4] if sources == 2 else 0
         window = src[source, pl.ds(first_source, count)].reshape(count * CH, WIDTH)
         passed[0:count] = jnp.dot(
             window, cols[...], preferred_element_type=F32
@@ -119,36 +123,48 @@
         ).astype(F32)
         act[a] = (value * keep).astype(BF16)
 
-    scale = flags[2].astype(F32)
+    scale = flags[3].astype(F32)
 
     def finish(y):
         window = act[pl.ds(y, 3)].reshape(3 * CH, WIDTH)
         total = gather_taps(jnp.dot(wm[...], window, preferred_element_type=F32))
-        own = joined[y + 2, own_at : own_at + CH, :].astype(F32)
+        own = joined[y + 2, own_ch, :].astype(F32)
         return (own + scale * total).astype(BF16)
 
-    @pl.loop(0, HALF)
-    def _(y):
-        out_a[y] = finish(y)
-
-    @pl.loop(0, HALF)
-    def _(y):
-        out_b[y] = finish(y + HALF)
-
-    out_first[...] = out_a[0:2]
-    out_last[...] = out_b[6:8]
-
-
-def run_level(flags, vals, wu, wm, sources, own, interpret=False):
+    if final:
+        (out,) = outs
+
+        @pl.loop(0, 16)
+        def _(y):
+            out[y] = finish(y)
+
+    else:
+        out_edge, out_inner, out_rim, out_near = outs
+
+        @pl.loop(0, HALF)
+        def _(y):
+            out_edge[y] = finish(y + at(0, 8))
+
+        @pl.loop(0, HALF)
+        def _(y):
+            out_inner[y] = finish(y + at(8, 8))
+
+        out_rim[...] = out_edge[pl.ds(at(0, 6), 2)]
+        out_near[...] = out_inner[pl.ds(at(6, 6), 2)]
+
+
+def run_level(flags, vals, wu, wm, sources, own, final, interpret=False):
     half = jax.ShapeDtypeStruct((HALF, CH, WIDTH), BF16)
     edge = jax.ShapeDtypeStruct((2, CH, WIDTH), BF16)
+    full = jax.ShapeDtypeStruct((2 * HALF, CH, WIDTH), BF16)
     operands = [p for s in sources for p in s] + list(own)
     vmem = pl.BlockSpec(memory_space=pltpu.VMEM)
+    out_shape = (full,) if final else (half, half, edge, edge)
     return pl.pallas_call(
-        functools.partial(level_kernel, len(sources)),
-        out_shape=(half, half, edge, edge),
+        functools.partial(level_kernel, len(sources), final),
+        out_shape=out_shape,
         in_specs=[pl.BlockSpec(memory_space=pltpu.SMEM)] + [vmem] * (3 + len(operands)),
-        out_specs=(vmem,) * 4,
+        out_specs=(vmem,) * len(out_shape),
         scratch_shapes=[
             pltpu.VMEM((len(sources), 32, CH, WIDTH), BF16),
             pltpu.VMEM((64, WIDTH), F32),
@@ -164,12 +180,23 @@
     )(flags, vals, wu, wm, *operands)
 
 
-def moved(x, axis, distance, wrap):
-    count = lax.axis_size(axis)
+def send(x, frame_to=lambda t: t, row_to=lambda r: r):
+    frames, rows = lax.axis_size("tm"), lax.axis_size("rows")
     route = [
-        (i, (i + distance) % count) for i in range(count) if wrap or 0 <= i + distance < count
+        (t * rows + r, (frame_to(t) % frames) * rows + row_to(r))
+        for t in range(frames)
+        for r in range(rows)
+        if 0 <= row_to(r) < rows
     ]
-    return lax.ppermute(x, axis, route)
+    return lax.ppermute(x, ("tm", "rows"), route)
+
+
+def off_chip(r):
+    return r + 1 if r % 2 else r - 1
+
+
+def on_chip(r):
+    return r ^ 1
 
 
 def level_values(packed, level):
@@ -186,41 +213,76 @@
 
 def shards(features, block_shift, quarter_pel, update_mask, uniting_weight, mixing_weight):
     band = features[0]
-    a, b = band[:HALF], band[HALF:]
-    first, last = band[:2], band[-2:]
     row = lax.axis_index("rows")
     rows = lax.axis_size("rows")
+    frames = lax.axis_size("tm")
+    turned = row % 2
+    edge = lax.dynamic_slice_in_dim(band, 8 * turned, HALF, axis=0)
+    inner = lax.dynamic_slice_in_dim(band, 8 - 8 * turned, HALF, axis=0)
+    rim = lax.dynamic_slice_in_dim(band, 14 * turned, 2, axis=0)
+    near = lax.dynamic_slice_in_dim(band, 14 - 14 * turned, 2, axis=0)
     own = jnp.stack([block_shift[:, :, 0], quarter_pel[:, :, 0]])
-    above = moved(own[:, :, :, 1:2], "rows", 1, False)
-    below = moved(own[:, :, :, 0:1], "rows", -1, False)
+    above = send(own[:, :, :, 1:2], row_to=lambda r: r + 1)
+    below = send(own[:, :, :, 0:1], row_to=lambda r: r - 1)
     packed = jnp.concatenate([above, own, below], axis=3)
     wu, wm = tap_weights(uniting_weight), tap_weights(mixing_weight)
-    frames = lax.axis_size("tm")
     for level in range(LEVELS - 1, -1, -1):
         distance = 2**level
-        steps = [distance] if 2 * distance == frames else [distance, -distance]
-        own_top = moved(last, "rows", 1, False)
-        own_bot = moved(first, "rows", -1, False)
-        sources = []
-        for step in steps:
-            ra = moved(a, "tm", step, True)
-            rb = moved(b, "tm", step, True)
-            sources.append((ra, rb))
-        sources = [
-            (moved(rb, "rows", 1, False), ra, rb, moved(ra, "rows", -1, False))
-            for ra, rb in sources
-        ]
+        swapped = jnp.int32(0)
+        if 2 * distance == frames:
+
+            def flip(t):
+                return t + distance
+
+            sources = [
+                (send(edge, flip, off_chip), send(edge, flip), send(inner, flip)),
+            ]
+        elif 4 * distance == frames:
+
+            def across(t):
+                return t + distance if t % (2 * distance) < distance else t - distance
+
+            def flip(t):
+                return t + 2 * distance
+
+            e, i = send(edge, across), send(inner, across)
+            sources = [
+                (send(edge, across, off_chip), e, i),
+                (send(e, flip, off_chip), send(e, flip), send(i, flip)),
+            ]
+            swapped = (lax.axis_index("tm") % (2 * distance) < distance).astype(jnp.int32)
+        else:
+            sources = []
+            for step in (distance, -distance):
+
+                def to(t, step=step):
+                    return t + step
+
+                sources.append((send(edge, to, off_chip), send(edge, to), send(inner, to)))
+        own_outer = send(rim, row_to=off_chip)
+        own_near = send(near, row_to=on_chip)
+        sources = [(h, e, i, send(i, row_to=on_chip)) for h, e, i in sources]
         flags = jnp.stack(
             [
+                turned,
                 (row > 0).astype(jnp.int32),
                 (row < rows - 1).astype(jnp.int32),
                 update_mask[level, 0],
+                swapped,
             ]
         )
-        a, b, first, last = run_level(
-            flags, level_values(packed, level), wu, wm, sources, (own_top, a, b, own_bot)
+        outs = run_level(
+            flags,
+            level_values(packed, level),
+            wu,
+            wm,
+            sources,
+            (own_outer, edge, inner, own_near),
+            level == 0,
         )
-    return jnp.concatenate([a, b])[None]
+        if level:
+            edge, inner, rim, near = outs
+    return outs[0][None]
 
 
 def solution(mesh):

time: 184 us -> 155 us (0.84)
  the two profiles are of different devices: /device:TPU:7 before, /device:TPU:9 now
where the time goes in v2:
time: 155 us
  starting transfers between devices  61.2 us (39%)
  Pallas kernels  48.4 us (31%)
  waiting for transfers between devices  31.3 us (20%)
  local copies, waits for them, and re-layouts  13.1 us (8%)
    ppermute x28, starting transfers between devices, send(): return lax.ppermute(x, ('tm', 'rows'), route)  61.2 us
    pallas_call x3, Pallas kernels, run_level(): pl.pallas_call(functools.partial(level_kernel, len(sources), final), out_...  48.4 us
    ppermute x28, waiting for transfers between devices, send(): return lax.ppermute(x, ('tm', 'rows'), route)  31.3 us
    another operation x3, local copies, waits for them, and re-layouts, shards(): jnp.stack([turned, (row > 0).astype(jnp.int32), (row < rows - 1).astype(j...  3.87 us
  transfers between devices with their start and end apart: 28, of which 9 were waited for; matrix products, arithmetic and copies ran while one was open for 6% of the time, Pallas kernels for 0%

profile of v2, /device:TPU:9, one launch (start us, length us, event | category | flops | bytes accessed | tf_op | source)
XLA Modules:
  0.0 154.7 jit_solution(13316790640519810949)
XLA Ops:
  0.0 1.1 dynamic-slice_bitcast_fusion
  1.1 5.1 %collective-permute-start.2 = (bf16[8,64,256]{2,1,0:T(8,128)(2,1)S(1)}, bf16[8,64,256]{2,1,0:T(8,128)(2,1)S(1)}, u32[]{:S(2)}, u32[]{:S(2)}) collective-permute-start(bf16[8,64,256]{2,1,0:T(8,128)(2,1)S(1)} %get-tuple-element.24.refs_5_), channel_id=1, source_target_pairs={{1,66},{2,65},{3,68},{4,67},{5,70},{6,69},{7,72},{8,71},{9,74},{10... | collective-permute-start | bytes 786440 | tf_op jit(solution)/shard_map/ppermute | solution.py:191
  6.2 0.1 collective-permute-start.3
  6.3 1.5 collective-permute-start.4
  7.8 2.7 %collective-permute-start = (s32[2,3,4,1,32]{4,3,2,1,0:T(1,128)S(1)}, s32[2,3,4,1,32]{4,3,2,1,0:T(1,128)S(1)}, u32[]{:S(2)}, u32[]{:S(2)}) collective-permute-start(s32[2,3,4,1,32]{4,3,2,1,0:T(1,128)S(1)} %get-tuple-element.28), channel_id=1, source_target_pairs={{0,1},{1,2},{2,3},{3,4},{4,5},{5,6},{6,7},{7,8},{8,9},{9,10},{10,1... | collective-permute-start | bytes 9224 | tf_op jit(solution)/shard_map/ppermute | solution.py:191
  10.5 1.9 %collective-permute-start.1 = (s32[2,3,4,1,32]{4,3,2,1,0:T(1,128)S(1)}, s32[2,3,4,1,32]{4,3,2,1,0:T(1,128)S(1)}, u32[]{:S(2)}, u32[]{:S(2)}) collective-permute-start(s32[2,3,4,1,32]{4,3,2,1,0:T(1,128)S(1)} %get-tuple-element.29), channel_id=1, source_target_pairs={{1,0},{2,1},{3,2},{4,3},{5,4},{6,5},{7,6},{8,7},{9,8},{10,9},{11,1... | collective-permute-start | bytes 9224 | tf_op jit(solution)/shard_map/ppermute | solution.py:191
  12.5 0.0 copy-start.6
  12.5 0.9 dynamic-slice_bitcast_fusion.2
  13.4 0.7 fusion.2
  14.1 0.3 copy.13
  14.4 1.0 reshape.30.wu
  15.4 0.1 copy.14
  15.5 0.8 reshape.31.wm
  16.3 1.3 stack.49.flags
  17.5 0.7 collective-permute-done
  18.2 5.9 %collective-permute-start.6 = (bf16[2,64,256]{2,1,0:T(8,128)(2,1)S(1)}, bf16[2,64,256]{2,1,0:T(8,128)(2,1)S(1)}, u32[]{:S(2)}, u32[]{:S(2)}) collective-permute-start(bf16[2,64,256]{2,1,0:T(8,128)(2,1)S(1)} %get-tuple-element.22), channel_id=1, source_target_pairs={{1,2},{2,1},{3,4},{4,3},{5,6},{6,5},{7,8},{8,7},{9,10},{10,9},{11,... | collective-permute-start | bytes 196616 | tf_op jit(solution)/shard_map/ppermute | solution.py:191
  24.1 0.1 collective-permute-start.7
  24.2 0.5 collective-permute-start.5
  24.8 0.6 pad.12
  25.4 0.6 collective-permute-done.6.refs_4_
  26.1 0.5 copy-done.31
  26.6 0.0 copy-done.32
  26.7 0.1 copy-done.7
  26.8 0.1 copy-done.8
  26.9 0.1 copy-done.25
  26.9 15.9 %shard_map.64 = (bf16[8,64,256]{2,1,0:T(8,128)(2,1)}, bf16[8,64,256]{2,1,0:T(8,128)(2,1)}, bf16[2,64,256]{2,1,0:T(8,128)(2,1)}, bf16[2,64,256]{2,1,0:T(8,128)(2,1)}) custom-call(s32[5]{0:T(128)} %stack.49.flags, s32[64,32]{1,0:T(8,128)} %bitcast.49, bf16[192,576]{1,0:T(8,128)(2,1)} %reshape.30.wu, bf16[192,192]{1,0:T(8,128)(2,1)} %reshape.31.wm, ...), custom_call_target="tpu_custom_call" | custom-call | flops 3000000000 | bytes 4000000 | tf_op jit(solution)/shard_map/pallas_call | solution.py:163
  42.8 3.6 %collective-permute-start.10 = (bf16[8,64,256]{2,1,0:T(8,128)(2,1)}, bf16[8,64,256]{2,1,0:T(8,128)(2,1)S(1)}, u32[]{:S(2)}, u32[]{:S(2)}) collective-permute-start(bf16[8,64,256]{2,1,0:T(8,128)(2,1)} %get-tuple-element.14.refs_10_), channel_id=1, source_target_pairs={{0,32},{1,33},{2,34},{3,35},{4,36},{5,37},{6,38},{7,39},{8,40},{9,... | collective-permute-start | bytes 786440 | tf_op jit(solution)/shard_map/ppermute | solution.py:191
  46.4 0.1 collective-permute-start.9
  46.5 3.9 %collective-permute-done.10.refs_2_ = bf16[8,64,256]{2,1,0:T(8,128)(2,1)S(1)} collective-permute-done((bf16[8,64,256]{2,1,0:T(8,128)(2,1)}, bf16[8,64,256]{2,1,0:T(8,128)(2,1)S(1)}, u32[]{:S(2)}, u32[]{:S(2)}) %collective-permute-start.10) | collective-permute-done | bytes 262176 | tf_op jit(solution)/shard_map/ppermute | solution.py:191
  50.4 2.7 %collective-permute-start.14 = (bf16[8,64,256]{2,1,0:T(8,128)(2,1)S(1)}, bf16[8,64,256]{2,1,0:T(8,128)(2,1)S(1)}, u32[]{:S(2)}, u32[]{:S(2)}) collective-permute-start(bf16[8,64,256]{2,1,0:T(8,128)(2,1)S(1)} %collective-permute-done.10.refs_2_), channel_id=1, source_target_pairs={{0,64},{1,65},{2,66},{3,67},{4,68},{5,69},{6,70},{7,71},{8,72},{9,... | collective-permute-start | bytes 786440 | tf_op jit(solution)/shard_map/ppermute | solution.py:191
  53.1 8.4 %collective-permute-start.16 = (bf16[2,64,256]{2,1,0:T(8,128)(2,1)}, bf16[2,64,256]{2,1,0:T(8,128)(2,1)S(1)}, u32[]{:S(2)}, u32[]{:S(2)}) collective-permute-start(bf16[2,64,256]{2,1,0:T(8,128)(2,1)} %get-tuple-element.15), channel_id=1, source_target_pairs={{1,2},{2,1},{3,4},{4,3},{5,6},{6,5},{7,8},{8,7},{9,10},{10,9},{11,... | collective-permute-start | bytes 196616 | tf_op jit(solution)/shard_map/ppermute | solution.py:191
  61.5 0.1 collective-permute-start.17
  61.6 6.9 %collective-permute-start.8 = (bf16[8,64,256]{2,1,0:T(8,128)(2,1)}, bf16[8,64,256]{2,1,0:T(8,128)(2,1)S(1)}, u32[]{:S(2)}, u32[]{:S(2)}) collective-permute-start(bf16[8,64,256]{2,1,0:T(8,128)(2,1)} %get-tuple-element.13.refs_9_), channel_id=1, source_target_pairs={{1,34},{2,33},{3,36},{4,35},{5,38},{6,37},{7,40},{8,39},{9,42},{10... | collective-permute-start | bytes 786440 | tf_op jit(solution)/shard_map/ppermute | solution.py:191
  68.5 0.1 collective-permute-start.11
  68.6 3.1 %collective-permute-start.12 = (bf16[8,64,256]{2,1,0:T(8,128)(2,1)S(1)}, bf16[8,64,256]{2,1,0:T(8,128)(2,1)S(1)}, u32[]{:S(2)}, u32[]{:S(2)}) collective-permute-start(bf16[8,64,256]{2,1,0:T(8,128)(2,1)S(1)} %collective-permute-done.9.refs_1_), channel_id=1, source_target_pairs={{1,66},{2,65},{3,68},{4,67},{5,70},{6,69},{7,72},{8,71},{9,74},{10... | collective-permute-start | bytes 786440 | tf_op jit(solution)/shard_map/ppermute | solution.py:191
  71.8 1.2 collective-permute-start.13
  73.0 0.2 collective-permute-start.15
  73.2 1.3 stack.48.flags
  74.5 0.6 pad.11
  75.1 1.0 collective-permute-done.8.refs_0_
  76.1 6.2 %collective-permute-done.12.refs_4_ = bf16[8,64,256]{2,1,0:T(8,128)(2,1)S(1)} collective-permute-done((bf16[8,64,256]{2,1,0:T(8,128)(2,1)S(1)}, bf16[8,64,256]{2,1,0:T(8,128)(2,1)S(1)}, u32[]{:S(2)}, u32[]{:S(2)}) %collective-permute-start.12) | collective-permute-done | bytes 262176 | tf_op jit(solution)/shard_map/ppermute | solution.py:191
  82.4 0.6 copy-done.15
  83.0 0.1 copy-done.18
  83.1 0.1 copy-done.20
  83.2 16.2 %shard_map.65 = (bf16[8,64,256]{2,1,0:T(8,128)(2,1)}, bf16[8,64,256]{2,1,0:T(8,128)(2,1)}, bf16[2,64,256]{2,1,0:T(8,128)(2,1)}, bf16[2,64,256]{2,1,0:T(8,128)(2,1)}) custom-call(s32[5]{0:T(128)} %stack.48.flags, s32[64,32]{1,0:T(8,128)} %bitcast.47, bf16[192,576]{1,0:T(8,128)(2,1)} %reshape.30.wu, bf16[192,192]{1,0:T(8,128)(2,1)} %reshape.31.wm, ...), custom_call_target="tpu_custom_call" | custom-call | flops 3000000000 | bytes 4000000 | tf_op jit(solution)/shard_map/pallas_call | solution.py:163
  99.4 0.7 collective-permute-start.20
  100.1 2.8 %collective-permute-start.24 = (bf16[8,64,256]{2,1,0:T(8,128)(2,1)}, bf16[8,64,256]{2,1,0:T(8,128)(2,1)S(1)}, u32[]{:S(2)}, u32[]{:S(2)}) collective-permute-start(bf16[8,64,256]{2,1,0:T(8,128)(2,1)} %get-tuple-element.18.refs_10_), channel_id=1, source_target_pairs={{0,112},{1,113},{2,114},{3,115},{4,116},{5,117},{6,118},{7,119},{8... | collective-permute-start | bytes 786440 | tf_op jit(solution)/shard_map/ppermute | solution.py:191
  103.0 2.9 %collective-permute-start.18 = (bf16[8,64,256]{2,1,0:T(8,128)(2,1)}, bf16[8,64,256]{2,1,0:T(8,128)(2,1)S(1)}, u32[]{:S(2)}, u32[]{:S(2)}) collective-permute-start(bf16[8,64,256]{2,1,0:T(8,128)(2,1)} %get-tuple-element.17.refs_9_), channel_id=1, source_target_pairs={{1,18},{2,17},{3,20},{4,19},{5,22},{6,21},{7,24},{8,23},{9,26},{10... | collective-permute-start | bytes 786440 | tf_op jit(solution)/shard_map/ppermute | solution.py:191
  105.9 3.6 %collective-permute-start.26 = (bf16[2,64,256]{2,1,0:T(8,128)(2,1)}, bf16[2,64,256]{2,1,0:T(8,128)(2,1)S(1)}, u32[]{:S(2)}, u32[]{:S(2)}) collective-permute-start(bf16[2,64,256]{2,1,0:T(8,128)(2,1)} %get-tuple-element.19), channel_id=1, source_target_pairs={{1,2},{2,1},{3,4},{4,3},{5,6},{6,5},{7,8},{8,7},{9,10},{10,9},{11,... | collective-permute-start | bytes 196616 | tf_op jit(solution)/shard_map/ppermute | solution.py:191
  109.5 0.5 collective-permute-start.27
  109.9 9.4 %collective-permute-done.26.refs_8_ = bf16[2,64,256]{2,1,0:T(8,128)(2,1)S(1)} collective-permute-done((bf16[2,64,256]{2,1,0:T(8,128)(2,1)}, bf16[2,64,256]{2,1,0:T(8,128)(2,1)S(1)}, u32[]{:S(2)}, u32[]{:S(2)}) %collective-permute-start.26) | collective-permute-done | bytes 65568 | tf_op jit(solution)/shard_map/ppermute | solution.py:191
  119.3 4.8 %collective-permute-start.22 = (bf16[8,64,256]{2,1,0:T(8,128)(2,1)}, bf16[8,64,256]{2,1,0:T(8,128)(2,1)S(1)}, u32[]{:S(2)}, u32[]{:S(2)}) collective-permute-start(bf16[8,64,256]{2,1,0:T(8,128)(2,1)} %get-tuple-element.17.refs_9_), channel_id=1, source_target_pairs={{1,114},{2,113},{3,116},{4,115},{5,118},{6,117},{7,120},{8,119},{9... | collective-permute-start | bytes 786440 | tf_op jit(solution)/shard_map/ppermute | solution.py:191
  124.2 0.7 collective-permute-start.23
  124.9 0.9 collective-permute-start.21
  125.9 0.1 collective-permute-start.25
  126.0 1.3 stack.44.flags
  127.3 0.6 pad.10
  127.9 1.7 %collective-permute-done.19.refs_1_ = bf16[8,64,256]{2,1,0:T(8,128)(2,1)S(1)} collective-permute-done((bf16[8,64,256]{2,1,0:T(8,128)(2,1)}, bf16[8,64,256]{2,1,0:T(8,128)(2,1)S(1)}, u32[]{:S(2)}, u32[]{:S(2)}) %collective-permute-start.19) | collective-permute-done | bytes 262176 | tf_op jit(solution)/shard_map/ppermute | solution.py:191
  129.7 2.3 %collective-permute-done.22.refs_4_ = bf16[8,64,256]{2,1,0:T(8,128)(2,1)S(1)} collective-permute-done((bf16[8,64,256]{2,1,0:T(8,128)(2,1)}, bf16[8,64,256]{2,1,0:T(8,128)(2,1)S(1)}, u32[]{:S(2)}, u32[]{:S(2)}) %collective-permute-start.22) | collective-permute-done | bytes 262176 | tf_op jit(solution)/shard_map/ppermute | solution.py:191
  132.0 5.5 %collective-permute-done.23.refs_5_ = bf16[8,64,256]{2,1,0:T(8,128)(2,1)S(1)} collective-permute-done((bf16[8,64,256]{2,1,0:T(8,128)(2,1)}, bf16[8,64,256]{2,1,0:T(8,128)(2,1)S(1)}, u32[]{:S(2)}, u32[]{:S(2)}) %collective-permute-start.23) | collective-permute-done | bytes 262176 | tf_op jit(solution)/shard_map/ppermute | solution.py:191
  137.6 0.6 copy-done.23
  138.2 0.1 copy-done.24
  138.3 0.1 copy-done.26
  138.4 16.3 %shard_map.66 = bf16[16,64,256]{2,1,0:T(8,128)(2,1)} custom-call(s32[5]{0:T(128)} %stack.44.flags, s32[64,32]{1,0:T(8,128)} %bitcast.48, bf16[192,576]{1,0:T(8,128)(2,1)} %reshape.30.wu, bf16[192,192]{1,0:T(8,128)(2,1)} %reshape.31.wm, bf16[8,64,256]{2,1,0:T(8,128)(2,1)} %copy-done.19, bf16[8,64,256]{2,1,0:T(8,128)(2,1)} %copy-done.21, ...), custom_call_target="tpu_custom_call" | custom-call | flops 3000000000 | bytes 4000000 | tf_op jit(solution)/shard_map/pallas_call | solution.py:163
  (80 shorter events, 0.3 us)
Async XLA Ops:
  0.0 7.8 %copy-start.4 = (s32[3,4,1,2,32]{4,3,2,1,0:T(2,128)S(1)}, s32[3,4,1,2,32]{4,3,2,1,0:T(2,128)}, u32[]{:S(2)}) copy-start(s32[3,4,1,2,32]{4,3,2,1,0:T(2,128)} %param.7) | copy-start | bytes 9220
  0.0 7.8 %copy-start.5 = (s32[3,4,1,2,32]{4,3,2,1,0:T(2,128)S(1)}, s32[3,4,1,2,32]{4,3,2,1,0:T(2,128)}, u32[]{:S(2)}) copy-start(s32[3,4,1,2,32]{4,3,2,1,0:T(2,128)} %param.8) | copy-start | bytes 9220
  1.1 13.2 %copy-start.1 = (bf16[8,64,256]{2,1,0:T(8,128)(2,1)}, bf16[8,64,256]{2,1,0:T(8,128)(2,1)S(1)}, u32[]{:S(2)}) copy-start(bf16[8,64,256]{2,1,0:T(8,128)(2,1)S(1)} %get-tuple-element.23.refs_6_) | copy-start | bytes 786436
  1.1 13.2 %copy-start.2 = (bf16[8,64,256]{2,1,0:T(8,128)(2,1)}, bf16[8,64,256]{2,1,0:T(8,128)(2,1)S(1)}, u32[]{:S(2)}) copy-start(bf16[8,64,256]{2,1,0:T(8,128)(2,1)S(1)} %get-tuple-element.24.refs_5_) | copy-start | bytes 786436
  1.1 13.0 %copy-start = (bf16[3,3,64,192]{3,2,1,0:T(8,128)(2,1)S(1)}, bf16[3,3,64,192]{3,2,1,0:T(8,128)(2,1)}, u32[]{:S(2)}) copy-start(bf16[3,3,64,192]{3,2,1,0:T(8,128)(2,1)} %param.10) | copy-start | bytes 663556
  1.1 24.9 %collective-permute-start.2 = (bf16[8,64,256]{2,1,0:T(8,128)(2,1)S(1)}, bf16[8,64,256]{2,1,0:T(8,128)(2,1)S(1)}, u32[]{:S(2)}, u32[]{:S(2)}) collective-permute-start(bf16[8,64,256]{2,1,0:T(8,128)(2,1)S(1)} %get-tuple-element.24.refs_5_), channel_id=1, source_target_pairs={{1,66},{2,65},{3,68},{4,67},{5,70},{6,69},{7,72},{8,71},{9,74},{10... | collective-permute-start | bytes 786440 | tf_op jit(solution)/shard_map/ppermute | solution.py:191
  6.2 19.8 %collective-permute-start.3 = (bf16[8,64,256]{2,1,0:T(8,128)(2,1)S(1)}, bf16[8,64,256]{2,1,0:T(8,128)(2,1)S(1)}, u32[]{:S(2)}, u32[]{:S(2)}) collective-permute-start(bf16[8,64,256]{2,1,0:T(8,128)(2,1)S(1)} %get-tuple-element.24.refs_5_), channel_id=1, source_target_pairs={{0,64},{1,65},{2,66},{3,67},{4,68},{5,69},{6,70},{7,71},{8,72},{9,... | collective-permute-start | bytes 786440 | tf_op jit(solution)/shard_map/ppermute | solution.py:191
  6.3 17.9 %collective-permute-start.4 = (bf16[8,64,256]{2,1,0:T(8,128)(2,1)S(1)}, bf16[8,64,256]{2,1,0:T(8,128)(2,1)S(1)}, u32[]{:S(2)}, u32[]{:S(2)}) collective-permute-start(bf16[8,64,256]{2,1,0:T(8,128)(2,1)S(1)} %get-tuple-element.23.refs_6_), channel_id=1, source_target_pairs={{0,64},{1,65},{2,66},{3,67},{4,68},{5,69},{6,70},{7,71},{8,72},{9,... | collective-permute-start | bytes 786440 | tf_op jit(solution)/shard_map/ppermute | solution.py:191
  7.8 10.4 %collective-permute-start = (s32[2,3,4,1,32]{4,3,2,1,0:T(1,128)S(1)}, s32[2,3,4,1,32]{4,3,2,1,0:T(1,128)S(1)}, u32[]{:S(2)}, u32[]{:S(2)}) collective-permute-start(s32[2,3,4,1,32]{4,3,2,1,0:T(1,128)S(1)} %get-tuple-element.28), channel_id=1, source_target_pairs={{0,1},{1,2},{2,3},{3,4},{4,5},{5,6},{6,7},{7,8},{8,9},{9,10},{10,1... | collective-permute-start | bytes 9224 | tf_op jit(solution)/shard_map/ppermute | solution.py:191
  10.5 13.5 %collective-permute-start.1 = (s32[2,3,4,1,32]{4,3,2,1,0:T(1,128)S(1)}, s32[2,3,4,1,32]{4,3,2,1,0:T(1,128)S(1)}, u32[]{:S(2)}, u32[]{:S(2)}) collective-permute-start(s32[2,3,4,1,32]{4,3,2,1,0:T(1,128)S(1)} %get-tuple-element.29), channel_id=1, source_target_pairs={{1,0},{2,1},{3,2},{4,3},{5,4},{6,5},{7,6},{8,7},{9,8},{10,9},{11,1... | collective-permute-start | bytes 9224 | tf_op jit(solution)/shard_map/ppermute | solution.py:191
  12.5 0.9 copy-start.6
  14.3 1.0 copy-start.3
  18.2 7.8 %collective-permute-start.6 = (bf16[2,64,256]{2,1,0:T(8,128)(2,1)S(1)}, bf16[2,64,256]{2,1,0:T(8,128)(2,1)S(1)}, u32[]{:S(2)}, u32[]{:S(2)}) collective-permute-start(bf16[2,64,256]{2,1,0:T(8,128)(2,1)S(1)} %get-tuple-element.22), channel_id=1, source_target_pairs={{1,2},{2,1},{3,4},{4,3},{5,6},{6,5},{7,8},{8,7},{9,10},{10,9},{11,... | collective-permute-start | bytes 196616 | tf_op jit(solution)/shard_map/ppermute | solution.py:191
  24.1 1.9 %collective-permute-start.7 = (bf16[2,64,256]{2,1,0:T(8,128)(2,1)S(1)}, bf16[2,64,256]{2,1,0:T(8,128)(2,1)S(1)}, u32[]{:S(2)}, u32[]{:S(2)}) collective-permute-start(bf16[2,64,256]{2,1,0:T(8,128)(2,1)S(1)} %get-tuple-element.21), channel_id=1, source_target_pairs={{0,1},{1,0},{2,3},{3,2},{4,5},{5,4},{6,7},{7,6},{8,9},{9,8},{10,11... | collective-permute-start | bytes 196616 | tf_op jit(solution)/shard_map/ppermute | solution.py:191
  24.2 1.9 %copy-start.11 = (bf16[8,64,256]{2,1,0:T(8,128)(2,1)}, bf16[8,64,256]{2,1,0:T(8,128)(2,1)S(1)}, u32[]{:S(2)}) copy-start(bf16[8,64,256]{2,1,0:T(8,128)(2,1)S(1)} %collective-permute-done.4.refs_2_) | copy-start | bytes 786436
  24.2 1.9 %collective-permute-start.5 = (bf16[8,64,256]{2,1,0:T(8,128)(2,1)S(1)}, bf16[8,64,256]{2,1,0:T(8,128)(2,1)S(1)}, u32[]{:S(2)}, u32[]{:S(2)}) collective-permute-start(bf16[8,64,256]{2,1,0:T(8,128)(2,1)S(1)} %collective-permute-done.4.refs_2_), channel_id=1, source_target_pairs={{0,1},{1,0},{2,3},{3,2},{4,5},{5,4},{6,7},{7,6},{8,9},{9,8},{10,11... | collective-permute-start | bytes 786440 | tf_op jit(solution)/shard_map/ppermute | solution.py:191
  26.0 0.6 copy-start.31
  26.0 0.6 copy-start.32
  26.0 0.7 copy-start.7
  26.0 0.8 copy-start.8
  26.1 0.9 copy-start.25
  42.8 7.6 %collective-permute-start.10 = (bf16[8,64,256]{2,1,0:T(8,128)(2,1)}, bf16[8,64,256]{2,1,0:T(8,128)(2,1)S(1)}, u32[]{:S(2)}, u32[]{:S(2)}) collective-permute-start(bf16[8,64,256]{2,1,0:T(8,128)(2,1)} %get-tuple-element.14.refs_10_), channel_id=1, source_target_pairs={{0,32},{1,33},{2,34},{3,35},{4,36},{5,37},{6,38},{7,39},{8,40},{9,... | collective-permute-start | bytes 786440 | tf_op jit(solution)/shard_map/ppermute | solution.py:191
  46.4 22.2 %collective-permute-start.9 = (bf16[8,64,256]{2,1,0:T(8,128)(2,1)}, bf16[8,64,256]{2,1,0:T(8,128)(2,1)S(1)}, u32[]{:S(2)}, u32[]{:S(2)}) collective-permute-start(bf16[8,64,256]{2,1,0:T(8,128)(2,1)} %get-tuple-element.13.refs_9_), channel_id=1, source_target_pairs={{0,32},{1,33},{2,34},{3,35},{4,36},{5,37},{6,38},{7,39},{8,40},{9,... | collective-permute-start | bytes 786440 | tf_op jit(solution)/shard_map/ppermute | solution.py:191
  50.4 31.9 %copy-start.9 = (bf16[8,64,256]{2,1,0:T(8,128)(2,1)}, bf16[8,64,256]{2,1,0:T(8,128)(2,1)S(1)}, u32[]{:S(2)}) copy-start(bf16[8,64,256]{2,1,0:T(8,128)(2,1)S(1)} %collective-permute-done.10.refs_2_) | copy-start | bytes 786436
  50.4 22.6 %collective-permute-start.14 = (bf16[8,64,256]{2,1,0:T(8,128)(2,1)S(1)}, bf16[8,64,256]{2,1,0:T(8,128)(2,1)S(1)}, u32[]{:S(2)}, u32[]{:S(2)}) collective-permute-start(bf16[8,64,256]{2,1,0:T(8,128)(2,1)S(1)} %collective-permute-done.10.refs_2_), channel_id=1, source_target_pairs={{0,64},{1,65},{2,66},{3,67},{4,68},{5,69},{6,70},{7,71},{8,72},{9,... | collective-permute-start | bytes 786440 | tf_op jit(solution)/shard_map/ppermute | solution.py:191
  53.1 15.4 %collective-permute-start.16 = (bf16[2,64,256]{2,1,0:T(8,128)(2,1)}, bf16[2,64,256]{2,1,0:T(8,128)(2,1)S(1)}, u32[]{:S(2)}, u32[]{:S(2)}) collective-permute-start(bf16[2,64,256]{2,1,0:T(8,128)(2,1)} %get-tuple-element.15), channel_id=1, source_target_pairs={{1,2},{2,1},{3,4},{4,3},{5,6},{6,5},{7,8},{8,7},{9,10},{10,9},{11,... | collective-permute-start | bytes 196616 | tf_op jit(solution)/shard_map/ppermute | solution.py:191
  61.5 10.3 %collective-permute-start.17 = (bf16[2,64,256]{2,1,0:T(8,128)(2,1)}, bf16[2,64,256]{2,1,0:T(8,128)(2,1)S(1)}, u32[]{:S(2)}, u32[]{:S(2)}) collective-permute-start(bf16[2,64,256]{2,1,0:T(8,128)(2,1)} %get-tuple-element.16), channel_id=1, source_target_pairs={{0,1},{1,0},{2,3},{3,2},{4,5},{5,4},{6,7},{7,6},{8,9},{9,8},{10,11... | collective-permute-start | bytes 196616 | tf_op jit(solution)/shard_map/ppermute | solution.py:191
  61.6 14.5 %collective-permute-start.8 = (bf16[8,64,256]{2,1,0:T(8,128)(2,1)}, bf16[8,64,256]{2,1,0:T(8,128)(2,1)S(1)}, u32[]{:S(2)}, u32[]{:S(2)}) collective-permute-start(bf16[8,64,256]{2,1,0:T(8,128)(2,1)} %get-tuple-element.13.refs_9_), channel_id=1, source_target_pairs={{1,34},{2,33},{3,36},{4,35},{5,38},{6,37},{7,40},{8,39},{9,42},{10... | collective-permute-start | bytes 786440 | tf_op jit(solution)/shard_map/ppermute | solution.py:191
  68.5 13.8 %copy-start.27 = (bf16[2,64,256]{2,1,0:T(8,128)(2,1)}, bf16[2,64,256]{2,1,0:T(8,128)(2,1)S(1)}, u32[]{:S(2)}) copy-start(bf16[2,64,256]{2,1,0:T(8,128)(2,1)S(1)} %collective-permute-done.16.refs_8_) | copy-start | bytes 196612
  68.5 7.6 %collective-permute-start.11 = (bf16[8,64,256]{2,1,0:T(8,128)(2,1)S(1)}, bf16[8,64,256]{2,1,0:T(8,128)(2,1)S(1)}, u32[]{:S(2)}, u32[]{:S(2)}) collective-permute-start(bf16[8,64,256]{2,1,0:T(8,128)(2,1)S(1)} %collective-permute-done.10.refs_2_), channel_id=1, source_target_pairs={{0,1},{1,0},{2,3},{3,2},{4,5},{5,4},{6,7},{7,6},{8,9},{9,8},{10,11... | collective-permute-start | bytes 786440 | tf_op jit(solution)/shard_map/ppermute | solution.py:191
  68.6 13.7 %copy-start.10 = (bf16[8,64,256]{2,1,0:T(8,128)(2,1)}, bf16[8,64,256]{2,1,0:T(8,128)(2,1)S(1)}, u32[]{:S(2)}) copy-start(bf16[8,64,256]{2,1,0:T(8,128)(2,1)S(1)} %collective-permute-done.9.refs_1_) | copy-start | bytes 786436
  68.6 13.7 %collective-permute-start.12 = (bf16[8,64,256]{2,1,0:T(8,128)(2,1)S(1)}, bf16[8,64,256]{2,1,0:T(8,128)(2,1)S(1)}, u32[]{:S(2)}, u32[]{:S(2)}) collective-permute-start(bf16[8,64,256]{2,1,0:T(8,128)(2,1)S(1)} %collective-permute-done.9.refs_1_), channel_id=1, source_target_pairs={{1,66},{2,65},{3,68},{4,67},{5,70},{6,69},{7,72},{8,71},{9,74},{10... | collective-permute-start | bytes 786440 | tf_op jit(solution)/shard_map/ppermute | solution.py:191
  71.8 10.6 %copy-start.28 = (bf16[2,64,256]{2,1,0:T(8,128)(2,1)}, bf16[2,64,256]{2,1,0:T(8,128)(2,1)S(1)}, u32[]{:S(2)}) copy-start(bf16[2,64,256]{2,1,0:T(8,128)(2,1)S(1)} %collective-permute-done.17.refs_11_) | copy-start | bytes 196612
  71.8 10.5 %collective-permute-start.13 = (bf16[8,64,256]{2,1,0:T(8,128)(2,1)S(1)}, bf16[8,64,256]{2,1,0:T(8,128)(2,1)S(1)}, u32[]{:S(2)}, u32[]{:S(2)}) collective-permute-start(bf16[8,64,256]{2,1,0:T(8,128)(2,1)S(1)} %collective-permute-done.9.refs_1_), channel_id=1, source_target_pairs={{0,64},{1,65},{2,66},{3,67},{4,68},{5,69},{6,70},{7,71},{8,72},{9,... | collective-permute-start | bytes 786440 | tf_op jit(solution)/shard_map/ppermute | solution.py:191
  73.0 9.4 %copy-start.12 = (bf16[8,64,256]{2,1,0:T(8,128)(2,1)}, bf16[8,64,256]{2,1,0:T(8,128)(2,1)S(1)}, u32[]{:S(2)}) copy-start(bf16[8,64,256]{2,1,0:T(8,128)(2,1)S(1)} %collective-permute-done.14.refs_6_) | copy-start | bytes 786436
  73.0 9.3 %collective-permute-start.15 = (bf16[8,64,256]{2,1,0:T(8,128)(2,1)S(1)}, bf16[8,64,256]{2,1,0:T(8,128)(2,1)S(1)}, u32[]{:S(2)}, u32[]{:S(2)}) collective-permute-start(bf16[8,64,256]{2,1,0:T(8,128)(2,1)S(1)} %collective-permute-done.14.refs_6_), channel_id=1, source_target_pairs={{0,1},{1,0},{2,3},{3,2},{4,5},{5,4},{6,7},{7,6},{8,9},{9,8},{10,11... | collective-permute-start | bytes 786440 | tf_op jit(solution)/shard_map/ppermute | solution.py:191
  76.1 6.3 %copy-start.13 = (bf16[8,64,256]{2,1,0:T(8,128)(2,1)}, bf16[8,64,256]{2,1,0:T(8,128)(2,1)S(1)}, u32[]{:S(2)}) copy-start(bf16[8,64,256]{2,1,0:T(8,128)(2,1)S(1)} %collective-permute-done.8.refs_0_) | copy-start | bytes 786436
  76.1 6.3 %copy-start.14 = (bf16[8,64,256]{2,1,0:T(8,128)(2,1)}, bf16[8,64,256]{2,1,0:T(8,128)(2,1)S(1)}, u32[]{:S(2)}) copy-start(bf16[8,64,256]{2,1,0:T(8,128)(2,1)S(1)} %collective-permute-done.11.refs_3_) | copy-start | bytes 786436
  82.3 0.7 copy-start.15
  82.3 0.8 copy-start.18
  82.3 0.9 copy-start.20
  99.4 24.8 %collective-permute-start.20 = (bf16[8,64,256]{2,1,0:T(8,128)(2,1)}, bf16[8,64,256]{2,1,0:T(8,128)(2,1)S(1)}, u32[]{:S(2)}, u32[]{:S(2)}) collective-permute-start(bf16[8,64,256]{2,1,0:T(8,128)(2,1)} %get-tuple-element.18.refs_10_), channel_id=1, source_target_pairs={{0,16},{1,17},{2,18},{3,19},{4,20},{5,21},{6,22},{7,23},{8,24},{9,... | collective-permute-start | bytes 786440 | tf_op jit(solution)/shard_map/ppermute | solution.py:191
  100.1 24.8 %collective-permute-start.24 = (bf16[8,64,256]{2,1,0:T(8,128)(2,1)}, bf16[8,64,256]{2,1,0:T(8,128)(2,1)S(1)}, u32[]{:S(2)}, u32[]{:S(2)}) collective-permute-start(bf16[8,64,256]{2,1,0:T(8,128)(2,1)} %get-tuple-element.18.refs_10_), channel_id=1, source_target_pairs={{0,112},{1,113},{2,114},{3,115},{4,116},{5,117},{6,118},{7,119},{8... | collective-permute-start | bytes 786440 | tf_op jit(solution)/shard_map/ppermute | solution.py:191
  103.0 22.9 %collective-permute-start.18 = (bf16[8,64,256]{2,1,0:T(8,128)(2,1)}, bf16[8,64,256]{2,1,0:T(8,128)(2,1)S(1)}, u32[]{:S(2)}, u32[]{:S(2)}) collective-permute-start(bf16[8,64,256]{2,1,0:T(8,128)(2,1)} %get-tuple-element.17.refs_9_), channel_id=1, source_target_pairs={{1,18},{2,17},{3,20},{4,19},{5,22},{6,21},{7,24},{8,23},{9,26},{10... | collective-permute-start | bytes 786440 | tf_op jit(solution)/shard_map/ppermute | solution.py:191
  105.9 13.4 %collective-permute-start.26 = (bf16[2,64,256]{2,1,0:T(8,128)(2,1)}, bf16[2,64,256]{2,1,0:T(8,128)(2,1)S(1)}, u32[]{:S(2)}, u32[]{:S(2)}) collective-permute-start(bf16[2,64,256]{2,1,0:T(8,128)(2,1)} %get-tuple-element.19), channel_id=1, source_target_pairs={{1,2},{2,1},{3,4},{4,3},{5,6},{6,5},{7,8},{8,7},{9,10},{10,9},{11,... | collective-permute-start | bytes 196616 | tf_op jit(solution)/shard_map/ppermute | solution.py:191
  109.5 9.8 %collective-permute-start.27 = (bf16[2,64,256]{2,1,0:T(8,128)(2,1)}, bf16[2,64,256]{2,1,0:T(8,128)(2,1)S(1)}, u32[]{:S(2)}, u32[]{:S(2)}) collective-permute-start(bf16[2,64,256]{2,1,0:T(8,128)(2,1)} %get-tuple-element.20), channel_id=1, source_target_pairs={{0,1},{1,0},{2,3},{3,2},{4,5},{5,4},{6,7},{7,6},{8,9},{9,8},{10,11... | collective-permute-start | bytes 196616 | tf_op jit(solution)/shard_map/ppermute | solution.py:191
  119.3 18.2 %copy-start.29 = (bf16[2,64,256]{2,1,0:T(8,128)(2,1)}, bf16[2,64,256]{2,1,0:T(8,128)(2,1)S(1)}, u32[]{:S(2)}) copy-start(bf16[2,64,256]{2,1,0:T(8,128)(2,1)S(1)} %collective-permute-done.26.refs_8_) | copy-start | bytes 196612
  119.3 10.4 %collective-permute-start.19 = (bf16[8,64,256]{2,1,0:T(8,128)(2,1)}, bf16[8,64,256]{2,1,0:T(8,128)(2,1)S(1)}, u32[]{:S(2)}, u32[]{:S(2)}) collective-permute-start(bf16[8,64,256]{2,1,0:T(8,128)(2,1)} %get-tuple-element.17.refs_9_), channel_id=1, source_target_pairs={{0,16},{1,17},{2,18},{3,19},{4,20},{5,21},{6,22},{7,23},{8,24},{9,... | collective-permute-start | bytes 786440 | tf_op jit(solution)/shard_map/ppermute | solution.py:191
  119.3 18.2 %copy-start.30 = (bf16[2,64,256]{2,1,0:T(8,128)(2,1)}, bf16[2,64,256]{2,1,0:T(8,128)(2,1)S(1)}, u32[]{:S(2)}) copy-start(bf16[2,64,256]{2,1,0:T(8,128)(2,1)S(1)} %collective-permute-done.27.refs_11_) | copy-start | bytes 196612
  119.3 12.6 %collective-permute-start.22 = (bf16[8,64,256]{2,1,0:T(8,128)(2,1)}, bf16[8,64,256]{2,1,0:T(8,128)(2,1)S(1)}, u32[]{:S(2)}, u32[]{:S(2)}) collective-permute-start(bf16[8,64,256]{2,1,0:T(8,128)(2,1)} %get-tuple-element.17.refs_9_), channel_id=1, source_target_pairs={{1,114},{2,113},{3,116},{4,115},{5,118},{6,117},{7,120},{8,119},{9... | collective-permute-start | bytes 786440 | tf_op jit(solution)/shard_map/ppermute | solution.py:191
  124.2 13.4 %copy-start.16 = (bf16[8,64,256]{2,1,0:T(8,128)(2,1)}, bf16[8,64,256]{2,1,0:T(8,128)(2,1)S(1)}, u32[]{:S(2)}) copy-start(bf16[8,64,256]{2,1,0:T(8,128)(2,1)S(1)} %collective-permute-done.20.refs_2_) | copy-start | bytes 786436
  124.2 13.3 %collective-permute-start.23 = (bf16[8,64,256]{2,1,0:T(8,128)(2,1)}, bf16[8,64,256]{2,1,0:T(8,128)(2,1)S(1)}, u32[]{:S(2)}, u32[]{:S(2)}) collective-permute-start(bf16[8,64,256]{2,1,0:T(8,128)(2,1)} %get-tuple-element.17.refs_9_), channel_id=1, source_target_pairs={{0,112},{1,113},{2,114},{3,115},{4,116},{5,117},{6,118},{7,119},{8... | collective-permute-start | bytes 786440 | tf_op jit(solution)/shard_map/ppermute | solution.py:191
  124.9 12.6 %copy-start.17 = (bf16[8,64,256]{2,1,0:T(8,128)(2,1)}, bf16[8,64,256]{2,1,0:T(8,128)(2,1)S(1)}, u32[]{:S(2)}) copy-start(bf16[8,64,256]{2,1,0:T(8,128)(2,1)S(1)} %collective-permute-done.24.refs_6_) | copy-start | bytes 786436
  124.9 12.6 %collective-permute-start.21 = (bf16[8,64,256]{2,1,0:T(8,128)(2,1)S(1)}, bf16[8,64,256]{2,1,0:T(8,128)(2,1)S(1)}, u32[]{:S(2)}, u32[]{:S(2)}) collective-permute-start(bf16[8,64,256]{2,1,0:T(8,128)(2,1)S(1)} %collective-permute-done.20.refs_2_), channel_id=1, source_target_pairs={{0,1},{1,0},{2,3},{3,2},{4,5},{5,4},{6,7},{7,6},{8,9},{9,8},{10,11... | collective-permute-start | bytes 786440 | tf_op jit(solution)/shard_map/ppermute | solution.py:191
  125.8 11.7 %copy-start.19 = (bf16[8,64,256]{2,1,0:T(8,128)(2,1)}, bf16[8,64,256]{2,1,0:T(8,128)(2,1)S(1)}, u32[]{:S(2)}) copy-start(bf16[8,64,256]{2,1,0:T(8,128)(2,1)S(1)} %collective-permute-done.18.refs_0_) | copy-start | bytes 786436
  125.9 11.6 %collective-permute-start.25 = (bf16[8,64,256]{2,1,0:T(8,128)(2,1)S(1)}, bf16[8,64,256]{2,1,0:T(8,128)(2,1)S(1)}, u32[]{:S(2)}, u32[]{:S(2)}) collective-permute-start(bf16[8,64,256]{2,1,0:T(8,128)(2,1)S(1)} %collective-permute-done.24.refs_6_), channel_id=1, source_target_pairs={{0,1},{1,0},{2,3},{3,2},{4,5},{5,4},{6,7},{7,6},{8,9},{9,8},{10,11... | collective-permute-start | bytes 786440 | tf_op jit(solution)/shard_map/ppermute | solution.py:191
  129.7 7.9 %copy-start.21 = (bf16[8,64,256]{2,1,0:T(8,128)(2,1)}, bf16[8,64,256]{2,1,0:T(8,128)(2,1)S(1)}, u32[]{:S(2)}) copy-start(bf16[8,64,256]{2,1,0:T(8,128)(2,1)S(1)} %collective-permute-done.19.refs_1_) | copy-start | bytes 786436
  132.0 5.6 %copy-start.22 = (bf16[8,64,256]{2,1,0:T(8,128)(2,1)}, bf16[8,64,256]{2,1,0:T(8,128)(2,1)S(1)}, u32[]{:S(2)}) copy-start(bf16[8,64,256]{2,1,0:T(8,128)(2,1)S(1)} %collective-permute-done.22.refs_4_) | copy-start | bytes 786436
  137.5 0.7 copy-start.23
  137.5 0.8 copy-start.24
  137.5 0.9 copy-start.26

commit v3 on v2

v3 whole, which is shorter than its diff:
```python
import functools

import jax
import jax.numpy as jnp
from jax import lax
from jax.experimental import pallas as pl
from jax.experimental.pallas import tpu as pltpu
from jax.sharding import PartitionSpec as P


LEVELS = 3
CH = 64
WIDTH = 256
HALF = 8
F32 = jnp.float32
BF16 = jnp.bfloat16


def pick_rows(v, bits, w0, w1, outs):
    b8, b4, b2, b1 = bits
    n8, n4, n2, n1 = outs + 8, outs + 4, outs + 2, outs + 1
    x8 = [jnp.where(b8, v[j + 8], v[j]) if j < outs + 3 else v[j] for j in range(n8)]
    x4 = [jnp.where(b4, x8[j + 4], x8[j]) for j in range(n4)]
    x2 = [jnp.where(b2, x4[j + 2], x4[j]) for j in range(n2)]
    x1 = [jnp.where(b1, x2[j + 1], x2[j]) for j in range(n1)]
    return [w0 * x1[i] + w1 * x1[i + 1] for i in range(outs)]


BLOCKS = ((1, 3, 19, 8, 2), (2, 11, 19, 8, 10), (0, 1, 13, 2, 0), (3, 19, 13, 2, 18))
OWN = slice(2 * CH, 3 * CH)


def turn(turned, place, size):
    return place + turned * (size - 2 * place)


def columns_kernel(vals, cols, table):
    block_of = lax.broadcasted_iota(jnp.int32, (32, WIDTH), 1) // 8
    spread = (block_of == lax.broadcasted_iota(jnp.int32, (32, WIDTH), 0)).astype(F32)
    table[...] = jnp.dot(
        vals[...].astype(F32).astype(BF16), spread.astype(BF16), preferred_element_type=F32
    )
    apart = lax.broadcasted_iota(jnp.int32, (WIDTH, WIDTH), 0) - lax.broadcasted_iota(
        jnp.int32, (WIDTH, WIDTH), 1
    )

    @pl.loop(0, cols.shape[0])
    def _(n):
        entry = table[pl.ds(pl.multiple_of(n * 8, 8), 8), :]
        off = apart - entry[1:2].astype(jnp.int32)
        fx = entry[3:4] * 0.25
        cols[n] = jnp.where(off == 0, 1.0 - fx, jnp.where(off == 1, fx, 0.0)).astype(BF16)


def make_columns(vals, interpret=False):
    count = vals.shape[0] // 8
    vmem = pl.BlockSpec(memory_space=pltpu.VMEM)
    return pl.pallas_call(
        columns_kernel,
        out_shape=(
            jax.ShapeDtypeStruct((count, WIDTH, WIDTH), BF16),
            jax.ShapeDtypeStruct((count * 8, WIDTH), F32),
        ),
        in_specs=[vmem],
        out_specs=(vmem, vmem),
        cost_estimate=pl.CostEstimate(
            flops=100_000_000, bytes_accessed=3_000_000, transcendentals=0
        ),
        interpret=interpret,
    )(vals)


def warp_into(flags, cols, table, source_of, base, passed, put_of):
    has_above = (flags[1] > 0).astype(F32)
    has_below = (flags[2] > 0).astype(F32)
    lanes = (16, WIDTH)

    @pl.loop(0, 2)
    def _(which):
        put = put_of(which)

        def column_pass(k):
            block, first, count, _, _ = BLOCKS[k]
            window = source_of(which, first, count).reshape(count * CH, WIDTH)
            passed[k][...] = jnp.dot(
                window, cols[base + which * 4 + block], preferred_element_type=F32
            ).reshape(count, CH, WIDTH)

        def row_pass(k):
            block, _, count, outs, start = BLOCKS[k]
            at = (base + which * 4 + block) * 8
            entry = table[pl.ds(pl.multiple_of(at, 8), 8), :]
            s = entry[0:1].astype(jnp.int32) + 5
            keep = {0: has_above, 3: has_below}.get(block, 1.0)
            bits = [jnp.broadcast_to((s & b) != 0, lanes) for b in (8, 4, 2, 1)]
            fy = entry[2:3] * 0.25
            w1 = jnp.broadcast_to(fy * keep, lanes)
            w0 = jnp.broadcast_to((1.0 - fy) * keep, lanes)
            for c in range(CH // 16):
                v = [passed[k][u, 16 * c : 16 * c + 16, :] for u in range(count)]
                for i, row in enumerate(pick_rows(v, bits, w0, w1, outs)):
                    put(start + i, 16 * c, row.astype(BF16))

        column_pass(0)
        for k in range(4):
            if k < 3:
                column_pass(k + 1)
            row_pass(k)


def convolve_band(flags, wu, wm, joined, act, final, outs):
    has_above = flags[1] > 0
    has_below = flags[2] > 0
    turned = flags[0]
    lane = lax.broadcasted_iota(jnp.int32, (CH, WIDTH), 1)
    not_first = lane > 0
    not_last = lane < WIDTH - 1

    def gather_taps(s):
        left = jnp.where(not_first, pltpu.roll(s[0:CH], 1, 1), 0.0)
        right = jnp.where(not_last, pltpu.roll(s[2 * CH :], WIDTH - 1, 1), 0.0)
        return s[CH : 2 * CH] + left + right

    def activate(a):
        window = joined[pl.ds(a, 3)].reshape(9 * CH, WIDTH)
        total = gather_taps(jnp.dot(wu[...], window, preferred_element_type=F32))
        half = 0.5 * total
        value = half + half * jnp.tanh(half)
        keep = jnp.where(
            a == 0, has_above, jnp.where(a == 17, has_below, True)
        ).astype(F32)
        act[a] = (value * keep).astype(BF16)

    @pl.loop(0, 6)
    def _(n):
        for k in range(3):
            activate(3 * n + k)

    scale = flags[3].astype(F32)

    def finish(y):
        window = act[pl.ds(y, 3)].reshape(3 * CH, WIDTH)
        total = gather_taps(jnp.dot(wm[...], window, preferred_element_type=F32))
        own = joined[y + 2, OWN, :].astype(F32)
        return (own + scale * total).astype(BF16)

    if final:
        (out,) = outs

        @pl.loop(0, 4)
        def _(n):
            for k in range(4):
                out[4 * n + k] = finish(4 * n + k)

    else:
        out_edge, out_inner, out_rim, out_near = outs

        @pl.loop(0, 4)
        def _(n):
            for k in range(2):
                y = 2 * n + k
                out_edge[y] = finish(y + turn(turned, 0, 8))
                out_inner[y] = finish(y + turn(turned, 8, 8))

        out_rim[...] = out_edge[pl.ds(turn(turned, 0, 6), 2)]
        out_near[...] = out_inner[pl.ds(turn(turned, 6, 6), 2)]


def stack_rows(target, turned, pieces):
    for p in range(4):
        target[pl.ds(turn(turned, 8 * p, 24), 8)] = pieces[p][...]


def level_kernel(sources, base, flags, cols, table, wu, wm, *refs):
    own_outer, own_edge, own_inner, own_near = refs[4 * sources : 4 * sources + 4]
    outs = refs[4 * sources + 4 : 4 * sources + 8]
    src, joined, act = refs[4 * sources + 8 : 4 * sources + 11]
    passed = refs[4 * sources + 11 :]
    turned = flags[0]
    for i in range(sources):
        stack_rows(src.at[i], turned, refs[4 * i : 4 * i + 4])
    joined[pl.ds(turn(turned, 0, 18), 2), OWN] = own_outer[...]
    joined[pl.ds(turn(turned, 2, 12), 8), OWN] = own_edge[...]
    joined[pl.ds(turn(turned, 10, 12), 8), OWN] = own_inner[...]
    joined[pl.ds(turn(turned, 18, 18), 2), OWN] = own_near[...]

    def source_of(which, first, count):
        return src[which ^ flags[4] if sources == 2 else 0, first : first + count]

    def put_of(which):
        def put(row, c, value):
            joined[row, pl.ds(pl.multiple_of(which * CH + c, 16), 16), :] = value

        return put

    warp_into(flags, cols, table, source_of, base, passed, put_of)
    convolve_band(flags, wu, wm, joined, act, False, outs)


def warp_kernel(base, flags, cols, table, outer, edge, inner, near, out, src, *passed):
    stack_rows(src, flags[0], (outer, edge, inner, near))

    def source_of(which, first, count):
        return src[first : first + count]

    def put_of(which):
        def put(row, c, value):
            out[which, row, c : c + 16, :] = value

        return put

    warp_into(flags, cols, table, source_of, base, passed, put_of)


def last_kernel(flags, wu, wm, outer, edge, inner, near, earlier, later, out, joined, act):
    turned = flags[0]
    joined[pl.ds(turn(turned, 0, 18), 2), OWN] = outer[pl.ds(turn(turned, 6, 6), 2)]
    joined[pl.ds(turn(turned, 2, 12), 8), OWN] = edge[...]
    joined[pl.ds(turn(turned, 10, 12), 8), OWN] = inner[...]
    joined[pl.ds(turn(turned, 18, 18), 2), OWN] = near[pl.ds(turn(turned, 0, 6), 2)]
    joined[:, 0:CH] = earlier[...]
    joined[:, CH : 2 * CH] = later[...]
    convolve_band(flags, wu, wm, joined, act, True, (out,))


def on_core(kernel, out_shape, scratch, cost, operands, interpret):
    vmem = pl.BlockSpec(memory_space=pltpu.VMEM)
    return pl.pallas_call(
        kernel,
        out_shape=out_shape,
        in_specs=[pl.BlockSpec(memory_space=pltpu.SMEM)] + [vmem] * (len(operands) - 1),
        out_specs=(vmem,) * len(out_shape),
        scratch_shapes=scratch,
        cost_estimate=pl.CostEstimate(
            flops=cost, bytes_accessed=4_000_000, transcendentals=300_000
        ),
        interpret=interpret,
    )(*operands)


def passed_buffers():
    return [pltpu.VMEM((count, CH, WIDTH), F32) for _, _, count, _, _ in BLOCKS]


def band_buffers():
    return [pltpu.VMEM((20, 3 * CH, WIDTH), BF16), pltpu.VMEM((18, CH, WIDTH), BF16)]


def run_level(flags, cols, table, base, wu, wm, sources, own, interpret=False):
    half = jax.ShapeDtypeStruct((HALF, CH, WIDTH), BF16)
    edge = jax.ShapeDtypeStruct((2, CH, WIDTH), BF16)
    operands = [flags, cols, table, wu, wm] + [p for s in sources for p in s] + list(own)
    scratch = [pltpu.VMEM((len(sources), 32, CH, WIDTH), BF16)]
    return on_core(
        functools.partial(level_kernel, len(sources), base),
        (half, half, edge, edge),
        scratch + band_buffers() + passed_buffers(),
        3_000_000_000,
        operands,
        interpret,
    )


def run_warp(flags, cols, table, base, pieces, interpret=False):
    return on_core(
        functools.partial(warp_kernel, base),
        (jax.ShapeDtypeStruct((2, 20, CH, WIDTH), BF16),),
        [pltpu.VMEM((32, CH, WIDTH), BF16)] + passed_buffers(),
        1_500_000_000,
        [flags, cols, table, *pieces],
        interpret,
    )[0]


def run_last(flags, wu, wm, own, warped, interpret=False):
    return on_core(
        last_kernel,
        (jax.ShapeDtypeStruct((2 * HALF, CH, WIDTH), BF16),),
        band_buffers(),
        1_500_000_000,
        [flags, wu, wm, *own, *warped],
        interpret,
    )[0]


def send(x, frame_to=lambda t: t, row_to=lambda r: r):
    frames, rows = lax.axis_size("tm"), lax.axis_size("rows")
    route = [
        (t * rows + r, (frame_to(t) % frames) * rows + row_to(r))
        for t in range(frames)
        for r in range(rows)
        if 0 <= row_to(r) < rows
    ]
    return lax.ppermute(x, ("tm", "rows"), route)


def off_chip(r):
    return r + 1 if r % 2 else r - 1


def on_chip(r):
    return r ^ 1


def level_values(t):
    t = t.reshape(2, 2, 2, 4, 32)
    t = jnp.transpose(t, (1, 3, 0, 2, 4)).reshape(2, 4, 4, 32)
    return jnp.pad(t, ((0, 0), (0, 0), (0, 4), (0, 0))).reshape(64, 32)


def tap_weights(w):
    o, j = w.shape[2], w.shape[3]
    return jnp.transpose(w, (1, 2, 0, 3)).reshape(3 * o, 3 * j)


def shards(features, block_shift, quarter_pel, update_mask, uniting_weight, mixing_weight):
    band = features[0]
    row = lax.axis_index("rows")
    rows = lax.axis_size("rows")
    turned = row % 2
    edge = lax.dynamic_slice_in_dim(band, 8 * turned, HALF, axis=0)
    inner = lax.dynamic_slice_in_dim(band, 8 - 8 * turned, HALF, axis=0)
    rim = lax.dynamic_slice_in_dim(band, 14 * turned, 2, axis=0)
    near = lax.dynamic_slice_in_dim(band, 14 - 14 * turned, 2, axis=0)
    wu, wm = tap_weights(uniting_weight), tap_weights(mixing_weight)

    def to_other(t):
        return t + 4

    def across(t):
        return t + 2 if t % 4 < 2 else t - 2

    def ahead(t):
        return t + 1

    def back(t):
        return t - 1

    e = send(edge, to_other)
    i = send(inner, to_other)
    h = send(edge, to_other, off_chip)
    own = jnp.stack([block_shift[:, :, 0], quarter_pel[:, :, 0]])
    above = send(own[:, :, :, 1:2], row_to=lambda r: r + 1)
    below = send(own[:, :, :, 0:1], row_to=lambda r: r - 1)
    packed = jnp.concatenate([above, own, below], axis=3)
    for_ahead = send(packed[:, 0, 0:2], back)
    for_back = send(packed[:, 0, 2:4], ahead)
    own_outer = send(rim, row_to=off_chip)
    own_near = send(near, row_to=on_chip)
    n = send(i, row_to=on_chip)
    cols, table = make_columns(
        jnp.concatenate(
            [
                level_values(packed[:, 2]),
                level_values(packed[:, 1]),
                level_values(jnp.concatenate([for_ahead, for_back], axis=1)),
            ]
        )
    )
    common = [turned, (row > 0).astype(jnp.int32), (row < rows - 1).astype(jnp.int32)]
    swapped = (lax.axis_index("tm") % 4 < 2).astype(jnp.int32)
    flags = [jnp.stack(common + [update_mask[k, 0], swapped]) for k in range(LEVELS)]

    edge, inner, rim, near = run_level(
        flags[2], cols, table, 0, wu, wm, [(h, e, i, n)], (own_outer, edge, inner, own_near)
    )

    own_outer = send(rim, row_to=off_chip)
    own_near = send(near, row_to=on_chip)
    e = send(edge, across)
    i = send(inner, across)
    h = send(edge, across, off_chip)
    xe = send(e, to_other)
    xh = send(e, to_other, off_chip)
    xi = send(i, to_other)
    n = send(i, row_to=on_chip)
    xn = send(xi, row_to=on_chip)
    edge, inner, _, _ = run_level(
        flags[1],
        cols,
        table,
        8,
        wu,
        wm,
        [(h, e, i, n), (xh, xe, xi, xn)],
        (own_outer, edge, inner, own_near),
    )

    outer = send(edge, row_to=off_chip)
    near = send(inner, row_to=on_chip)
    own = (outer, edge, inner, near)
    warped = run_warp(flags[0], cols, table, 16, own)
    earlier = send(warped[0], ahead)
    later = send(warped[1], back)
    return run_last(flags[0], wu, wm, own, (earlier, later))[None]


def solution(mesh):
    placed = (
        P("tm", "rows", None, None),
        P(None, None, "tm", "rows", None),
        P(None, None, "tm", "rows", None),
        P(None, "tm"),
        P(),
        P(),
    )
    return jax.shard_map(
        shards, mesh=mesh, in_specs=placed, out_specs=P("tm", "rows", None, None), check_vma=False
    )
```

time: 155 us -> 144 us (0.929)
  the two profiles are of different devices: /device:TPU:9 before, /device:TPU:13 now
where the time goes in v3:
time: 144 us
  starting transfers between devices  47.3 us (33%)
  waiting for transfers between devices  42.7 us (30%)
  Pallas kernels  37 us (26%)
  local copies, waits for them, and re-layouts  14.6 us (10%)
  other arithmetic  1.54 us (1%)
    ppermute x24, starting transfers between devices, send(): return lax.ppermute(x, ('tm', 'rows'), route)  47.3 us
    ppermute x24, waiting for transfers between devices, send(): return lax.ppermute(x, ('tm', 'rows'), route)  42.7 us
    pallas_call x4, Pallas kernels, on_core(): pl.pallas_call(kernel, out_shape=out_shape, in_specs=[pl.BlockSpec(memory...  33 us
    unnamed x54, local copies, waits for them, and re-layouts  4.49 us
    pallas_call x1, Pallas kernels, make_columns(): pl.pallas_call(columns_kernel, out_shape=(jax.ShapeDtypeStruct((count, WI...  4.02 us
    another operation x3, local copies, waits for them, and re-layouts, shards(): jnp.stack(common + [update_mask[k, 0], swapped])  3.85 us
  transfers between devices with their start and end apart: 24, of which 9 were waited for; matrix products, arithmetic and copies ran while one was open for 6% of the time, Pallas kernels for 3%

profile of v3, /device:TPU:13, one launch (start us, length us, event | category | flops | bytes accessed | tf_op | source)
XLA Modules:
  0.0 143.6 jit_solution(10651758671191192298)
XLA Ops:
  0.0 1.1 dynamic-slice_bitcast_fusion
  1.2 0.0 copy-start.6
  1.2 0.0 copy-start.7
  1.2 1.0 collective-permute-start.5
  2.2 3.3 %collective-permute-start.4 = (bf16[8,64,256]{2,1,0:T(8,128)(2,1)S(1)}, bf16[8,64,256]{2,1,0:T(8,128)(2,1)S(1)}, u32[]{:S(2)}, u32[]{:S(2)}) collective-permute-start(bf16[8,64,256]{2,1,0:T(8,128)(2,1)S(1)} %get-tuple-element.26.refs_5_), channel_id=1, source_target_pairs={{1,66},{2,65},{3,68},{4,67},{5,70},{6,69},{7,72},{8,71},{9,74},{10... | collective-permute-start | bytes 786440 | tf_op jit(solution)/shard_map/ppermute | solution.py:294
  5.6 0.8 fusion
  6.4 4.0 %collective-permute-start = (s32[2,3,4,1,32]{4,3,2,1,0:T(1,128)S(1)}, s32[2,3,4,1,32]{4,3,2,1,0:T(1,128)S(1)}, u32[]{:S(2)}, u32[]{:S(2)}) collective-permute-start(s32[2,3,4,1,32]{4,3,2,1,0:T(1,128)S(1)} %get-tuple-element.31), channel_id=1, source_target_pairs={{0,1},{1,2},{2,3},{3,4},{4,5},{5,6},{6,7},{7,8},{8,9},{9,10},{10,1... | collective-permute-start | bytes 9224 | tf_op jit(solution)/shard_map/ppermute | solution.py:294
  10.4 1.9 %collective-permute-start.1 = (s32[2,3,4,1,32]{4,3,2,1,0:T(1,128)S(1)}, s32[2,3,4,1,32]{4,3,2,1,0:T(1,128)S(1)}, u32[]{:S(2)}, u32[]{:S(2)}) collective-permute-start(s32[2,3,4,1,32]{4,3,2,1,0:T(1,128)S(1)} %get-tuple-element.32), channel_id=1, source_target_pairs={{1,0},{2,1},{3,2},{4,3},{5,4},{6,5},{7,6},{8,7},{9,8},{10,9},{11,1... | collective-permute-start | bytes 9224 | tf_op jit(solution)/shard_map/ppermute | solution.py:294
  12.3 1.0 collective-permute-start.6
  13.3 0.9 dynamic-slice_bitcast_fusion.2
  14.2 0.6 fusion.2
  14.8 0.1 copy.37
  14.9 0.8 reshape.32.wm
  15.7 0.3 copy.36
  16.0 1.0 reshape.31.wu
  16.9 1.3 stack.51.flags
  18.3 0.0 collective-permute-done.1
  18.3 4.1 %collective-permute-start.2 = (s32[2,2,4,32]{3,2,1,0:T(4,128)S(1)}, s32[2,2,4,32]{3,2,1,0:T(4,128)S(1)}, u32[]{:S(2)}, u32[]{:S(2)}) collective-permute-start(s32[2,2,4,32]{3,2,1,0:T(4,128)S(1)} %get-tuple-element.29), channel_id=1, source_target_pairs={{0,112},{1,113},{2,114},{3,115},{4,116},{5,117},{6,118},{7,119},{8... | collective-permute-start | bytes 6152 | tf_op jit(solution)/shard_map/ppermute | solution.py:294
  22.4 0.0 collective-permute-start.3
  22.4 0.0 collective-permute-done.6.refs_2_
  22.5 1.3 collective-permute-start.7
  23.9 0.0 collective-permute-done.2
  23.9 1.1 collective-permute-start.9
  25.0 2.0 %collective-permute-done.3 = s32[2,2,4,32]{3,2,1,0:T(4,128)S(1)} collective-permute-done((s32[2,2,4,32]{3,2,1,0:T(4,128)S(1)}, s32[2,2,4,32]{3,2,1,0:T(4,128)S(1)}, u32[]{:S(2)}, u32[]{:S(2)}) %collective-permute-start.3) | collective-permute-done | bytes 2080 | tf_op jit(solution)/shard_map/ppermute | solution.py:294
  27.0 7.7 %collective-permute-start.8 = (bf16[2,64,256]{2,1,0:T(8,128)(2,1)S(1)}, bf16[2,64,256]{2,1,0:T(8,128)(2,1)S(1)}, u32[]{:S(2)}, u32[]{:S(2)}) collective-permute-start(bf16[2,64,256]{2,1,0:T(8,128)(2,1)S(1)} %get-tuple-element.24), channel_id=1, source_target_pairs={{1,2},{2,1},{3,4},{4,3},{5,6},{6,5},{7,8},{8,7},{9,10},{10,9},{11,... | collective-permute-start | bytes 196616 | tf_op jit(solution)/shard_map/ppermute | solution.py:294
  34.8 0.7 pad_add_fusion.vals
  35.5 4.0 %shard_map.64 = (bf16[24,256,256]{2,1,0:T(8,128)(2,1)}, f32[192,256]{1,0:T(8,128)}) custom-call(s32[192,32]{1,0:T(8,128)} %pad_add_fusion.vals), custom_call_target="tpu_custom_call" | custom-call | flops 100000000 | bytes 3000000 | tf_op jit(solution)/shard_map/pallas_call | solution.py:58
  39.5 0.0 copy-start.12
  39.6 0.5 copy-done.25
  40.1 0.0 copy-done.26
  40.2 0.1 copy-done.11
  40.3 0.1 copy-done.12
  40.3 0.1 copy-done.15
  40.4 10.0 %shard_map.65 = (bf16[8,64,256]{2,1,0:T(8,128)(2,1)}, bf16[8,64,256]{2,1,0:T(8,128)(2,1)}, bf16[2,64,256]{2,1,0:T(8,128)(2,1)}, bf16[2,64,256]{2,1,0:T(8,128)(2,1)}) custom-call(s32[5]{0:T(128)} %stack.51.flags, bf16[24,256,256]{2,1,0:T(8,128)(2,1)} %get-tuple-element.13.cols, f32[192,256]{1,0:T(8,128)} %get-tuple-element.14.table, ...), custom_call_target="tpu_custom_call" | custom-call | flops 3000000000 | bytes 4000000 | tf_op jit(solution)/shard_map/pallas_call | solution.py:228
  50.5 3.0 %collective-permute-start.11 = (bf16[8,64,256]{2,1,0:T(8,128)(2,1)}, bf16[8,64,256]{2,1,0:T(8,128)(2,1)S(1)}, u32[]{:S(2)}, u32[]{:S(2)}) collective-permute-start(bf16[8,64,256]{2,1,0:T(8,128)(2,1)} %get-tuple-element.15.refs_9_), channel_id=1, source_target_pairs={{0,32},{1,33},{2,34},{3,35},{4,36},{5,37},{6,38},{7,39},{8,40},{9,... | collective-permute-start | bytes 786440 | tf_op jit(solution)/shard_map/ppermute | solution.py:294
  53.4 7.1 %collective-permute-done.12.refs_2_ = bf16[8,64,256]{2,1,0:T(8,128)(2,1)S(1)} collective-permute-done((bf16[8,64,256]{2,1,0:T(8,128)(2,1)}, bf16[8,64,256]{2,1,0:T(8,128)(2,1)S(1)}, u32[]{:S(2)}, u32[]{:S(2)}) %collective-permute-start.12) | collective-permute-done | bytes 262176 | tf_op jit(solution)/shard_map/ppermute | solution.py:294
  60.5 0.9 collective-permute-start.16
  61.4 3.8 %collective-permute-start.18 = (bf16[2,64,256]{2,1,0:T(8,128)(2,1)}, bf16[2,64,256]{2,1,0:T(8,128)(2,1)S(1)}, u32[]{:S(2)}, u32[]{:S(2)}) collective-permute-start(bf16[2,64,256]{2,1,0:T(8,128)(2,1)} %get-tuple-element.17), channel_id=1, source_target_pairs={{1,2},{2,1},{3,4},{4,3},{5,6},{6,5},{7,8},{8,7},{9,10},{10,9},{11,... | collective-permute-start | bytes 196616 | tf_op jit(solution)/shard_map/ppermute | solution.py:294
  65.2 0.1 collective-permute-start.19
  65.3 3.8 %collective-permute-start.10 = (bf16[8,64,256]{2,1,0:T(8,128)(2,1)}, bf16[8,64,256]{2,1,0:T(8,128)(2,1)S(1)}, u32[]{:S(2)}, u32[]{:S(2)}) collective-permute-start(bf16[8,64,256]{2,1,0:T(8,128)(2,1)} %get-tuple-element.15.refs_9_), channel_id=1, source_target_pairs={{1,34},{2,33},{3,36},{4,35},{5,38},{6,37},{7,40},{8,39},{9,42},{10... | collective-permute-start | bytes 786440 | tf_op jit(solution)/shard_map/ppermute | solution.py:294
  69.0 0.6 collective-permute-done.18.refs_8_
  69.6 0.6 collective-permute-start.15
  70.3 3.8 %collective-permute-start.14 = (bf16[8,64,256]{2,1,0:T(8,128)(2,1)S(1)}, bf16[8,64,256]{2,1,0:T(8,128)(2,1)S(1)}, u32[]{:S(2)}, u32[]{:S(2)}) collective-permute-start(bf16[8,64,256]{2,1,0:T(8,128)(2,1)S(1)} %collective-permute-done.11.refs_1_), channel_id=1, source_target_pairs={{1,66},{2,65},{3,68},{4,67},{5,70},{6,69},{7,72},{8,71},{9,74},{10... | collective-permute-start | bytes 786440 | tf_op jit(solution)/shard_map/ppermute | solution.py:294
  74.1 0.1 collective-permute-start.17
  74.1 1.2 stack.49.flags
  75.4 5.5 %collective-permute-done.10.refs_0_ = bf16[8,64,256]{2,1,0:T(8,128)(2,1)S(1)} collective-permute-done((bf16[8,64,256]{2,1,0:T(8,128)(2,1)}, bf16[8,64,256]{2,1,0:T(8,128)(2,1)S(1)}, u32[]{:S(2)}, u32[]{:S(2)}) %collective-permute-start.10) | collective-permute-done | bytes 262176 | tf_op jit(solution)/shard_map/ppermute | solution.py:294
  80.8 1.4 collective-permute-done.15.refs_5_
  82.2 1.1 collective-permute-done.14.refs_4_
  83.4 0.6 copy-done.21
  84.0 0.7 copy-done.22
  84.7 10.4 %shard_map.66 = (bf16[8,64,256]{2,1,0:T(8,128)(2,1)}, bf16[8,64,256]{2,1,0:T(8,128)(2,1)}, bf16[2,64,256]{2,1,0:T(8,128)(2,1)}, bf16[2,64,256]{2,1,0:T(8,128)(2,1)}) custom-call(s32[5]{0:T(128)} %stack.49.flags, bf16[24,256,256]{2,1,0:T(8,128)(2,1)} %get-tuple-element.13.cols, f32[192,256]{1,0:T(8,128)} %get-tuple-element.14.table, ...), custom_call_target="tpu_custom_call" | custom-call | flops 3000000000 | bytes 4000000 | tf_op jit(solution)/shard_map/pallas_call | solution.py:228
  95.2 3.9 %collective-permute-start.20 = (bf16[8,64,256]{2,1,0:T(8,128)(2,1)}, bf16[8,64,256]{2,1,0:T(8,128)(2,1)S(1)}, u32[]{:S(2)}, u32[]{:S(2)}) collective-permute-start(bf16[8,64,256]{2,1,0:T(8,128)(2,1)} %get-tuple-element.19.edge), channel_id=1, source_target_pairs={{1,2},{2,1},{3,4},{4,3},{5,6},{6,5},{7,8},{8,7},{9,10},{10,9},{11,... | collective-permute-start | bytes 786440 | tf_op jit(solution)/shard_map/ppermute | solution.py:294
  99.1 0.1 collective-permute-start.21
  99.2 1.3 stack.48.flags
  100.5 6.9 %collective-permute-done.20.outer = bf16[8,64,256]{2,1,0:T(8,128)(2,1)S(1)} collective-permute-done((bf16[8,64,256]{2,1,0:T(8,128)(2,1)}, bf16[8,64,256]{2,1,0:T(8,128)(2,1)S(1)}, u32[]{:S(2)}, u32[]{:S(2)}) %collective-permute-start.20) | collective-permute-done | bytes 262176 | tf_op jit(solution)/shard_map/ppermute | solution.py:294
  107.4 0.7 copy-done.3
  108.1 0.7 copy-done.4
  108.8 5.4 %shard_map.67 = bf16[2,20,64,256]{3,2,1,0:T(8,128)(2,1)} custom-call(s32[5]{0:T(128)} %stack.48.flags, bf16[24,256,256]{2,1,0:T(8,128)(2,1)} %get-tuple-element.13.cols, f32[192,256]{1,0:T(8,128)} %get-tuple-element.14.table, bf16[8,64,256]{2,1,0:T(8,128)(2,1)} %copy-done.3, bf16[8,64,256]{2,1,0:T(8,128)(2,1)} %get-tuple-element.19.edge, ...), custom_call_target="tpu_custom_call" | custom-call | flops 1500000000 | bytes 4000000 | tf_op jit(solution)/shard_map/pallas_call | solution.py:228
  114.2 1.4 slice_bitcast_fusion
  115.7 1.8 %collective-permute-start.23 = (bf16[20,64,256]{2,1,0:T(8,128)(2,1)S(1)}, bf16[20,64,256]{2,1,0:T(8,128)(2,1)S(1)}, u32[]{:S(2)}, u32[]{:S(2)}) collective-permute-start(bf16[20,64,256]{2,1,0:T(8,128)(2,1)S(1)} %get-tuple-element.21), channel_id=1, source_target_pairs={{0,112},{1,113},{2,114},{3,115},{4,116},{5,117},{6,118},{7,119},{8... | collective-permute-start | bytes 1966088 | tf_op jit(solution)/shard_map/ppermute | solution.py:294
  117.4 14.3 %collective-permute-done.23.later = bf16[20,64,256]{2,1,0:T(8,128)(2,1)S(1)} collective-permute-done((bf16[20,64,256]{2,1,0:T(8,128)(2,1)S(1)}, bf16[20,64,256]{2,1,0:T(8,128)(2,1)S(1)}, u32[]{:S(2)}, u32[]{:S(2)}) %collective-permute-start.23) | collective-permute-done | bytes 655392 | tf_op jit(solution)/shard_map/ppermute | solution.py:294
  131.7 3.9 %collective-permute-done.22.earlier = bf16[20,64,256]{2,1,0:T(8,128)(2,1)S(1)} collective-permute-done((bf16[20,64,256]{2,1,0:T(8,128)(2,1)S(1)}, bf16[20,64,256]{2,1,0:T(8,128)(2,1)S(1)}, u32[]{:S(2)}, u32[]{:S(2)}) %collective-permute-start.22) | collective-permute-done | bytes 655392 | tf_op jit(solution)/shard_map/ppermute | solution.py:294
  135.6 0.9 copy-done.10
  136.5 7.1 %shard_map.68 = bf16[16,64,256]{2,1,0:T(8,128)(2,1)} custom-call(s32[5]{0:T(128)} %stack.48.flags, bf16[192,576]{1,0:T(8,128)(2,1)} %reshape.31.wu, bf16[192,192]{1,0:T(8,128)(2,1)} %reshape.32.wm, bf16[8,64,256]{2,1,0:T(8,128)(2,1)} %copy-done.3, bf16[8,64,256]{2,1,0:T(8,128)(2,1)} %get-tuple-element.19.edge, bf16[8,64,256]{2,1,0:T(8,128)(2,1)} %get-tuple-element.20.inner, ...), custom_call_target="tpu_custom_call" | custom-call | flops 1500000000 | bytes 4000000 | tf_op jit(solution)/shard_map/pallas_call | solution.py:228
  (66 shorter events, 0.2 us)
Async XLA Ops:
  0.0 14.2 %copy-start.8 = (s32[3,1]{0,1:T(1,128)S(1)}, s32[3,1]{0,1:T(1,128)}, u32[]{:S(2)}) copy-start(s32[3,1]{0,1:T(1,128)} %param.9) | copy-start | bytes 40
  0.0 14.8 %copy-start.5 = (bf16[3,3,64,64]{3,2,1,0:T(8,128)(2,1)S(1)}, bf16[3,3,64,64]{3,2,1,0:T(8,128)(2,1)}, u32[]{:S(2)}) copy-start(bf16[3,3,64,64]{3,2,1,0:T(8,128)(2,1)} %param.11) | copy-start | bytes 221188
  0.0 15.7 %copy-start = (bf16[3,3,64,192]{3,2,1,0:T(8,128)(2,1)S(1)}, bf16[3,3,64,192]{3,2,1,0:T(8,128)(2,1)}, u32[]{:S(2)}) copy-start(bf16[3,3,64,192]{3,2,1,0:T(8,128)(2,1)} %param.10) | copy-start | bytes 663556
  1.2 22.7 %copy-start.1 = (bf16[8,64,256]{2,1,0:T(8,128)(2,1)}, bf16[8,64,256]{2,1,0:T(8,128)(2,1)S(1)}, u32[]{:S(2)}) copy-start(bf16[8,64,256]{2,1,0:T(8,128)(2,1)S(1)} %get-tuple-element.25.refs_6_) | copy-start | bytes 786436
  1.2 22.7 %copy-start.2 = (bf16[8,64,256]{2,1,0:T(8,128)(2,1)}, bf16[8,64,256]{2,1,0:T(8,128)(2,1)S(1)}, u32[]{:S(2)}) copy-start(bf16[8,64,256]{2,1,0:T(8,128)(2,1)S(1)} %get-tuple-element.26.refs_5_) | copy-start | bytes 786436
  1.2 17.1 %copy-start.6 = (s32[3,4,1,2,32]{4,3,2,1,0:T(2,128)S(1)}, s32[3,4,1,2,32]{4,3,2,1,0:T(2,128)}, u32[]{:S(2)}) copy-start(s32[3,4,1,2,32]{4,3,2,1,0:T(2,128)} %param.7) | copy-start | bytes 9220
  1.2 17.1 %copy-start.7 = (s32[3,4,1,2,32]{4,3,2,1,0:T(2,128)S(1)}, s32[3,4,1,2,32]{4,3,2,1,0:T(2,128)}, u32[]{:S(2)}) copy-start(s32[3,4,1,2,32]{4,3,2,1,0:T(2,128)} %param.8) | copy-start | bytes 9220
  1.2 38.3 %collective-permute-start.5 = (bf16[8,64,256]{2,1,0:T(8,128)(2,1)S(1)}, bf16[8,64,256]{2,1,0:T(8,128)(2,1)S(1)}, u32[]{:S(2)}, u32[]{:S(2)}) collective-permute-start(bf16[8,64,256]{2,1,0:T(8,128)(2,1)S(1)} %get-tuple-element.26.refs_5_), channel_id=1, source_target_pairs={{0,64},{1,65},{2,66},{3,67},{4,68},{5,69},{6,70},{7,71},{8,72},{9,... | collective-permute-start | bytes 786440 | tf_op jit(solution)/shard_map/ppermute | solution.py:294
  2.2 37.3 %collective-permute-start.4 = (bf16[8,64,256]{2,1,0:T(8,128)(2,1)S(1)}, bf16[8,64,256]{2,1,0:T(8,128)(2,1)S(1)}, u32[]{:S(2)}, u32[]{:S(2)}) collective-permute-start(bf16[8,64,256]{2,1,0:T(8,128)(2,1)S(1)} %get-tuple-element.26.refs_5_), channel_id=1, source_target_pairs={{1,66},{2,65},{3,68},{4,67},{5,70},{6,69},{7,72},{8,71},{9,74},{10... | collective-permute-start | bytes 786440 | tf_op jit(solution)/shard_map/ppermute | solution.py:294
  6.4 11.9 %collective-permute-start = (s32[2,3,4,1,32]{4,3,2,1,0:T(1,128)S(1)}, s32[2,3,4,1,32]{4,3,2,1,0:T(1,128)S(1)}, u32[]{:S(2)}, u32[]{:S(2)}) collective-permute-start(s32[2,3,4,1,32]{4,3,2,1,0:T(1,128)S(1)} %get-tuple-element.31), channel_id=1, source_target_pairs={{0,1},{1,2},{2,3},{3,4},{4,5},{5,6},{6,7},{7,8},{8,9},{9,10},{10,1... | collective-permute-start | bytes 9224 | tf_op jit(solution)/shard_map/ppermute | solution.py:294
  10.4 7.9 %collective-permute-start.1 = (s32[2,3,4,1,32]{4,3,2,1,0:T(1,128)S(1)}, s32[2,3,4,1,32]{4,3,2,1,0:T(1,128)S(1)}, u32[]{:S(2)}, u32[]{:S(2)}) collective-permute-start(s32[2,3,4,1,32]{4,3,2,1,0:T(1,128)S(1)} %get-tuple-element.32), channel_id=1, source_target_pairs={{1,0},{2,1},{3,2},{4,3},{5,4},{6,5},{7,6},{8,7},{9,8},{10,9},{11,1... | collective-permute-start | bytes 9224 | tf_op jit(solution)/shard_map/ppermute | solution.py:294
  12.3 10.2 %collective-permute-start.6 = (bf16[8,64,256]{2,1,0:T(8,128)(2,1)S(1)}, bf16[8,64,256]{2,1,0:T(8,128)(2,1)S(1)}, u32[]{:S(2)}, u32[]{:S(2)}) collective-permute-start(bf16[8,64,256]{2,1,0:T(8,128)(2,1)S(1)} %get-tuple-element.25.refs_6_), channel_id=1, source_target_pairs={{0,64},{1,65},{2,66},{3,67},{4,68},{5,69},{6,70},{7,71},{8,72},{9,... | collective-permute-start | bytes 786440 | tf_op jit(solution)/shard_map/ppermute | solution.py:294
  18.3 5.6 %collective-permute-start.2 = (s32[2,2,4,32]{3,2,1,0:T(4,128)S(1)}, s32[2,2,4,32]{3,2,1,0:T(4,128)S(1)}, u32[]{:S(2)}, u32[]{:S(2)}) collective-permute-start(s32[2,2,4,32]{3,2,1,0:T(4,128)S(1)} %get-tuple-element.29), channel_id=1, source_target_pairs={{0,112},{1,113},{2,114},{3,115},{4,116},{5,117},{6,118},{7,119},{8... | collective-permute-start | bytes 6152 | tf_op jit(solution)/shard_map/ppermute | solution.py:294
  22.4 4.6 %collective-permute-start.3 = (s32[2,2,4,32]{3,2,1,0:T(4,128)S(1)}, s32[2,2,4,32]{3,2,1,0:T(4,128)S(1)}, u32[]{:S(2)}, u32[]{:S(2)}) collective-permute-start(s32[2,2,4,32]{3,2,1,0:T(4,128)S(1)} %get-tuple-element.30), channel_id=1, source_target_pairs={{0,16},{1,17},{2,18},{3,19},{4,20},{5,21},{6,22},{7,23},{8,24},{9,... | collective-permute-start | bytes 6152 | tf_op jit(solution)/shard_map/ppermute | solution.py:294
  22.5 17.1 %copy-start.13 = (bf16[8,64,256]{2,1,0:T(8,128)(2,1)}, bf16[8,64,256]{2,1,0:T(8,128)(2,1)S(1)}, u32[]{:S(2)}) copy-start(bf16[8,64,256]{2,1,0:T(8,128)(2,1)S(1)} %collective-permute-done.6.refs_2_) | copy-start | bytes 786436
  22.5 17.1 %collective-permute-start.7 = (bf16[8,64,256]{2,1,0:T(8,128)(2,1)S(1)}, bf16[8,64,256]{2,1,0:T(8,128)(2,1)S(1)}, u32[]{:S(2)}, u32[]{:S(2)}) collective-permute-start(bf16[8,64,256]{2,1,0:T(8,128)(2,1)S(1)} %collective-permute-done.6.refs_2_), channel_id=1, source_target_pairs={{0,1},{1,0},{2,3},{3,2},{4,5},{5,4},{6,7},{7,6},{8,9},{9,8},{10,11... | collective-permute-start | bytes 786440 | tf_op jit(solution)/shard_map/ppermute | solution.py:294
  23.9 15.6 %collective-permute-start.9 = (bf16[2,64,256]{2,1,0:T(8,128)(2,1)S(1)}, bf16[2,64,256]{2,1,0:T(8,128)(2,1)S(1)}, u32[]{:S(2)}, u32[]{:S(2)}) collective-permute-start(bf16[2,64,256]{2,1,0:T(8,128)(2,1)S(1)} %get-tuple-element.23), channel_id=1, source_target_pairs={{0,1},{1,0},{2,3},{3,2},{4,5},{5,4},{6,7},{7,6},{8,9},{9,8},{10,11... | collective-permute-start | bytes 196616 | tf_op jit(solution)/shard_map/ppermute | solution.py:294
  27.0 12.5 %collective-permute-start.8 = (bf16[2,64,256]{2,1,0:T(8,128)(2,1)S(1)}, bf16[2,64,256]{2,1,0:T(8,128)(2,1)S(1)}, u32[]{:S(2)}, u32[]{:S(2)}) collective-permute-start(bf16[2,64,256]{2,1,0:T(8,128)(2,1)S(1)} %get-tuple-element.24), channel_id=1, source_target_pairs={{1,2},{2,1},{3,4},{4,3},{5,6},{6,5},{7,8},{8,7},{9,10},{10,9},{11,... | collective-permute-start | bytes 196616 | tf_op jit(solution)/shard_map/ppermute | solution.py:294
  39.5 0.6 copy-start.25
  39.5 0.7 copy-start.26
  39.5 0.7 copy-start.11
  39.5 0.8 copy-start.12
  39.6 0.9 copy-start.15
  50.5 10.0 %collective-permute-start.12 = (bf16[8,64,256]{2,1,0:T(8,128)(2,1)}, bf16[8,64,256]{2,1,0:T(8,128)(2,1)S(1)}, u32[]{:S(2)}, u32[]{:S(2)}) collective-permute-start(bf16[8,64,256]{2,1,0:T(8,128)(2,1)} %get-tuple-element.16.refs_10_), channel_id=1, source_target_pairs={{0,32},{1,33},{2,34},{3,35},{4,36},{5,37},{6,38},{7,39},{8,40},{9,... | collective-permute-start | bytes 786440 | tf_op jit(solution)/shard_map/ppermute | solution.py:294
  50.5 19.2 %collective-permute-start.11 = (bf16[8,64,256]{2,1,0:T(8,128)(2,1)}, bf16[8,64,256]{2,1,0:T(8,128)(2,1)S(1)}, u32[]{:S(2)}, u32[]{:S(2)}) collective-permute-start(bf16[8,64,256]{2,1,0:T(8,128)(2,1)} %get-tuple-element.15.refs_9_), channel_id=1, source_target_pairs={{0,32},{1,33},{2,34},{3,35},{4,36},{5,37},{6,38},{7,39},{8,40},{9,... | collective-permute-start | bytes 786440 | tf_op jit(solution)/shard_map/ppermute | solution.py:294
  60.5 22.9 %copy-start.14 = (bf16[8,64,256]{2,1,0:T(8,128)(2,1)}, bf16[8,64,256]{2,1,0:T(8,128)(2,1)S(1)}, u32[]{:S(2)}) copy-start(bf16[8,64,256]{2,1,0:T(8,128)(2,1)S(1)} %collective-permute-done.12.refs_2_) | copy-start | bytes 786436
  60.5 13.5 %collective-permute-start.16 = (bf16[8,64,256]{2,1,0:T(8,128)(2,1)S(1)}, bf16[8,64,256]{2,1,0:T(8,128)(2,1)S(1)}, u32[]{:S(2)}, u32[]{:S(2)}) collective-permute-start(bf16[8,64,256]{2,1,0:T(8,128)(2,1)S(1)} %collective-permute-done.12.refs_2_), channel_id=1, source_target_pairs={{0,64},{1,65},{2,66},{3,67},{4,68},{5,69},{6,70},{7,71},{8,72},{9,... | collective-permute-start | bytes 786440 | tf_op jit(solution)/shard_map/ppermute | solution.py:294
  61.4 8.2 %collective-permute-start.18 = (bf16[2,64,256]{2,1,0:T(8,128)(2,1)}, bf16[2,64,256]{2,1,0:T(8,128)(2,1)S(1)}, u32[]{:S(2)}, u32[]{:S(2)}) collective-permute-start(bf16[2,64,256]{2,1,0:T(8,128)(2,1)} %get-tuple-element.17), channel_id=1, source_target_pairs={{1,2},{2,1},{3,4},{4,3},{5,6},{6,5},{7,8},{8,7},{9,10},{10,9},{11,... | collective-permute-start | bytes 196616 | tf_op jit(solution)/shard_map/ppermute | solution.py:294
  65.2 5.1 %collective-permute-start.19 = (bf16[2,64,256]{2,1,0:T(8,128)(2,1)}, bf16[2,64,256]{2,1,0:T(8,128)(2,1)S(1)}, u32[]{:S(2)}, u32[]{:S(2)}) collective-permute-start(bf16[2,64,256]{2,1,0:T(8,128)(2,1)} %get-tuple-element.18), channel_id=1, source_target_pairs={{0,1},{1,0},{2,3},{3,2},{4,5},{5,4},{6,7},{7,6},{8,9},{9,8},{10,11... | collective-permute-start | bytes 196616 | tf_op jit(solution)/shard_map/ppermute | solution.py:294
  65.3 15.6 %collective-permute-start.10 = (bf16[8,64,256]{2,1,0:T(8,128)(2,1)}, bf16[8,64,256]{2,1,0:T(8,128)(2,1)S(1)}, u32[]{:S(2)}, u32[]{:S(2)}) collective-permute-start(bf16[8,64,256]{2,1,0:T(8,128)(2,1)} %get-tuple-element.15.refs_9_), channel_id=1, source_target_pairs={{1,34},{2,33},{3,36},{4,35},{5,38},{6,37},{7,40},{8,39},{9,42},{10... | collective-permute-start | bytes 786440 | tf_op jit(solution)/shard_map/ppermute | solution.py:294
  69.6 13.7 %copy-start.23 = (bf16[2,64,256]{2,1,0:T(8,128)(2,1)}, bf16[2,64,256]{2,1,0:T(8,128)(2,1)S(1)}, u32[]{:S(2)}) copy-start(bf16[2,64,256]{2,1,0:T(8,128)(2,1)S(1)} %collective-permute-done.18.refs_8_) | copy-start | bytes 196612
  69.6 11.2 %collective-permute-start.13 = (bf16[8,64,256]{2,1,0:T(8,128)(2,1)S(1)}, bf16[8,64,256]{2,1,0:T(8,128)(2,1)S(1)}, u32[]{:S(2)}, u32[]{:S(2)}) collective-permute-start(bf16[8,64,256]{2,1,0:T(8,128)(2,1)S(1)} %collective-permute-done.12.refs_2_), channel_id=1, source_target_pairs={{0,1},{1,0},{2,3},{3,2},{4,5},{5,4},{6,7},{7,6},{8,9},{9,8},{10,11... | collective-permute-start | bytes 786440 | tf_op jit(solution)/shard_map/ppermute | solution.py:294
  69.6 13.7 %copy-start.16 = (bf16[8,64,256]{2,1,0:T(8,128)(2,1)}, bf16[8,64,256]{2,1,0:T(8,128)(2,1)S(1)}, u32[]{:S(2)}) copy-start(bf16[8,64,256]{2,1,0:T(8,128)(2,1)S(1)} %collective-permute-done.11.refs_1_) | copy-start | bytes 786436
  69.6 12.6 %collective-permute-start.15 = (bf16[8,64,256]{2,1,0:T(8,128)(2,1)S(1)}, bf16[8,64,256]{2,1,0:T(8,128)(2,1)S(1)}, u32[]{:S(2)}, u32[]{:S(2)}) collective-permute-start(bf16[8,64,256]{2,1,0:T(8,128)(2,1)S(1)} %collective-permute-done.11.refs_1_), channel_id=1, source_target_pairs={{0,64},{1,65},{2,66},{3,67},{4,68},{5,69},{6,70},{7,71},{8,72},{9,... | collective-permute-start | bytes 786440 | tf_op jit(solution)/shard_map/ppermute | solution.py:294
  70.3 13.1 %copy-start.24 = (bf16[2,64,256]{2,1,0:T(8,128)(2,1)}, bf16[2,64,256]{2,1,0:T(8,128)(2,1)S(1)}, u32[]{:S(2)}) copy-start(bf16[2,64,256]{2,1,0:T(8,128)(2,1)S(1)} %collective-permute-done.19.refs_11_) | copy-start | bytes 196612
  70.3 13.1 %collective-permute-start.14 = (bf16[8,64,256]{2,1,0:T(8,128)(2,1)S(1)}, bf16[8,64,256]{2,1,0:T(8,128)(2,1)S(1)}, u32[]{:S(2)}, u32[]{:S(2)}) collective-permute-start(bf16[8,64,256]{2,1,0:T(8,128)(2,1)S(1)} %collective-permute-done.11.refs_1_), channel_id=1, source_target_pairs={{1,66},{2,65},{3,68},{4,67},{5,70},{6,69},{7,72},{8,71},{9,74},{10... | collective-permute-start | bytes 786440 | tf_op jit(solution)/shard_map/ppermute | solution.py:294
  74.0 9.3 %copy-start.17 = (bf16[8,64,256]{2,1,0:T(8,128)(2,1)}, bf16[8,64,256]{2,1,0:T(8,128)(2,1)S(1)}, u32[]{:S(2)}) copy-start(bf16[8,64,256]{2,1,0:T(8,128)(2,1)S(1)} %collective-permute-done.16.refs_6_) | copy-start | bytes 786436
  74.1 9.3 %collective-permute-start.17 = (bf16[8,64,256]{2,1,0:T(8,128)(2,1)S(1)}, bf16[8,64,256]{2,1,0:T(8,128)(2,1)S(1)}, u32[]{:S(2)}, u32[]{:S(2)}) collective-permute-start(bf16[8,64,256]{2,1,0:T(8,128)(2,1)S(1)} %collective-permute-done.16.refs_6_), channel_id=1, source_target_pairs={{0,1},{1,0},{2,3},{3,2},{4,5},{5,4},{6,7},{7,6},{8,9},{9,8},{10,11... | collective-permute-start | bytes 786440 | tf_op jit(solution)/shard_map/ppermute | solution.py:294
  80.8 2.6 %copy-start.18 = (bf16[8,64,256]{2,1,0:T(8,128)(2,1)}, bf16[8,64,256]{2,1,0:T(8,128)(2,1)S(1)}, u32[]{:S(2)}) copy-start(bf16[8,64,256]{2,1,0:T(8,128)(2,1)S(1)} %collective-permute-done.10.refs_0_) | copy-start | bytes 786436
  80.8 2.6 %copy-start.19 = (bf16[8,64,256]{2,1,0:T(8,128)(2,1)}, bf16[8,64,256]{2,1,0:T(8,128)(2,1)S(1)}, u32[]{:S(2)}) copy-start(bf16[8,64,256]{2,1,0:T(8,128)(2,1)S(1)} %collective-permute-done.13.refs_3_) | copy-start | bytes 786436
  82.2 1.2 copy-start.20
  83.3 0.7 copy-start.21
  84.0 0.7 copy-start.22
  95.2 12.2 %collective-permute-start.20 = (bf16[8,64,256]{2,1,0:T(8,128)(2,1)}, bf16[8,64,256]{2,1,0:T(8,128)(2,1)S(1)}, u32[]{:S(2)}, u32[]{:S(2)}) collective-permute-start(bf16[8,64,256]{2,1,0:T(8,128)(2,1)} %get-tuple-element.19.edge), channel_id=1, source_target_pairs={{1,2},{2,1},{3,4},{4,3},{5,6},{6,5},{7,8},{8,7},{9,10},{10,9},{11,... | collective-permute-start | bytes 786440 | tf_op jit(solution)/shard_map/ppermute | solution.py:294
  99.1 8.3 %collective-permute-start.21 = (bf16[8,64,256]{2,1,0:T(8,128)(2,1)}, bf16[8,64,256]{2,1,0:T(8,128)(2,1)S(1)}, u32[]{:S(2)}, u32[]{:S(2)}) collective-permute-start(bf16[8,64,256]{2,1,0:T(8,128)(2,1)} %get-tuple-element.20.inner), channel_id=1, source_target_pairs={{0,1},{1,0},{2,3},{3,2},{4,5},{5,4},{6,7},{7,6},{8,9},{9,8},{10,11... | collective-permute-start | bytes 786440 | tf_op jit(solution)/shard_map/ppermute | solution.py:294
  107.4 0.7 copy-start.3
  108.1 0.7 copy-start.4
  115.7 16.1 %collective-permute-start.23 = (bf16[20,64,256]{2,1,0:T(8,128)(2,1)S(1)}, bf16[20,64,256]{2,1,0:T(8,128)(2,1)S(1)}, u32[]{:S(2)}, u32[]{:S(2)}) collective-permute-start(bf16[20,64,256]{2,1,0:T(8,128)(2,1)S(1)} %get-tuple-element.21), channel_id=1, source_target_pairs={{0,112},{1,113},{2,114},{3,115},{4,116},{5,117},{6,118},{7,119},{8... | collective-permute-start | bytes 1966088 | tf_op jit(solution)/shard_map/ppermute | solution.py:294
  117.4 18.2 %collective-permute-start.22 = (bf16[20,64,256]{2,1,0:T(8,128)(2,1)S(1)}, bf16[20,64,256]{2,1,0:T(8,128)(2,1)S(1)}, u32[]{:S(2)}, u32[]{:S(2)}) collective-permute-start(bf16[20,64,256]{2,1,0:T(8,128)(2,1)S(1)} %get-tuple-element.22), channel_id=1, source_target_pairs={{0,16},{1,17},{2,18},{3,19},{4,20},{5,21},{6,22},{7,23},{8,24},{9,... | collective-permute-start | bytes 1966088 | tf_op jit(solution)/shard_map/ppermute | solution.py:294
  131.7 3.9 %copy-start.9 = (bf16[20,64,256]{2,1,0:T(8,128)(2,1)}, bf16[20,64,256]{2,1,0:T(8,128)(2,1)S(1)}, u32[]{:S(2)}) copy-start(bf16[20,64,256]{2,1,0:T(8,128)(2,1)S(1)} %collective-permute-done.23.later) | copy-start | bytes 1966084
  135.6 0.9 copy-start.10

commit v4 on v3

--- a/solution.py
+++ b/solution.py
@@ -12,6 +12,7 @@
 CH = 64
 WIDTH = 256
 HALF = 8
+VMEM_LIMIT = 28 << 20
 F32 = jnp.float32
 BF16 = jnp.bfloat16
 
@@ -37,9 +38,7 @@
 def columns_kernel(vals, cols, table):
     block_of = lax.broadcasted_iota(jnp.int32, (32, WIDTH), 1) // 8
     spread = (block_of == lax.broadcasted_iota(jnp.int32, (32, WIDTH), 0)).astype(F32)
-    table[...] = jnp.dot(
-        vals[...].astype(F32).astype(BF16), spread.astype(BF16), preferred_element_type=F32
-    )
+    table[...] = jnp.dot(vals[...], spread.astype(BF16), preferred_element_type=F32)
     apart = lax.broadcasted_iota(jnp.int32, (WIDTH, WIDTH), 0) - lax.broadcasted_iota(
         jnp.int32, (WIDTH, WIDTH), 1
     )
@@ -70,7 +69,7 @@
     )(vals)
 
 
-def warp_into(flags, cols, table, source_of, base, passed, put_of):
+def warp_into(flags, cols, table, source_of, passed, put_of):
     has_above = (flags[1] > 0).astype(F32)
     has_below = (flags[2] > 0).astype(F32)
     lanes = (16, WIDTH)
@@ -83,12 +82,12 @@
             block, first, count, _, _ = BLOCKS[k]
             window = source_of(which, first, count).reshape(count * CH, WIDTH)
             passed[k][...] = jnp.dot(
-                window, cols[base + which * 4 + block], preferred_element_type=F32
+                window, cols[which * 4 + block], preferred_element_type=F32
             ).reshape(count, CH, WIDTH)
 
         def row_pass(k):
             block, _, count, outs, start = BLOCKS[k]
-            at = (base + which * 4 + block) * 8
+            at = (which * 4 + block) * 8
             entry = table[pl.ds(pl.multiple_of(at, 8), 8), :]
             s = entry[0:1].astype(jnp.int32) + 5
             keep = {0: has_above, 3: has_below}.get(block, 1.0)
@@ -171,7 +170,7 @@
         target[pl.ds(turn(turned, 8 * p, 24), 8)] = pieces[p][...]
 
 
-def level_kernel(sources, base, flags, cols, table, wu, wm, *refs):
+def level_kernel(sources, flags, cols, table, wu, wm, *refs):
     own_outer, own_edge, own_inner, own_near = refs[4 * sources : 4 * sources + 4]
     outs = refs[4 * sources + 4 : 4 * sources + 8]
     src, joined, act = refs[4 * sources + 8 : 4 * sources + 11]
@@ -179,10 +178,10 @@
     turned = flags[0]
     for i in range(sources):
         stack_rows(src.at[i], turned, refs[4 * i : 4 * i + 4])
-    joined[pl.ds(turn(turned, 0, 18), 2), OWN] = own_outer[...]
+    joined[pl.ds(turn(turned, 0, 18), 2), OWN] = own_outer[0:2]
     joined[pl.ds(turn(turned, 2, 12), 8), OWN] = own_edge[...]
     joined[pl.ds(turn(turned, 10, 12), 8), OWN] = own_inner[...]
-    joined[pl.ds(turn(turned, 18, 18), 2), OWN] = own_near[...]
+    joined[pl.ds(turn(turned, 18, 18), 2), OWN] = own_near[0:2]
 
     def source_of(which, first, count):
         return src[which ^ flags[4] if sources == 2 else 0, first : first + count]
@@ -193,11 +192,11 @@
 
         return put
 
-    warp_into(flags, cols, table, source_of, base, passed, put_of)
+    warp_into(flags, cols, table, source_of, passed, put_of)
     convolve_band(flags, wu, wm, joined, act, False, outs)
 
 
-def warp_kernel(base, flags, cols, table, outer, edge, inner, near, out, src, *passed):
+def warp_kernel(flags, cols, table, outer, edge, inner, near, ahead, back, src, both, *passed):
     stack_rows(src, flags[0], (outer, edge, inner, near))
 
     def source_of(which, first, count):
@@ -205,11 +204,13 @@
 
     def put_of(which):
         def put(row, c, value):
-            out[which, row, c : c + 16, :] = value
+            both[which, row, c : c + 16, :] = value
 
         return put
 
-    warp_into(flags, cols, table, source_of, base, passed, put_of)
+    warp_into(flags, cols, table, source_of, passed, put_of)
+    ahead[...] = both[0]
+    back[...] = both[1]
 
 
 def last_kernel(flags, wu, wm, outer, edge, inner, near, earlier, later, out, joined, act):
@@ -231,6 +232,7 @@
         in_specs=[pl.BlockSpec(memory_space=pltpu.SMEM)] + [vmem] * (len(operands) - 1),
         out_specs=(vmem,) * len(out_shape),
         scratch_shapes=scratch,
+        compiler_params=pltpu.CompilerParams(vmem_limit_bytes=VMEM_LIMIT),
         cost_estimate=pl.CostEstimate(
             flops=cost, bytes_accessed=4_000_000, transcendentals=300_000
         ),
@@ -246,13 +248,13 @@
     return [pltpu.VMEM((20, 3 * CH, WIDTH), BF16), pltpu.VMEM((18, CH, WIDTH), BF16)]
 
 
-def run_level(flags, cols, table, base, wu, wm, sources, own, interpret=False):
+def run_level(flags, cols, table, wu, wm, sources, own, interpret=False):
     half = jax.ShapeDtypeStruct((HALF, CH, WIDTH), BF16)
     edge = jax.ShapeDtypeStruct((2, CH, WIDTH), BF16)
     operands = [flags, cols, table, wu, wm] + [p for s in sources for p in s] + list(own)
     scratch = [pltpu.VMEM((len(sources), 32, CH, WIDTH), BF16)]
     return on_core(
-        functools.partial(level_kernel, len(sources), base),
+        functools.partial(level_kernel, len(sources)),
         (half, half, edge, edge),
         scratch + band_buffers() + passed_buffers(),
         3_000_000_000,
@@ -261,15 +263,16 @@
     )
 
 
-def run_warp(flags, cols, table, base, pieces, interpret=False):
+def run_warp(flags, cols, table, pieces, interpret=False):
     return on_core(
-        functools.partial(warp_kernel, base),
-        (jax.ShapeDtypeStruct((2, 20, CH, WIDTH), BF16),),
-        [pltpu.VMEM((32, CH, WIDTH), BF16)] + passed_buffers(),
+        warp_kernel,
+        (jax.ShapeDtypeStruct((20, CH, WIDTH), BF16),) * 2,
+        [pltpu.VMEM((32, CH, WIDTH), BF16), pltpu.VMEM((2, 20, CH, WIDTH), BF16)]
+        + passed_buffers(),
         1_500_000_000,
         [flags, cols, table, *pieces],
         interpret,
-    )[0]
+    )
 
 
 def run_last(flags, wu, wm, own, warped, interpret=False):
@@ -311,6 +314,15 @@
 def tap_weights(w):
     o, j = w.shape[2], w.shape[3]
     return jnp.transpose(w, (1, 2, 0, 3)).reshape(3 * o, 3 * j)
+
+
+def with_table(rows, entries):
+    plane = jnp.pad(entries.reshape(3, WIDTH), ((0, CH - 3), (0, 0)))
+    return jnp.concatenate([rows, plane[None]])
+
+
+def table_of(payload):
+    return payload[2, 0:3].reshape(2, LEVELS, 4, 1, 32)
 
 
 def shards(features, block_shift, quarter_pel, update_mask, uniting_weight, mixing_weight):
@@ -323,46 +335,44 @@
     rim = lax.dynamic_slice_in_dim(band, 14 * turned, 2, axis=0)
     near = lax.dynamic_slice_in_dim(band, 14 - 14 * turned, 2, axis=0)
     wu, wm = tap_weights(uniting_weight), tap_weights(mixing_weight)
-
-    def to_other(t):
-        return t + 4
-
-    def across(t):
-        return t + 2 if t % 4 < 2 else t - 2
-
-    def ahead(t):
-        return t + 1
-
-    def back(t):
-        return t - 1
-
-    e = send(edge, to_other)
-    i = send(inner, to_other)
-    h = send(edge, to_other, off_chip)
-    own = jnp.stack([block_shift[:, :, 0], quarter_pel[:, :, 0]])
-    above = send(own[:, :, :, 1:2], row_to=lambda r: r + 1)
-    below = send(own[:, :, :, 0:1], row_to=lambda r: r - 1)
-    packed = jnp.concatenate([above, own, below], axis=3)
-    for_ahead = send(packed[:, 0, 0:2], back)
-    for_back = send(packed[:, 0, 2:4], ahead)
-    own_outer = send(rim, row_to=off_chip)
-    own_near = send(near, row_to=on_chip)
-    n = send(i, row_to=on_chip)
-    cols, table = make_columns(
-        jnp.concatenate(
-            [
-                level_values(packed[:, 2]),
-                level_values(packed[:, 1]),
-                level_values(jnp.concatenate([for_ahead, for_back], axis=1)),
-            ]
-        )
-    )
     common = [turned, (row > 0).astype(jnp.int32), (row < rows - 1).astype(jnp.int32)]
     swapped = (lax.axis_index("tm") % 4 < 2).astype(jnp.int32)
     flags = [jnp.stack(common + [update_mask[k, 0], swapped]) for k in range(LEVELS)]
 
+    def to_other(t):
+        return t + 4
+
+    def across(t):
+        return t + 2 if t % 4 < 2 else t - 2
+
+    def ahead(t):
+        return t + 1
+
+    def back(t):
+        return t - 1
+
+    own = jnp.stack([block_shift[:, :, 0], quarter_pel[:, :, 0]]).astype(BF16)
+    at_edge = jnp.where(turned == 1, own[:, :, :, 1], own[:, :, :, 0])
+    at_near = jnp.where(turned == 1, own[:, :, :, 0], own[:, :, :, 1])
+
+    e = send(edge, to_other)
+    h = send(edge, to_other, off_chip)
+    i = send(inner, to_other)
+    own_outer = send(with_table(rim, at_edge), row_to=off_chip)
+    own_near = send(with_table(near, at_near), row_to=on_chip)
+    n = send(i, row_to=on_chip)
+    outer_table, near_table = table_of(own_outer), table_of(own_near)
+    packed = jnp.concatenate(
+        [
+            jnp.where(turned == 1, near_table, outer_table),
+            own,
+            jnp.where(turned == 1, outer_table, near_table),
+        ],
+        axis=3,
+    )
+    cols, table = make_columns(level_values(packed[:, 2]))
     edge, inner, rim, near = run_level(
-        flags[2], cols, table, 0, wu, wm, [(h, e, i, n)], (own_outer, edge, inner, own_near)
+        flags[2], cols, table, wu, wm, [(h, e, i, n)], (own_outer, edge, inner, own_near)
     )
 
     own_outer = send(rim, row_to=off_chip)
@@ -374,12 +384,14 @@
     xh = send(e, to_other, off_chip)
     xi = send(i, to_other)
     n = send(i, row_to=on_chip)
+    for_ahead = send(packed[:, 0, 0:2], back)
+    for_back = send(packed[:, 0, 2:4], ahead)
     xn = send(xi, row_to=on_chip)
+    cols, table = make_columns(level_values(packed[:, 1]))
     edge, inner, _, _ = run_level(
         flags[1],
         cols,
         table,
-        8,
         wu,
         wm,
         [(h, e, i, n), (xh, xe, xi, xn)],
@@ -388,10 +400,13 @@
 
     outer = send(edge, row_to=off_chip)
     near = send(inner, row_to=on_chip)
+    cols, table = make_columns(
+        level_values(jnp.concatenate([for_ahead, for_back], axis=1))
+    )
     own = (outer, edge, inner, near)
-    warped = run_warp(flags[0], cols, table, 16, own)
-    earlier = send(warped[0], ahead)
-    later = send(warped[1], back)
+    to_ahead, to_back = run_warp(flags[0], cols, table, own)
+    earlier = send(to_ahead, ahead)
+    later = send(to_back, back)
     return run_last(flags[0], wu, wm, own, (earlier, later))[None]
 
 

time: 144 us -> 129 us (0.90)
  the two profiles are of different devices: /device:TPU:13 before, /device:TPU:8 now
where the time goes in v4:
time: 129 us; the launch traced here: 128 us
  starting transfers between devices  40 us (31%)
  waiting for transfers between devices  39 us (30%)
  Pallas kernels  30.6 us (24%)
  local copies, waits for them, and re-layouts  17.8 us (14%)
    ppermute x22, starting transfers between devices, send(): return lax.ppermute(x, ('tm', 'rows'), route)  40 us
    ppermute x22, waiting for transfers between devices, send(): return lax.ppermute(x, ('tm', 'rows'), route)  39 us
    pallas_call x4, Pallas kernels, on_core(): pl.pallas_call(kernel, out_shape=out_shape, in_specs=[pl.BlockSpec(memory...  23.7 us
    unnamed x30, local copies, waits for them, and re-layouts  10.1 us
    pallas_call x3, Pallas kernels, make_columns(): pl.pallas_call(columns_kernel, out_shape=(jax.ShapeDtypeStruct((count, WI...  6.91 us
  transfers between devices with their start and end apart: 22, of which 8 were waited for; matrix products, arithmetic and copies ran while one was open for 5% of the time, Pallas kernels for 5%

profile of v4, /device:TPU:8, one launch (start us, length us, event | category | flops | bytes accessed | tf_op | source)
XLA Modules:
  0.0 128.0 jit_solution(1149189359277150874)
XLA Ops:
  0.0 1.1 dynamic-slice_bitcast_fusion
  1.1 4.0 %collective-permute-start.2 = (bf16[8,64,256]{2,1,0:T(8,128)(2,1)S(1)}, bf16[8,64,256]{2,1,0:T(8,128)(2,1)S(1)}, u32[]{:S(2)}, u32[]{:S(2)}) collective-permute-start(bf16[8,64,256]{2,1,0:T(8,128)(2,1)S(1)} %get-tuple-element.36.refs_5_), channel_id=1, source_target_pairs={{1,66},{2,65},{3,68},{4,67},{5,70},{6,69},{7,72},{8,71},{9,74},{10... | collective-permute-start | bytes 786440 | tf_op jit(solution)/shard_map/ppermute | solution.py:297
  5.1 0.3 collective-permute-start.3
  5.4 0.1 fusion
  5.5 0.1 select_n.83
  5.6 0.9 dynamic-slice_bitcast_fusion.3
  6.5 0.7 collective-permute-start
  7.2 0.1 select_n.86
  7.4 4.0 %collective-permute-start.1 = (bf16[3,64,256]{2,1,0:T(8,128)(2,1)S(1)}, bf16[3,64,256]{2,1,0:T(8,128)(2,1)S(1)}, u32[]{:S(2)}, u32[]{:S(2)}) collective-permute-start(bf16[3,64,256]{2,1,0:T(8,128)(2,1)S(1)} %pad_maximum_fusion.1), channel_id=1, source_target_pairs={{1,2},{2,1},{3,4},{4,3},{5,6},{6,5},{7,8},{8,7},{9,10},{10,9},{11,... | collective-permute-start | bytes 294920 | tf_op jit(solution)/shard_map/ppermute | solution.py:297
  11.4 0.4 collective-permute-start.4
  11.8 0.6 fusion.4
  12.4 0.3 copy.16
  12.6 0.3 reshape.85.wu
  12.9 0.6 copy-done.11
  13.5 0.1 copy.17
  13.7 0.2 reshape.86.wm
  13.8 0.7 stack.52.flags
  14.6 2.1 %collective-permute-done.1.refs_4_ = bf16[3,64,256]{2,1,0:T(8,128)(2,1)S(1)} collective-permute-done((bf16[3,64,256]{2,1,0:T(8,128)(2,1)S(1)}, bf16[3,64,256]{2,1,0:T(8,128)(2,1)S(1)}, u32[]{:S(2)}, u32[]{:S(2)}) %collective-permute-start.1) | collective-permute-done | bytes 98336 | tf_op jit(solution)/shard_map/ppermute | solution.py:297
  16.7 0.1 select_n.93
  16.8 0.1 select_n.94
  16.9 5.0 %collective-permute-done.4.refs_2_ = bf16[8,64,256]{2,1,0:T(8,128)(2,1)S(1)} collective-permute-done((bf16[8,64,256]{2,1,0:T(8,128)(2,1)S(1)}, bf16[8,64,256]{2,1,0:T(8,128)(2,1)S(1)}, u32[]{:S(2)}, u32[]{:S(2)}) %collective-permute-start.4) | collective-permute-done | bytes 262176 | tf_op jit(solution)/shard_map/ppermute | solution.py:297
  22.0 0.6 pad.20
  22.6 2.3 %shard_map.65 = (bf16[8,256,256]{2,1,0:T(8,128)(2,1)}, f32[64,256]{1,0:T(8,128)}) custom-call(bf16[64,32]{1,0:T(8,128)(2,1)} %bitcast.60), custom_call_target="tpu_custom_call" | custom-call | flops 100000000 | bytes 3000000 | tf_op jit(solution)/shard_map/pallas_call | solution.py:57
  24.9 1.2 copy-done.5
  26.2 0.8 copy-done.8
  27.0 7.2 %shard_map.66 = (bf16[8,64,256]{2,1,0:T(8,128)(2,1)S(1)}, bf16[8,64,256]{2,1,0:T(8,128)(2,1)S(1)}, bf16[2,64,256]{2,1,0:T(8,128)(2,1)S(1)}, bf16[2,64,256]{2,1,0:T(8,128)(2,1)S(1)}) custom-call(s32[5]{0:T(128)S(1)} %stack.52.flags, bf16[8,256,256]{2,1,0:T(8,128)(2,1)S(1)} %copy-done.5, f32[64,256]{1,0:T(8,128)S(1)} %copy-done.8, ...), custom_call_target="tpu_custom_call" | custom-call | flops 3000000000 | bytes 4000000 | tf_op jit(solution)/shard_map/pallas_call | solution.py:229
  34.2 4.0 %collective-permute-start.8 = (bf16[8,64,256]{2,1,0:T(8,128)(2,1)S(1)}, bf16[8,64,256]{2,1,0:T(8,128)(2,1)S(1)}, u32[]{:S(2)}, u32[]{:S(2)}) collective-permute-start(bf16[8,64,256]{2,1,0:T(8,128)(2,1)S(1)} %get-tuple-element.24.refs_10_), channel_id=1, source_target_pairs={{0,32},{1,33},{2,34},{3,35},{4,36},{5,37},{6,38},{7,39},{8,40},{9,... | collective-permute-start | bytes 786440 | tf_op jit(solution)/shard_map/ppermute | solution.py:297
  38.2 0.1 collective-permute-start.7
  38.3 7.1 %collective-permute-done.8.refs_2_ = bf16[8,64,256]{2,1,0:T(8,128)(2,1)S(1)} collective-permute-done((bf16[8,64,256]{2,1,0:T(8,128)(2,1)S(1)}, bf16[8,64,256]{2,1,0:T(8,128)(2,1)S(1)}, u32[]{:S(2)}, u32[]{:S(2)}) %collective-permute-start.8) | collective-permute-done | bytes 262176 | tf_op jit(solution)/shard_map/ppermute | solution.py:297
  45.3 0.7 collective-permute-start.12
  46.1 2.0 %collective-permute-start.14 = (bf16[2,64,256]{2,1,0:T(8,128)(2,1)S(1)}, bf16[2,64,256]{2,1,0:T(8,128)(2,1)S(1)}, u32[]{:S(2)}, u32[]{:S(2)}) collective-permute-start(bf16[2,64,256]{2,1,0:T(8,128)(2,1)S(1)} %get-tuple-element.25), channel_id=1, source_target_pairs={{1,2},{2,1},{3,4},{4,3},{5,6},{6,5},{7,8},{8,7},{9,10},{10,9},{11,... | collective-permute-start | bytes 196616 | tf_op jit(solution)/shard_map/ppermute | solution.py:297
  48.1 1.5 %collective-permute-start.15 = (bf16[2,64,256]{2,1,0:T(8,128)(2,1)S(1)}, bf16[2,64,256]{2,1,0:T(8,128)(2,1)S(1)}, u32[]{:S(2)}, u32[]{:S(2)}) collective-permute-start(bf16[2,64,256]{2,1,0:T(8,128)(2,1)S(1)} %get-tuple-element.26), channel_id=1, source_target_pairs={{0,1},{1,0},{2,3},{3,2},{4,5},{5,4},{6,7},{7,6},{8,9},{9,8},{10,11... | collective-permute-start | bytes 196616 | tf_op jit(solution)/shard_map/ppermute | solution.py:297
  49.6 7.5 %collective-permute-start.6 = (bf16[8,64,256]{2,1,0:T(8,128)(2,1)S(1)}, bf16[8,64,256]{2,1,0:T(8,128)(2,1)S(1)}, u32[]{:S(2)}, u32[]{:S(2)}) collective-permute-start(bf16[8,64,256]{2,1,0:T(8,128)(2,1)S(1)} %get-tuple-element.23.refs_9_), channel_id=1, source_target_pairs={{1,34},{2,33},{3,36},{4,35},{5,38},{6,37},{7,40},{8,39},{9,42},{10... | collective-permute-start | bytes 786440 | tf_op jit(solution)/shard_map/ppermute | solution.py:297
  57.1 3.7 %collective-permute-start.10 = (bf16[8,64,256]{2,1,0:T(8,128)(2,1)S(1)}, bf16[8,64,256]{2,1,0:T(8,128)(2,1)S(1)}, u32[]{:S(2)}, u32[]{:S(2)}) collective-permute-start(bf16[8,64,256]{2,1,0:T(8,128)(2,1)S(1)} %collective-permute-done.7.refs_1_), channel_id=1, source_target_pairs={{1,66},{2,65},{3,68},{4,67},{5,70},{6,69},{7,72},{8,71},{9,74},{10... | collective-permute-start | bytes 786440 | tf_op jit(solution)/shard_map/ppermute | solution.py:297
  60.8 0.1 collective-permute-start.11
  60.9 0.1 collective-permute-start.9
  61.0 0.5 collective-permute-start.13
  61.5 0.7 stack.50.flags
  62.2 0.6 pad.19
  62.8 2.3 %shard_map.64 = (bf16[8,256,256]{2,1,0:T(8,128)(2,1)}, f32[64,256]{1,0:T(8,128)}) custom-call(bf16[64,32]{1,0:T(8,128)(2,1)} %bitcast.61), custom_call_target="tpu_custom_call" | custom-call | flops 100000000 | bytes 3000000 | tf_op jit(solution)/shard_map/pallas_call | solution.py:57
  65.1 5.1 %collective-permute-done.10.refs_4_ = bf16[8,64,256]{2,1,0:T(8,128)(2,1)S(1)} collective-permute-done((bf16[8,64,256]{2,1,0:T(8,128)(2,1)S(1)}, bf16[8,64,256]{2,1,0:T(8,128)(2,1)S(1)}, u32[]{:S(2)}, u32[]{:S(2)}) %collective-permute-start.10) | collective-permute-done | bytes 262176 | tf_op jit(solution)/shard_map/ppermute | solution.py:297
  70.2 0.8 collective-permute-done.11.refs_5_
  71.1 0.7 copy-done
  71.8 0.7 copy-done.2
  72.5 0.9 copy-done.1
  73.4 0.9 copy-done.3
  74.4 1.2 copy-done.4
  75.6 0.8 copy-done.7
  76.5 7.8 %shard_map.67 = (bf16[8,64,256]{2,1,0:T(8,128)(2,1)S(1)}, bf16[8,64,256]{2,1,0:T(8,128)(2,1)S(1)}, bf16[2,64,256]{2,1,0:T(8,128)(2,1)}, bf16[2,64,256]{2,1,0:T(8,128)(2,1)}) custom-call(s32[5]{0:T(128)S(1)} %stack.50.flags, bf16[8,256,256]{2,1,0:T(8,128)(2,1)S(1)} %copy-done.4, f32[64,256]{1,0:T(8,128)S(1)} %copy-done.7, bf16[192,576]{1,0:T(8,128)(2,1)S(1)} %reshape.85.wu, ...), custom_call_target="tpu_custom_call" | custom-call | flops 3000000000 | bytes 4000000 | tf_op jit(solution)/shard_map/pallas_call | solution.py:229
  84.3 4.1 %collective-permute-start.16 = (bf16[8,64,256]{2,1,0:T(8,128)(2,1)S(1)}, bf16[8,64,256]{2,1,0:T(8,128)(2,1)S(1)}, u32[]{:S(2)}, u32[]{:S(2)}) collective-permute-start(bf16[8,64,256]{2,1,0:T(8,128)(2,1)S(1)} %get-tuple-element.27.edge), channel_id=1, source_target_pairs={{1,2},{2,1},{3,4},{4,3},{5,6},{6,5},{7,8},{8,7},{9,10},{10,9},{11,... | collective-permute-start | bytes 786440 | tf_op jit(solution)/shard_map/ppermute | solution.py:297
  88.4 0.1 collective-permute-start.17
  88.5 1.8 %collective-permute-start.18 = (bf16[2,2,4,32]{3,2,1,0:T(4,128)(2,1)S(1)}, bf16[2,2,4,32]{3,2,1,0:T(4,128)(2,1)S(1)}, u32[]{:S(2)}, u32[]{:S(2)}) collective-permute-start(bf16[2,2,4,32]{3,2,1,0:T(4,128)(2,1)S(1)} %get-tuple-element.41), channel_id=1, source_target_pairs={{0,112},{1,113},{2,114},{3,115},{4,116},{5,117},{6,118},{7,119},{8... | collective-permute-start | bytes 3080 | tf_op jit(solution)/shard_map/ppermute | solution.py:297
  90.3 0.3 collective-permute-start.19
  90.6 0.7 stack.49.flags
  91.3 2.9 %collective-permute-done.18 = bf16[2,2,4,32]{3,2,1,0:T(4,128)(2,1)S(1)} collective-permute-done((bf16[2,2,4,32]{3,2,1,0:T(4,128)(2,1)S(1)}, bf16[2,2,4,32]{3,2,1,0:T(4,128)(2,1)S(1)}, u32[]{:S(2)}, u32[]{:S(2)}) %collective-permute-start.18) | collective-permute-done | bytes 1056 | tf_op jit(solution)/shard_map/ppermute | solution.py:297
  94.2 2.1 %collective-permute-done.19 = bf16[2,2,4,32]{3,2,1,0:T(4,128)(2,1)S(1)} collective-permute-done((bf16[2,2,4,32]{3,2,1,0:T(4,128)(2,1)S(1)}, bf16[2,2,4,32]{3,2,1,0:T(4,128)(2,1)S(1)}, u32[]{:S(2)}, u32[]{:S(2)}) %collective-permute-start.19) | collective-permute-done | bytes 1056 | tf_op jit(solution)/shard_map/ppermute | solution.py:297
  96.4 0.6 pad.21
  97.0 2.3 %shard_map.68 = (bf16[8,256,256]{2,1,0:T(8,128)(2,1)}, f32[64,256]{1,0:T(8,128)}) custom-call(bf16[64,32]{1,0:T(8,128)(2,1)} %bitcast.59), custom_call_target="tpu_custom_call" | custom-call | flops 100000000 | bytes 3000000 | tf_op jit(solution)/shard_map/pallas_call | solution.py:57
  99.3 1.2 copy-done.6
  100.6 0.8 copy-done.9
  101.4 2.8 %shard_map.69 = (bf16[20,64,256]{2,1,0:T(8,128)(2,1)S(1)}, bf16[20,64,256]{2,1,0:T(8,128)(2,1)S(1)}) custom-call(s32[5]{0:T(128)S(1)} %stack.49.flags, bf16[8,256,256]{2,1,0:T(8,128)(2,1)S(1)} %copy-done.6, f32[64,256]{1,0:T(8,128)S(1)} %copy-done.9, bf16[8,64,256]{2,1,0:T(8,128)(2,1)S(1)} %collective-permute-done.16.outer, ...), custom_call_target="tpu_custom_call" | custom-call | flops 1500000000 | bytes 4000000 | tf_op jit(solution)/shard_map/pallas_call | solution.py:229
  104.3 4.1 %collective-permute-start.21 = (bf16[20,64,256]{2,1,0:T(8,128)(2,1)S(1)}, bf16[20,64,256]{2,1,0:T(8,128)(2,1)S(1)}, u32[]{:S(2)}, u32[]{:S(2)}) collective-permute-start(bf16[20,64,256]{2,1,0:T(8,128)(2,1)S(1)} %get-tuple-element.32), channel_id=1, source_target_pairs={{0,112},{1,113},{2,114},{3,115},{4,116},{5,117},{6,118},{7,119},{8... | collective-permute-start | bytes 1966088 | tf_op jit(solution)/shard_map/ppermute | solution.py:297
  108.4 13.7 %collective-permute-done.20.earlier = bf16[20,64,256]{2,1,0:T(8,128)(2,1)S(1)} collective-permute-done((bf16[20,64,256]{2,1,0:T(8,128)(2,1)S(1)}, bf16[20,64,256]{2,1,0:T(8,128)(2,1)S(1)}, u32[]{:S(2)}, u32[]{:S(2)}) %collective-permute-start.20) | collective-permute-done | bytes 655392 | tf_op jit(solution)/shard_map/ppermute | solution.py:297
  122.1 5.9 %shard_map.70 = bf16[16,64,256]{2,1,0:T(8,128)(2,1)} custom-call(s32[5]{0:T(128)S(1)} %stack.49.flags, bf16[192,576]{1,0:T(8,128)(2,1)S(1)} %reshape.85.wu, bf16[192,192]{1,0:T(8,128)(2,1)S(1)} %reshape.86.wm, bf16[8,64,256]{2,1,0:T(8,128)(2,1)S(1)} %collective-permute-done.16.outer, bf16[8,64,256]{2,1,0:T(8,128)(2,1)S(1)} %get-tuple-element.27.edge, ...), custom_call_target="tpu_custom_call" | custom-call | flops 1500000000 | bytes 4000000 | tf_op jit(solution)/shard_map/pallas_call | solution.py:229
  (48 shorter events, 0.3 us)
Async XLA Ops:
  0.0 5.4 %copy-start.13 = (s32[3,4,1,2,32]{4,3,2,1,0:T(2,128)S(1)}, s32[3,4,1,2,32]{4,3,2,1,0:T(2,128)}, u32[]{:S(2)}) copy-start(s32[3,4,1,2,32]{4,3,2,1,0:T(2,128)} %param.8) | copy-start | bytes 9220
  1.1 4.3 %copy-start.12 = (s32[3,4,1,2,32]{4,3,2,1,0:T(2,128)S(1)}, s32[3,4,1,2,32]{4,3,2,1,0:T(2,128)}, u32[]{:S(2)}) copy-start(s32[3,4,1,2,32]{4,3,2,1,0:T(2,128)} %param.7) | copy-start | bytes 9220
  1.1 23.8 %collective-permute-start.2 = (bf16[8,64,256]{2,1,0:T(8,128)(2,1)S(1)}, bf16[8,64,256]{2,1,0:T(8,128)(2,1)S(1)}, u32[]{:S(2)}, u32[]{:S(2)}) collective-permute-start(bf16[8,64,256]{2,1,0:T(8,128)(2,1)S(1)} %get-tuple-element.36.refs_5_), channel_id=1, source_target_pairs={{1,66},{2,65},{3,68},{4,67},{5,70},{6,69},{7,72},{8,71},{9,74},{10... | collective-permute-start | bytes 786440 | tf_op jit(solution)/shard_map/ppermute | solution.py:297
  5.1 19.8 %collective-permute-start.3 = (bf16[8,64,256]{2,1,0:T(8,128)(2,1)S(1)}, bf16[8,64,256]{2,1,0:T(8,128)(2,1)S(1)}, u32[]{:S(2)}, u32[]{:S(2)}) collective-permute-start(bf16[8,64,256]{2,1,0:T(8,128)(2,1)S(1)} %get-tuple-element.36.refs_5_), channel_id=1, source_target_pairs={{0,64},{1,65},{2,66},{3,67},{4,68},{5,69},{6,70},{7,71},{8,72},{9,... | collective-permute-start | bytes 786440 | tf_op jit(solution)/shard_map/ppermute | solution.py:297
  6.5 5.8 %copy-start.10 = (bf16[3,3,64,192]{3,2,1,0:T(8,128)(2,1)S(1)}, bf16[3,3,64,192]{3,2,1,0:T(8,128)(2,1)}, u32[]{:S(2)}) copy-start(bf16[3,3,64,192]{3,2,1,0:T(8,128)(2,1)} %param.10) | copy-start | bytes 663556
  6.5 8.0 %collective-permute-start = (bf16[3,64,256]{2,1,0:T(8,128)(2,1)S(1)}, bf16[3,64,256]{2,1,0:T(8,128)(2,1)S(1)}, u32[]{:S(2)}, u32[]{:S(2)}) collective-permute-start(bf16[3,64,256]{2,1,0:T(8,128)(2,1)S(1)} %pad_maximum_fusion), channel_id=1, source_target_pairs={{0,1},{1,0},{2,3},{3,2},{4,5},{5,4},{6,7},{7,6},{8,9},{9,8},{10,11... | collective-permute-start | bytes 294920 | tf_op jit(solution)/shard_map/ppermute | solution.py:297
  7.3 4.4 %copy-start.14 = (s32[3,1]{0,1:T(1,128)S(1)}, s32[3,1]{0,1:T(1,128)}, u32[]{:S(2)}) copy-start(s32[3,1]{0,1:T(1,128)} %param.9) | copy-start | bytes 40
  7.4 9.4 %collective-permute-start.1 = (bf16[3,64,256]{2,1,0:T(8,128)(2,1)S(1)}, bf16[3,64,256]{2,1,0:T(8,128)(2,1)S(1)}, u32[]{:S(2)}, u32[]{:S(2)}) collective-permute-start(bf16[3,64,256]{2,1,0:T(8,128)(2,1)S(1)} %pad_maximum_fusion.1), channel_id=1, source_target_pairs={{1,2},{2,1},{3,4},{4,3},{5,6},{6,5},{7,8},{8,7},{9,10},{10,9},{11,... | collective-permute-start | bytes 294920 | tf_op jit(solution)/shard_map/ppermute | solution.py:297
  11.4 10.5 %collective-permute-start.4 = (bf16[8,64,256]{2,1,0:T(8,128)(2,1)S(1)}, bf16[8,64,256]{2,1,0:T(8,128)(2,1)S(1)}, u32[]{:S(2)}, u32[]{:S(2)}) collective-permute-start(bf16[8,64,256]{2,1,0:T(8,128)(2,1)S(1)} %get-tuple-element.35.refs_6_), channel_id=1, source_target_pairs={{0,64},{1,65},{2,66},{3,67},{4,68},{5,69},{6,70},{7,71},{8,72},{9,... | collective-permute-start | bytes 786440 | tf_op jit(solution)/shard_map/ppermute | solution.py:297
  12.6 0.9 copy-start.11
  21.9 3.0 %collective-permute-start.5 = (bf16[8,64,256]{2,1,0:T(8,128)(2,1)S(1)}, bf16[8,64,256]{2,1,0:T(8,128)(2,1)S(1)}, u32[]{:S(2)}, u32[]{:S(2)}) collective-permute-start(bf16[8,64,256]{2,1,0:T(8,128)(2,1)S(1)} %collective-permute-done.4.refs_2_), channel_id=1, source_target_pairs={{0,1},{1,0},{2,3},{3,2},{4,5},{5,4},{6,7},{7,6},{8,9},{9,8},{10,11... | collective-permute-start | bytes 786440 | tf_op jit(solution)/shard_map/ppermute | solution.py:297
  24.9 1.2 copy-start.5
  26.2 0.8 copy-start.8
  34.2 11.1 %collective-permute-start.8 = (bf16[8,64,256]{2,1,0:T(8,128)(2,1)S(1)}, bf16[8,64,256]{2,1,0:T(8,128)(2,1)S(1)}, u32[]{:S(2)}, u32[]{:S(2)}) collective-permute-start(bf16[8,64,256]{2,1,0:T(8,128)(2,1)S(1)} %get-tuple-element.24.refs_10_), channel_id=1, source_target_pairs={{0,32},{1,33},{2,34},{3,35},{4,36},{5,37},{6,38},{7,39},{8,40},{9,... | collective-permute-start | bytes 786440 | tf_op jit(solution)/shard_map/ppermute | solution.py:297
  38.2 18.9 %collective-permute-start.7 = (bf16[8,64,256]{2,1,0:T(8,128)(2,1)S(1)}, bf16[8,64,256]{2,1,0:T(8,128)(2,1)S(1)}, u32[]{:S(2)}, u32[]{:S(2)}) collective-permute-start(bf16[8,64,256]{2,1,0:T(8,128)(2,1)S(1)} %get-tuple-element.23.refs_9_), channel_id=1, source_target_pairs={{0,32},{1,33},{2,34},{3,35},{4,36},{5,37},{6,38},{7,39},{8,40},{9,... | collective-permute-start | bytes 786440 | tf_op jit(solution)/shard_map/ppermute | solution.py:297
  45.3 15.7 %collective-permute-start.12 = (bf16[8,64,256]{2,1,0:T(8,128)(2,1)S(1)}, bf16[8,64,256]{2,1,0:T(8,128)(2,1)S(1)}, u32[]{:S(2)}, u32[]{:S(2)}) collective-permute-start(bf16[8,64,256]{2,1,0:T(8,128)(2,1)S(1)} %collective-permute-done.8.refs_2_), channel_id=1, source_target_pairs={{0,64},{1,65},{2,66},{3,67},{4,68},{5,69},{6,70},{7,71},{8,72},{9,... | collective-permute-start | bytes 786440 | tf_op jit(solution)/shard_map/ppermute | solution.py:297
  46.1 14.8 %collective-permute-start.14 = (bf16[2,64,256]{2,1,0:T(8,128)(2,1)S(1)}, bf16[2,64,256]{2,1,0:T(8,128)(2,1)S(1)}, u32[]{:S(2)}, u32[]{:S(2)}) collective-permute-start(bf16[2,64,256]{2,1,0:T(8,128)(2,1)S(1)} %get-tuple-element.25), channel_id=1, source_target_pairs={{1,2},{2,1},{3,4},{4,3},{5,6},{6,5},{7,8},{8,7},{9,10},{10,9},{11,... | collective-permute-start | bytes 196616 | tf_op jit(solution)/shard_map/ppermute | solution.py:297
  48.1 12.8 %collective-permute-start.15 = (bf16[2,64,256]{2,1,0:T(8,128)(2,1)S(1)}, bf16[2,64,256]{2,1,0:T(8,128)(2,1)S(1)}, u32[]{:S(2)}, u32[]{:S(2)}) collective-permute-start(bf16[2,64,256]{2,1,0:T(8,128)(2,1)S(1)} %get-tuple-element.26), channel_id=1, source_target_pairs={{0,1},{1,0},{2,3},{3,2},{4,5},{5,4},{6,7},{7,6},{8,9},{9,8},{10,11... | collective-permute-start | bytes 196616 | tf_op jit(solution)/shard_map/ppermute | solution.py:297
  49.6 15.5 %collective-permute-start.6 = (bf16[8,64,256]{2,1,0:T(8,128)(2,1)S(1)}, bf16[8,64,256]{2,1,0:T(8,128)(2,1)S(1)}, u32[]{:S(2)}, u32[]{:S(2)}) collective-permute-start(bf16[8,64,256]{2,1,0:T(8,128)(2,1)S(1)} %get-tuple-element.23.refs_9_), channel_id=1, source_target_pairs={{1,34},{2,33},{3,36},{4,35},{5,38},{6,37},{7,40},{8,39},{9,42},{10... | collective-permute-start | bytes 786440 | tf_op jit(solution)/shard_map/ppermute | solution.py:297
  57.1 13.1 %collective-permute-start.10 = (bf16[8,64,256]{2,1,0:T(8,128)(2,1)S(1)}, bf16[8,64,256]{2,1,0:T(8,128)(2,1)S(1)}, u32[]{:S(2)}, u32[]{:S(2)}) collective-permute-start(bf16[8,64,256]{2,1,0:T(8,128)(2,1)S(1)} %collective-permute-done.7.refs_1_), channel_id=1, source_target_pairs={{1,66},{2,65},{3,68},{4,67},{5,70},{6,69},{7,72},{8,71},{9,74},{10... | collective-permute-start | bytes 786440 | tf_op jit(solution)/shard_map/ppermute | solution.py:297
  60.8 10.2 %collective-permute-start.11 = (bf16[8,64,256]{2,1,0:T(8,128)(2,1)S(1)}, bf16[8,64,256]{2,1,0:T(8,128)(2,1)S(1)}, u32[]{:S(2)}, u32[]{:S(2)}) collective-permute-start(bf16[8,64,256]{2,1,0:T(8,128)(2,1)S(1)} %collective-permute-done.7.refs_1_), channel_id=1, source_target_pairs={{0,64},{1,65},{2,66},{3,67},{4,68},{5,69},{6,70},{7,71},{8,72},{9,... | collective-permute-start | bytes 786440 | tf_op jit(solution)/shard_map/ppermute | solution.py:297
  60.9 10.1 %collective-permute-start.9 = (bf16[8,64,256]{2,1,0:T(8,128)(2,1)S(1)}, bf16[8,64,256]{2,1,0:T(8,128)(2,1)S(1)}, u32[]{:S(2)}, u32[]{:S(2)}) collective-permute-start(bf16[8,64,256]{2,1,0:T(8,128)(2,1)S(1)} %collective-permute-done.8.refs_2_), channel_id=1, source_target_pairs={{0,1},{1,0},{2,3},{3,2},{4,5},{5,4},{6,7},{7,6},{8,9},{9,8},{10,11... | collective-permute-start | bytes 786440 | tf_op jit(solution)/shard_map/ppermute | solution.py:297
  61.0 10.8 %collective-permute-start.13 = (bf16[8,64,256]{2,1,0:T(8,128)(2,1)S(1)}, bf16[8,64,256]{2,1,0:T(8,128)(2,1)S(1)}, u32[]{:S(2)}, u32[]{:S(2)}) collective-permute-start(bf16[8,64,256]{2,1,0:T(8,128)(2,1)S(1)} %collective-permute-done.12.refs_6_), channel_id=1, source_target_pairs={{0,1},{1,0},{2,3},{3,2},{4,5},{5,4},{6,7},{7,6},{8,9},{9,8},{10,11... | collective-permute-start | bytes 786440 | tf_op jit(solution)/shard_map/ppermute | solution.py:297
  71.1 0.7 copy-start
  71.8 0.7 copy-start.2
  72.5 0.9 copy-start.1
  73.4 0.9 copy-start.3
  74.4 1.2 copy-start.4
  75.6 0.8 copy-start.7
  84.3 15.0 %collective-permute-start.16 = (bf16[8,64,256]{2,1,0:T(8,128)(2,1)S(1)}, bf16[8,64,256]{2,1,0:T(8,128)(2,1)S(1)}, u32[]{:S(2)}, u32[]{:S(2)}) collective-permute-start(bf16[8,64,256]{2,1,0:T(8,128)(2,1)S(1)} %get-tuple-element.27.edge), channel_id=1, source_target_pairs={{1,2},{2,1},{3,4},{4,3},{5,6},{6,5},{7,8},{8,7},{9,10},{10,9},{11,... | collective-permute-start | bytes 786440 | tf_op jit(solution)/shard_map/ppermute | solution.py:297
  88.4 10.9 %collective-permute-start.17 = (bf16[8,64,256]{2,1,0:T(8,128)(2,1)S(1)}, bf16[8,64,256]{2,1,0:T(8,128)(2,1)S(1)}, u32[]{:S(2)}, u32[]{:S(2)}) collective-permute-start(bf16[8,64,256]{2,1,0:T(8,128)(2,1)S(1)} %get-tuple-element.28.inner), channel_id=1, source_target_pairs={{0,1},{1,0},{2,3},{3,2},{4,5},{5,4},{6,7},{7,6},{8,9},{9,8},{10,11... | collective-permute-start | bytes 786440 | tf_op jit(solution)/shard_map/ppermute | solution.py:297
  88.5 5.7 %collective-permute-start.18 = (bf16[2,2,4,32]{3,2,1,0:T(4,128)(2,1)S(1)}, bf16[2,2,4,32]{3,2,1,0:T(4,128)(2,1)S(1)}, u32[]{:S(2)}, u32[]{:S(2)}) collective-permute-start(bf16[2,2,4,32]{3,2,1,0:T(4,128)(2,1)S(1)} %get-tuple-element.41), channel_id=1, source_target_pairs={{0,112},{1,113},{2,114},{3,115},{4,116},{5,117},{6,118},{7,119},{8... | collective-permute-start | bytes 3080 | tf_op jit(solution)/shard_map/ppermute | solution.py:297
  90.3 6.0 %collective-permute-start.19 = (bf16[2,2,4,32]{3,2,1,0:T(4,128)(2,1)S(1)}, bf16[2,2,4,32]{3,2,1,0:T(4,128)(2,1)S(1)}, u32[]{:S(2)}, u32[]{:S(2)}) collective-permute-start(bf16[2,2,4,32]{3,2,1,0:T(4,128)(2,1)S(1)} %get-tuple-element.42), channel_id=1, source_target_pairs={{0,16},{1,17},{2,18},{3,19},{4,20},{5,21},{6,22},{7,23},{8,24},{9,... | collective-permute-start | bytes 3080 | tf_op jit(solution)/shard_map/ppermute | solution.py:297
  99.3 1.2 copy-start.6
  100.6 0.8 copy-start.9
  104.2 17.9 %collective-permute-start.20 = (bf16[20,64,256]{2,1,0:T(8,128)(2,1)S(1)}, bf16[20,64,256]{2,1,0:T(8,128)(2,1)S(1)}, u32[]{:S(2)}, u32[]{:S(2)}) collective-permute-start(bf16[20,64,256]{2,1,0:T(8,128)(2,1)S(1)} %get-tuple-element.31), channel_id=1, source_target_pairs={{0,16},{1,17},{2,18},{3,19},{4,20},{5,21},{6,22},{7,23},{8,24},{9,... | collective-permute-start | bytes 1966088 | tf_op jit(solution)/shard_map/ppermute | solution.py:297
  104.3 17.8 %collective-permute-start.21 = (bf16[20,64,256]{2,1,0:T(8,128)(2,1)S(1)}, bf16[20,64,256]{2,1,0:T(8,128)(2,1)S(1)}, u32[]{:S(2)}, u32[]{:S(2)}) collective-permute-start(bf16[20,64,256]{2,1,0:T(8,128)(2,1)S(1)} %get-tuple-element.32), channel_id=1, source_target_pairs={{0,112},{1,113},{2,114},{3,115},{4,116},{5,117},{6,118},{7,119},{8... | collective-permute-start | bytes 1966088 | tf_op jit(solution)/shard_map/ppermute | solution.py:297

commit v5 on v4

--- a/solution.py
+++ b/solution.py
@@ -12,7 +12,7 @@
 CH = 64
 WIDTH = 256
 HALF = 8
-VMEM_LIMIT = 28 << 20
+VMEM_LIMIT = 16 << 20
 F32 = jnp.float32
 BF16 = jnp.bfloat16
 
@@ -62,6 +62,7 @@
         ),
         in_specs=[vmem],
         out_specs=(vmem, vmem),
+        compiler_params=pltpu.CompilerParams(vmem_limit_bytes=VMEM_LIMIT),
         cost_estimate=pl.CostEstimate(
             flops=100_000_000, bytes_accessed=3_000_000, transcendentals=0
         ),
@@ -130,10 +131,10 @@
         ).astype(F32)
         act[a] = (value * keep).astype(BF16)
 
-    @pl.loop(0, 6)
+    @pl.loop(0, 3)
     def _(n):
-        for k in range(3):
-            activate(3 * n + k)
+        for k in range(6):
+            activate(6 * n + k)
 
     scale = flags[3].astype(F32)
 
@@ -146,18 +147,18 @@
     if final:
         (out,) = outs
 
-        @pl.loop(0, 4)
+        @pl.loop(0, 2)
+        def _(n):
+            for k in range(8):
+                out[8 * n + k] = finish(8 * n + k)
+
+    else:
+        out_edge, out_inner, out_rim, out_near = outs
+
+        @pl.loop(0, 2)
         def _(n):
             for k in range(4):
-                out[4 * n + k] = finish(4 * n + k)
-
-    else:
-        out_edge, out_inner, out_rim, out_near = outs
-
-        @pl.loop(0, 4)
-        def _(n):
-            for k in range(2):
-                y = 2 * n + k
+                y = 4 * n + k
                 out_edge[y] = finish(y + turn(turned, 0, 8))
                 out_inner[y] = finish(y + turn(turned, 8, 8))
 
@@ -379,9 +380,9 @@
     own_near = send(near, row_to=on_chip)
     e = send(edge, across)
     i = send(inner, across)
-    h = send(edge, across, off_chip)
     xe = send(e, to_other)
     xh = send(e, to_other, off_chip)
+    h = send(xe, to_other, off_chip)
     xi = send(i, to_other)
     n = send(i, row_to=on_chip)
     for_ahead = send(packed[:, 0, 0:2], back)

time: 129 us -> 118 us (0.915)
  Pallas kernels: 30.6 us -> 21.9 us
  local copies, waits for them, and re-layouts: 17.8 us -> 9.9 us
  waiting for transfers between devices: 39 us -> 46.3 us
    ppermute x22, waiting for transfers between devices: 39 us -> 46.3 us  [send(): return lax.ppermute(x, ('tm', 'rows'), route)]
    unnamed x30 -> x18, local copies, waits for them, and re-layouts: 10.1 us -> 3.92 us
    pallas_call x3, Pallas kernels: 6.91 us -> 1.73 us  [make_columns(): pl.pallas_call(columns_kernel, out_shape=(jax.ShapeDtypeStruct((count, WI...]
    pallas_call x4, Pallas kernels: 23.7 us -> 20.2 us  [on_core(): pl.pallas_call(kernel, out_shape=out_shape, in_specs=[pl.BlockSpec(memory...]
    pad x3, local copies, waits for them, and re-layouts: 1.84 us -> 0.03 us  [level_values(): return jnp.pad(t, ((0, 0), (0, 0), (0, 4), (0, 0))).reshape(64, 32)]
  transfers between devices with their start and end apart: 22 -> 22, of which waited for: 8 -> 10; matrix products, arithmetic and copies ran while one was open for 5% -> 4% of each run, Pallas kernels for 5% -> 1%
where the time goes in v5:
time: 118 us
  waiting for transfers between devices  46.3 us (39%)
  starting transfers between devices  39.2 us (33%)
  Pallas kernels  21.9 us (19%)
  local copies, waits for them, and re-layouts  9.9 us (8%)
    ppermute x22, waiting for transfers between devices, send(): return lax.ppermute(x, ('tm', 'rows'), route)  46.3 us
    ppermute x22, starting transfers between devices, send(): return lax.ppermute(x, ('tm', 'rows'), route)  39.2 us
    pallas_call x4, Pallas kernels, on_core(): pl.pallas_call(kernel, out_shape=out_shape, in_specs=[pl.BlockSpec(memory...  20.2 us
    unnamed x18, local copies, waits for them, and re-layouts  3.92 us
  transfers between devices with their start and end apart: 22, of which 10 were waited for; matrix products, arithmetic and copies ran while one was open for 4% of the time, Pallas kernels for 1%

profile of v5, /device:TPU:8, one launch (start us, length us, event | category | flops | bytes accessed | tf_op | source)
XLA Modules:
  0.0 117.8 jit_solution(2446595255488060728)
XLA Ops:
  0.0 1.1 dynamic-slice_bitcast_fusion
  1.1 0.0 copy-start.6
  1.1 4.0 %collective-permute-start.2 = (bf16[8,64,256]{2,1,0:T(8,128)(2,1)S(1)}, bf16[8,64,256]{2,1,0:T(8,128)(2,1)S(1)}, u32[]{:S(2)}, u32[]{:S(2)}) collective-permute-start(bf16[8,64,256]{2,1,0:T(8,128)(2,1)S(1)} %get-tuple-element.36.refs_5_), channel_id=1, source_target_pairs={{1,66},{2,65},{3,68},{4,67},{5,70},{6,69},{7,72},{8,71},{9,74},{10... | collective-permute-start | bytes 786440 | tf_op jit(solution)/shard_map/ppermute | solution.py:298
  5.1 0.3 collective-permute-start.3
  5.4 0.1 fusion
  5.5 0.1 select_n.83
  5.6 0.9 dynamic-slice_bitcast_fusion.3
  6.5 0.0 copy-start.4
  6.5 0.7 collective-permute-start
  7.2 0.1 select_n.86
  7.3 0.0 copy-start.8
  7.4 4.0 %collective-permute-start.1 = (bf16[3,64,256]{2,1,0:T(8,128)(2,1)S(1)}, bf16[3,64,256]{2,1,0:T(8,128)(2,1)S(1)}, u32[]{:S(2)}, u32[]{:S(2)}) collective-permute-start(bf16[3,64,256]{2,1,0:T(8,128)(2,1)S(1)} %pad_maximum_fusion.1), channel_id=1, source_target_pairs={{1,2},{2,1},{3,4},{4,3},{5,6},{6,5},{7,8},{8,7},{9,10},{10,9},{11,... | collective-permute-start | bytes 294920 | tf_op jit(solution)/shard_map/ppermute | solution.py:298
  11.4 0.4 collective-permute-start.4
  11.8 0.6 fusion.4
  12.4 0.3 copy.16
  12.6 0.0 copy-start.5
  12.6 0.3 reshape.85.wu
  12.9 0.6 copy-done.5
  13.5 0.1 copy.17
  13.7 0.2 reshape.86.wm
  13.8 0.7 stack.52.flags
  14.6 2.1 %collective-permute-done.1.refs_4_ = bf16[3,64,256]{2,1,0:T(8,128)(2,1)S(1)} collective-permute-done((bf16[3,64,256]{2,1,0:T(8,128)(2,1)S(1)}, bf16[3,64,256]{2,1,0:T(8,128)(2,1)S(1)}, u32[]{:S(2)}, u32[]{:S(2)}) %collective-permute-start.1) | collective-permute-done | bytes 98336 | tf_op jit(solution)/shard_map/ppermute | solution.py:298
  16.7 0.1 select_n.93
  16.8 0.1 select_n.94
  16.9 5.0 %collective-permute-done.4.refs_2_ = bf16[8,64,256]{2,1,0:T(8,128)(2,1)S(1)} collective-permute-done((bf16[8,64,256]{2,1,0:T(8,128)(2,1)S(1)}, bf16[8,64,256]{2,1,0:T(8,128)(2,1)S(1)}, u32[]{:S(2)}, u32[]{:S(2)}) %collective-permute-start.4) | collective-permute-done | bytes 262176 | tf_op jit(solution)/shard_map/ppermute | solution.py:298
  21.9 0.0 collective-permute-start.5
  21.9 0.1 pad_maximum_fusion.2
  22.0 0.6 shard_map.65
  22.6 0.0 collective-permute-done.2.refs_0_
  22.6 0.8 collective-permute-done.5.refs_3_
  23.4 6.0 %shard_map.66 = (bf16[8,64,256]{2,1,0:T(8,128)(2,1)S(1)}, bf16[8,64,256]{2,1,0:T(8,128)(2,1)S(1)}, bf16[2,64,256]{2,1,0:T(8,128)(2,1)S(1)}, bf16[2,64,256]{2,1,0:T(8,128)(2,1)S(1)}) custom-call(s32[5]{0:T(128)S(1)} %stack.52.flags, bf16[8,256,256]{2,1,0:T(8,128)(2,1)S(1)} %get-tuple-element.21.cols, f32[64,256]{1,0:T(8,128)S(1)} %get-tuple-element.22.table, ...), custom_call_target="tpu_custom_call" | custom-call | flops 3000000000 | bytes 4000000 | tf_op jit(solution)/shard_map/pallas_call | solution.py:230
  29.4 4.0 %collective-permute-start.9 = (bf16[8,64,256]{2,1,0:T(8,128)(2,1)S(1)}, bf16[8,64,256]{2,1,0:T(8,128)(2,1)S(1)}, u32[]{:S(2)}, u32[]{:S(2)}) collective-permute-start(bf16[8,64,256]{2,1,0:T(8,128)(2,1)S(1)} %get-tuple-element.24.refs_10_), channel_id=1, source_target_pairs={{0,32},{1,33},{2,34},{3,35},{4,36},{5,37},{6,38},{7,39},{8,40},{9,... | collective-permute-start | bytes 786440 | tf_op jit(solution)/shard_map/ppermute | solution.py:298
  33.4 0.1 collective-permute-start.6
  33.5 7.1 %collective-permute-done.9.refs_2_ = bf16[8,64,256]{2,1,0:T(8,128)(2,1)S(1)} collective-permute-done((bf16[8,64,256]{2,1,0:T(8,128)(2,1)S(1)}, bf16[8,64,256]{2,1,0:T(8,128)(2,1)S(1)}, u32[]{:S(2)}, u32[]{:S(2)}) %collective-permute-start.9) | collective-permute-done | bytes 262176 | tf_op jit(solution)/shard_map/ppermute | solution.py:298
  40.6 0.7 collective-permute-start.12
  41.3 4.4 %collective-permute-done.6.refs_1_ = bf16[8,64,256]{2,1,0:T(8,128)(2,1)S(1)} collective-permute-done((bf16[8,64,256]{2,1,0:T(8,128)(2,1)S(1)}, bf16[8,64,256]{2,1,0:T(8,128)(2,1)S(1)}, u32[]{:S(2)}, u32[]{:S(2)}) %collective-permute-start.6) | collective-permute-done | bytes 262176 | tf_op jit(solution)/shard_map/ppermute | solution.py:298
  45.6 0.7 collective-permute-start.7
  46.3 3.5 %collective-permute-start.11 = (bf16[8,64,256]{2,1,0:T(8,128)(2,1)S(1)}, bf16[8,64,256]{2,1,0:T(8,128)(2,1)S(1)}, u32[]{:S(2)}, u32[]{:S(2)}) collective-permute-start(bf16[8,64,256]{2,1,0:T(8,128)(2,1)S(1)} %collective-permute-done.6.refs_1_), channel_id=1, source_target_pairs={{1,66},{2,65},{3,68},{4,67},{5,70},{6,69},{7,72},{8,71},{9,74},{10... | collective-permute-start | bytes 786440 | tf_op jit(solution)/shard_map/ppermute | solution.py:298
  49.9 0.2 collective-permute-start.13
  50.1 3.4 %collective-permute-done.7.refs_5_ = bf16[8,64,256]{2,1,0:T(8,128)(2,1)S(1)} collective-permute-done((bf16[8,64,256]{2,1,0:T(8,128)(2,1)S(1)}, bf16[8,64,256]{2,1,0:T(8,128)(2,1)S(1)}, u32[]{:S(2)}, u32[]{:S(2)}) %collective-permute-start.7) | collective-permute-done | bytes 262176 | tf_op jit(solution)/shard_map/ppermute | solution.py:298
  53.4 1.9 %collective-permute-start.8 = (bf16[8,64,256]{2,1,0:T(8,128)(2,1)S(1)}, bf16[8,64,256]{2,1,0:T(8,128)(2,1)S(1)}, u32[]{:S(2)}, u32[]{:S(2)}) collective-permute-start(bf16[8,64,256]{2,1,0:T(8,128)(2,1)S(1)} %collective-permute-done.7.refs_5_), channel_id=1, source_target_pairs={{1,66},{2,65},{3,68},{4,67},{5,70},{6,69},{7,72},{8,71},{9,74},{10... | collective-permute-start | bytes 786440 | tf_op jit(solution)/shard_map/ppermute | solution.py:298
  55.3 5.2 %collective-permute-start.14 = (bf16[2,64,256]{2,1,0:T(8,128)(2,1)S(1)}, bf16[2,64,256]{2,1,0:T(8,128)(2,1)S(1)}, u32[]{:S(2)}, u32[]{:S(2)}) collective-permute-start(bf16[2,64,256]{2,1,0:T(8,128)(2,1)S(1)} %get-tuple-element.25), channel_id=1, source_target_pairs={{1,2},{2,1},{3,4},{4,3},{5,6},{6,5},{7,8},{8,7},{9,10},{10,9},{11,... | collective-permute-start | bytes 196616 | tf_op jit(solution)/shard_map/ppermute | solution.py:298
  60.6 3.5 %collective-permute-done.14.refs_8_ = bf16[2,64,256]{2,1,0:T(8,128)(2,1)S(1)} collective-permute-done((bf16[2,64,256]{2,1,0:T(8,128)(2,1)S(1)}, bf16[2,64,256]{2,1,0:T(8,128)(2,1)S(1)}, u32[]{:S(2)}, u32[]{:S(2)}) %collective-permute-start.14) | collective-permute-done | bytes 65568 | tf_op jit(solution)/shard_map/ppermute | solution.py:298
  64.1 0.2 collective-permute-start.15
  64.3 0.7 stack.50.flags
  65.0 0.6 shard_map.64
  65.7 0.7 copy-done
  66.4 0.7 copy-done.2
  67.1 0.9 copy-done.1
  68.0 0.9 copy-done.3
  69.0 6.7 %shard_map.67 = (bf16[8,64,256]{2,1,0:T(8,128)(2,1)S(1)}, bf16[8,64,256]{2,1,0:T(8,128)(2,1)S(1)}, bf16[2,64,256]{2,1,0:T(8,128)(2,1)}, bf16[2,64,256]{2,1,0:T(8,128)(2,1)}) custom-call(s32[5]{0:T(128)S(1)} %stack.50.flags, bf16[8,256,256]{2,1,0:T(8,128)(2,1)S(1)} %get-tuple-element.19.cols, f32[64,256]{1,0:T(8,128)S(1)} %get-tuple-element.20.table, ...), custom_call_target="tpu_custom_call" | custom-call | flops 3000000000 | bytes 4000000 | tf_op jit(solution)/shard_map/pallas_call | solution.py:230
  75.7 4.4 %collective-permute-start.16 = (bf16[8,64,256]{2,1,0:T(8,128)(2,1)S(1)}, bf16[8,64,256]{2,1,0:T(8,128)(2,1)S(1)}, u32[]{:S(2)}, u32[]{:S(2)}) collective-permute-start(bf16[8,64,256]{2,1,0:T(8,128)(2,1)S(1)} %get-tuple-element.27.edge), channel_id=1, source_target_pairs={{1,2},{2,1},{3,4},{4,3},{5,6},{6,5},{7,8},{8,7},{9,10},{10,9},{11,... | collective-permute-start | bytes 786440 | tf_op jit(solution)/shard_map/ppermute | solution.py:298
  80.0 0.4 collective-permute-start.17
  80.5 4.3 %collective-permute-start.18 = (bf16[2,2,4,32]{3,2,1,0:T(4,128)(2,1)S(1)}, bf16[2,2,4,32]{3,2,1,0:T(4,128)(2,1)S(1)}, u32[]{:S(2)}, u32[]{:S(2)}) collective-permute-start(bf16[2,2,4,32]{3,2,1,0:T(4,128)(2,1)S(1)} %get-tuple-element.41), channel_id=1, source_target_pairs={{0,112},{1,113},{2,114},{3,115},{4,116},{5,117},{6,118},{7,119},{8... | collective-permute-start | bytes 3080 | tf_op jit(solution)/shard_map/ppermute | solution.py:298
  84.7 0.0 collective-permute-start.19
  84.7 0.7 stack.49.flags
  85.5 1.0 collective-permute-done.18
  86.4 4.7 %collective-permute-done.19 = bf16[2,2,4,32]{3,2,1,0:T(4,128)(2,1)S(1)} collective-permute-done((bf16[2,2,4,32]{3,2,1,0:T(4,128)(2,1)S(1)}, bf16[2,2,4,32]{3,2,1,0:T(4,128)(2,1)S(1)}, u32[]{:S(2)}, u32[]{:S(2)}) %collective-permute-start.19) | collective-permute-done | bytes 1056 | tf_op jit(solution)/shard_map/ppermute | solution.py:298
  91.1 0.6 shard_map.68
  91.8 2.8 %shard_map.69 = (bf16[20,64,256]{2,1,0:T(8,128)(2,1)S(1)}, bf16[20,64,256]{2,1,0:T(8,128)(2,1)S(1)}) custom-call(s32[5]{0:T(128)S(1)} %stack.49.flags, bf16[8,256,256]{2,1,0:T(8,128)(2,1)S(1)} %get-tuple-element.29.cols, f32[64,256]{1,0:T(8,128)S(1)} %get-tuple-element.30.table, bf16[8,64,256]{2,1,0:T(8,128)(2,1)S(1)} %collective-permute-done.16.outer, ...), custom_call_target="tpu_custom_call" | custom-call | flops 1500000000 | bytes 4000000 | tf_op jit(solution)/shard_map/pallas_call | solution.py:230
  94.5 0.1 collective-permute-start.20
  94.6 4.1 %collective-permute-start.21 = (bf16[20,64,256]{2,1,0:T(8,128)(2,1)S(1)}, bf16[20,64,256]{2,1,0:T(8,128)(2,1)S(1)}, u32[]{:S(2)}, u32[]{:S(2)}) collective-permute-start(bf16[20,64,256]{2,1,0:T(8,128)(2,1)S(1)} %get-tuple-element.32), channel_id=1, source_target_pairs={{0,112},{1,113},{2,114},{3,115},{4,116},{5,117},{6,118},{7,119},{8... | collective-permute-start | bytes 1966088 | tf_op jit(solution)/shard_map/ppermute | solution.py:298
  98.7 14.4 %collective-permute-done.20.earlier = bf16[20,64,256]{2,1,0:T(8,128)(2,1)S(1)} collective-permute-done((bf16[20,64,256]{2,1,0:T(8,128)(2,1)S(1)}, bf16[20,64,256]{2,1,0:T(8,128)(2,1)S(1)}, u32[]{:S(2)}, u32[]{:S(2)}) %collective-permute-start.20) | collective-permute-done | bytes 655392 | tf_op jit(solution)/shard_map/ppermute | solution.py:298
  113.1 4.7 %shard_map.70 = bf16[16,64,256]{2,1,0:T(8,128)(2,1)} custom-call(s32[5]{0:T(128)S(1)} %stack.49.flags, bf16[192,576]{1,0:T(8,128)(2,1)S(1)} %reshape.85.wu, bf16[192,192]{1,0:T(8,128)(2,1)S(1)} %reshape.86.wm, bf16[8,64,256]{2,1,0:T(8,128)(2,1)S(1)} %collective-permute-done.16.outer, bf16[8,64,256]{2,1,0:T(8,128)(2,1)S(1)} %get-tuple-element.27.edge, ...), custom_call_target="tpu_custom_call" | custom-call | flops 1500000000 | bytes 4000000 | tf_op jit(solution)/shard_map/pallas_call | solution.py:230
  (36 shorter events, 0.2 us)
Async XLA Ops:
  0.0 5.4 %copy-start.7 = (s32[3,4,1,2,32]{4,3,2,1,0:T(2,128)S(1)}, s32[3,4,1,2,32]{4,3,2,1,0:T(2,128)}, u32[]{:S(2)}) copy-start(s32[3,4,1,2,32]{4,3,2,1,0:T(2,128)} %param.8) | copy-start | bytes 9220
  1.1 4.3 %copy-start.6 = (s32[3,4,1,2,32]{4,3,2,1,0:T(2,128)S(1)}, s32[3,4,1,2,32]{4,3,2,1,0:T(2,128)}, u32[]{:S(2)}) copy-start(s32[3,4,1,2,32]{4,3,2,1,0:T(2,128)} %param.7) | copy-start | bytes 9220
  1.1 21.5 %collective-permute-start.2 = (bf16[8,64,256]{2,1,0:T(8,128)(2,1)S(1)}, bf16[8,64,256]{2,1,0:T(8,128)(2,1)S(1)}, u32[]{:S(2)}, u32[]{:S(2)}) collective-permute-start(bf16[8,64,256]{2,1,0:T(8,128)(2,1)S(1)} %get-tuple-element.36.refs_5_), channel_id=1, source_target_pairs={{1,66},{2,65},{3,68},{4,67},{5,70},{6,69},{7,72},{8,71},{9,74},{10... | collective-permute-start | bytes 786440 | tf_op jit(solution)/shard_map/ppermute | solution.py:298
  5.1 17.5 %collective-permute-start.3 = (bf16[8,64,256]{2,1,0:T(8,128)(2,1)S(1)}, bf16[8,64,256]{2,1,0:T(8,128)(2,1)S(1)}, u32[]{:S(2)}, u32[]{:S(2)}) collective-permute-start(bf16[8,64,256]{2,1,0:T(8,128)(2,1)S(1)} %get-tuple-element.36.refs_5_), channel_id=1, source_target_pairs={{0,64},{1,65},{2,66},{3,67},{4,68},{5,69},{6,70},{7,71},{8,72},{9,... | collective-permute-start | bytes 786440 | tf_op jit(solution)/shard_map/ppermute | solution.py:298
  6.5 5.9 %copy-start.4 = (bf16[3,3,64,192]{3,2,1,0:T(8,128)(2,1)S(1)}, bf16[3,3,64,192]{3,2,1,0:T(8,128)(2,1)}, u32[]{:S(2)}) copy-start(bf16[3,3,64,192]{3,2,1,0:T(8,128)(2,1)} %param.10) | copy-start | bytes 663556
  6.5 8.0 %collective-permute-start = (bf16[3,64,256]{2,1,0:T(8,128)(2,1)S(1)}, bf16[3,64,256]{2,1,0:T(8,128)(2,1)S(1)}, u32[]{:S(2)}, u32[]{:S(2)}) collective-permute-start(bf16[3,64,256]{2,1,0:T(8,128)(2,1)S(1)} %pad_maximum_fusion), channel_id=1, source_target_pairs={{0,1},{1,0},{2,3},{3,2},{4,5},{5,4},{6,7},{7,6},{8,9},{9,8},{10,11... | collective-permute-start | bytes 294920 | tf_op jit(solution)/shard_map/ppermute | solution.py:298
  7.3 4.4 %copy-start.8 = (s32[3,1]{0,1:T(1,128)S(1)}, s32[3,1]{0,1:T(1,128)}, u32[]{:S(2)}) copy-start(s32[3,1]{0,1:T(1,128)} %param.9) | copy-start | bytes 40
  7.4 9.4 %collective-permute-start.1 = (bf16[3,64,256]{2,1,0:T(8,128)(2,1)S(1)}, bf16[3,64,256]{2,1,0:T(8,128)(2,1)S(1)}, u32[]{:S(2)}, u32[]{:S(2)}) collective-permute-start(bf16[3,64,256]{2,1,0:T(8,128)(2,1)S(1)} %pad_maximum_fusion.1), channel_id=1, source_target_pairs={{1,2},{2,1},{3,4},{4,3},{5,6},{6,5},{7,8},{8,7},{9,10},{10,9},{11,... | collective-permute-start | bytes 294920 | tf_op jit(solution)/shard_map/ppermute | solution.py:298
  11.4 10.5 %collective-permute-start.4 = (bf16[8,64,256]{2,1,0:T(8,128)(2,1)S(1)}, bf16[8,64,256]{2,1,0:T(8,128)(2,1)S(1)}, u32[]{:S(2)}, u32[]{:S(2)}) collective-permute-start(bf16[8,64,256]{2,1,0:T(8,128)(2,1)S(1)} %get-tuple-element.35.refs_6_), channel_id=1, source_target_pairs={{0,64},{1,65},{2,66},{3,67},{4,68},{5,69},{6,70},{7,71},{8,72},{9,... | collective-permute-start | bytes 786440 | tf_op jit(solution)/shard_map/ppermute | solution.py:298
  12.6 0.9 copy-start.5
  21.9 1.5 %collective-permute-start.5 = (bf16[8,64,256]{2,1,0:T(8,128)(2,1)S(1)}, bf16[8,64,256]{2,1,0:T(8,128)(2,1)S(1)}, u32[]{:S(2)}, u32[]{:S(2)}) collective-permute-start(bf16[8,64,256]{2,1,0:T(8,128)(2,1)S(1)} %collective-permute-done.4.refs_2_), channel_id=1, source_target_pairs={{0,1},{1,0},{2,3},{3,2},{4,5},{5,4},{6,7},{7,6},{8,9},{9,8},{10,11... | collective-permute-start | bytes 786440 | tf_op jit(solution)/shard_map/ppermute | solution.py:298
  29.4 11.1 %collective-permute-start.9 = (bf16[8,64,256]{2,1,0:T(8,128)(2,1)S(1)}, bf16[8,64,256]{2,1,0:T(8,128)(2,1)S(1)}, u32[]{:S(2)}, u32[]{:S(2)}) collective-permute-start(bf16[8,64,256]{2,1,0:T(8,128)(2,1)S(1)} %get-tuple-element.24.refs_10_), channel_id=1, source_target_pairs={{0,32},{1,33},{2,34},{3,35},{4,36},{5,37},{6,38},{7,39},{8,40},{9,... | collective-permute-start | bytes 786440 | tf_op jit(solution)/shard_map/ppermute | solution.py:298
  33.4 12.2 %collective-permute-start.6 = (bf16[8,64,256]{2,1,0:T(8,128)(2,1)S(1)}, bf16[8,64,256]{2,1,0:T(8,128)(2,1)S(1)}, u32[]{:S(2)}, u32[]{:S(2)}) collective-permute-start(bf16[8,64,256]{2,1,0:T(8,128)(2,1)S(1)} %get-tuple-element.23.refs_9_), channel_id=1, source_target_pairs={{0,32},{1,33},{2,34},{3,35},{4,36},{5,37},{6,38},{7,39},{8,40},{9,... | collective-permute-start | bytes 786440 | tf_op jit(solution)/shard_map/ppermute | solution.py:298
  40.6 9.3 %collective-permute-start.12 = (bf16[8,64,256]{2,1,0:T(8,128)(2,1)S(1)}, bf16[8,64,256]{2,1,0:T(8,128)(2,1)S(1)}, u32[]{:S(2)}, u32[]{:S(2)}) collective-permute-start(bf16[8,64,256]{2,1,0:T(8,128)(2,1)S(1)} %collective-permute-done.9.refs_2_), channel_id=1, source_target_pairs={{0,64},{1,65},{2,66},{3,67},{4,68},{5,69},{6,70},{7,71},{8,72},{9,... | collective-permute-start | bytes 786440 | tf_op jit(solution)/shard_map/ppermute | solution.py:298
  45.6 7.8 %collective-permute-start.7 = (bf16[8,64,256]{2,1,0:T(8,128)(2,1)S(1)}, bf16[8,64,256]{2,1,0:T(8,128)(2,1)S(1)}, u32[]{:S(2)}, u32[]{:S(2)}) collective-permute-start(bf16[8,64,256]{2,1,0:T(8,128)(2,1)S(1)} %collective-permute-done.6.refs_1_), channel_id=1, source_target_pairs={{0,64},{1,65},{2,66},{3,67},{4,68},{5,69},{6,70},{7,71},{8,72},{9,... | collective-permute-start | bytes 786440 | tf_op jit(solution)/shard_map/ppermute | solution.py:298
  46.3 19.3 %collective-permute-start.10 = (bf16[8,64,256]{2,1,0:T(8,128)(2,1)S(1)}, bf16[8,64,256]{2,1,0:T(8,128)(2,1)S(1)}, u32[]{:S(2)}, u32[]{:S(2)}) collective-permute-start(bf16[8,64,256]{2,1,0:T(8,128)(2,1)S(1)} %collective-permute-done.9.refs_2_), channel_id=1, source_target_pairs={{0,1},{1,0},{2,3},{3,2},{4,5},{5,4},{6,7},{7,6},{8,9},{9,8},{10,11... | collective-permute-start | bytes 786440 | tf_op jit(solution)/shard_map/ppermute | solution.py:298
  46.3 19.3 %collective-permute-start.11 = (bf16[8,64,256]{2,1,0:T(8,128)(2,1)S(1)}, bf16[8,64,256]{2,1,0:T(8,128)(2,1)S(1)}, u32[]{:S(2)}, u32[]{:S(2)}) collective-permute-start(bf16[8,64,256]{2,1,0:T(8,128)(2,1)S(1)} %collective-permute-done.6.refs_1_), channel_id=1, source_target_pairs={{1,66},{2,65},{3,68},{4,67},{5,70},{6,69},{7,72},{8,71},{9,74},{10... | collective-permute-start | bytes 786440 | tf_op jit(solution)/shard_map/ppermute | solution.py:298
  49.9 15.8 %collective-permute-start.13 = (bf16[8,64,256]{2,1,0:T(8,128)(2,1)S(1)}, bf16[8,64,256]{2,1,0:T(8,128)(2,1)S(1)}, u32[]{:S(2)}, u32[]{:S(2)}) collective-permute-start(bf16[8,64,256]{2,1,0:T(8,128)(2,1)S(1)} %collective-permute-done.12.refs_6_), channel_id=1, source_target_pairs={{0,1},{1,0},{2,3},{3,2},{4,5},{5,4},{6,7},{7,6},{8,9},{9,8},{10,11... | collective-permute-start | bytes 786440 | tf_op jit(solution)/shard_map/ppermute | solution.py:298
  53.4 12.9 %collective-permute-start.8 = (bf16[8,64,256]{2,1,0:T(8,128)(2,1)S(1)}, bf16[8,64,256]{2,1,0:T(8,128)(2,1)S(1)}, u32[]{:S(2)}, u32[]{:S(2)}) collective-permute-start(bf16[8,64,256]{2,1,0:T(8,128)(2,1)S(1)} %collective-permute-done.7.refs_5_), channel_id=1, source_target_pairs={{1,66},{2,65},{3,68},{4,67},{5,70},{6,69},{7,72},{8,71},{9,74},{10... | collective-permute-start | bytes 786440 | tf_op jit(solution)/shard_map/ppermute | solution.py:298
  55.3 8.7 %collective-permute-start.14 = (bf16[2,64,256]{2,1,0:T(8,128)(2,1)S(1)}, bf16[2,64,256]{2,1,0:T(8,128)(2,1)S(1)}, u32[]{:S(2)}, u32[]{:S(2)}) collective-permute-start(bf16[2,64,256]{2,1,0:T(8,128)(2,1)S(1)} %get-tuple-element.25), channel_id=1, source_target_pairs={{1,2},{2,1},{3,4},{4,3},{5,6},{6,5},{7,8},{8,7},{9,10},{10,9},{11,... | collective-permute-start | bytes 196616 | tf_op jit(solution)/shard_map/ppermute | solution.py:298
  64.1 1.5 %collective-permute-start.15 = (bf16[2,64,256]{2,1,0:T(8,128)(2,1)S(1)}, bf16[2,64,256]{2,1,0:T(8,128)(2,1)S(1)}, u32[]{:S(2)}, u32[]{:S(2)}) collective-permute-start(bf16[2,64,256]{2,1,0:T(8,128)(2,1)S(1)} %get-tuple-element.26), channel_id=1, source_target_pairs={{0,1},{1,0},{2,3},{3,2},{4,5},{5,4},{6,7},{7,6},{8,9},{9,8},{10,11... | collective-permute-start | bytes 196616 | tf_op jit(solution)/shard_map/ppermute | solution.py:298
  65.6 0.7 copy-start
  66.3 0.7 copy-start.2
  67.1 0.9 copy-start.1
  68.0 0.9 copy-start.3
  75.7 16.1 %collective-permute-start.16 = (bf16[8,64,256]{2,1,0:T(8,128)(2,1)S(1)}, bf16[8,64,256]{2,1,0:T(8,128)(2,1)S(1)}, u32[]{:S(2)}, u32[]{:S(2)}) collective-permute-start(bf16[8,64,256]{2,1,0:T(8,128)(2,1)S(1)} %get-tuple-element.27.edge), channel_id=1, source_target_pairs={{1,2},{2,1},{3,4},{4,3},{5,6},{6,5},{7,8},{8,7},{9,10},{10,9},{11,... | collective-permute-start | bytes 786440 | tf_op jit(solution)/shard_map/ppermute | solution.py:298
  80.0 11.7 %collective-permute-start.17 = (bf16[8,64,256]{2,1,0:T(8,128)(2,1)S(1)}, bf16[8,64,256]{2,1,0:T(8,128)(2,1)S(1)}, u32[]{:S(2)}, u32[]{:S(2)}) collective-permute-start(bf16[8,64,256]{2,1,0:T(8,128)(2,1)S(1)} %get-tuple-element.28.inner), channel_id=1, source_target_pairs={{0,1},{1,0},{2,3},{3,2},{4,5},{5,4},{6,7},{7,6},{8,9},{9,8},{10,11... | collective-permute-start | bytes 786440 | tf_op jit(solution)/shard_map/ppermute | solution.py:298
  80.5 6.0 %collective-permute-start.18 = (bf16[2,2,4,32]{3,2,1,0:T(4,128)(2,1)S(1)}, bf16[2,2,4,32]{3,2,1,0:T(4,128)(2,1)S(1)}, u32[]{:S(2)}, u32[]{:S(2)}) collective-permute-start(bf16[2,2,4,32]{3,2,1,0:T(4,128)(2,1)S(1)} %get-tuple-element.41), channel_id=1, source_target_pairs={{0,112},{1,113},{2,114},{3,115},{4,116},{5,117},{6,118},{7,119},{8... | collective-permute-start | bytes 3080 | tf_op jit(solution)/shard_map/ppermute | solution.py:298
  84.7 6.4 %collective-permute-start.19 = (bf16[2,2,4,32]{3,2,1,0:T(4,128)(2,1)S(1)}, bf16[2,2,4,32]{3,2,1,0:T(4,128)(2,1)S(1)}, u32[]{:S(2)}, u32[]{:S(2)}) collective-permute-start(bf16[2,2,4,32]{3,2,1,0:T(4,128)(2,1)S(1)} %get-tuple-element.42), channel_id=1, source_target_pairs={{0,16},{1,17},{2,18},{3,19},{4,20},{5,21},{6,22},{7,23},{8,24},{9,... | collective-permute-start | bytes 3080 | tf_op jit(solution)/shard_map/ppermute | solution.py:298
  94.5 18.6 %collective-permute-start.20 = (bf16[20,64,256]{2,1,0:T(8,128)(2,1)S(1)}, bf16[20,64,256]{2,1,0:T(8,128)(2,1)S(1)}, u32[]{:S(2)}, u32[]{:S(2)}) collective-permute-start(bf16[20,64,256]{2,1,0:T(8,128)(2,1)S(1)} %get-tuple-element.31), channel_id=1, source_target_pairs={{0,16},{1,17},{2,18},{3,19},{4,20},{5,21},{6,22},{7,23},{8,24},{9,... | collective-permute-start | bytes 1966088 | tf_op jit(solution)/shard_map/ppermute | solution.py:298
  94.6 18.5 %collective-permute-start.21 = (bf16[20,64,256]{2,1,0:T(8,128)(2,1)S(1)}, bf16[20,64,256]{2,1,0:T(8,128)(2,1)S(1)}, u32[]{:S(2)}, u32[]{:S(2)}) collective-permute-start(bf16[20,64,256]{2,1,0:T(8,128)(2,1)S(1)} %get-tuple-element.32), channel_id=1, source_target_pairs={{0,112},{1,113},{2,114},{3,115},{4,116},{5,117},{6,118},{7,119},{8... | collective-permute-start | bytes 1966088 | tf_op jit(solution)/shard_map/ppermute | solution.py:298

commit v6 on v5

--- a/solution.py
+++ b/solution.py
@@ -371,7 +371,20 @@
         ],
         axis=3,
     )
-    cols, table = make_columns(level_values(packed[:, 2]))
+    values, later_values, ahead_entries, back_entries, wu, wm, *flags = (
+        lax.optimization_barrier(
+            (
+                level_values(packed[:, 2]),
+                level_values(packed[:, 1]),
+                packed[:, 0, 0:2],
+                packed[:, 0, 2:4],
+                wu,
+                wm,
+                *flags,
+            )
+        )
+    )
+    cols, table = make_columns(values)
     edge, inner, rim, near = run_level(
         flags[2], cols, table, wu, wm, [(h, e, i, n)], (own_outer, edge, inner, own_near)
     )
@@ -385,10 +398,10 @@
     h = send(xe, to_other, off_chip)
     xi = send(i, to_other)
     n = send(i, row_to=on_chip)
-    for_ahead = send(packed[:, 0, 0:2], back)
-    for_back = send(packed[:, 0, 2:4], ahead)
+    for_ahead = send(ahead_entries, back)
+    for_back = send(back_entries, ahead)
     xn = send(xi, row_to=on_chip)
-    cols, table = make_columns(level_values(packed[:, 1]))
+    cols, table = make_columns(later_values)
     edge, inner, _, _ = run_level(
         flags[1],
         cols,

time: 118 us -> 114 us (0.966)
  local copies, waits for them, and re-layouts: 9.9 us -> 7.2 us
  waiting for transfers between devices: 46.3 us -> 45 us
    unnamed x18 -> x10, local copies, waits for them, and re-layouts: 3.92 us -> 1.28 us
    ppermute x22, waiting for transfers between devices: 46.3 us -> 45 us  [send(): return lax.ppermute(x, ('tm', 'rows'), route)]
  transfers between devices with their start and end apart: 22 -> 22, of which waited for: 10 -> 11; matrix products, arithmetic and copies ran while one was open for 4% -> 4% of each run, Pallas kernels for 1% -> 2%
where the time goes in v6:
time: 114 us
  waiting for transfers between devices  45 us (39%)
  starting transfers between devices  39 us (34%)
  Pallas kernels  21.9 us (19%)
  local copies, waits for them, and re-layouts  7.2 us (6%)
    ppermute x22, waiting for transfers between devices, send(): return lax.ppermute(x, ('tm', 'rows'), route)  45 us
    ppermute x22, starting transfers between devices, send(): return lax.ppermute(x, ('tm', 'rows'), route)  39 us
    pallas_call x4, Pallas kernels, on_core(): pl.pallas_call(kernel, out_shape=out_shape, in_specs=[pl.BlockSpec(memory...  20.2 us
  transfers between devices with their start and end apart: 22, of which 11 were waited for; matrix products, arithmetic and copies ran while one was open for 4% of the time, Pallas kernels for 2%

profile of v6, /device:TPU:8, one launch (start us, length us, event | category | flops | bytes accessed | tf_op | source)
XLA Modules:
  0.0 113.7 jit_solution(7292630452193675781)
XLA Ops:
  0.0 1.1 dynamic-slice_bitcast_fusion
  1.1 0.0 copy-start.2
  1.1 4.0 %collective-permute-start.2 = (bf16[8,64,256]{2,1,0:T(8,128)(2,1)S(1)}, bf16[8,64,256]{2,1,0:T(8,128)(2,1)S(1)}, u32[]{:S(2)}, u32[]{:S(2)}) collective-permute-start(bf16[8,64,256]{2,1,0:T(8,128)(2,1)S(1)} %get-tuple-element.54.refs_5_), channel_id=1, source_target_pairs={{1,66},{2,65},{3,68},{4,67},{5,70},{6,69},{7,72},{8,71},{9,74},{10... | collective-permute-start | bytes 786440 | tf_op jit(solution)/shard_map/ppermute | solution.py:298
  5.1 0.3 collective-permute-start.3
  5.4 0.1 fusion
  5.5 0.1 select_n.82
  5.6 0.9 dynamic-slice_bitcast_fusion.3
  6.5 0.0 copy-start
  6.5 0.7 collective-permute-start
  7.2 0.1 select_n.85
  7.3 4.0 %collective-permute-start.1 = (bf16[3,64,256]{2,1,0:T(8,128)(2,1)S(1)}, bf16[3,64,256]{2,1,0:T(8,128)(2,1)S(1)}, u32[]{:S(2)}, u32[]{:S(2)}) collective-permute-start(bf16[3,64,256]{2,1,0:T(8,128)(2,1)S(1)} %pad_maximum_fusion.1), channel_id=1, source_target_pairs={{1,2},{2,1},{3,4},{4,3},{5,6},{6,5},{7,8},{8,7},{9,10},{10,9},{11,... | collective-permute-start | bytes 294920 | tf_op jit(solution)/shard_map/ppermute | solution.py:298
  11.4 0.4 collective-permute-start.4
  11.8 0.7 copy-done.4
  12.4 0.6 fusion.4
  13.0 0.7 stack.50.flags
  13.8 0.7 stack.51.flags
  14.5 0.6 stack.52.flags
  15.1 0.3 copy.22
  15.4 0.0 copy-start.1
  15.4 0.3 reshape.89.wu
  15.7 0.6 copy-done.1
  16.3 0.1 copy.23
  16.4 0.2 reshape.90.wm
  16.6 0.0 collective-permute-done.refs_7_
  16.6 0.1 collective-permute-done.1.refs_4_
  16.7 0.1 select_n.93
  16.8 0.1 select_n.94
  16.9 0.1 pad_maximum_fusion.2
  17.0 4.9 %collective-permute-done.4.refs_2_ = bf16[8,64,256]{2,1,0:T(8,128)(2,1)S(1)} collective-permute-done((bf16[8,64,256]{2,1,0:T(8,128)(2,1)S(1)}, bf16[8,64,256]{2,1,0:T(8,128)(2,1)S(1)}, u32[]{:S(2)}, u32[]{:S(2)}) %collective-permute-start.4) | collective-permute-done | bytes 262176 | tf_op jit(solution)/shard_map/ppermute | solution.py:298
  21.9 0.0 collective-permute-start.5
  22.0 0.6 shard_map.65
  22.6 0.0 collective-permute-done.2.refs_0_
  22.6 0.0 collective-permute-done.3.refs_1_
  22.6 0.8 collective-permute-done.5.refs_3_
  23.4 6.0 %shard_map.66 = (bf16[8,64,256]{2,1,0:T(8,128)(2,1)S(1)}, bf16[8,64,256]{2,1,0:T(8,128)(2,1)S(1)}, bf16[2,64,256]{2,1,0:T(8,128)(2,1)S(1)}, bf16[2,64,256]{2,1,0:T(8,128)(2,1)S(1)}) custom-call(s32[5]{0:T(128)S(1)} %stack.52.flags, bf16[8,256,256]{2,1,0:T(8,128)(2,1)S(1)} %get-tuple-element.37.cols, f32[64,256]{1,0:T(8,128)S(1)} %get-tuple-element.38.table, ...), custom_call_target="tpu_custom_call" | custom-call | flops 3000000000 | bytes 4000000 | tf_op jit(solution)/shard_map/pallas_call | solution.py:230
  29.4 4.0 %collective-permute-start.9 = (bf16[8,64,256]{2,1,0:T(8,128)(2,1)S(1)}, bf16[8,64,256]{2,1,0:T(8,128)(2,1)S(1)}, u32[]{:S(2)}, u32[]{:S(2)}) collective-permute-start(bf16[8,64,256]{2,1,0:T(8,128)(2,1)S(1)} %get-tuple-element.40.refs_10_), channel_id=1, source_target_pairs={{0,32},{1,33},{2,34},{3,35},{4,36},{5,37},{6,38},{7,39},{8,40},{9,... | collective-permute-start | bytes 786440 | tf_op jit(solution)/shard_map/ppermute | solution.py:298
  33.4 0.1 collective-permute-start.6
  33.5 7.1 %collective-permute-done.9.refs_2_ = bf16[8,64,256]{2,1,0:T(8,128)(2,1)S(1)} collective-permute-done((bf16[8,64,256]{2,1,0:T(8,128)(2,1)S(1)}, bf16[8,64,256]{2,1,0:T(8,128)(2,1)S(1)}, u32[]{:S(2)}, u32[]{:S(2)}) %collective-permute-start.9) | collective-permute-done | bytes 262176 | tf_op jit(solution)/shard_map/ppermute | solution.py:298
  40.6 0.7 collective-permute-start.12
  41.2 4.4 %collective-permute-done.6.refs_1_ = bf16[8,64,256]{2,1,0:T(8,128)(2,1)S(1)} collective-permute-done((bf16[8,64,256]{2,1,0:T(8,128)(2,1)S(1)}, bf16[8,64,256]{2,1,0:T(8,128)(2,1)S(1)}, u32[]{:S(2)}, u32[]{:S(2)}) %collective-permute-start.6) | collective-permute-done | bytes 262176 | tf_op jit(solution)/shard_map/ppermute | solution.py:298
  45.6 0.7 collective-permute-start.7
  46.3 3.5 %collective-permute-start.11 = (bf16[8,64,256]{2,1,0:T(8,128)(2,1)S(1)}, bf16[8,64,256]{2,1,0:T(8,128)(2,1)S(1)}, u32[]{:S(2)}, u32[]{:S(2)}) collective-permute-start(bf16[8,64,256]{2,1,0:T(8,128)(2,1)S(1)} %collective-permute-done.6.refs_1_), channel_id=1, source_target_pairs={{1,66},{2,65},{3,68},{4,67},{5,70},{6,69},{7,72},{8,71},{9,74},{10... | collective-permute-start | bytes 786440 | tf_op jit(solution)/shard_map/ppermute | solution.py:298
  49.9 0.2 collective-permute-start.13
  50.0 3.4 %collective-permute-done.7.refs_5_ = bf16[8,64,256]{2,1,0:T(8,128)(2,1)S(1)} collective-permute-done((bf16[8,64,256]{2,1,0:T(8,128)(2,1)S(1)}, bf16[8,64,256]{2,1,0:T(8,128)(2,1)S(1)}, u32[]{:S(2)}, u32[]{:S(2)}) %collective-permute-start.7) | collective-permute-done | bytes 262176 | tf_op jit(solution)/shard_map/ppermute | solution.py:298
  53.4 1.9 %collective-permute-start.8 = (bf16[8,64,256]{2,1,0:T(8,128)(2,1)S(1)}, bf16[8,64,256]{2,1,0:T(8,128)(2,1)S(1)}, u32[]{:S(2)}, u32[]{:S(2)}) collective-permute-start(bf16[8,64,256]{2,1,0:T(8,128)(2,1)S(1)} %collective-permute-done.7.refs_5_), channel_id=1, source_target_pairs={{1,66},{2,65},{3,68},{4,67},{5,70},{6,69},{7,72},{8,71},{9,74},{10... | collective-permute-start | bytes 786440 | tf_op jit(solution)/shard_map/ppermute | solution.py:298
  55.3 5.3 %collective-permute-start.14 = (bf16[2,64,256]{2,1,0:T(8,128)(2,1)S(1)}, bf16[2,64,256]{2,1,0:T(8,128)(2,1)S(1)}, u32[]{:S(2)}, u32[]{:S(2)}) collective-permute-start(bf16[2,64,256]{2,1,0:T(8,128)(2,1)S(1)} %get-tuple-element.41), channel_id=1, source_target_pairs={{1,2},{2,1},{3,4},{4,3},{5,6},{6,5},{7,8},{8,7},{9,10},{10,9},{11,... | collective-permute-start | bytes 196616 | tf_op jit(solution)/shard_map/ppermute | solution.py:298
  60.6 3.5 %collective-permute-done.14.refs_8_ = bf16[2,64,256]{2,1,0:T(8,128)(2,1)S(1)} collective-permute-done((bf16[2,64,256]{2,1,0:T(8,128)(2,1)S(1)}, bf16[2,64,256]{2,1,0:T(8,128)(2,1)S(1)}, u32[]{:S(2)}, u32[]{:S(2)}) %collective-permute-start.14) | collective-permute-done | bytes 65568 | tf_op jit(solution)/shard_map/ppermute | solution.py:298
  64.0 0.2 collective-permute-start.15
  64.3 0.6 shard_map.64
  64.9 0.4 collective-permute-done.15.refs_11_
  65.3 0.0 collective-permute-done.10.refs_3_
  65.3 6.7 %shard_map.67 = (bf16[8,64,256]{2,1,0:T(8,128)(2,1)S(1)}, bf16[8,64,256]{2,1,0:T(8,128)(2,1)S(1)}, bf16[2,64,256]{2,1,0:T(8,128)(2,1)}, bf16[2,64,256]{2,1,0:T(8,128)(2,1)}) custom-call(s32[5]{0:T(128)S(1)} %stack.51.flags, bf16[8,256,256]{2,1,0:T(8,128)(2,1)S(1)} %get-tuple-element.33.cols, f32[64,256]{1,0:T(8,128)S(1)} %get-tuple-element.34.table, ...), custom_call_target="tpu_custom_call" | custom-call | flops 3000000000 | bytes 4000000 | tf_op jit(solution)/shard_map/pallas_call | solution.py:230
  72.0 4.6 %collective-permute-start.16 = (bf16[8,64,256]{2,1,0:T(8,128)(2,1)S(1)}, bf16[8,64,256]{2,1,0:T(8,128)(2,1)S(1)}, u32[]{:S(2)}, u32[]{:S(2)}) collective-permute-start(bf16[8,64,256]{2,1,0:T(8,128)(2,1)S(1)} %get-tuple-element.43.edge), channel_id=1, source_target_pairs={{1,2},{2,1},{3,4},{4,3},{5,6},{6,5},{7,8},{8,7},{9,10},{10,9},{11,... | collective-permute-start | bytes 786440 | tf_op jit(solution)/shard_map/ppermute | solution.py:298
  76.7 0.1 collective-permute-start.17
  76.8 4.2 %collective-permute-start.18 = (bf16[2,2,4,32]{3,2,1,0:T(4,128)(2,1)S(1)}, bf16[2,2,4,32]{3,2,1,0:T(4,128)(2,1)S(1)}, u32[]{:S(2)}, u32[]{:S(2)}) collective-permute-start(bf16[2,2,4,32]{3,2,1,0:T(4,128)(2,1)S(1)} %get-tuple-element.45), channel_id=1, source_target_pairs={{0,112},{1,113},{2,114},{3,115},{4,116},{5,117},{6,118},{7,119},{8... | collective-permute-start | bytes 3080 | tf_op jit(solution)/shard_map/ppermute | solution.py:298
  80.9 0.0 collective-permute-start.19
  80.9 1.8 %collective-permute-done.18 = bf16[2,2,4,32]{3,2,1,0:T(4,128)(2,1)S(1)} collective-permute-done((bf16[2,2,4,32]{3,2,1,0:T(4,128)(2,1)S(1)}, bf16[2,2,4,32]{3,2,1,0:T(4,128)(2,1)S(1)}, u32[]{:S(2)}, u32[]{:S(2)}) %collective-permute-start.18) | collective-permute-done | bytes 1056 | tf_op jit(solution)/shard_map/ppermute | solution.py:298
  82.7 4.7 %collective-permute-done.19 = bf16[2,2,4,32]{3,2,1,0:T(4,128)(2,1)S(1)} collective-permute-done((bf16[2,2,4,32]{3,2,1,0:T(4,128)(2,1)S(1)}, bf16[2,2,4,32]{3,2,1,0:T(4,128)(2,1)S(1)}, u32[]{:S(2)}, u32[]{:S(2)}) %collective-permute-start.19) | collective-permute-done | bytes 1056 | tf_op jit(solution)/shard_map/ppermute | solution.py:298
  87.4 0.6 shard_map.68
  88.0 2.8 %shard_map.69 = (bf16[20,64,256]{2,1,0:T(8,128)(2,1)S(1)}, bf16[20,64,256]{2,1,0:T(8,128)(2,1)S(1)}) custom-call(s32[5]{0:T(128)S(1)} %stack.50.flags, bf16[8,256,256]{2,1,0:T(8,128)(2,1)S(1)} %get-tuple-element.47.cols, f32[64,256]{1,0:T(8,128)S(1)} %get-tuple-element.48.table, bf16[8,64,256]{2,1,0:T(8,128)(2,1)S(1)} %collective-permute-done.16.outer, ...), custom_call_target="tpu_custom_call" | custom-call | flops 1500000000 | bytes 4000000 | tf_op jit(solution)/shard_map/pallas_call | solution.py:230
  90.8 0.1 collective-permute-start.20
  90.9 4.1 %collective-permute-start.21 = (bf16[20,64,256]{2,1,0:T(8,128)(2,1)S(1)}, bf16[20,64,256]{2,1,0:T(8,128)(2,1)S(1)}, u32[]{:S(2)}, u32[]{:S(2)}) collective-permute-start(bf16[20,64,256]{2,1,0:T(8,128)(2,1)S(1)} %get-tuple-element.50), channel_id=1, source_target_pairs={{0,112},{1,113},{2,114},{3,115},{4,116},{5,117},{6,118},{7,119},{8... | collective-permute-start | bytes 1966088 | tf_op jit(solution)/shard_map/ppermute | solution.py:298
  95.0 14.0 %collective-permute-done.20.earlier = bf16[20,64,256]{2,1,0:T(8,128)(2,1)S(1)} collective-permute-done((bf16[20,64,256]{2,1,0:T(8,128)(2,1)S(1)}, bf16[20,64,256]{2,1,0:T(8,128)(2,1)S(1)}, u32[]{:S(2)}, u32[]{:S(2)}) %collective-permute-start.20) | collective-permute-done | bytes 655392 | tf_op jit(solution)/shard_map/ppermute | solution.py:298
  109.0 4.7 %shard_map.70 = bf16[16,64,256]{2,1,0:T(8,128)(2,1)} custom-call(s32[5]{0:T(128)S(1)} %stack.50.flags, bf16[192,576]{1,0:T(8,128)(2,1)S(1)} %reshape.89.wu, bf16[192,192]{1,0:T(8,128)(2,1)S(1)} %reshape.90.wm, bf16[8,64,256]{2,1,0:T(8,128)(2,1)S(1)} %collective-permute-done.16.outer, bf16[8,64,256]{2,1,0:T(8,128)(2,1)S(1)} %get-tuple-element.43.edge, ...), custom_call_target="tpu_custom_call" | custom-call | flops 1500000000 | bytes 4000000 | tf_op jit(solution)/shard_map/pallas_call | solution.py:230
  (28 shorter events, 0.2 us)
Async XLA Ops:
  0.0 5.4 %copy-start.3 = (s32[3,4,1,2,32]{4,3,2,1,0:T(2,128)S(1)}, s32[3,4,1,2,32]{4,3,2,1,0:T(2,128)}, u32[]{:S(2)}) copy-start(s32[3,4,1,2,32]{4,3,2,1,0:T(2,128)} %param.8) | copy-start | bytes 9220
  1.1 4.3 %copy-start.2 = (s32[3,4,1,2,32]{4,3,2,1,0:T(2,128)S(1)}, s32[3,4,1,2,32]{4,3,2,1,0:T(2,128)}, u32[]{:S(2)}) copy-start(s32[3,4,1,2,32]{4,3,2,1,0:T(2,128)} %param.7) | copy-start | bytes 9220
  1.1 21.5 %collective-permute-start.2 = (bf16[8,64,256]{2,1,0:T(8,128)(2,1)S(1)}, bf16[8,64,256]{2,1,0:T(8,128)(2,1)S(1)}, u32[]{:S(2)}, u32[]{:S(2)}) collective-permute-start(bf16[8,64,256]{2,1,0:T(8,128)(2,1)S(1)} %get-tuple-element.54.refs_5_), channel_id=1, source_target_pairs={{1,66},{2,65},{3,68},{4,67},{5,70},{6,69},{7,72},{8,71},{9,74},{10... | collective-permute-start | bytes 786440 | tf_op jit(solution)/shard_map/ppermute | solution.py:298
  5.1 17.5 %collective-permute-start.3 = (bf16[8,64,256]{2,1,0:T(8,128)(2,1)S(1)}, bf16[8,64,256]{2,1,0:T(8,128)(2,1)S(1)}, u32[]{:S(2)}, u32[]{:S(2)}) collective-permute-start(bf16[8,64,256]{2,1,0:T(8,128)(2,1)S(1)} %get-tuple-element.54.refs_5_), channel_id=1, source_target_pairs={{0,64},{1,65},{2,66},{3,67},{4,68},{5,69},{6,70},{7,71},{8,72},{9,... | collective-permute-start | bytes 786440 | tf_op jit(solution)/shard_map/ppermute | solution.py:298
  6.5 8.6 %copy-start = (bf16[3,3,64,192]{3,2,1,0:T(8,128)(2,1)S(1)}, bf16[3,3,64,192]{3,2,1,0:T(8,128)(2,1)}, u32[]{:S(2)}) copy-start(bf16[3,3,64,192]{3,2,1,0:T(8,128)(2,1)} %param.10) | copy-start | bytes 663556
  6.5 10.0 %collective-permute-start = (bf16[3,64,256]{2,1,0:T(8,128)(2,1)S(1)}, bf16[3,64,256]{2,1,0:T(8,128)(2,1)S(1)}, u32[]{:S(2)}, u32[]{:S(2)}) collective-permute-start(bf16[3,64,256]{2,1,0:T(8,128)(2,1)S(1)} %pad_maximum_fusion), channel_id=1, source_target_pairs={{0,1},{1,0},{2,3},{3,2},{4,5},{5,4},{6,7},{7,6},{8,9},{9,8},{10,11... | collective-permute-start | bytes 294920 | tf_op jit(solution)/shard_map/ppermute | solution.py:298
  7.3 9.4 %collective-permute-start.1 = (bf16[3,64,256]{2,1,0:T(8,128)(2,1)S(1)}, bf16[3,64,256]{2,1,0:T(8,128)(2,1)S(1)}, u32[]{:S(2)}, u32[]{:S(2)}) collective-permute-start(bf16[3,64,256]{2,1,0:T(8,128)(2,1)S(1)} %pad_maximum_fusion.1), channel_id=1, source_target_pairs={{1,2},{2,1},{3,4},{4,3},{5,6},{6,5},{7,8},{8,7},{9,10},{10,9},{11,... | collective-permute-start | bytes 294920 | tf_op jit(solution)/shard_map/ppermute | solution.py:298
  11.4 10.5 %collective-permute-start.4 = (bf16[8,64,256]{2,1,0:T(8,128)(2,1)S(1)}, bf16[8,64,256]{2,1,0:T(8,128)(2,1)S(1)}, u32[]{:S(2)}, u32[]{:S(2)}) collective-permute-start(bf16[8,64,256]{2,1,0:T(8,128)(2,1)S(1)} %get-tuple-element.53.refs_6_), channel_id=1, source_target_pairs={{0,64},{1,65},{2,66},{3,67},{4,68},{5,69},{6,70},{7,71},{8,72},{9,... | collective-permute-start | bytes 786440 | tf_op jit(solution)/shard_map/ppermute | solution.py:298
  11.8 0.7 copy-start.4
  15.4 0.9 copy-start.1
  21.9 1.5 %collective-permute-start.5 = (bf16[8,64,256]{2,1,0:T(8,128)(2,1)S(1)}, bf16[8,64,256]{2,1,0:T(8,128)(2,1)S(1)}, u32[]{:S(2)}, u32[]{:S(2)}) collective-permute-start(bf16[8,64,256]{2,1,0:T(8,128)(2,1)S(1)} %collective-permute-done.4.refs_2_), channel_id=1, source_target_pairs={{0,1},{1,0},{2,3},{3,2},{4,5},{5,4},{6,7},{7,6},{8,9},{9,8},{10,11... | collective-permute-start | bytes 786440 | tf_op jit(solution)/shard_map/ppermute | solution.py:298
  29.4 11.1 %collective-permute-start.9 = (bf16[8,64,256]{2,1,0:T(8,128)(2,1)S(1)}, bf16[8,64,256]{2,1,0:T(8,128)(2,1)S(1)}, u32[]{:S(2)}, u32[]{:S(2)}) collective-permute-start(bf16[8,64,256]{2,1,0:T(8,128)(2,1)S(1)} %get-tuple-element.40.refs_10_), channel_id=1, source_target_pairs={{0,32},{1,33},{2,34},{3,35},{4,36},{5,37},{6,38},{7,39},{8,40},{9,... | collective-permute-start | bytes 786440 | tf_op jit(solution)/shard_map/ppermute | solution.py:298
  33.4 12.2 %collective-permute-start.6 = (bf16[8,64,256]{2,1,0:T(8,128)(2,1)S(1)}, bf16[8,64,256]{2,1,0:T(8,128)(2,1)S(1)}, u32[]{:S(2)}, u32[]{:S(2)}) collective-permute-start(bf16[8,64,256]{2,1,0:T(8,128)(2,1)S(1)} %get-tuple-element.39.refs_9_), channel_id=1, source_target_pairs={{0,32},{1,33},{2,34},{3,35},{4,36},{5,37},{6,38},{7,39},{8,40},{9,... | collective-permute-start | bytes 786440 | tf_op jit(solution)/shard_map/ppermute | solution.py:298
  40.6 9.3 %collective-permute-start.12 = (bf16[8,64,256]{2,1,0:T(8,128)(2,1)S(1)}, bf16[8,64,256]{2,1,0:T(8,128)(2,1)S(1)}, u32[]{:S(2)}, u32[]{:S(2)}) collective-permute-start(bf16[8,64,256]{2,1,0:T(8,128)(2,1)S(1)} %collective-permute-done.9.refs_2_), channel_id=1, source_target_pairs={{0,64},{1,65},{2,66},{3,67},{4,68},{5,69},{6,70},{7,71},{8,72},{9,... | collective-permute-start | bytes 786440 | tf_op jit(solution)/shard_map/ppermute | solution.py:298
  45.6 7.8 %collective-permute-start.7 = (bf16[8,64,256]{2,1,0:T(8,128)(2,1)S(1)}, bf16[8,64,256]{2,1,0:T(8,128)(2,1)S(1)}, u32[]{:S(2)}, u32[]{:S(2)}) collective-permute-start(bf16[8,64,256]{2,1,0:T(8,128)(2,1)S(1)} %collective-permute-done.6.refs_1_), channel_id=1, source_target_pairs={{0,64},{1,65},{2,66},{3,67},{4,68},{5,69},{6,70},{7,71},{8,72},{9,... | collective-permute-start | bytes 786440 | tf_op jit(solution)/shard_map/ppermute | solution.py:298
  46.3 19.0 %collective-permute-start.10 = (bf16[8,64,256]{2,1,0:T(8,128)(2,1)S(1)}, bf16[8,64,256]{2,1,0:T(8,128)(2,1)S(1)}, u32[]{:S(2)}, u32[]{:S(2)}) collective-permute-start(bf16[8,64,256]{2,1,0:T(8,128)(2,1)S(1)} %collective-permute-done.9.refs_2_), channel_id=1, source_target_pairs={{0,1},{1,0},{2,3},{3,2},{4,5},{5,4},{6,7},{7,6},{8,9},{9,8},{10,11... | collective-permute-start | bytes 786440 | tf_op jit(solution)/shard_map/ppermute | solution.py:298
  46.3 19.0 %collective-permute-start.11 = (bf16[8,64,256]{2,1,0:T(8,128)(2,1)S(1)}, bf16[8,64,256]{2,1,0:T(8,128)(2,1)S(1)}, u32[]{:S(2)}, u32[]{:S(2)}) collective-permute-start(bf16[8,64,256]{2,1,0:T(8,128)(2,1)S(1)} %collective-permute-done.6.refs_1_), channel_id=1, source_target_pairs={{1,66},{2,65},{3,68},{4,67},{5,70},{6,69},{7,72},{8,71},{9,74},{10... | collective-permute-start | bytes 786440 | tf_op jit(solution)/shard_map/ppermute | solution.py:298
  49.9 15.5 %collective-permute-start.13 = (bf16[8,64,256]{2,1,0:T(8,128)(2,1)S(1)}, bf16[8,64,256]{2,1,0:T(8,128)(2,1)S(1)}, u32[]{:S(2)}, u32[]{:S(2)}) collective-permute-start(bf16[8,64,256]{2,1,0:T(8,128)(2,1)S(1)} %collective-permute-done.12.refs_6_), channel_id=1, source_target_pairs={{0,1},{1,0},{2,3},{3,2},{4,5},{5,4},{6,7},{7,6},{8,9},{9,8},{10,11... | collective-permute-start | bytes 786440 | tf_op jit(solution)/shard_map/ppermute | solution.py:298
  53.4 11.9 %collective-permute-start.8 = (bf16[8,64,256]{2,1,0:T(8,128)(2,1)S(1)}, bf16[8,64,256]{2,1,0:T(8,128)(2,1)S(1)}, u32[]{:S(2)}, u32[]{:S(2)}) collective-permute-start(bf16[8,64,256]{2,1,0:T(8,128)(2,1)S(1)} %collective-permute-done.7.refs_5_), channel_id=1, source_target_pairs={{1,66},{2,65},{3,68},{4,67},{5,70},{6,69},{7,72},{8,71},{9,74},{10... | collective-permute-start | bytes 786440 | tf_op jit(solution)/shard_map/ppermute | solution.py:298
  55.3 8.7 %collective-permute-start.14 = (bf16[2,64,256]{2,1,0:T(8,128)(2,1)S(1)}, bf16[2,64,256]{2,1,0:T(8,128)(2,1)S(1)}, u32[]{:S(2)}, u32[]{:S(2)}) collective-permute-start(bf16[2,64,256]{2,1,0:T(8,128)(2,1)S(1)} %get-tuple-element.41), channel_id=1, source_target_pairs={{1,2},{2,1},{3,4},{4,3},{5,6},{6,5},{7,8},{8,7},{9,10},{10,9},{11,... | collective-permute-start | bytes 196616 | tf_op jit(solution)/shard_map/ppermute | solution.py:298
  64.0 1.3 %collective-permute-start.15 = (bf16[2,64,256]{2,1,0:T(8,128)(2,1)S(1)}, bf16[2,64,256]{2,1,0:T(8,128)(2,1)S(1)}, u32[]{:S(2)}, u32[]{:S(2)}) collective-permute-start(bf16[2,64,256]{2,1,0:T(8,128)(2,1)S(1)} %get-tuple-element.42), channel_id=1, source_target_pairs={{0,1},{1,0},{2,3},{3,2},{4,5},{5,4},{6,7},{7,6},{8,9},{9,8},{10,11... | collective-permute-start | bytes 196616 | tf_op jit(solution)/shard_map/ppermute | solution.py:298
  72.0 16.0 %collective-permute-start.16 = (bf16[8,64,256]{2,1,0:T(8,128)(2,1)S(1)}, bf16[8,64,256]{2,1,0:T(8,128)(2,1)S(1)}, u32[]{:S(2)}, u32[]{:S(2)}) collective-permute-start(bf16[8,64,256]{2,1,0:T(8,128)(2,1)S(1)} %get-tuple-element.43.edge), channel_id=1, source_target_pairs={{1,2},{2,1},{3,4},{4,3},{5,6},{6,5},{7,8},{8,7},{9,10},{10,9},{11,... | collective-permute-start | bytes 786440 | tf_op jit(solution)/shard_map/ppermute | solution.py:298
  76.7 11.4 %collective-permute-start.17 = (bf16[8,64,256]{2,1,0:T(8,128)(2,1)S(1)}, bf16[8,64,256]{2,1,0:T(8,128)(2,1)S(1)}, u32[]{:S(2)}, u32[]{:S(2)}) collective-permute-start(bf16[8,64,256]{2,1,0:T(8,128)(2,1)S(1)} %get-tuple-element.44.inner), channel_id=1, source_target_pairs={{0,1},{1,0},{2,3},{3,2},{4,5},{5,4},{6,7},{7,6},{8,9},{9,8},{10,11... | collective-permute-start | bytes 786440 | tf_op jit(solution)/shard_map/ppermute | solution.py:298
  76.8 6.0 %collective-permute-start.18 = (bf16[2,2,4,32]{3,2,1,0:T(4,128)(2,1)S(1)}, bf16[2,2,4,32]{3,2,1,0:T(4,128)(2,1)S(1)}, u32[]{:S(2)}, u32[]{:S(2)}) collective-permute-start(bf16[2,2,4,32]{3,2,1,0:T(4,128)(2,1)S(1)} %get-tuple-element.45), channel_id=1, source_target_pairs={{0,112},{1,113},{2,114},{3,115},{4,116},{5,117},{6,118},{7,119},{8... | collective-permute-start | bytes 3080 | tf_op jit(solution)/shard_map/ppermute | solution.py:298
  80.9 6.5 %collective-permute-start.19 = (bf16[2,2,4,32]{3,2,1,0:T(4,128)(2,1)S(1)}, bf16[2,2,4,32]{3,2,1,0:T(4,128)(2,1)S(1)}, u32[]{:S(2)}, u32[]{:S(2)}) collective-permute-start(bf16[2,2,4,32]{3,2,1,0:T(4,128)(2,1)S(1)} %get-tuple-element.46), channel_id=1, source_target_pairs={{0,16},{1,17},{2,18},{3,19},{4,20},{5,21},{6,22},{7,23},{8,24},{9,... | collective-permute-start | bytes 3080 | tf_op jit(solution)/shard_map/ppermute | solution.py:298
  90.8 18.2 %collective-permute-start.20 = (bf16[20,64,256]{2,1,0:T(8,128)(2,1)S(1)}, bf16[20,64,256]{2,1,0:T(8,128)(2,1)S(1)}, u32[]{:S(2)}, u32[]{:S(2)}) collective-permute-start(bf16[20,64,256]{2,1,0:T(8,128)(2,1)S(1)} %get-tuple-element.49), channel_id=1, source_target_pairs={{0,16},{1,17},{2,18},{3,19},{4,20},{5,21},{6,22},{7,23},{8,24},{9,... | collective-permute-start | bytes 1966088 | tf_op jit(solution)/shard_map/ppermute | solution.py:298
  90.9 18.1 %collective-permute-start.21 = (bf16[20,64,256]{2,1,0:T(8,128)(2,1)S(1)}, bf16[20,64,256]{2,1,0:T(8,128)(2,1)S(1)}, u32[]{:S(2)}, u32[]{:S(2)}) collective-permute-start(bf16[20,64,256]{2,1,0:T(8,128)(2,1)S(1)} %get-tuple-element.50), channel_id=1, source_target_pairs={{0,112},{1,113},{2,114},{3,115},{4,116},{5,117},{6,118},{7,119},{8... | collective-permute-start | bytes 1966088 | tf_op jit(solution)/shard_map/ppermute | solution.py:298

commit v7 on v6

--- a/solution.py
+++ b/solution.py
@@ -70,100 +70,87 @@
     )(vals)
 
 
+def column_pass(buffer, window, matrix):
+    count = window.shape[0]
+    buffer[...] = jnp.dot(
+        window.reshape(count * CH, WIDTH), matrix, preferred_element_type=F32
+    ).reshape(count, CH, WIDTH)
+
+
+def row_pass(buffer, entry, keep, outs, put):
+    lanes = (16, WIDTH)
+    s = entry[0:1].astype(jnp.int32) + 5
+    bits = [jnp.broadcast_to((s & b) != 0, lanes) for b in (8, 4, 2, 1)]
+    fy = entry[2:3] * 0.25
+    w1 = jnp.broadcast_to(fy * keep, lanes)
+    w0 = jnp.broadcast_to((1.0 - fy) * keep, lanes)
+    for c in range(CH // 16):
+        v = [buffer[u, 16 * c : 16 * c + 16, :] for u in range(buffer.shape[0])]
+        for i, row in enumerate(pick_rows(v, bits, w0, w1, outs)):
+            put(i, 16 * c, row.astype(BF16))
+
+
+def entry_at(table, n):
+    return table[pl.ds(pl.multiple_of(n * 8, 8), 8), :]
+
+
 def warp_into(flags, cols, table, source_of, passed, put_of):
     has_above = (flags[1] > 0).astype(F32)
     has_below = (flags[2] > 0).astype(F32)
-    lanes = (16, WIDTH)
 
     @pl.loop(0, 2)
     def _(which):
         put = put_of(which)
 
-        def column_pass(k):
+        def columns(k):
             block, first, count, _, _ = BLOCKS[k]
-            window = source_of(which, first, count).reshape(count * CH, WIDTH)
-            passed[k][...] = jnp.dot(
-                window, cols[which * 4 + block], preferred_element_type=F32
-            ).reshape(count, CH, WIDTH)
-
-        def row_pass(k):
-            block, _, count, outs, start = BLOCKS[k]
-            at = (which * 4 + block) * 8
-            entry = table[pl.ds(pl.multiple_of(at, 8), 8), :]
-            s = entry[0:1].astype(jnp.int32) + 5
+            column_pass(passed[k], source_of(which, first, count), cols[which * 4 + block])
+
+        def rows(k):
+            block, _, _, outs, start = BLOCKS[k]
             keep = {0: has_above, 3: has_below}.get(block, 1.0)
-            bits = [jnp.broadcast_to((s & b) != 0, lanes) for b in (8, 4, 2, 1)]
-            fy = entry[2:3] * 0.25
-            w1 = jnp.broadcast_to(fy * keep, lanes)
-            w0 = jnp.broadcast_to((1.0 - fy) * keep, lanes)
-            for c in range(CH // 16):
-                v = [passed[k][u, 16 * c : 16 * c + 16, :] for u in range(count)]
-                for i, row in enumerate(pick_rows(v, bits, w0, w1, outs)):
-                    put(start + i, 16 * c, row.astype(BF16))
-
-        column_pass(0)
+            row_pass(
+                passed[k],
+                entry_at(table, which * 4 + block),
+                keep,
+                outs,
+                lambda i, c, value: put(start + i, c, value),
+            )
+
+        columns(0)
         for k in range(4):
             if k < 3:
-                column_pass(k + 1)
-            row_pass(k)
-
-
-def convolve_band(flags, wu, wm, joined, act, final, outs):
-    has_above = flags[1] > 0
-    has_below = flags[2] > 0
-    turned = flags[0]
-    lane = lax.broadcasted_iota(jnp.int32, (CH, WIDTH), 1)
-    not_first = lane > 0
-    not_last = lane < WIDTH - 1
-
-    def gather_taps(s):
-        left = jnp.where(not_first, pltpu.roll(s[0:CH], 1, 1), 0.0)
-        right = jnp.where(not_last, pltpu.roll(s[2 * CH :], WIDTH - 1, 1), 0.0)
+                columns(k + 1)
+            rows(k)
+
+
+class Convolutions:
+    def __init__(self, flags, wu, wm, joined, act):
+        self.flags, self.wu, self.wm, self.joined, self.act = flags, wu, wm, joined, act
+        lane = lax.broadcasted_iota(jnp.int32, (CH, WIDTH), 1)
+        self.not_first = lane > 0
+        self.not_last = lane < WIDTH - 1
+
+    def gather_taps(self, s):
+        left = jnp.where(self.not_first, pltpu.roll(s[0:CH], 1, 1), 0.0)
+        right = jnp.where(self.not_last, pltpu.roll(s[2 * CH :], WIDTH - 1, 1), 0.0)
         return s[CH : 2 * CH] + left + right
 
-    def activate(a):
-        window = joined[pl.ds(a, 3)].reshape(9 * CH, WIDTH)
-        total = gather_taps(jnp.dot(wu[...], window, preferred_element_type=F32))
+    def activate(self, a):
+        window = self.joined[pl.ds(a, 3)].reshape(9 * CH, WIDTH)
+        total = self.gather_taps(jnp.dot(self.wu[...], window, preferred_element_type=F32))
         half = 0.5 * total
         value = half + half * jnp.tanh(half)
-        keep = jnp.where(
-            a == 0, has_above, jnp.where(a == 17, has_below, True)
-        ).astype(F32)
-        act[a] = (value * keep).astype(BF16)
-
-    @pl.loop(0, 3)
-    def _(n):
-        for k in range(6):
-            activate(6 * n + k)
-
-    scale = flags[3].astype(F32)
-
-    def finish(y):
-        window = act[pl.ds(y, 3)].reshape(3 * CH, WIDTH)
-        total = gather_taps(jnp.dot(wm[...], window, preferred_element_type=F32))
-        own = joined[y + 2, OWN, :].astype(F32)
-        return (own + scale * total).astype(BF16)
-
-    if final:
-        (out,) = outs
-
-        @pl.loop(0, 2)
-        def _(n):
-            for k in range(8):
-                out[8 * n + k] = finish(8 * n + k)
-
-    else:
-        out_edge, out_inner, out_rim, out_near = outs
-
-        @pl.loop(0, 2)
-        def _(n):
-            for k in range(4):
-                y = 4 * n + k
-                out_edge[y] = finish(y + turn(turned, 0, 8))
-                out_inner[y] = finish(y + turn(turned, 8, 8))
-
-        out_rim[...] = out_edge[pl.ds(turn(turned, 0, 6), 2)]
-        out_near[...] = out_inner[pl.ds(turn(turned, 6, 6), 2)]
+        inside = jnp.where(
+            a == 0, self.flags[1] > 0, jnp.where(a == 17, self.flags[2] > 0, True)
+        )
+        self.act[a] = (value * inside.astype(F32)).astype(BF16)
+
+    def finish(self, y):
+        window = self.act[pl.ds(y, 3)].reshape(3 * CH, WIDTH)
+        total = self.gather_taps(jnp.dot(self.wm[...], window, preferred_element_type=F32))
+        own = self.joined[y + 2, OWN, :].astype(F32)
+        return (own + self.flags[3].astype(F32) * total).astype(BF16)
 
 
 def stack_rows(target, turned, pieces):
@@ -171,7 +158,8 @@
         target[pl.ds(turn(turned, 8 * p, 24), 8)] = pieces[p][...]
 
 
-def level_kernel(sources, flags, cols, table, wu, wm, *refs):
+def level_kernel(sources, level, flags, cols, table, wu, wm, *refs):
+    flags = flags.at[level]
     own_outer, own_edge, own_inner, own_near = refs[4 * sources : 4 * sources + 4]
     outs = refs[4 * sources + 4 : 4 * sources + 8]
     src, joined, act = refs[4 * sources + 8 : 4 * sources + 11]
@@ -194,35 +182,119 @@
         return put
 
     warp_into(flags, cols, table, source_of, passed, put_of)
-    convolve_band(flags, wu, wm, joined, act, False, outs)
-
-
-def warp_kernel(flags, cols, table, outer, edge, inner, near, ahead, back, src, both, *passed):
-    stack_rows(src, flags[0], (outer, edge, inner, near))
-
-    def source_of(which, first, count):
-        return src[first : first + count]
-
-    def put_of(which):
-        def put(row, c, value):
-            both[which, row, c : c + 16, :] = value
-
-        return put
-
-    warp_into(flags, cols, table, source_of, passed, put_of)
+    conv = Convolutions(flags, wu, wm, joined, act)
+
+    @pl.loop(0, 3)
+    def _(n):
+        for k in range(6):
+            conv.activate(6 * n + k)
+
+    out_edge, out_inner, out_rim, out_near = outs
+
+    @pl.loop(0, 2)
+    def _(n):
+        for k in range(4):
+            y = 4 * n + k
+            out_edge[y] = conv.finish(y + turn(turned, 0, 8))
+            out_inner[y] = conv.finish(y + turn(turned, 8, 8))
+
+    out_rim[...] = out_edge[pl.ds(turn(turned, 0, 6), 2)]
+    out_near[...] = out_inner[pl.ds(turn(turned, 6, 6), 2)]
+
+
+def warp_half_kernel(is_outer, flags, cols, table, *refs):
+    flags = flags.at[0]
+    pieces, (ahead, back, src, both, main_rows, halo_rows) = refs[:3], refs[3:]
+    turned = flags[0]
+    part = turned if is_outer else 1 - turned
+    for p in range(3):
+        place = p if is_outer else p + 1
+        src[pl.ds(turn(turned, 8 * place, 24), 8)] = pieces[p][...]
+    keep = (jnp.where(part == 1, flags[2], flags[1]) > 0).astype(F32)
+
+    @pl.loop(0, 2)
+    def _(which):
+        def put_from(start):
+            def put(i, c, value):
+                both[which, start + i, c : c + 16, :] = value
+
+            return put
+
+        main, halo = which * 4 + 1 + part, which * 4 + 3 * part
+        column_pass(main_rows, src[pl.ds(3 + 8 * part, 19)], cols[main])
+        column_pass(halo_rows, src[pl.ds(1 + 18 * part, 13)], cols[halo])
+        row_pass(main_rows, entry_at(table, main), 1.0, 8, put_from(2 - 2 * part))
+        row_pass(halo_rows, entry_at(table, halo), keep, 2, put_from(8 * part))
+
     ahead[...] = both[0]
     back[...] = both[1]
 
 
-def last_kernel(flags, wu, wm, outer, edge, inner, near, earlier, later, out, joined, act):
+def last_inner_kernel(
+    flags, wu, wm, inner, near, earlier, later, out_act, out_rows, joined, act
+):
+    flags = flags.at[0]
     turned = flags[0]
+    part = 1 - turned
+    joined[pl.ds(turn(turned, 10, 12), 8), OWN] = inner[...]
+    joined[pl.ds(turn(turned, 18, 18), 2), OWN] = near[pl.ds(turn(turned, 0, 6), 2)]
+    joined[pl.ds(10 * part, 10), 0:CH] = earlier[...]
+    joined[pl.ds(10 * part, 10), CH : 2 * CH] = later[...]
+    conv = Convolutions(flags, wu, wm, joined, act)
+
+    @pl.loop(0, 2)
+    def _(n):
+        for k in range(4):
+            conv.activate(10 * part + 4 * n + k)
+
+    for k in range(6):
+        out_rows[k] = conv.finish(10 * part + k)
+    out_act[...] = act[pl.ds(10 * part, 8)]
+
+
+def last_outer_kernel(
+    flags,
+    wu,
+    wm,
+    outer,
+    edge,
+    inner,
+    near,
+    inner_earlier,
+    inner_later,
+    inner_act,
+    inner_rows,
+    earlier,
+    later,
+    out,
+    joined,
+    act,
+):
+    flags = flags.at[0]
+    turned = flags[0]
+    part = turned
     joined[pl.ds(turn(turned, 0, 18), 2), OWN] = outer[pl.ds(turn(turned, 6, 6), 2)]
     joined[pl.ds(turn(turned, 2, 12), 8), OWN] = edge[...]
     joined[pl.ds(turn(turned, 10, 12), 8), OWN] = inner[...]
     joined[pl.ds(turn(turned, 18, 18), 2), OWN] = near[pl.ds(turn(turned, 0, 6), 2)]
-    joined[:, 0:CH] = earlier[...]
-    joined[:, CH : 2 * CH] = later[...]
-    convolve_band(flags, wu, wm, joined, act, True, (out,))
+    joined[pl.ds(10 * part, 10), 0:CH] = earlier[...]
+    joined[pl.ds(10 * part, 10), CH : 2 * CH] = later[...]
+    joined[pl.ds(10 - 10 * part, 10), 0:CH] = inner_earlier[...]
+    joined[pl.ds(10 - 10 * part, 10), CH : 2 * CH] = inner_later[...]
+    act[pl.ds(10 - 10 * part, 8)] = inner_act[...]
+    out[pl.ds(10 - 10 * part, 6)] = inner_rows[...]
+    conv = Convolutions(flags, wu, wm, joined, act)
+
+    @pl.loop(0, 2)
+    def _(n):
+        for k in range(5):
+            conv.activate(8 * part + 5 * n + k)
+
+    @pl.loop(0, 2)
+    def _(n):
+        for k in range(5):
+            y = 6 * part + 5 * n + k
+            out[y] = conv.finish(y)
 
 
 def on_core(kernel, out_shape, scratch, cost, operands, interpret):
@@ -249,13 +321,13 @@
     return [pltpu.VMEM((20, 3 * CH, WIDTH), BF16), pltpu.VMEM((18, CH, WIDTH), BF16)]
 
 
-def run_level(flags, cols, table, wu, wm, sources, own, interpret=False):
+def run_level(level, flags, cols, table, wu, wm, sources, own, interpret=False):
     half = jax.ShapeDtypeStruct((HALF, CH, WIDTH), BF16)
     edge = jax.ShapeDtypeStruct((2, CH, WIDTH), BF16)
     operands = [flags, cols, table, wu, wm] + [p for s in sources for p in s] + list(own)
     scratch = [pltpu.VMEM((len(sources), 32, CH, WIDTH), BF16)]
     return on_core(
-        functools.partial(level_kernel, len(sources)),
+        functools.partial(level_kernel, len(sources), level),
         (half, half, edge, edge),
         scratch + band_buffers() + passed_buffers(),
         3_000_000_000,
@@ -264,25 +336,43 @@
     )
 
 
-def run_warp(flags, cols, table, pieces, interpret=False):
+def run_warp_half(is_outer, flags, cols, table, pieces, interpret=False):
     return on_core(
-        warp_kernel,
-        (jax.ShapeDtypeStruct((20, CH, WIDTH), BF16),) * 2,
-        [pltpu.VMEM((32, CH, WIDTH), BF16), pltpu.VMEM((2, 20, CH, WIDTH), BF16)]
-        + passed_buffers(),
-        1_500_000_000,
+        functools.partial(warp_half_kernel, is_outer),
+        (jax.ShapeDtypeStruct((10, CH, WIDTH), BF16),) * 2,
+        [
+            pltpu.VMEM((32, CH, WIDTH), BF16),
+            pltpu.VMEM((2, 10, CH, WIDTH), BF16),
+            pltpu.VMEM((19, CH, WIDTH), F32),
+            pltpu.VMEM((13, CH, WIDTH), F32),
+        ],
+        800_000_000,
         [flags, cols, table, *pieces],
         interpret,
     )
 
 
-def run_last(flags, wu, wm, own, warped, interpret=False):
+def run_last_inner(flags, wu, wm, operands, interpret=False):
     return on_core(
-        last_kernel,
+        last_inner_kernel,
+        (
+            jax.ShapeDtypeStruct((8, CH, WIDTH), BF16),
+            jax.ShapeDtypeStruct((6, CH, WIDTH), BF16),
+        ),
+        band_buffers(),
+        600_000_000,
+        [flags, wu, wm, *operands],
+        interpret,
+    )
+
+
+def run_last_outer(flags, wu, wm, operands, interpret=False):
+    return on_core(
+        last_outer_kernel,
         (jax.ShapeDtypeStruct((2 * HALF, CH, WIDTH), BF16),),
         band_buffers(),
-        1_500_000_000,
-        [flags, wu, wm, *own, *warped],
+        900_000_000,
+        [flags, wu, wm, *operands],
         interpret,
     )[0]
 
@@ -338,7 +428,9 @@
     wu, wm = tap_weights(uniting_weight), tap_weights(mixing_weight)
     common = [turned, (row > 0).astype(jnp.int32), (row < rows - 1).astype(jnp.int32)]
     swapped = (lax.axis_index("tm") % 4 < 2).astype(jnp.int32)
-    flags = [jnp.stack(common + [update_mask[k, 0], swapped]) for k in range(LEVELS)]
+    flags = jnp.stack(
+        [value for k in range(LEVELS) for value in common + [update_mask[k, 0], swapped]]
+    ).reshape(LEVELS, 5)
 
     def to_other(t):
         return t + 4
@@ -371,7 +463,7 @@
         ],
         axis=3,
     )
-    values, later_values, ahead_entries, back_entries, wu, wm, *flags = (
+    values, later_values, ahead_entries, back_entries, wu, wm, flags = (
         lax.optimization_barrier(
             (
                 level_values(packed[:, 2]),
@@ -380,13 +472,13 @@
                 packed[:, 0, 2:4],
                 wu,
                 wm,
-                *flags,
+                flags,
             )
         )
     )
     cols, table = make_columns(values)
     edge, inner, rim, near = run_level(
-        flags[2], cols, table, wu, wm, [(h, e, i, n)], (own_outer, edge, inner, own_near)
+        2, flags, cols, table, wu, wm, [(h, e, i, n)], (own_outer, edge, inner, own_near)
     )
 
     own_outer = send(rim, row_to=off_chip)
@@ -403,7 +495,8 @@
     xn = send(xi, row_to=on_chip)
     cols, table = make_columns(later_values)
     edge, inner, _, _ = run_level(
-        flags[1],
+        1,
+        flags,
         cols,
         table,
         wu,
@@ -417,11 +510,33 @@
     cols, table = make_columns(
         level_values(jnp.concatenate([for_ahead, for_back], axis=1))
     )
-    own = (outer, edge, inner, near)
-    to_ahead, to_back = run_warp(flags[0], cols, table, own)
-    earlier = send(to_ahead, ahead)
-    later = send(to_back, back)
-    return run_last(flags[0], wu, wm, own, (earlier, later))[None]
+    halves = run_warp_half(False, flags, cols, table, (edge, inner, near))
+    inner_earlier = send(halves[0], ahead)
+    inner_later = send(halves[1], back)
+    halves = run_warp_half(True, flags, cols, table, (outer, edge, inner))
+    earlier = send(halves[0], ahead)
+    later = send(halves[1], back)
+    inner_act, inner_rows = run_last_inner(
+        flags, wu, wm, (inner, near, inner_earlier, inner_later)
+    )
+    refined = run_last_outer(
+        flags,
+        wu,
+        wm,
+        (
+            outer,
+            edge,
+            inner,
+            near,
+            inner_earlier,
+            inner_later,
+            inner_act,
+            inner_rows,
+            earlier,
+            later,
+        ),
+    )
+    return refined[None]
 
 
 def solution(mesh):

time: 114 us -> 113 us (level)
  waiting for transfers between devices: 45 us -> 37.5 us
  starting transfers between devices: 39 us -> 43.1 us
  Pallas kernels: 21.9 us -> 24.1 us
    ppermute x22 -> x24, waiting for transfers between devices: 45 us -> 37.5 us  [send(): return lax.ppermute(x, ('tm', 'rows'), route)]
    ppermute x22 -> x24, starting transfers between devices: 39 us -> 43.1 us  [send(): return lax.ppermute(x, ('tm', 'rows'), route)]
    pallas_call x4 -> x6, Pallas kernels: 20.2 us -> 22.4 us  [on_core(): pl.pallas_call(kernel, out_shape=out_shape, in_specs=[pl.BlockSpec(memory...]
  transfers between devices with their start and end apart: 22 -> 24, of which waited for: 11 -> 12; matrix products, arithmetic and copies ran while one was open for 4% -> 4% of each run, Pallas kernels for 2% -> 7%
where the time goes in v7:
time: 113 us; the launch traced here: 112 us
  starting transfers between devices  43.1 us (38%)
  waiting for transfers between devices  37.5 us (33%)
  Pallas kernels  24.1 us (21%)
  local copies, waits for them, and re-layouts  7.15 us (6%)
    ppermute x24, starting transfers between devices, send(): return lax.ppermute(x, ('tm', 'rows'), route)  43.1 us
    ppermute x24, waiting for transfers between devices, send(): return lax.ppermute(x, ('tm', 'rows'), route)  37.5 us
    pallas_call x6, Pallas kernels, on_core(): pl.pallas_call(kernel, out_shape=out_shape, in_specs=[pl.BlockSpec(memory...  22.4 us
  transfers between devices with their start and end apart: 24, of which 12 were waited for; matrix products, arithmetic and copies ran while one was open for 4% of the time, Pallas kernels for 7%

profile of v7, /device:TPU:8, one launch (start us, length us, event | category | flops | bytes accessed | tf_op | source)
XLA Modules:
  0.0 112.4 jit_solution(16323316800035293202)
XLA Ops:
  0.0 1.1 dynamic-slice_bitcast_fusion
  1.1 0.0 copy-start.2
  1.1 4.0 %collective-permute-start.2 = (bf16[8,64,256]{2,1,0:T(8,128)(2,1)S(1)}, bf16[8,64,256]{2,1,0:T(8,128)(2,1)S(1)}, u32[]{:S(2)}, u32[]{:S(2)}) collective-permute-start(bf16[8,64,256]{2,1,0:T(8,128)(2,1)S(1)} %get-tuple-element.58.refs_5_), channel_id=1, source_target_pairs={{1,66},{2,65},{3,68},{4,67},{5,70},{6,69},{7,72},{8,71},{9,74},{10... | collective-permute-start | bytes 786440 | tf_op jit(solution)/shard_map/ppermute | solution.py:388
  5.1 0.3 collective-permute-start.3
  5.4 0.1 fusion
  5.5 0.1 select_n.82
  5.6 0.9 dynamic-slice_bitcast_fusion.3
  6.5 0.0 copy-start
  6.6 0.7 collective-permute-start
  7.2 0.1 select_n.85
  7.4 4.0 %collective-permute-start.1 = (bf16[3,64,256]{2,1,0:T(8,128)(2,1)S(1)}, bf16[3,64,256]{2,1,0:T(8,128)(2,1)S(1)}, u32[]{:S(2)}, u32[]{:S(2)}) collective-permute-start(bf16[3,64,256]{2,1,0:T(8,128)(2,1)S(1)} %pad_maximum_fusion.1), channel_id=1, source_target_pairs={{1,2},{2,1},{3,4},{4,3},{5,6},{6,5},{7,8},{8,7},{9,10},{10,9},{11,... | collective-permute-start | bytes 294920 | tf_op jit(solution)/shard_map/ppermute | solution.py:388
  11.4 0.4 collective-permute-start.4
  11.8 0.7 copy-done.4
  12.4 0.6 fusion.4
  13.0 1.9 %stack.44 = s32[15]{0:T(128)S(1)} concatenate(s32[1]{0:T(128)} %bitcast.19, s32[1]{0:T(128)} %bitcast.20, s32[1]{0:T(128)} %bitcast.21, s32[1]{0:T(128)} %bitcast.22, s32[1]{0:T(128)} %bitcast.23, s32[1]{0:T(128)} %bitcast.19, s32[1]{0:T(128)} %bitcast.20, s32[1]{0:T(128)} %bitcast.21, s32[1]{0:T(128)} %bitcast.24, s32[1]{0:T(128)} %bitcast.23, s32[1]{0:T(128)} %bitcast.19, ...), dimensions={0} | concatenate | bytes 120 | tf_op jit(solution)/shard_map/stack | solution.py:431
  15.0 0.1 reshape.94.flags
  15.1 0.3 copy.22
  15.3 0.0 copy-start.1
  15.3 0.3 reshape.92.wu
  15.6 0.6 copy-done.1
  16.2 0.1 copy.23
  16.4 0.2 reshape.93.wm
  16.5 0.0 collective-permute-done.refs_7_
  16.5 0.2 collective-permute-done.1.refs_4_
  16.7 0.1 select_n.93
  16.8 0.1 select_n.94
  16.9 0.1 pad_maximum_fusion.2
  17.0 4.9 %collective-permute-done.4.refs_2_ = bf16[8,64,256]{2,1,0:T(8,128)(2,1)S(1)} collective-permute-done((bf16[8,64,256]{2,1,0:T(8,128)(2,1)S(1)}, bf16[8,64,256]{2,1,0:T(8,128)(2,1)S(1)}, u32[]{:S(2)}, u32[]{:S(2)}) %collective-permute-start.4) | collective-permute-done | bytes 262176 | tf_op jit(solution)/shard_map/ppermute | solution.py:388
  21.9 0.0 collective-permute-start.5
  22.0 0.6 shard_map.65
  22.6 0.8 collective-permute-done.5.refs_3_
  23.4 6.0 %shard_map.66 = (bf16[8,64,256]{2,1,0:T(8,128)(2,1)S(1)}, bf16[8,64,256]{2,1,0:T(8,128)(2,1)S(1)}, bf16[2,64,256]{2,1,0:T(8,128)(2,1)S(1)}, bf16[2,64,256]{2,1,0:T(8,128)(2,1)S(1)}) custom-call(s32[3,5]{1,0:T(4,128)S(1)} %reshape.94.flags, bf16[8,256,256]{2,1,0:T(8,128)(2,1)S(1)} %get-tuple-element.37.cols, f32[64,256]{1,0:T(8,128)S(1)} %get-tuple-element.38.table, ...), custom_call_target="tpu_custom_call" | custom-call | flops 3000000000 | bytes 4000000 | tf_op jit(solution)/shard_map/pallas_call | solution.py:302
  29.5 4.0 %collective-permute-start.9 = (bf16[8,64,256]{2,1,0:T(8,128)(2,1)S(1)}, bf16[8,64,256]{2,1,0:T(8,128)(2,1)S(1)}, u32[]{:S(2)}, u32[]{:S(2)}) collective-permute-start(bf16[8,64,256]{2,1,0:T(8,128)(2,1)S(1)} %get-tuple-element.40.refs_10_), channel_id=1, source_target_pairs={{0,32},{1,33},{2,34},{3,35},{4,36},{5,37},{6,38},{7,39},{8,40},{9,... | collective-permute-start | bytes 786440 | tf_op jit(solution)/shard_map/ppermute | solution.py:388
  33.4 0.1 collective-permute-start.6
  33.5 7.1 %collective-permute-done.9.refs_2_ = bf16[8,64,256]{2,1,0:T(8,128)(2,1)S(1)} collective-permute-done((bf16[8,64,256]{2,1,0:T(8,128)(2,1)S(1)}, bf16[8,64,256]{2,1,0:T(8,128)(2,1)S(1)}, u32[]{:S(2)}, u32[]{:S(2)}) %collective-permute-start.9) | collective-permute-done | bytes 262176 | tf_op jit(solution)/shard_map/ppermute | solution.py:388
  40.6 0.7 collective-permute-start.12
  41.3 4.4 %collective-permute-done.6.refs_1_ = bf16[8,64,256]{2,1,0:T(8,128)(2,1)S(1)} collective-permute-done((bf16[8,64,256]{2,1,0:T(8,128)(2,1)S(1)}, bf16[8,64,256]{2,1,0:T(8,128)(2,1)S(1)}, u32[]{:S(2)}, u32[]{:S(2)}) %collective-permute-start.6) | collective-permute-done | bytes 262176 | tf_op jit(solution)/shard_map/ppermute | solution.py:388
  45.7 0.7 collective-permute-start.7
  46.4 3.5 %collective-permute-start.11 = (bf16[8,64,256]{2,1,0:T(8,128)(2,1)S(1)}, bf16[8,64,256]{2,1,0:T(8,128)(2,1)S(1)}, u32[]{:S(2)}, u32[]{:S(2)}) collective-permute-start(bf16[8,64,256]{2,1,0:T(8,128)(2,1)S(1)} %collective-permute-done.6.refs_1_), channel_id=1, source_target_pairs={{1,66},{2,65},{3,68},{4,67},{5,70},{6,69},{7,72},{8,71},{9,74},{10... | collective-permute-start | bytes 786440 | tf_op jit(solution)/shard_map/ppermute | solution.py:388
  49.9 0.2 collective-permute-start.13
  50.1 3.4 %collective-permute-done.7.refs_5_ = bf16[8,64,256]{2,1,0:T(8,128)(2,1)S(1)} collective-permute-done((bf16[8,64,256]{2,1,0:T(8,128)(2,1)S(1)}, bf16[8,64,256]{2,1,0:T(8,128)(2,1)S(1)}, u32[]{:S(2)}, u32[]{:S(2)}) %collective-permute-start.7) | collective-permute-done | bytes 262176 | tf_op jit(solution)/shard_map/ppermute | solution.py:388
  53.4 1.9 %collective-permute-start.8 = (bf16[8,64,256]{2,1,0:T(8,128)(2,1)S(1)}, bf16[8,64,256]{2,1,0:T(8,128)(2,1)S(1)}, u32[]{:S(2)}, u32[]{:S(2)}) collective-permute-start(bf16[8,64,256]{2,1,0:T(8,128)(2,1)S(1)} %collective-permute-done.7.refs_5_), channel_id=1, source_target_pairs={{1,66},{2,65},{3,68},{4,67},{5,70},{6,69},{7,72},{8,71},{9,74},{10... | collective-permute-start | bytes 786440 | tf_op jit(solution)/shard_map/ppermute | solution.py:388
  55.4 5.3 %collective-permute-start.14 = (bf16[2,64,256]{2,1,0:T(8,128)(2,1)S(1)}, bf16[2,64,256]{2,1,0:T(8,128)(2,1)S(1)}, u32[]{:S(2)}, u32[]{:S(2)}) collective-permute-start(bf16[2,64,256]{2,1,0:T(8,128)(2,1)S(1)} %get-tuple-element.41), channel_id=1, source_target_pairs={{1,2},{2,1},{3,4},{4,3},{5,6},{6,5},{7,8},{8,7},{9,10},{10,9},{11,... | collective-permute-start | bytes 196616 | tf_op jit(solution)/shard_map/ppermute | solution.py:388
  60.6 3.5 %collective-permute-done.14.refs_8_ = bf16[2,64,256]{2,1,0:T(8,128)(2,1)S(1)} collective-permute-done((bf16[2,64,256]{2,1,0:T(8,128)(2,1)S(1)}, bf16[2,64,256]{2,1,0:T(8,128)(2,1)S(1)}, u32[]{:S(2)}, u32[]{:S(2)}) %collective-permute-start.14) | collective-permute-done | bytes 65568 | tf_op jit(solution)/shard_map/ppermute | solution.py:388
  64.1 0.2 collective-permute-start.15
  64.3 0.6 shard_map.64
  64.9 0.4 collective-permute-done.15.refs_11_
  65.4 6.7 %shard_map.67 = (bf16[8,64,256]{2,1,0:T(8,128)(2,1)S(1)}, bf16[8,64,256]{2,1,0:T(8,128)(2,1)S(1)}, bf16[2,64,256]{2,1,0:T(8,128)(2,1)}, bf16[2,64,256]{2,1,0:T(8,128)(2,1)}) custom-call(s32[3,5]{1,0:T(4,128)S(1)} %reshape.94.flags, bf16[8,256,256]{2,1,0:T(8,128)(2,1)S(1)} %get-tuple-element.34.cols, f32[64,256]{1,0:T(8,128)S(1)} %get-tuple-element.35.table, ...), custom_call_target="tpu_custom_call" | custom-call | flops 3000000000 | bytes 4000000 | tf_op jit(solution)/shard_map/pallas_call | solution.py:302
  72.1 0.2 collective-permute-start.17
  72.3 4.5 %collective-permute-start.16 = (bf16[8,64,256]{2,1,0:T(8,128)(2,1)S(1)}, bf16[8,64,256]{2,1,0:T(8,128)(2,1)S(1)}, u32[]{:S(2)}, u32[]{:S(2)}) collective-permute-start(bf16[8,64,256]{2,1,0:T(8,128)(2,1)S(1)} %get-tuple-element.43.refs_0_.refs_1_.edge), channel_id=1, source_target_pairs={{1,2},{2,1},{3,4},{4,3},{5,6},{6,5},{7,8},{8,7},{9,10},{10,9},{11,... | collective-permute-start | bytes 786440 | tf_op jit(solution)/shard_map/ppermute | solution.py:388
  76.9 4.0 %collective-permute-start.18 = (bf16[2,2,4,32]{3,2,1,0:T(4,128)(2,1)S(1)}, bf16[2,2,4,32]{3,2,1,0:T(4,128)(2,1)S(1)}, u32[]{:S(2)}, u32[]{:S(2)}) collective-permute-start(bf16[2,2,4,32]{3,2,1,0:T(4,128)(2,1)S(1)} %get-tuple-element.45), channel_id=1, source_target_pairs={{0,112},{1,113},{2,114},{3,115},{4,116},{5,117},{6,118},{7,119},{8... | collective-permute-start | bytes 3080 | tf_op jit(solution)/shard_map/ppermute | solution.py:388
  80.9 2.3 %collective-permute-done.18 = bf16[2,2,4,32]{3,2,1,0:T(4,128)(2,1)S(1)} collective-permute-done((bf16[2,2,4,32]{3,2,1,0:T(4,128)(2,1)S(1)}, bf16[2,2,4,32]{3,2,1,0:T(4,128)(2,1)S(1)}, u32[]{:S(2)}, u32[]{:S(2)}) %collective-permute-start.18) | collective-permute-done | bytes 1056 | tf_op jit(solution)/shard_map/ppermute | solution.py:388
  83.1 4.7 %collective-permute-done.19 = bf16[2,2,4,32]{3,2,1,0:T(4,128)(2,1)S(1)} collective-permute-done((bf16[2,2,4,32]{3,2,1,0:T(4,128)(2,1)S(1)}, bf16[2,2,4,32]{3,2,1,0:T(4,128)(2,1)S(1)}, u32[]{:S(2)}, u32[]{:S(2)}) %collective-permute-start.19) | collective-permute-done | bytes 1056 | tf_op jit(solution)/shard_map/ppermute | solution.py:388
  87.8 0.6 shard_map.68
  88.4 1.9 %shard_map.69 = (bf16[10,64,256]{2,1,0:T(8,128)(2,1)S(1)}, bf16[10,64,256]{2,1,0:T(8,128)(2,1)S(1)}) custom-call(s32[3,5]{1,0:T(4,128)S(1)} %reshape.94.flags, bf16[8,256,256]{2,1,0:T(8,128)(2,1)S(1)} %get-tuple-element.47.cols, f32[64,256]{1,0:T(8,128)S(1)} %get-tuple-element.48.table, bf16[8,64,256]{2,1,0:T(8,128)(2,1)S(1)} %get-tuple-element.43.refs_0_.refs_1_.edge, ...), custom_call_target="tpu_custom_call" | custom-call | flops 800000000 | bytes 4000000 | tf_op jit(solution)/shard_map/pallas_call | solution.py:302
  90.3 0.1 collective-permute-start.20
  90.4 4.1 %collective-permute-start.21 = (bf16[10,64,256]{2,1,0:T(8,128)(2,1)S(1)}, bf16[10,64,256]{2,1,0:T(8,128)(2,1)S(1)}, u32[]{:S(2)}, u32[]{:S(2)}) collective-permute-start(bf16[10,64,256]{2,1,0:T(8,128)(2,1)S(1)} %get-tuple-element.50), channel_id=1, source_target_pairs={{0,112},{1,113},{2,114},{3,115},{4,116},{5,117},{6,118},{7,119},{8... | collective-permute-start | bytes 983048 | tf_op jit(solution)/shard_map/ppermute | solution.py:388
  94.5 1.9 %shard_map.71 = (bf16[10,64,256]{2,1,0:T(8,128)(2,1)S(1)}, bf16[10,64,256]{2,1,0:T(8,128)(2,1)S(1)}) custom-call(s32[3,5]{1,0:T(4,128)S(1)} %reshape.94.flags, bf16[8,256,256]{2,1,0:T(8,128)(2,1)S(1)} %get-tuple-element.47.cols, f32[64,256]{1,0:T(8,128)S(1)} %get-tuple-element.48.table, bf16[8,64,256]{2,1,0:T(8,128)(2,1)S(1)} %collective-permute-done.16.refs_0_.outer, ...), custom_call_target="tpu_custom_call" | custom-call | flops 800000000 | bytes 4000000 | tf_op jit(solution)/shard_map/pallas_call | solution.py:302
  96.4 0.1 collective-permute-start.22
  96.5 4.1 %collective-permute-start.23 = (bf16[10,64,256]{2,1,0:T(8,128)(2,1)S(1)}, bf16[10,64,256]{2,1,0:T(8,128)(2,1)S(1)}, u32[]{:S(2)}, u32[]{:S(2)}) collective-permute-start(bf16[10,64,256]{2,1,0:T(8,128)(2,1)S(1)} %get-tuple-element.54), channel_id=1, source_target_pairs={{0,112},{1,113},{2,114},{3,115},{4,116},{5,117},{6,118},{7,119},{8... | collective-permute-start | bytes 983048 | tf_op jit(solution)/shard_map/ppermute | solution.py:388
  100.7 2.4 %collective-permute-done.20.earlier.inner_earlier = bf16[10,64,256]{2,1,0:T(8,128)(2,1)S(1)} collective-permute-done((bf16[10,64,256]{2,1,0:T(8,128)(2,1)S(1)}, bf16[10,64,256]{2,1,0:T(8,128)(2,1)S(1)}, u32[]{:S(2)}, u32[]{:S(2)}) %collective-permute-start.20) | collective-permute-done | bytes 327712 | tf_op jit(solution)/shard_map/ppermute | solution.py:388
  103.1 2.2 %shard_map.70 = (bf16[8,64,256]{2,1,0:T(8,128)(2,1)S(1)}, bf16[6,64,256]{2,1,0:T(8,128)(2,1)S(1)}) custom-call(s32[3,5]{1,0:T(4,128)S(1)} %reshape.94.flags, bf16[192,576]{1,0:T(8,128)(2,1)S(1)} %reshape.92.wu, bf16[192,192]{1,0:T(8,128)(2,1)S(1)} %reshape.93.wm, bf16[8,64,256]{2,1,0:T(8,128)(2,1)S(1)} %get-tuple-element.44.refs_1_.inner.refs_2_, ...), custom_call_target="tpu_custom_call" | custom-call | flops 600000000 | bytes 4000000 | tf_op jit(solution)/shard_map/pallas_call | solution.py:302
  105.3 3.4 %collective-permute-done.22.earlier = bf16[10,64,256]{2,1,0:T(8,128)(2,1)S(1)} collective-permute-done((bf16[10,64,256]{2,1,0:T(8,128)(2,1)S(1)}, bf16[10,64,256]{2,1,0:T(8,128)(2,1)S(1)}, u32[]{:S(2)}, u32[]{:S(2)}) %collective-permute-start.22) | collective-permute-done | bytes 327712 | tf_op jit(solution)/shard_map/ppermute | solution.py:388
  108.8 3.6 %shard_map.72 = bf16[16,64,256]{2,1,0:T(8,128)(2,1)} custom-call(s32[3,5]{1,0:T(4,128)S(1)} %reshape.94.flags, bf16[192,576]{1,0:T(8,128)(2,1)S(1)} %reshape.92.wu, bf16[192,192]{1,0:T(8,128)(2,1)S(1)} %reshape.93.wm, bf16[8,64,256]{2,1,0:T(8,128)(2,1)S(1)} %collective-permute-done.16.refs_0_.outer, ...), custom_call_target="tpu_custom_call" | custom-call | flops 900000000 | bytes 4000000 | tf_op jit(solution)/shard_map/pallas_call | solution.py:302
  (33 shorter events, 0.2 us)
Async XLA Ops:
  0.0 5.4 %copy-start.3 = (s32[3,4,1,2,32]{4,3,2,1,0:T(2,128)S(1)}, s32[3,4,1,2,32]{4,3,2,1,0:T(2,128)}, u32[]{:S(2)}) copy-start(s32[3,4,1,2,32]{4,3,2,1,0:T(2,128)} %param.8) | copy-start | bytes 9220
  1.1 4.3 %copy-start.2 = (s32[3,4,1,2,32]{4,3,2,1,0:T(2,128)S(1)}, s32[3,4,1,2,32]{4,3,2,1,0:T(2,128)}, u32[]{:S(2)}) copy-start(s32[3,4,1,2,32]{4,3,2,1,0:T(2,128)} %param.7) | copy-start | bytes 9220
  1.1 21.5 %collective-permute-start.2 = (bf16[8,64,256]{2,1,0:T(8,128)(2,1)S(1)}, bf16[8,64,256]{2,1,0:T(8,128)(2,1)S(1)}, u32[]{:S(2)}, u32[]{:S(2)}) collective-permute-start(bf16[8,64,256]{2,1,0:T(8,128)(2,1)S(1)} %get-tuple-element.58.refs_5_), channel_id=1, source_target_pairs={{1,66},{2,65},{3,68},{4,67},{5,70},{6,69},{7,72},{8,71},{9,74},{10... | collective-permute-start | bytes 786440 | tf_op jit(solution)/shard_map/ppermute | solution.py:388
  5.1 17.5 %collective-permute-start.3 = (bf16[8,64,256]{2,1,0:T(8,128)(2,1)S(1)}, bf16[8,64,256]{2,1,0:T(8,128)(2,1)S(1)}, u32[]{:S(2)}, u32[]{:S(2)}) collective-permute-start(bf16[8,64,256]{2,1,0:T(8,128)(2,1)S(1)} %get-tuple-element.58.refs_5_), channel_id=1, source_target_pairs={{0,64},{1,65},{2,66},{3,67},{4,68},{5,69},{6,70},{7,71},{8,72},{9,... | collective-permute-start | bytes 786440 | tf_op jit(solution)/shard_map/ppermute | solution.py:388
  6.5 8.5 %copy-start = (bf16[3,3,64,192]{3,2,1,0:T(8,128)(2,1)S(1)}, bf16[3,3,64,192]{3,2,1,0:T(8,128)(2,1)}, u32[]{:S(2)}) copy-start(bf16[3,3,64,192]{3,2,1,0:T(8,128)(2,1)} %param.10) | copy-start | bytes 663556
  6.6 10.0 %collective-permute-start = (bf16[3,64,256]{2,1,0:T(8,128)(2,1)S(1)}, bf16[3,64,256]{2,1,0:T(8,128)(2,1)S(1)}, u32[]{:S(2)}, u32[]{:S(2)}) collective-permute-start(bf16[3,64,256]{2,1,0:T(8,128)(2,1)S(1)} %pad_maximum_fusion), channel_id=1, source_target_pairs={{0,1},{1,0},{2,3},{3,2},{4,5},{5,4},{6,7},{7,6},{8,9},{9,8},{10,11... | collective-permute-start | bytes 294920 | tf_op jit(solution)/shard_map/ppermute | solution.py:388
  7.4 9.4 %collective-permute-start.1 = (bf16[3,64,256]{2,1,0:T(8,128)(2,1)S(1)}, bf16[3,64,256]{2,1,0:T(8,128)(2,1)S(1)}, u32[]{:S(2)}, u32[]{:S(2)}) collective-permute-start(bf16[3,64,256]{2,1,0:T(8,128)(2,1)S(1)} %pad_maximum_fusion.1), channel_id=1, source_target_pairs={{1,2},{2,1},{3,4},{4,3},{5,6},{6,5},{7,8},{8,7},{9,10},{10,9},{11,... | collective-permute-start | bytes 294920 | tf_op jit(solution)/shard_map/ppermute | solution.py:388
  11.4 10.5 %collective-permute-start.4 = (bf16[8,64,256]{2,1,0:T(8,128)(2,1)S(1)}, bf16[8,64,256]{2,1,0:T(8,128)(2,1)S(1)}, u32[]{:S(2)}, u32[]{:S(2)}) collective-permute-start(bf16[8,64,256]{2,1,0:T(8,128)(2,1)S(1)} %get-tuple-element.57.refs_6_), channel_id=1, source_target_pairs={{0,64},{1,65},{2,66},{3,67},{4,68},{5,69},{6,70},{7,71},{8,72},{9,... | collective-permute-start | bytes 786440 | tf_op jit(solution)/shard_map/ppermute | solution.py:388
  11.8 0.7 copy-start.4
  15.3 0.9 copy-start.1
  21.9 1.5 %collective-permute-start.5 = (bf16[8,64,256]{2,1,0:T(8,128)(2,1)S(1)}, bf16[8,64,256]{2,1,0:T(8,128)(2,1)S(1)}, u32[]{:S(2)}, u32[]{:S(2)}) collective-permute-start(bf16[8,64,256]{2,1,0:T(8,128)(2,1)S(1)} %collective-permute-done.4.refs_2_), channel_id=1, source_target_pairs={{0,1},{1,0},{2,3},{3,2},{4,5},{5,4},{6,7},{7,6},{8,9},{9,8},{10,11... | collective-permute-start | bytes 786440 | tf_op jit(solution)/shard_map/ppermute | solution.py:388
  29.5 11.1 %collective-permute-start.9 = (bf16[8,64,256]{2,1,0:T(8,128)(2,1)S(1)}, bf16[8,64,256]{2,1,0:T(8,128)(2,1)S(1)}, u32[]{:S(2)}, u32[]{:S(2)}) collective-permute-start(bf16[8,64,256]{2,1,0:T(8,128)(2,1)S(1)} %get-tuple-element.40.refs_10_), channel_id=1, source_target_pairs={{0,32},{1,33},{2,34},{3,35},{4,36},{5,37},{6,38},{7,39},{8,40},{9,... | collective-permute-start | bytes 786440 | tf_op jit(solution)/shard_map/ppermute | solution.py:388
  33.4 12.2 %collective-permute-start.6 = (bf16[8,64,256]{2,1,0:T(8,128)(2,1)S(1)}, bf16[8,64,256]{2,1,0:T(8,128)(2,1)S(1)}, u32[]{:S(2)}, u32[]{:S(2)}) collective-permute-start(bf16[8,64,256]{2,1,0:T(8,128)(2,1)S(1)} %get-tuple-element.39.refs_9_), channel_id=1, source_target_pairs={{0,32},{1,33},{2,34},{3,35},{4,36},{5,37},{6,38},{7,39},{8,40},{9,... | collective-permute-start | bytes 786440 | tf_op jit(solution)/shard_map/ppermute | solution.py:388
  40.6 9.3 %collective-permute-start.12 = (bf16[8,64,256]{2,1,0:T(8,128)(2,1)S(1)}, bf16[8,64,256]{2,1,0:T(8,128)(2,1)S(1)}, u32[]{:S(2)}, u32[]{:S(2)}) collective-permute-start(bf16[8,64,256]{2,1,0:T(8,128)(2,1)S(1)} %collective-permute-done.9.refs_2_), channel_id=1, source_target_pairs={{0,64},{1,65},{2,66},{3,67},{4,68},{5,69},{6,70},{7,71},{8,72},{9,... | collective-permute-start | bytes 786440 | tf_op jit(solution)/shard_map/ppermute | solution.py:388
  45.7 7.8 %collective-permute-start.7 = (bf16[8,64,256]{2,1,0:T(8,128)(2,1)S(1)}, bf16[8,64,256]{2,1,0:T(8,128)(2,1)S(1)}, u32[]{:S(2)}, u32[]{:S(2)}) collective-permute-start(bf16[8,64,256]{2,1,0:T(8,128)(2,1)S(1)} %collective-permute-done.6.refs_1_), channel_id=1, source_target_pairs={{0,64},{1,65},{2,66},{3,67},{4,68},{5,69},{6,70},{7,71},{8,72},{9,... | collective-permute-start | bytes 786440 | tf_op jit(solution)/shard_map/ppermute | solution.py:388
  46.3 19.0 %collective-permute-start.10 = (bf16[8,64,256]{2,1,0:T(8,128)(2,1)S(1)}, bf16[8,64,256]{2,1,0:T(8,128)(2,1)S(1)}, u32[]{:S(2)}, u32[]{:S(2)}) collective-permute-start(bf16[8,64,256]{2,1,0:T(8,128)(2,1)S(1)} %collective-permute-done.9.refs_2_), channel_id=1, source_target_pairs={{0,1},{1,0},{2,3},{3,2},{4,5},{5,4},{6,7},{7,6},{8,9},{9,8},{10,11... | collective-permute-start | bytes 786440 | tf_op jit(solution)/shard_map/ppermute | solution.py:388
  46.4 19.0 %collective-permute-start.11 = (bf16[8,64,256]{2,1,0:T(8,128)(2,1)S(1)}, bf16[8,64,256]{2,1,0:T(8,128)(2,1)S(1)}, u32[]{:S(2)}, u32[]{:S(2)}) collective-permute-start(bf16[8,64,256]{2,1,0:T(8,128)(2,1)S(1)} %collective-permute-done.6.refs_1_), channel_id=1, source_target_pairs={{1,66},{2,65},{3,68},{4,67},{5,70},{6,69},{7,72},{8,71},{9,74},{10... | collective-permute-start | bytes 786440 | tf_op jit(solution)/shard_map/ppermute | solution.py:388
  49.9 15.5 %collective-permute-start.13 = (bf16[8,64,256]{2,1,0:T(8,128)(2,1)S(1)}, bf16[8,64,256]{2,1,0:T(8,128)(2,1)S(1)}, u32[]{:S(2)}, u32[]{:S(2)}) collective-permute-start(bf16[8,64,256]{2,1,0:T(8,128)(2,1)S(1)} %collective-permute-done.12.refs_6_), channel_id=1, source_target_pairs={{0,1},{1,0},{2,3},{3,2},{4,5},{5,4},{6,7},{7,6},{8,9},{9,8},{10,11... | collective-permute-start | bytes 786440 | tf_op jit(solution)/shard_map/ppermute | solution.py:388
  53.4 11.9 %collective-permute-start.8 = (bf16[8,64,256]{2,1,0:T(8,128)(2,1)S(1)}, bf16[8,64,256]{2,1,0:T(8,128)(2,1)S(1)}, u32[]{:S(2)}, u32[]{:S(2)}) collective-permute-start(bf16[8,64,256]{2,1,0:T(8,128)(2,1)S(1)} %collective-permute-done.7.refs_5_), channel_id=1, source_target_pairs={{1,66},{2,65},{3,68},{4,67},{5,70},{6,69},{7,72},{8,71},{9,74},{10... | collective-permute-start | bytes 786440 | tf_op jit(solution)/shard_map/ppermute | solution.py:388
  55.4 8.7 %collective-permute-start.14 = (bf16[2,64,256]{2,1,0:T(8,128)(2,1)S(1)}, bf16[2,64,256]{2,1,0:T(8,128)(2,1)S(1)}, u32[]{:S(2)}, u32[]{:S(2)}) collective-permute-start(bf16[2,64,256]{2,1,0:T(8,128)(2,1)S(1)} %get-tuple-element.41), channel_id=1, source_target_pairs={{1,2},{2,1},{3,4},{4,3},{5,6},{6,5},{7,8},{8,7},{9,10},{10,9},{11,... | collective-permute-start | bytes 196616 | tf_op jit(solution)/shard_map/ppermute | solution.py:388
  64.1 1.3 %collective-permute-start.15 = (bf16[2,64,256]{2,1,0:T(8,128)(2,1)S(1)}, bf16[2,64,256]{2,1,0:T(8,128)(2,1)S(1)}, u32[]{:S(2)}, u32[]{:S(2)}) collective-permute-start(bf16[2,64,256]{2,1,0:T(8,128)(2,1)S(1)} %get-tuple-element.42), channel_id=1, source_target_pairs={{0,1},{1,0},{2,3},{3,2},{4,5},{5,4},{6,7},{7,6},{8,9},{9,8},{10,11... | collective-permute-start | bytes 196616 | tf_op jit(solution)/shard_map/ppermute | solution.py:388
  72.1 16.3 %collective-permute-start.17 = (bf16[8,64,256]{2,1,0:T(8,128)(2,1)S(1)}, bf16[8,64,256]{2,1,0:T(8,128)(2,1)S(1)}, u32[]{:S(2)}, u32[]{:S(2)}) collective-permute-start(bf16[8,64,256]{2,1,0:T(8,128)(2,1)S(1)} %get-tuple-element.44.refs_1_.inner.refs_2_), channel_id=1, source_target_pairs={{0,1},{1,0},{2,3},{3,2},{4,5},{5,4},{6,7},{7,6},{8,9},{9,8},{10,11... | collective-permute-start | bytes 786440 | tf_op jit(solution)/shard_map/ppermute | solution.py:388
  72.3 22.2 %collective-permute-start.16 = (bf16[8,64,256]{2,1,0:T(8,128)(2,1)S(1)}, bf16[8,64,256]{2,1,0:T(8,128)(2,1)S(1)}, u32[]{:S(2)}, u32[]{:S(2)}) collective-permute-start(bf16[8,64,256]{2,1,0:T(8,128)(2,1)S(1)} %get-tuple-element.43.refs_0_.refs_1_.edge), channel_id=1, source_target_pairs={{1,2},{2,1},{3,4},{4,3},{5,6},{6,5},{7,8},{8,7},{9,10},{10,9},{11,... | collective-permute-start | bytes 786440 | tf_op jit(solution)/shard_map/ppermute | solution.py:388
  76.9 6.2 %collective-permute-start.18 = (bf16[2,2,4,32]{3,2,1,0:T(4,128)(2,1)S(1)}, bf16[2,2,4,32]{3,2,1,0:T(4,128)(2,1)S(1)}, u32[]{:S(2)}, u32[]{:S(2)}) collective-permute-start(bf16[2,2,4,32]{3,2,1,0:T(4,128)(2,1)S(1)} %get-tuple-element.45), channel_id=1, source_target_pairs={{0,112},{1,113},{2,114},{3,115},{4,116},{5,117},{6,118},{7,119},{8... | collective-permute-start | bytes 3080 | tf_op jit(solution)/shard_map/ppermute | solution.py:388
  80.8 6.9 %collective-permute-start.19 = (bf16[2,2,4,32]{3,2,1,0:T(4,128)(2,1)S(1)}, bf16[2,2,4,32]{3,2,1,0:T(4,128)(2,1)S(1)}, u32[]{:S(2)}, u32[]{:S(2)}) collective-permute-start(bf16[2,2,4,32]{3,2,1,0:T(4,128)(2,1)S(1)} %get-tuple-element.46), channel_id=1, source_target_pairs={{0,16},{1,17},{2,18},{3,19},{4,20},{5,21},{6,22},{7,23},{8,24},{9,... | collective-permute-start | bytes 3080 | tf_op jit(solution)/shard_map/ppermute | solution.py:388
  90.3 12.8 %collective-permute-start.20 = (bf16[10,64,256]{2,1,0:T(8,128)(2,1)S(1)}, bf16[10,64,256]{2,1,0:T(8,128)(2,1)S(1)}, u32[]{:S(2)}, u32[]{:S(2)}) collective-permute-start(bf16[10,64,256]{2,1,0:T(8,128)(2,1)S(1)} %get-tuple-element.49), channel_id=1, source_target_pairs={{0,16},{1,17},{2,18},{3,19},{4,20},{5,21},{6,22},{7,23},{8,24},{9,... | collective-permute-start | bytes 983048 | tf_op jit(solution)/shard_map/ppermute | solution.py:388
  90.4 12.7 %collective-permute-start.21 = (bf16[10,64,256]{2,1,0:T(8,128)(2,1)S(1)}, bf16[10,64,256]{2,1,0:T(8,128)(2,1)S(1)}, u32[]{:S(2)}, u32[]{:S(2)}) collective-permute-start(bf16[10,64,256]{2,1,0:T(8,128)(2,1)S(1)} %get-tuple-element.50), channel_id=1, source_target_pairs={{0,112},{1,113},{2,114},{3,115},{4,116},{5,117},{6,118},{7,119},{8... | collective-permute-start | bytes 983048 | tf_op jit(solution)/shard_map/ppermute | solution.py:388
  96.4 12.3 %collective-permute-start.22 = (bf16[10,64,256]{2,1,0:T(8,128)(2,1)S(1)}, bf16[10,64,256]{2,1,0:T(8,128)(2,1)S(1)}, u32[]{:S(2)}, u32[]{:S(2)}) collective-permute-start(bf16[10,64,256]{2,1,0:T(8,128)(2,1)S(1)} %get-tuple-element.53), channel_id=1, source_target_pairs={{0,16},{1,17},{2,18},{3,19},{4,20},{5,21},{6,22},{7,23},{8,24},{9,... | collective-permute-start | bytes 983048 | tf_op jit(solution)/shard_map/ppermute | solution.py:388
  96.5 12.2 %collective-permute-start.23 = (bf16[10,64,256]{2,1,0:T(8,128)(2,1)S(1)}, bf16[10,64,256]{2,1,0:T(8,128)(2,1)S(1)}, u32[]{:S(2)}, u32[]{:S(2)}) collective-permute-start(bf16[10,64,256]{2,1,0:T(8,128)(2,1)S(1)} %get-tuple-element.54), channel_id=1, source_target_pairs={{0,112},{1,113},{2,114},{3,115},{4,116},{5,117},{6,118},{7,119},{8... | collective-permute-start | bytes 983048 | tf_op jit(solution)/shard_map/ppermute | solution.py:388

commit v8 on v7

--- a/solution.py
+++ b/solution.py
@@ -35,10 +35,19 @@
     return place + turned * (size - 2 * place)
 
 
-def columns_kernel(vals, cols, table):
+def columns_kernel(first, second, cols, table, vals):
+    vals[...] = jnp.zeros_like(vals)
+    for ref, entries in enumerate((first, second)):
+        for k in range(4):
+            rows = entries[k // 2, k % 2].astype(F32)
+            for block in range(4):
+                at = (ref * 4 + block) * 8 + k
+                vals[at : at + 1, :] = rows[block : block + 1]
     block_of = lax.broadcasted_iota(jnp.int32, (32, WIDTH), 1) // 8
     spread = (block_of == lax.broadcasted_iota(jnp.int32, (32, WIDTH), 0)).astype(F32)
-    table[...] = jnp.dot(vals[...], spread.astype(BF16), preferred_element_type=F32)
+    table[...] = jnp.dot(
+        vals[...].astype(BF16), spread.astype(BF16), preferred_element_type=F32
+    )
     apart = lax.broadcasted_iota(jnp.int32, (WIDTH, WIDTH), 0) - lax.broadcasted_iota(
         jnp.int32, (WIDTH, WIDTH), 1
     )
@@ -51,23 +60,23 @@
         cols[n] = jnp.where(off == 0, 1.0 - fx, jnp.where(off == 1, fx, 0.0)).astype(BF16)
 
 
-def make_columns(vals, interpret=False):
-    count = vals.shape[0] // 8
+def make_columns(first, second, interpret=False):
     vmem = pl.BlockSpec(memory_space=pltpu.VMEM)
     return pl.pallas_call(
         columns_kernel,
         out_shape=(
-            jax.ShapeDtypeStruct((count, WIDTH, WIDTH), BF16),
-            jax.ShapeDtypeStruct((count * 8, WIDTH), F32),
+            jax.ShapeDtypeStruct((8, WIDTH, WIDTH), BF16),
+            jax.ShapeDtypeStruct((64, WIDTH), F32),
         ),
-        in_specs=[vmem],
+        in_specs=[vmem, vmem],
         out_specs=(vmem, vmem),
+        scratch_shapes=[pltpu.VMEM((64, 32), F32)],
         compiler_params=pltpu.CompilerParams(vmem_limit_bytes=VMEM_LIMIT),
         cost_estimate=pl.CostEstimate(
             flops=100_000_000, bytes_accessed=3_000_000, transcendentals=0
         ),
         interpret=interpret,
-    )(vals)
+    )(first, second)
 
 
 def column_pass(buffer, window, matrix):
@@ -396,12 +405,6 @@
     return r ^ 1
 
 
-def level_values(t):
-    t = t.reshape(2, 2, 2, 4, 32)
-    t = jnp.transpose(t, (1, 3, 0, 2, 4)).reshape(2, 4, 4, 32)
-    return jnp.pad(t, ((0, 0), (0, 0), (0, 4), (0, 0))).reshape(64, 32)
-
-
 def tap_weights(w):
     o, j = w.shape[2], w.shape[3]
     return jnp.transpose(w, (1, 2, 0, 3)).reshape(3 * o, 3 * j)
@@ -463,20 +466,11 @@
         ],
         axis=3,
     )
-    values, later_values, ahead_entries, back_entries, wu, wm, flags = (
-        lax.optimization_barrier(
-            (
-                level_values(packed[:, 2]),
-                level_values(packed[:, 1]),
-                packed[:, 0, 0:2],
-                packed[:, 0, 2:4],
-                wu,
-                wm,
-                flags,
-            )
-        )
-    )
-    cols, table = make_columns(values)
+    *entries, wu, wm, flags = lax.optimization_barrier(
+        tuple(packed[:, k, j : j + 2] for k in (2, 1, 0) for j in (0, 2))
+        + (wu, wm, flags)
+    )
+    cols, table = make_columns(entries[0], entries[1])
     edge, inner, rim, near = run_level(
         2, flags, cols, table, wu, wm, [(h, e, i, n)], (own_outer, edge, inner, own_near)
     )
@@ -490,10 +484,11 @@
     h = send(xe, to_other, off_chip)
     xi = send(i, to_other)
     n = send(i, row_to=on_chip)
-    for_ahead = send(ahead_entries, back)
-    for_back = send(back_entries, ahead)
+    for_ahead = send(entries[4], back)
+    for_back = send(entries[5], ahead)
     xn = send(xi, row_to=on_chip)
-    cols, table = make_columns(later_values)
+    cols, table = make_columns(entries[2], entries[3])
+    next_cols, next_table = make_columns(for_ahead, for_back)
     edge, inner, _, _ = run_level(
         1,
         flags,
@@ -507,18 +502,13 @@
 
     outer = send(edge, row_to=off_chip)
     near = send(inner, row_to=on_chip)
-    cols, table = make_columns(
-        level_values(jnp.concatenate([for_ahead, for_back], axis=1))
-    )
-    halves = run_warp_half(False, flags, cols, table, (edge, inner, near))
+    halves = run_warp_half(False, flags, next_cols, next_table, (edge, inner, near))
     inner_earlier = send(halves[0], ahead)
     inner_later = send(halves[1], back)
-    halves = run_warp_half(True, flags, cols, table, (outer, edge, inner))
+    halves = run_warp_half(True, flags, next_cols, next_table, (outer, edge, inner))
     earlier = send(halves[0], ahead)
     later = send(halves[1], back)
-    inner_act, inner_rows = run_last_inner(
-        flags, wu, wm, (inner, near, inner_earlier, inner_later)
-    )
+    inner_act, inner_rows = run_last_inner(flags, wu, wm, (inner, near, inner_earlier, inner_later))
     refined = run_last_outer(
         flags,
         wu,

time: 113 us -> 113 us (level)
  no operation moved by 1% of the time
where the time goes in v8:
time: 113 us; the launch traced here: 112 us
  starting transfers between devices  43.1 us (38%)
  waiting for transfers between devices  38 us (34%)
  Pallas kernels  24.1 us (21%)
  local copies, waits for them, and re-layouts  6.53 us (6%)
    ppermute x24, starting transfers between devices, send(): return lax.ppermute(x, ('tm', 'rows'), route)  43.1 us
    ppermute x24, waiting for transfers between devices, send(): return lax.ppermute(x, ('tm', 'rows'), route)  38 us
    pallas_call x6, Pallas kernels, on_core(): pl.pallas_call(kernel, out_shape=out_shape, in_specs=[pl.BlockSpec(memory...  22.4 us
  transfers between devices with their start and end apart: 24, of which 12 were waited for; matrix products, arithmetic and copies ran while one was open for 4% of the time, Pallas kernels for 7%

profile of v8, /device:TPU:8, one launch (start us, length us, event | category | flops | bytes accessed | tf_op | source)
XLA Modules:
  0.0 112.3 jit_solution(2064511184773189010)
XLA Ops:
  0.0 1.1 dynamic-slice_bitcast_fusion
  1.1 0.0 copy-start.2
  1.1 4.0 %collective-permute-start.2 = (bf16[8,64,256]{2,1,0:T(8,128)(2,1)S(1)}, bf16[8,64,256]{2,1,0:T(8,128)(2,1)S(1)}, u32[]{:S(2)}, u32[]{:S(2)}) collective-permute-start(bf16[8,64,256]{2,1,0:T(8,128)(2,1)S(1)} %get-tuple-element.62.refs_5_), channel_id=1, source_target_pairs={{1,66},{2,65},{3,68},{4,67},{5,70},{6,69},{7,72},{8,71},{9,74},{10... | collective-permute-start | bytes 786440 | tf_op jit(solution)/shard_map/ppermute | solution.py:397
  5.1 0.3 collective-permute-start.3
  5.5 0.1 select_n.82
  5.6 0.9 dynamic-slice_bitcast_fusion.3
  6.5 0.0 copy-start
  6.5 0.7 collective-permute-start
  7.2 0.1 select_n.85
  7.4 0.0 copy-start.4
  7.4 4.0 %collective-permute-start.1 = (bf16[3,64,256]{2,1,0:T(8,128)(2,1)S(1)}, bf16[3,64,256]{2,1,0:T(8,128)(2,1)S(1)}, u32[]{:S(2)}, u32[]{:S(2)}) collective-permute-start(bf16[3,64,256]{2,1,0:T(8,128)(2,1)S(1)} %pad_maximum_fusion.1), channel_id=1, source_target_pairs={{1,2},{2,1},{3,4},{4,3},{5,6},{6,5},{7,8},{8,7},{9,10},{10,9},{11,... | collective-permute-start | bytes 294920 | tf_op jit(solution)/shard_map/ppermute | solution.py:397
  11.4 0.4 collective-permute-start.4
  11.8 0.6 fusion.2
  12.4 1.9 %stack.44 = s32[15]{0:T(128)S(1)} concatenate(s32[1]{0:T(128)} %bitcast.16, s32[1]{0:T(128)} %bitcast.17, s32[1]{0:T(128)} %bitcast.18, s32[1]{0:T(128)} %bitcast.19, s32[1]{0:T(128)} %bitcast.20, s32[1]{0:T(128)} %bitcast.16, s32[1]{0:T(128)} %bitcast.17, s32[1]{0:T(128)} %bitcast.18, s32[1]{0:T(128)} %bitcast.21, s32[1]{0:T(128)} %bitcast.20, s32[1]{0:T(128)} %bitcast.16, ...), dimensions={0} | concatenate | bytes 120 | tf_op jit(solution)/shard_map/stack | solution.py:434
  14.4 0.1 reshape.69.flags
  14.5 0.3 copy.17
  14.7 0.0 copy-start.1
  14.7 0.3 reshape.67.wu
  15.0 0.6 copy-done.1
  15.6 0.1 copy.18
  15.8 0.2 reshape.68.wm
  15.9 0.0 collective-permute-done.refs_7_
  15.9 0.8 collective-permute-done.1.refs_4_
  16.7 0.1 select_n.87
  16.8 0.1 select_n.89
  16.9 5.0 %collective-permute-done.4.refs_2_ = bf16[8,64,256]{2,1,0:T(8,128)(2,1)S(1)} collective-permute-done((bf16[8,64,256]{2,1,0:T(8,128)(2,1)S(1)}, bf16[8,64,256]{2,1,0:T(8,128)(2,1)S(1)}, u32[]{:S(2)}, u32[]{:S(2)}) %collective-permute-start.4) | collective-permute-done | bytes 262176 | tf_op jit(solution)/shard_map/ppermute | solution.py:397
  21.9 0.0 collective-permute-start.5
  21.9 0.1 pad_maximum_fusion.2
  22.0 0.6 shard_map.65
  22.6 0.0 collective-permute-done.3.refs_1_
  22.6 0.8 collective-permute-done.5.refs_3_
  23.4 6.0 %shard_map.66 = (bf16[8,64,256]{2,1,0:T(8,128)(2,1)S(1)}, bf16[8,64,256]{2,1,0:T(8,128)(2,1)S(1)}, bf16[2,64,256]{2,1,0:T(8,128)(2,1)S(1)}, bf16[2,64,256]{2,1,0:T(8,128)(2,1)S(1)}) custom-call(s32[3,5]{1,0:T(4,128)S(1)} %reshape.69.flags, bf16[8,256,256]{2,1,0:T(8,128)(2,1)S(1)} %get-tuple-element.41.cols, f32[64,256]{1,0:T(8,128)S(1)} %get-tuple-element.42.table, ...), custom_call_target="tpu_custom_call" | custom-call | flops 3000000000 | bytes 4000000 | tf_op jit(solution)/shard_map/pallas_call | solution.py:311
  29.5 4.0 %collective-permute-start.9 = (bf16[8,64,256]{2,1,0:T(8,128)(2,1)S(1)}, bf16[8,64,256]{2,1,0:T(8,128)(2,1)S(1)}, u32[]{:S(2)}, u32[]{:S(2)}) collective-permute-start(bf16[8,64,256]{2,1,0:T(8,128)(2,1)S(1)} %get-tuple-element.44.refs_10_), channel_id=1, source_target_pairs={{0,32},{1,33},{2,34},{3,35},{4,36},{5,37},{6,38},{7,39},{8,40},{9,... | collective-permute-start | bytes 786440 | tf_op jit(solution)/shard_map/ppermute | solution.py:397
  33.4 0.1 collective-permute-start.6
  33.5 7.1 %collective-permute-done.9.refs_2_ = bf16[8,64,256]{2,1,0:T(8,128)(2,1)S(1)} collective-permute-done((bf16[8,64,256]{2,1,0:T(8,128)(2,1)S(1)}, bf16[8,64,256]{2,1,0:T(8,128)(2,1)S(1)}, u32[]{:S(2)}, u32[]{:S(2)}) %collective-permute-start.9) | collective-permute-done | bytes 262176 | tf_op jit(solution)/shard_map/ppermute | solution.py:397
  40.6 0.7 collective-permute-start.12
  41.3 4.4 %collective-permute-done.6.refs_1_ = bf16[8,64,256]{2,1,0:T(8,128)(2,1)S(1)} collective-permute-done((bf16[8,64,256]{2,1,0:T(8,128)(2,1)S(1)}, bf16[8,64,256]{2,1,0:T(8,128)(2,1)S(1)}, u32[]{:S(2)}, u32[]{:S(2)}) %collective-permute-start.6) | collective-permute-done | bytes 262176 | tf_op jit(solution)/shard_map/ppermute | solution.py:397
  45.7 0.7 collective-permute-start.7
  46.4 3.5 %collective-permute-start.11 = (bf16[8,64,256]{2,1,0:T(8,128)(2,1)S(1)}, bf16[8,64,256]{2,1,0:T(8,128)(2,1)S(1)}, u32[]{:S(2)}, u32[]{:S(2)}) collective-permute-start(bf16[8,64,256]{2,1,0:T(8,128)(2,1)S(1)} %collective-permute-done.6.refs_1_), channel_id=1, source_target_pairs={{1,66},{2,65},{3,68},{4,67},{5,70},{6,69},{7,72},{8,71},{9,74},{10... | collective-permute-start | bytes 786440 | tf_op jit(solution)/shard_map/ppermute | solution.py:397
  49.9 0.2 collective-permute-start.13
  50.1 3.3 %collective-permute-done.7.refs_5_ = bf16[8,64,256]{2,1,0:T(8,128)(2,1)S(1)} collective-permute-done((bf16[8,64,256]{2,1,0:T(8,128)(2,1)S(1)}, bf16[8,64,256]{2,1,0:T(8,128)(2,1)S(1)}, u32[]{:S(2)}, u32[]{:S(2)}) %collective-permute-start.7) | collective-permute-done | bytes 262176 | tf_op jit(solution)/shard_map/ppermute | solution.py:397
  53.4 1.9 %collective-permute-start.8 = (bf16[8,64,256]{2,1,0:T(8,128)(2,1)S(1)}, bf16[8,64,256]{2,1,0:T(8,128)(2,1)S(1)}, u32[]{:S(2)}, u32[]{:S(2)}) collective-permute-start(bf16[8,64,256]{2,1,0:T(8,128)(2,1)S(1)} %collective-permute-done.7.refs_5_), channel_id=1, source_target_pairs={{1,66},{2,65},{3,68},{4,67},{5,70},{6,69},{7,72},{8,71},{9,74},{10... | collective-permute-start | bytes 786440 | tf_op jit(solution)/shard_map/ppermute | solution.py:397
  55.4 5.3 %collective-permute-start.14 = (bf16[2,64,256]{2,1,0:T(8,128)(2,1)S(1)}, bf16[2,64,256]{2,1,0:T(8,128)(2,1)S(1)}, u32[]{:S(2)}, u32[]{:S(2)}) collective-permute-start(bf16[2,64,256]{2,1,0:T(8,128)(2,1)S(1)} %get-tuple-element.45), channel_id=1, source_target_pairs={{1,2},{2,1},{3,4},{4,3},{5,6},{6,5},{7,8},{8,7},{9,10},{10,9},{11,... | collective-permute-start | bytes 196616 | tf_op jit(solution)/shard_map/ppermute | solution.py:397
  60.6 3.4 %collective-permute-done.14.refs_8_ = bf16[2,64,256]{2,1,0:T(8,128)(2,1)S(1)} collective-permute-done((bf16[2,64,256]{2,1,0:T(8,128)(2,1)S(1)}, bf16[2,64,256]{2,1,0:T(8,128)(2,1)S(1)}, u32[]{:S(2)}, u32[]{:S(2)}) %collective-permute-start.14) | collective-permute-done | bytes 65568 | tf_op jit(solution)/shard_map/ppermute | solution.py:397
  64.1 0.3 collective-permute-start.15
  64.3 0.6 shard_map.64
  64.9 0.4 collective-permute-done.15.refs_11_
  65.3 6.7 %shard_map.67 = (bf16[8,64,256]{2,1,0:T(8,128)(2,1)S(1)}, bf16[8,64,256]{2,1,0:T(8,128)(2,1)S(1)}, bf16[2,64,256]{2,1,0:T(8,128)(2,1)}, bf16[2,64,256]{2,1,0:T(8,128)(2,1)}) custom-call(s32[3,5]{1,0:T(4,128)S(1)} %reshape.69.flags, bf16[8,256,256]{2,1,0:T(8,128)(2,1)S(1)} %get-tuple-element.37.cols, f32[64,256]{1,0:T(8,128)S(1)} %get-tuple-element.38.table, ...), custom_call_target="tpu_custom_call" | custom-call | flops 3000000000 | bytes 4000000 | tf_op jit(solution)/shard_map/pallas_call | solution.py:311
  72.1 0.3 collective-permute-start.17
  72.3 4.5 %collective-permute-start.16 = (bf16[8,64,256]{2,1,0:T(8,128)(2,1)S(1)}, bf16[8,64,256]{2,1,0:T(8,128)(2,1)S(1)}, u32[]{:S(2)}, u32[]{:S(2)}) collective-permute-start(bf16[8,64,256]{2,1,0:T(8,128)(2,1)S(1)} %get-tuple-element.47.refs_0_.refs_1_.edge), channel_id=1, source_target_pairs={{1,2},{2,1},{3,4},{4,3},{5,6},{6,5},{7,8},{8,7},{9,10},{10,9},{11,... | collective-permute-start | bytes 786440 | tf_op jit(solution)/shard_map/ppermute | solution.py:397
  76.9 4.0 %collective-permute-start.18 = (bf16[2,2,4,32]{3,2,1,0:T(4,128)(2,1)S(1)}, bf16[2,2,4,32]{3,2,1,0:T(4,128)(2,1)S(1)}, u32[]{:S(2)}, u32[]{:S(2)}) collective-permute-start(bf16[2,2,4,32]{3,2,1,0:T(4,128)(2,1)S(1)} %get-tuple-element.49), channel_id=1, source_target_pairs={{0,112},{1,113},{2,114},{3,115},{4,116},{5,117},{6,118},{7,119},{8... | collective-permute-start | bytes 3080 | tf_op jit(solution)/shard_map/ppermute | solution.py:397
  80.8 2.3 %collective-permute-done.18.first = bf16[2,2,4,32]{3,2,1,0:T(4,128)(2,1)S(1)} collective-permute-done((bf16[2,2,4,32]{3,2,1,0:T(4,128)(2,1)S(1)}, bf16[2,2,4,32]{3,2,1,0:T(4,128)(2,1)S(1)}, u32[]{:S(2)}, u32[]{:S(2)}) %collective-permute-start.18) | collective-permute-done | bytes 1056 | tf_op jit(solution)/shard_map/ppermute | solution.py:397
  83.1 4.7 %collective-permute-done.19.second = bf16[2,2,4,32]{3,2,1,0:T(4,128)(2,1)S(1)} collective-permute-done((bf16[2,2,4,32]{3,2,1,0:T(4,128)(2,1)S(1)}, bf16[2,2,4,32]{3,2,1,0:T(4,128)(2,1)S(1)}, u32[]{:S(2)}, u32[]{:S(2)}) %collective-permute-start.19) | collective-permute-done | bytes 1056 | tf_op jit(solution)/shard_map/ppermute | solution.py:397
  87.8 0.6 shard_map.68
  88.4 1.9 %shard_map.69 = (bf16[10,64,256]{2,1,0:T(8,128)(2,1)S(1)}, bf16[10,64,256]{2,1,0:T(8,128)(2,1)S(1)}) custom-call(s32[3,5]{1,0:T(4,128)S(1)} %reshape.69.flags, bf16[8,256,256]{2,1,0:T(8,128)(2,1)S(1)} %get-tuple-element.51.cols, f32[64,256]{1,0:T(8,128)S(1)} %get-tuple-element.52.table, bf16[8,64,256]{2,1,0:T(8,128)(2,1)S(1)} %get-tuple-element.47.refs_0_.refs_1_.edge, ...), custom_call_target="tpu_custom_call" | custom-call | flops 800000000 | bytes 4000000 | tf_op jit(solution)/shard_map/pallas_call | solution.py:311
  90.3 0.1 collective-permute-start.20
  90.4 4.1 %collective-permute-start.21 = (bf16[10,64,256]{2,1,0:T(8,128)(2,1)S(1)}, bf16[10,64,256]{2,1,0:T(8,128)(2,1)S(1)}, u32[]{:S(2)}, u32[]{:S(2)}) collective-permute-start(bf16[10,64,256]{2,1,0:T(8,128)(2,1)S(1)} %get-tuple-element.54), channel_id=1, source_target_pairs={{0,112},{1,113},{2,114},{3,115},{4,116},{5,117},{6,118},{7,119},{8... | collective-permute-start | bytes 983048 | tf_op jit(solution)/shard_map/ppermute | solution.py:397
  94.5 1.9 %shard_map.71 = (bf16[10,64,256]{2,1,0:T(8,128)(2,1)S(1)}, bf16[10,64,256]{2,1,0:T(8,128)(2,1)S(1)}) custom-call(s32[3,5]{1,0:T(4,128)S(1)} %reshape.69.flags, bf16[8,256,256]{2,1,0:T(8,128)(2,1)S(1)} %get-tuple-element.51.cols, f32[64,256]{1,0:T(8,128)S(1)} %get-tuple-element.52.table, bf16[8,64,256]{2,1,0:T(8,128)(2,1)S(1)} %collective-permute-done.16.refs_0_.outer, ...), custom_call_target="tpu_custom_call" | custom-call | flops 800000000 | bytes 4000000 | tf_op jit(solution)/shard_map/pallas_call | solution.py:311
  96.4 0.1 collective-permute-start.22
  96.5 4.1 %collective-permute-start.23 = (bf16[10,64,256]{2,1,0:T(8,128)(2,1)S(1)}, bf16[10,64,256]{2,1,0:T(8,128)(2,1)S(1)}, u32[]{:S(2)}, u32[]{:S(2)}) collective-permute-start(bf16[10,64,256]{2,1,0:T(8,128)(2,1)S(1)} %get-tuple-element.58), channel_id=1, source_target_pairs={{0,112},{1,113},{2,114},{3,115},{4,116},{5,117},{6,118},{7,119},{8... | collective-permute-start | bytes 983048 | tf_op jit(solution)/shard_map/ppermute | solution.py:397
  100.6 2.4 %collective-permute-done.20.earlier.inner_earlier = bf16[10,64,256]{2,1,0:T(8,128)(2,1)S(1)} collective-permute-done((bf16[10,64,256]{2,1,0:T(8,128)(2,1)S(1)}, bf16[10,64,256]{2,1,0:T(8,128)(2,1)S(1)}, u32[]{:S(2)}, u32[]{:S(2)}) %collective-permute-start.20) | collective-permute-done | bytes 327712 | tf_op jit(solution)/shard_map/ppermute | solution.py:397
  103.1 2.2 %shard_map.70 = (bf16[8,64,256]{2,1,0:T(8,128)(2,1)S(1)}, bf16[6,64,256]{2,1,0:T(8,128)(2,1)S(1)}) custom-call(s32[3,5]{1,0:T(4,128)S(1)} %reshape.69.flags, bf16[192,576]{1,0:T(8,128)(2,1)S(1)} %reshape.67.wu, bf16[192,192]{1,0:T(8,128)(2,1)S(1)} %reshape.68.wm, bf16[8,64,256]{2,1,0:T(8,128)(2,1)S(1)} %get-tuple-element.48.refs_1_.inner.refs_2_, ...), custom_call_target="tpu_custom_call" | custom-call | flops 600000000 | bytes 4000000 | tf_op jit(solution)/shard_map/pallas_call | solution.py:311
  105.3 3.4 %collective-permute-done.22.earlier = bf16[10,64,256]{2,1,0:T(8,128)(2,1)S(1)} collective-permute-done((bf16[10,64,256]{2,1,0:T(8,128)(2,1)S(1)}, bf16[10,64,256]{2,1,0:T(8,128)(2,1)S(1)}, u32[]{:S(2)}, u32[]{:S(2)}) %collective-permute-start.22) | collective-permute-done | bytes 327712 | tf_op jit(solution)/shard_map/ppermute | solution.py:397
  108.7 3.6 %shard_map.72 = bf16[16,64,256]{2,1,0:T(8,128)(2,1)} custom-call(s32[3,5]{1,0:T(4,128)S(1)} %reshape.69.flags, bf16[192,576]{1,0:T(8,128)(2,1)S(1)} %reshape.67.wu, bf16[192,192]{1,0:T(8,128)(2,1)S(1)} %reshape.68.wm, bf16[8,64,256]{2,1,0:T(8,128)(2,1)S(1)} %collective-permute-done.16.refs_0_.outer, ...), custom_call_target="tpu_custom_call" | custom-call | flops 900000000 | bytes 4000000 | tf_op jit(solution)/shard_map/pallas_call | solution.py:311
  (30 shorter events, 0.2 us)
Async XLA Ops:
  0.0 5.4 %copy-start.3 = (s32[3,4,1,2,32]{4,3,2,1,0:T(2,128)S(1)}, s32[3,4,1,2,32]{4,3,2,1,0:T(2,128)}, u32[]{:S(2)}) copy-start(s32[3,4,1,2,32]{4,3,2,1,0:T(2,128)} %param.8) | copy-start | bytes 9220
  1.1 4.3 %copy-start.2 = (s32[3,4,1,2,32]{4,3,2,1,0:T(2,128)S(1)}, s32[3,4,1,2,32]{4,3,2,1,0:T(2,128)}, u32[]{:S(2)}) copy-start(s32[3,4,1,2,32]{4,3,2,1,0:T(2,128)} %param.7) | copy-start | bytes 9220
  1.1 21.5 %collective-permute-start.2 = (bf16[8,64,256]{2,1,0:T(8,128)(2,1)S(1)}, bf16[8,64,256]{2,1,0:T(8,128)(2,1)S(1)}, u32[]{:S(2)}, u32[]{:S(2)}) collective-permute-start(bf16[8,64,256]{2,1,0:T(8,128)(2,1)S(1)} %get-tuple-element.62.refs_5_), channel_id=1, source_target_pairs={{1,66},{2,65},{3,68},{4,67},{5,70},{6,69},{7,72},{8,71},{9,74},{10... | collective-permute-start | bytes 786440 | tf_op jit(solution)/shard_map/ppermute | solution.py:397
  5.1 17.5 %collective-permute-start.3 = (bf16[8,64,256]{2,1,0:T(8,128)(2,1)S(1)}, bf16[8,64,256]{2,1,0:T(8,128)(2,1)S(1)}, u32[]{:S(2)}, u32[]{:S(2)}) collective-permute-start(bf16[8,64,256]{2,1,0:T(8,128)(2,1)S(1)} %get-tuple-element.62.refs_5_), channel_id=1, source_target_pairs={{0,64},{1,65},{2,66},{3,67},{4,68},{5,69},{6,70},{7,71},{8,72},{9,... | collective-permute-start | bytes 786440 | tf_op jit(solution)/shard_map/ppermute | solution.py:397
  6.5 8.0 %copy-start = (bf16[3,3,64,192]{3,2,1,0:T(8,128)(2,1)S(1)}, bf16[3,3,64,192]{3,2,1,0:T(8,128)(2,1)}, u32[]{:S(2)}) copy-start(bf16[3,3,64,192]{3,2,1,0:T(8,128)(2,1)} %param.10) | copy-start | bytes 663556
  6.5 9.4 %collective-permute-start = (bf16[3,64,256]{2,1,0:T(8,128)(2,1)S(1)}, bf16[3,64,256]{2,1,0:T(8,128)(2,1)S(1)}, u32[]{:S(2)}, u32[]{:S(2)}) collective-permute-start(bf16[3,64,256]{2,1,0:T(8,128)(2,1)S(1)} %pad_maximum_fusion), channel_id=1, source_target_pairs={{0,1},{1,0},{2,3},{3,2},{4,5},{5,4},{6,7},{7,6},{8,9},{9,8},{10,11... | collective-permute-start | bytes 294920 | tf_op jit(solution)/shard_map/ppermute | solution.py:397
  7.4 4.4 %copy-start.4 = (s32[3,1]{0,1:T(1,128)S(1)}, s32[3,1]{0,1:T(1,128)}, u32[]{:S(2)}) copy-start(s32[3,1]{0,1:T(1,128)} %param.9) | copy-start | bytes 40
  7.4 9.4 %collective-permute-start.1 = (bf16[3,64,256]{2,1,0:T(8,128)(2,1)S(1)}, bf16[3,64,256]{2,1,0:T(8,128)(2,1)S(1)}, u32[]{:S(2)}, u32[]{:S(2)}) collective-permute-start(bf16[3,64,256]{2,1,0:T(8,128)(2,1)S(1)} %pad_maximum_fusion.1), channel_id=1, source_target_pairs={{1,2},{2,1},{3,4},{4,3},{5,6},{6,5},{7,8},{8,7},{9,10},{10,9},{11,... | collective-permute-start | bytes 294920 | tf_op jit(solution)/shard_map/ppermute | solution.py:397
  11.4 10.5 %collective-permute-start.4 = (bf16[8,64,256]{2,1,0:T(8,128)(2,1)S(1)}, bf16[8,64,256]{2,1,0:T(8,128)(2,1)S(1)}, u32[]{:S(2)}, u32[]{:S(2)}) collective-permute-start(bf16[8,64,256]{2,1,0:T(8,128)(2,1)S(1)} %get-tuple-element.61.refs_6_), channel_id=1, source_target_pairs={{0,64},{1,65},{2,66},{3,67},{4,68},{5,69},{6,70},{7,71},{8,72},{9,... | collective-permute-start | bytes 786440 | tf_op jit(solution)/shard_map/ppermute | solution.py:397
  14.7 0.9 copy-start.1
  21.9 1.5 %collective-permute-start.5 = (bf16[8,64,256]{2,1,0:T(8,128)(2,1)S(1)}, bf16[8,64,256]{2,1,0:T(8,128)(2,1)S(1)}, u32[]{:S(2)}, u32[]{:S(2)}) collective-permute-start(bf16[8,64,256]{2,1,0:T(8,128)(2,1)S(1)} %collective-permute-done.4.refs_2_), channel_id=1, source_target_pairs={{0,1},{1,0},{2,3},{3,2},{4,5},{5,4},{6,7},{7,6},{8,9},{9,8},{10,11... | collective-permute-start | bytes 786440 | tf_op jit(solution)/shard_map/ppermute | solution.py:397
  29.5 11.1 %collective-permute-start.9 = (bf16[8,64,256]{2,1,0:T(8,128)(2,1)S(1)}, bf16[8,64,256]{2,1,0:T(8,128)(2,1)S(1)}, u32[]{:S(2)}, u32[]{:S(2)}) collective-permute-start(bf16[8,64,256]{2,1,0:T(8,128)(2,1)S(1)} %get-tuple-element.44.refs_10_), channel_id=1, source_target_pairs={{0,32},{1,33},{2,34},{3,35},{4,36},{5,37},{6,38},{7,39},{8,40},{9,... | collective-permute-start | bytes 786440 | tf_op jit(solution)/shard_map/ppermute | solution.py:397
  33.4 12.2 %collective-permute-start.6 = (bf16[8,64,256]{2,1,0:T(8,128)(2,1)S(1)}, bf16[8,64,256]{2,1,0:T(8,128)(2,1)S(1)}, u32[]{:S(2)}, u32[]{:S(2)}) collective-permute-start(bf16[8,64,256]{2,1,0:T(8,128)(2,1)S(1)} %get-tuple-element.43.refs_9_), channel_id=1, source_target_pairs={{0,32},{1,33},{2,34},{3,35},{4,36},{5,37},{6,38},{7,39},{8,40},{9,... | collective-permute-start | bytes 786440 | tf_op jit(solution)/shard_map/ppermute | solution.py:397
  40.6 9.3 %collective-permute-start.12 = (bf16[8,64,256]{2,1,0:T(8,128)(2,1)S(1)}, bf16[8,64,256]{2,1,0:T(8,128)(2,1)S(1)}, u32[]{:S(2)}, u32[]{:S(2)}) collective-permute-start(bf16[8,64,256]{2,1,0:T(8,128)(2,1)S(1)} %collective-permute-done.9.refs_2_), channel_id=1, source_target_pairs={{0,64},{1,65},{2,66},{3,67},{4,68},{5,69},{6,70},{7,71},{8,72},{9,... | collective-permute-start | bytes 786440 | tf_op jit(solution)/shard_map/ppermute | solution.py:397
  45.7 7.8 %collective-permute-start.7 = (bf16[8,64,256]{2,1,0:T(8,128)(2,1)S(1)}, bf16[8,64,256]{2,1,0:T(8,128)(2,1)S(1)}, u32[]{:S(2)}, u32[]{:S(2)}) collective-permute-start(bf16[8,64,256]{2,1,0:T(8,128)(2,1)S(1)} %collective-permute-done.6.refs_1_), channel_id=1, source_target_pairs={{0,64},{1,65},{2,66},{3,67},{4,68},{5,69},{6,70},{7,71},{8,72},{9,... | collective-permute-start | bytes 786440 | tf_op jit(solution)/shard_map/ppermute | solution.py:397
  46.4 19.0 %collective-permute-start.10 = (bf16[8,64,256]{2,1,0:T(8,128)(2,1)S(1)}, bf16[8,64,256]{2,1,0:T(8,128)(2,1)S(1)}, u32[]{:S(2)}, u32[]{:S(2)}) collective-permute-start(bf16[8,64,256]{2,1,0:T(8,128)(2,1)S(1)} %collective-permute-done.9.refs_2_), channel_id=1, source_target_pairs={{0,1},{1,0},{2,3},{3,2},{4,5},{5,4},{6,7},{7,6},{8,9},{9,8},{10,11... | collective-permute-start | bytes 786440 | tf_op jit(solution)/shard_map/ppermute | solution.py:397
  46.4 19.0 %collective-permute-start.11 = (bf16[8,64,256]{2,1,0:T(8,128)(2,1)S(1)}, bf16[8,64,256]{2,1,0:T(8,128)(2,1)S(1)}, u32[]{:S(2)}, u32[]{:S(2)}) collective-permute-start(bf16[8,64,256]{2,1,0:T(8,128)(2,1)S(1)} %collective-permute-done.6.refs_1_), channel_id=1, source_target_pairs={{1,66},{2,65},{3,68},{4,67},{5,70},{6,69},{7,72},{8,71},{9,74},{10... | collective-permute-start | bytes 786440 | tf_op jit(solution)/shard_map/ppermute | solution.py:397
  49.9 15.4 %collective-permute-start.13 = (bf16[8,64,256]{2,1,0:T(8,128)(2,1)S(1)}, bf16[8,64,256]{2,1,0:T(8,128)(2,1)S(1)}, u32[]{:S(2)}, u32[]{:S(2)}) collective-permute-start(bf16[8,64,256]{2,1,0:T(8,128)(2,1)S(1)} %collective-permute-done.12.refs_6_), channel_id=1, source_target_pairs={{0,1},{1,0},{2,3},{3,2},{4,5},{5,4},{6,7},{7,6},{8,9},{9,8},{10,11... | collective-permute-start | bytes 786440 | tf_op jit(solution)/shard_map/ppermute | solution.py:397
  53.4 11.9 %collective-permute-start.8 = (bf16[8,64,256]{2,1,0:T(8,128)(2,1)S(1)}, bf16[8,64,256]{2,1,0:T(8,128)(2,1)S(1)}, u32[]{:S(2)}, u32[]{:S(2)}) collective-permute-start(bf16[8,64,256]{2,1,0:T(8,128)(2,1)S(1)} %collective-permute-done.7.refs_5_), channel_id=1, source_target_pairs={{1,66},{2,65},{3,68},{4,67},{5,70},{6,69},{7,72},{8,71},{9,74},{10... | collective-permute-start | bytes 786440 | tf_op jit(solution)/shard_map/ppermute | solution.py:397
  55.4 8.7 %collective-permute-start.14 = (bf16[2,64,256]{2,1,0:T(8,128)(2,1)S(1)}, bf16[2,64,256]{2,1,0:T(8,128)(2,1)S(1)}, u32[]{:S(2)}, u32[]{:S(2)}) collective-permute-start(bf16[2,64,256]{2,1,0:T(8,128)(2,1)S(1)} %get-tuple-element.45), channel_id=1, source_target_pairs={{1,2},{2,1},{3,4},{4,3},{5,6},{6,5},{7,8},{8,7},{9,10},{10,9},{11,... | collective-permute-start | bytes 196616 | tf_op jit(solution)/shard_map/ppermute | solution.py:397
  64.1 1.3 %collective-permute-start.15 = (bf16[2,64,256]{2,1,0:T(8,128)(2,1)S(1)}, bf16[2,64,256]{2,1,0:T(8,128)(2,1)S(1)}, u32[]{:S(2)}, u32[]{:S(2)}) collective-permute-start(bf16[2,64,256]{2,1,0:T(8,128)(2,1)S(1)} %get-tuple-element.46), channel_id=1, source_target_pairs={{0,1},{1,0},{2,3},{3,2},{4,5},{5,4},{6,7},{7,6},{8,9},{9,8},{10,11... | collective-permute-start | bytes 196616 | tf_op jit(solution)/shard_map/ppermute | solution.py:397
  72.1 16.3 %collective-permute-start.17 = (bf16[8,64,256]{2,1,0:T(8,128)(2,1)S(1)}, bf16[8,64,256]{2,1,0:T(8,128)(2,1)S(1)}, u32[]{:S(2)}, u32[]{:S(2)}) collective-permute-start(bf16[8,64,256]{2,1,0:T(8,128)(2,1)S(1)} %get-tuple-element.48.refs_1_.inner.refs_2_), channel_id=1, source_target_pairs={{0,1},{1,0},{2,3},{3,2},{4,5},{5,4},{6,7},{7,6},{8,9},{9,8},{10,11... | collective-permute-start | bytes 786440 | tf_op jit(solution)/shard_map/ppermute | solution.py:397
  72.3 22.2 %collective-permute-start.16 = (bf16[8,64,256]{2,1,0:T(8,128)(2,1)S(1)}, bf16[8,64,256]{2,1,0:T(8,128)(2,1)S(1)}, u32[]{:S(2)}, u32[]{:S(2)}) collective-permute-start(bf16[8,64,256]{2,1,0:T(8,128)(2,1)S(1)} %get-tuple-element.47.refs_0_.refs_1_.edge), channel_id=1, source_target_pairs={{1,2},{2,1},{3,4},{4,3},{5,6},{6,5},{7,8},{8,7},{9,10},{10,9},{11,... | collective-permute-start | bytes 786440 | tf_op jit(solution)/shard_map/ppermute | solution.py:397
  76.9 6.3 %collective-permute-start.18 = (bf16[2,2,4,32]{3,2,1,0:T(4,128)(2,1)S(1)}, bf16[2,2,4,32]{3,2,1,0:T(4,128)(2,1)S(1)}, u32[]{:S(2)}, u32[]{:S(2)}) collective-permute-start(bf16[2,2,4,32]{3,2,1,0:T(4,128)(2,1)S(1)} %get-tuple-element.49), channel_id=1, source_target_pairs={{0,112},{1,113},{2,114},{3,115},{4,116},{5,117},{6,118},{7,119},{8... | collective-permute-start | bytes 3080 | tf_op jit(solution)/shard_map/ppermute | solution.py:397
  80.8 6.9 %collective-permute-start.19 = (bf16[2,2,4,32]{3,2,1,0:T(4,128)(2,1)S(1)}, bf16[2,2,4,32]{3,2,1,0:T(4,128)(2,1)S(1)}, u32[]{:S(2)}, u32[]{:S(2)}) collective-permute-start(bf16[2,2,4,32]{3,2,1,0:T(4,128)(2,1)S(1)} %get-tuple-element.50), channel_id=1, source_target_pairs={{0,16},{1,17},{2,18},{3,19},{4,20},{5,21},{6,22},{7,23},{8,24},{9,... | collective-permute-start | bytes 3080 | tf_op jit(solution)/shard_map/ppermute | solution.py:397
  90.3 12.8 %collective-permute-start.20 = (bf16[10,64,256]{2,1,0:T(8,128)(2,1)S(1)}, bf16[10,64,256]{2,1,0:T(8,128)(2,1)S(1)}, u32[]{:S(2)}, u32[]{:S(2)}) collective-permute-start(bf16[10,64,256]{2,1,0:T(8,128)(2,1)S(1)} %get-tuple-element.53), channel_id=1, source_target_pairs={{0,16},{1,17},{2,18},{3,19},{4,20},{5,21},{6,22},{7,23},{8,24},{9,... | collective-permute-start | bytes 983048 | tf_op jit(solution)/shard_map/ppermute | solution.py:397
  90.4 12.7 %collective-permute-start.21 = (bf16[10,64,256]{2,1,0:T(8,128)(2,1)S(1)}, bf16[10,64,256]{2,1,0:T(8,128)(2,1)S(1)}, u32[]{:S(2)}, u32[]{:S(2)}) collective-permute-start(bf16[10,64,256]{2,1,0:T(8,128)(2,1)S(1)} %get-tuple-element.54), channel_id=1, source_target_pairs={{0,112},{1,113},{2,114},{3,115},{4,116},{5,117},{6,118},{7,119},{8... | collective-permute-start | bytes 983048 | tf_op jit(solution)/shard_map/ppermute | solution.py:397
  96.4 12.3 %collective-permute-start.22 = (bf16[10,64,256]{2,1,0:T(8,128)(2,1)S(1)}, bf16[10,64,256]{2,1,0:T(8,128)(2,1)S(1)}, u32[]{:S(2)}, u32[]{:S(2)}) collective-permute-start(bf16[10,64,256]{2,1,0:T(8,128)(2,1)S(1)} %get-tuple-element.57), channel_id=1, source_target_pairs={{0,16},{1,17},{2,18},{3,19},{4,20},{5,21},{6,22},{7,23},{8,24},{9,... | collective-permute-start | bytes 983048 | tf_op jit(solution)/shard_map/ppermute | solution.py:397
  96.5 12.2 %collective-permute-start.23 = (bf16[10,64,256]{2,1,0:T(8,128)(2,1)S(1)}, bf16[10,64,256]{2,1,0:T(8,128)(2,1)S(1)}, u32[]{:S(2)}, u32[]{:S(2)}) collective-permute-start(bf16[10,64,256]{2,1,0:T(8,128)(2,1)S(1)} %get-tuple-element.58), channel_id=1, source_target_pairs={{0,112},{1,113},{2,114},{3,115},{4,116},{5,117},{6,118},{7,119},{8... | collective-permute-start | bytes 983048 | tf_op jit(solution)/shard_map/ppermute | solution.py:397

commit v9 on v8

--- a/solution.py
+++ b/solution.py
@@ -134,8 +134,9 @@
 
 
 class Convolutions:
-    def __init__(self, flags, wu, wm, joined, act):
-        self.flags, self.wu, self.wm, self.joined, self.act = flags, wu, wm, joined, act
+    def __init__(self, flags, update, wu, wm, joined, act):
+        self.flags, self.update, self.wu, self.wm = flags, update, wu, wm
+        self.joined, self.act = joined, act
         lane = lax.broadcasted_iota(jnp.int32, (CH, WIDTH), 1)
         self.not_first = lane > 0
         self.not_last = lane < WIDTH - 1
@@ -159,7 +160,7 @@
         window = self.act[pl.ds(y, 3)].reshape(3 * CH, WIDTH)
         total = self.gather_taps(jnp.dot(self.wm[...], window, preferred_element_type=F32))
         own = self.joined[y + 2, OWN, :].astype(F32)
-        return (own + self.flags[3].astype(F32) * total).astype(BF16)
+        return (own + self.update.astype(F32) * total).astype(BF16)
 
 
 def stack_rows(target, turned, pieces):
@@ -167,8 +168,7 @@
         target[pl.ds(turn(turned, 8 * p, 24), 8)] = pieces[p][...]
 
 
-def level_kernel(sources, level, flags, cols, table, wu, wm, *refs):
-    flags = flags.at[level]
+def level_kernel(sources, level, flags, mask, cols, table, wu, wm, *refs):
     own_outer, own_edge, own_inner, own_near = refs[4 * sources : 4 * sources + 4]
     outs = refs[4 * sources + 4 : 4 * sources + 8]
     src, joined, act = refs[4 * sources + 8 : 4 * sources + 11]
@@ -182,7 +182,7 @@
     joined[pl.ds(turn(turned, 18, 18), 2), OWN] = own_near[0:2]
 
     def source_of(which, first, count):
-        return src[which ^ flags[4] if sources == 2 else 0, first : first + count]
+        return src[which ^ flags[3] if sources == 2 else 0, first : first + count]
 
     def put_of(which):
         def put(row, c, value):
@@ -191,7 +191,7 @@
         return put
 
     warp_into(flags, cols, table, source_of, passed, put_of)
-    conv = Convolutions(flags, wu, wm, joined, act)
+    conv = Convolutions(flags, mask[level, 0], wu, wm, joined, act)
 
     @pl.loop(0, 3)
     def _(n):
@@ -211,8 +211,7 @@
     out_near[...] = out_inner[pl.ds(turn(turned, 6, 6), 2)]
 
 
-def warp_half_kernel(is_outer, flags, cols, table, *refs):
-    flags = flags.at[0]
+def warp_half_kernel(is_outer, flags, mask, cols, table, *refs):
     pieces, (ahead, back, src, both, main_rows, halo_rows) = refs[:3], refs[3:]
     turned = flags[0]
     part = turned if is_outer else 1 - turned
@@ -240,16 +239,15 @@
 
 
 def last_inner_kernel(
-    flags, wu, wm, inner, near, earlier, later, out_act, out_rows, joined, act
+    flags, mask, wu, wm, inner, near, earlier, later, out_act, out_rows, joined, act
 ):
-    flags = flags.at[0]
     turned = flags[0]
     part = 1 - turned
     joined[pl.ds(turn(turned, 10, 12), 8), OWN] = inner[...]
     joined[pl.ds(turn(turned, 18, 18), 2), OWN] = near[pl.ds(turn(turned, 0, 6), 2)]
     joined[pl.ds(10 * part, 10), 0:CH] = earlier[...]
     joined[pl.ds(10 * part, 10), CH : 2 * CH] = later[...]
-    conv = Convolutions(flags, wu, wm, joined, act)
+    conv = Convolutions(flags, mask[0, 0], wu, wm, joined, act)
 
     @pl.loop(0, 2)
     def _(n):
@@ -263,6 +261,7 @@
 
 def last_outer_kernel(
     flags,
+    mask,
     wu,
     wm,
     outer,
@@ -279,7 +278,6 @@
     joined,
     act,
 ):
-    flags = flags.at[0]
     turned = flags[0]
     part = turned
     joined[pl.ds(turn(turned, 0, 18), 2), OWN] = outer[pl.ds(turn(turned, 6, 6), 2)]
@@ -292,7 +290,7 @@
     joined[pl.ds(10 - 10 * part, 10), CH : 2 * CH] = inner_later[...]
     act[pl.ds(10 - 10 * part, 8)] = inner_act[...]
     out[pl.ds(10 - 10 * part, 6)] = inner_rows[...]
-    conv = Convolutions(flags, wu, wm, joined, act)
+    conv = Convolutions(flags, mask[0, 0], wu, wm, joined, act)
 
     @pl.loop(0, 2)
     def _(n):
@@ -311,7 +309,7 @@
     return pl.pallas_call(
         kernel,
         out_shape=out_shape,
-        in_specs=[pl.BlockSpec(memory_space=pltpu.SMEM)] + [vmem] * (len(operands) - 1),
+        in_specs=[pl.BlockSpec(memory_space=pltpu.SMEM)] * 2 + [vmem] * (len(operands) - 2),
         out_specs=(vmem,) * len(out_shape),
         scratch_shapes=scratch,
         compiler_params=pltpu.CompilerParams(vmem_limit_bytes=VMEM_LIMIT),
@@ -333,7 +331,7 @@
 def run_level(level, flags, cols, table, wu, wm, sources, own, interpret=False):
     half = jax.ShapeDtypeStruct((HALF, CH, WIDTH), BF16)
     edge = jax.ShapeDtypeStruct((2, CH, WIDTH), BF16)
-    operands = [flags, cols, table, wu, wm] + [p for s in sources for p in s] + list(own)
+    operands = [*flags, cols, table, wu, wm] + [p for s in sources for p in s] + list(own)
     scratch = [pltpu.VMEM((len(sources), 32, CH, WIDTH), BF16)]
     return on_core(
         functools.partial(level_kernel, len(sources), level),
@@ -356,7 +354,7 @@
             pltpu.VMEM((13, CH, WIDTH), F32),
         ],
         800_000_000,
-        [flags, cols, table, *pieces],
+        [*flags, cols, table, *pieces],
         interpret,
     )
 
@@ -370,7 +368,7 @@
         ),
         band_buffers(),
         600_000_000,
-        [flags, wu, wm, *operands],
+        [*flags, wu, wm, *operands],
         interpret,
     )
 
@@ -381,7 +379,7 @@
         (jax.ShapeDtypeStruct((2 * HALF, CH, WIDTH), BF16),),
         band_buffers(),
         900_000_000,
-        [flags, wu, wm, *operands],
+        [*flags, wu, wm, *operands],
         interpret,
     )[0]
 
@@ -405,9 +403,28 @@
     return r ^ 1
 
 
-def tap_weights(w):
-    o, j = w.shape[2], w.shape[3]
-    return jnp.transpose(w, (1, 2, 0, 3)).reshape(3 * o, 3 * j)
+def weights_kernel(uniting, mixing, wu, wm):
+    for ty in range(3):
+        for tx in range(3):
+            rows = slice(tx * CH, tx * CH + CH)
+            wu[rows, ty * 3 * CH : (ty + 1) * 3 * CH] = uniting[ty, tx]
+            wm[rows, ty * CH : (ty + 1) * CH] = mixing[ty, tx]
+
+
+def tap_weights(uniting, mixing, interpret=False):
+    vmem = pl.BlockSpec(memory_space=pltpu.VMEM)
+    return pl.pallas_call(
+        weights_kernel,
+        out_shape=(
+            jax.ShapeDtypeStruct((3 * CH, 9 * CH), BF16),
+            jax.ShapeDtypeStruct((3 * CH, 3 * CH), BF16),
+        ),
+        in_specs=[vmem, vmem],
+        out_specs=(vmem, vmem),
+        compiler_params=pltpu.CompilerParams(vmem_limit_bytes=VMEM_LIMIT),
+        cost_estimate=pl.CostEstimate(flops=0, bytes_accessed=600_000, transcendentals=0),
+        interpret=interpret,
+    )(uniting, mixing)
 
 
 def with_table(rows, entries):
@@ -428,12 +445,10 @@
     inner = lax.dynamic_slice_in_dim(band, 8 - 8 * turned, HALF, axis=0)
     rim = lax.dynamic_slice_in_dim(band, 14 * turned, 2, axis=0)
     near = lax.dynamic_slice_in_dim(band, 14 - 14 * turned, 2, axis=0)
-    wu, wm = tap_weights(uniting_weight), tap_weights(mixing_weight)
     common = [turned, (row > 0).astype(jnp.int32), (row < rows - 1).astype(jnp.int32)]
     swapped = (lax.axis_index("tm") % 4 < 2).astype(jnp.int32)
-    flags = jnp.stack(
-        [value for k in range(LEVELS) for value in common + [update_mask[k, 0], swapped]]
-    ).reshape(LEVELS, 5)
+    spot = lax.iota(jnp.int32, 4)
+    flags = sum(jnp.where(spot == k, value, 0) for k, value in enumerate(common + [swapped]))
 
     def to_other(t):
         return t + 4
@@ -457,6 +472,7 @@
     own_outer = send(with_table(rim, at_edge), row_to=off_chip)
     own_near = send(with_table(near, at_near), row_to=on_chip)
     n = send(i, row_to=on_chip)
+    wu, wm = tap_weights(uniting_weight, mixing_weight)
     outer_table, near_table = table_of(own_outer), table_of(own_near)
     packed = jnp.concatenate(
         [
@@ -470,6 +486,7 @@
         tuple(packed[:, k, j : j + 2] for k in (2, 1, 0) for j in (0, 2))
         + (wu, wm, flags)
     )
+    flags = (flags, update_mask)
     cols, table = make_columns(entries[0], entries[1])
     edge, inner, rim, near = run_level(
         2, flags, cols, table, wu, wm, [(h, e, i, n)], (own_outer, edge, inner, own_near)

time: 113 us -> 113 us (level)
  waiting for transfers between devices: 38 us -> 41.4 us
  local copies, waits for them, and re-layouts: 6.53 us -> 3.14 us
    ppermute x24, waiting for transfers between devices: 38 us -> 41.4 us  [send(): return lax.ppermute(x, ('tm', 'rows'), route)]
    another operation x1 -> x0, local copies, waits for them, and re-layouts: 1.94 us -> none  [shards(): jnp.stack([value for k in range(LEVELS) for value in common + [update_mas...]
  transfers between devices with their start and end apart: 24 -> 24, of which waited for: 12 -> 12; matrix products, arithmetic and copies ran while one was open for 4% -> 1% of each run, Pallas kernels for 7% -> 7%
where the time goes in v9:
time: 113 us; the launch traced here: 112 us
  starting transfers between devices  43.1 us (38%)
  waiting for transfers between devices  41.4 us (37%)
  Pallas kernels  24.3 us (22%)
  local copies, waits for them, and re-layouts  3.14 us (3%)
    ppermute x24, starting transfers between devices, send(): return lax.ppermute(x, ('tm', 'rows'), route)  43.1 us
    ppermute x24, waiting for transfers between devices, send(): return lax.ppermute(x, ('tm', 'rows'), route)  41.4 us
    pallas_call x6, Pallas kernels, on_core(): pl.pallas_call(kernel, out_shape=out_shape, in_specs=[pl.BlockSpec(memory...  22.4 us
  transfers between devices with their start and end apart: 24, of which 12 were waited for; matrix products, arithmetic and copies ran while one was open for 1% of the time, Pallas kernels for 7%

profile of v9, /device:TPU:8, one launch (start us, length us, event | category | flops | bytes accessed | tf_op | source)
XLA Modules:
  0.0 112.4 jit_solution(10152108761724106146)
XLA Ops:
  0.0 1.1 dynamic-slice_bitcast_fusion
  1.1 0.0 copy-start.2
  1.1 4.0 %collective-permute-start.2 = (bf16[8,64,256]{2,1,0:T(8,128)(2,1)S(1)}, bf16[8,64,256]{2,1,0:T(8,128)(2,1)S(1)}, u32[]{:S(2)}, u32[]{:S(2)}) collective-permute-start(bf16[8,64,256]{2,1,0:T(8,128)(2,1)S(1)} %get-tuple-element.66.refs_5_), channel_id=1, source_target_pairs={{1,66},{2,65},{3,68},{4,67},{5,70},{6,69},{7,72},{8,71},{9,74},{10... | collective-permute-start | bytes 786440 | tf_op jit(solution)/shard_map/ppermute | solution.py:395
  5.1 0.3 collective-permute-start.3
  5.5 0.1 select_n.95
  5.6 0.9 dynamic-slice_bitcast_fusion.3
  6.5 0.0 copy-start
  6.5 0.7 collective-permute-start
  7.2 0.0 copy-start.1
  7.2 0.1 select_n.98
  7.4 4.0 %collective-permute-start.1 = (bf16[3,64,256]{2,1,0:T(8,128)(2,1)S(1)}, bf16[3,64,256]{2,1,0:T(8,128)(2,1)S(1)}, u32[]{:S(2)}, u32[]{:S(2)}) collective-permute-start(bf16[3,64,256]{2,1,0:T(8,128)(2,1)S(1)} %pad_maximum_fusion.1), channel_id=1, source_target_pairs={{1,2},{2,1},{3,4},{4,3},{5,6},{6,5},{7,8},{8,7},{9,10},{10,9},{11,... | collective-permute-start | bytes 294920 | tf_op jit(solution)/shard_map/ppermute | solution.py:395
  11.4 0.4 collective-permute-start.4
  11.8 0.6 copy-done.4
  12.4 0.1 copy.26.mask
  12.5 0.1 shard_map.64
  12.7 4.1 %collective-permute-done.1.refs_4_ = bf16[3,64,256]{2,1,0:T(8,128)(2,1)S(1)} collective-permute-done((bf16[3,64,256]{2,1,0:T(8,128)(2,1)S(1)}, bf16[3,64,256]{2,1,0:T(8,128)(2,1)S(1)}, u32[]{:S(2)}, u32[]{:S(2)}) %collective-permute-start.1) | collective-permute-done | bytes 98336 | tf_op jit(solution)/shard_map/ppermute | solution.py:395
  16.7 0.1 select_n.100
  16.8 0.1 select_n.102
  16.9 5.0 %collective-permute-done.4.refs_2_ = bf16[8,64,256]{2,1,0:T(8,128)(2,1)S(1)} collective-permute-done((bf16[8,64,256]{2,1,0:T(8,128)(2,1)S(1)}, bf16[8,64,256]{2,1,0:T(8,128)(2,1)S(1)}, u32[]{:S(2)}, u32[]{:S(2)}) %collective-permute-start.4) | collective-permute-done | bytes 262176 | tf_op jit(solution)/shard_map/ppermute | solution.py:395
  21.9 0.0 collective-permute-start.5
  21.9 0.1 pad_maximum_fusion.2
  22.0 0.6 shard_map.66
  22.6 0.0 collective-permute-done.2.refs_0_
  22.6 0.8 collective-permute-done.5.refs_3_
  23.4 6.0 %shard_map.67 = (bf16[8,64,256]{2,1,0:T(8,128)(2,1)S(1)}, bf16[8,64,256]{2,1,0:T(8,128)(2,1)S(1)}, bf16[2,64,256]{2,1,0:T(8,128)(2,1)S(1)}, bf16[2,64,256]{2,1,0:T(8,128)(2,1)S(1)}) custom-call(s32[4]{0:T(128)S(1)} %fusion.4.flags, s32[3,1]{1,0:T(4,128)S(1)} %copy.26.mask, bf16[8,256,256]{2,1,0:T(8,128)(2,1)S(1)} %get-tuple-element.45.cols, ...), custom_call_target="tpu_custom_call" | custom-call | flops 3000000000 | bytes 4000000 | tf_op jit(solution)/shard_map/pallas_call | solution.py:309
  29.5 4.0 %collective-permute-start.9 = (bf16[8,64,256]{2,1,0:T(8,128)(2,1)S(1)}, bf16[8,64,256]{2,1,0:T(8,128)(2,1)S(1)}, u32[]{:S(2)}, u32[]{:S(2)}) collective-permute-start(bf16[8,64,256]{2,1,0:T(8,128)(2,1)S(1)} %get-tuple-element.48.refs_10_), channel_id=1, source_target_pairs={{0,32},{1,33},{2,34},{3,35},{4,36},{5,37},{6,38},{7,39},{8,40},{9,... | collective-permute-start | bytes 786440 | tf_op jit(solution)/shard_map/ppermute | solution.py:395
  33.4 0.1 collective-permute-start.6
  33.5 7.1 %collective-permute-done.9.refs_2_ = bf16[8,64,256]{2,1,0:T(8,128)(2,1)S(1)} collective-permute-done((bf16[8,64,256]{2,1,0:T(8,128)(2,1)S(1)}, bf16[8,64,256]{2,1,0:T(8,128)(2,1)S(1)}, u32[]{:S(2)}, u32[]{:S(2)}) %collective-permute-start.9) | collective-permute-done | bytes 262176 | tf_op jit(solution)/shard_map/ppermute | solution.py:395
  40.6 0.7 collective-permute-start.12
  41.3 4.4 %collective-permute-done.6.refs_1_ = bf16[8,64,256]{2,1,0:T(8,128)(2,1)S(1)} collective-permute-done((bf16[8,64,256]{2,1,0:T(8,128)(2,1)S(1)}, bf16[8,64,256]{2,1,0:T(8,128)(2,1)S(1)}, u32[]{:S(2)}, u32[]{:S(2)}) %collective-permute-start.6) | collective-permute-done | bytes 262176 | tf_op jit(solution)/shard_map/ppermute | solution.py:395
  45.7 0.7 collective-permute-start.7
  46.3 0.0 collective-permute-start.10
  46.4 3.5 %collective-permute-start.11 = (bf16[8,64,256]{2,1,0:T(8,128)(2,1)S(1)}, bf16[8,64,256]{2,1,0:T(8,128)(2,1)S(1)}, u32[]{:S(2)}, u32[]{:S(2)}) collective-permute-start(bf16[8,64,256]{2,1,0:T(8,128)(2,1)S(1)} %collective-permute-done.6.refs_1_), channel_id=1, source_target_pairs={{1,66},{2,65},{3,68},{4,67},{5,70},{6,69},{7,72},{8,71},{9,74},{10... | collective-permute-start | bytes 786440 | tf_op jit(solution)/shard_map/ppermute | solution.py:395
  49.9 0.0 collective-permute-done.12.refs_6_
  49.9 0.2 collective-permute-start.13
  50.1 3.3 %collective-permute-done.7.refs_5_ = bf16[8,64,256]{2,1,0:T(8,128)(2,1)S(1)} collective-permute-done((bf16[8,64,256]{2,1,0:T(8,128)(2,1)S(1)}, bf16[8,64,256]{2,1,0:T(8,128)(2,1)S(1)}, u32[]{:S(2)}, u32[]{:S(2)}) %collective-permute-start.7) | collective-permute-done | bytes 262176 | tf_op jit(solution)/shard_map/ppermute | solution.py:395
  53.5 1.9 %collective-permute-start.8 = (bf16[8,64,256]{2,1,0:T(8,128)(2,1)S(1)}, bf16[8,64,256]{2,1,0:T(8,128)(2,1)S(1)}, u32[]{:S(2)}, u32[]{:S(2)}) collective-permute-start(bf16[8,64,256]{2,1,0:T(8,128)(2,1)S(1)} %collective-permute-done.7.refs_5_), channel_id=1, source_target_pairs={{1,66},{2,65},{3,68},{4,67},{5,70},{6,69},{7,72},{8,71},{9,74},{10... | collective-permute-start | bytes 786440 | tf_op jit(solution)/shard_map/ppermute | solution.py:395
  55.4 5.2 %collective-permute-start.14 = (bf16[2,64,256]{2,1,0:T(8,128)(2,1)S(1)}, bf16[2,64,256]{2,1,0:T(8,128)(2,1)S(1)}, u32[]{:S(2)}, u32[]{:S(2)}) collective-permute-start(bf16[2,64,256]{2,1,0:T(8,128)(2,1)S(1)} %get-tuple-element.49), channel_id=1, source_target_pairs={{1,2},{2,1},{3,4},{4,3},{5,6},{6,5},{7,8},{8,7},{9,10},{10,9},{11,... | collective-permute-start | bytes 196616 | tf_op jit(solution)/shard_map/ppermute | solution.py:395
  60.6 3.5 %collective-permute-done.14.refs_8_ = bf16[2,64,256]{2,1,0:T(8,128)(2,1)S(1)} collective-permute-done((bf16[2,64,256]{2,1,0:T(8,128)(2,1)S(1)}, bf16[2,64,256]{2,1,0:T(8,128)(2,1)S(1)}, u32[]{:S(2)}, u32[]{:S(2)}) %collective-permute-start.14) | collective-permute-done | bytes 65568 | tf_op jit(solution)/shard_map/ppermute | solution.py:395
  64.1 0.2 collective-permute-start.15
  64.3 0.6 shard_map.65
  64.9 0.4 collective-permute-done.15.refs_11_
  65.3 0.0 collective-permute-done.10.refs_3_
  65.3 0.0 collective-permute-done.11.refs_4_
  65.3 0.0 collective-permute-done.13.refs_7_
  65.3 0.0 collective-permute-done.8.refs_0_
  65.4 6.7 %shard_map.68 = (bf16[8,64,256]{2,1,0:T(8,128)(2,1)S(1)}, bf16[8,64,256]{2,1,0:T(8,128)(2,1)S(1)}, bf16[2,64,256]{2,1,0:T(8,128)(2,1)}, bf16[2,64,256]{2,1,0:T(8,128)(2,1)}) custom-call(s32[4]{0:T(128)S(1)} %fusion.4.flags, s32[3,1]{1,0:T(4,128)S(1)} %copy.26.mask, bf16[8,256,256]{2,1,0:T(8,128)(2,1)S(1)} %get-tuple-element.41.cols, ...), custom_call_target="tpu_custom_call" | custom-call | flops 3000000000 | bytes 4000000 | tf_op jit(solution)/shard_map/pallas_call | solution.py:309
  72.1 0.2 collective-permute-start.17
  72.3 4.5 %collective-permute-start.16 = (bf16[8,64,256]{2,1,0:T(8,128)(2,1)S(1)}, bf16[8,64,256]{2,1,0:T(8,128)(2,1)S(1)}, u32[]{:S(2)}, u32[]{:S(2)}) collective-permute-start(bf16[8,64,256]{2,1,0:T(8,128)(2,1)S(1)} %get-tuple-element.51.refs_0_.refs_1_.edge), channel_id=1, source_target_pairs={{1,2},{2,1},{3,4},{4,3},{5,6},{6,5},{7,8},{8,7},{9,10},{10,9},{11,... | collective-permute-start | bytes 786440 | tf_op jit(solution)/shard_map/ppermute | solution.py:395
  76.9 4.0 %collective-permute-start.18 = (bf16[2,2,4,32]{3,2,1,0:T(4,128)(2,1)S(1)}, bf16[2,2,4,32]{3,2,1,0:T(4,128)(2,1)S(1)}, u32[]{:S(2)}, u32[]{:S(2)}) collective-permute-start(bf16[2,2,4,32]{3,2,1,0:T(4,128)(2,1)S(1)} %get-tuple-element.53), channel_id=1, source_target_pairs={{0,112},{1,113},{2,114},{3,115},{4,116},{5,117},{6,118},{7,119},{8... | collective-permute-start | bytes 3080 | tf_op jit(solution)/shard_map/ppermute | solution.py:395
  80.8 2.3 %collective-permute-done.18.first = bf16[2,2,4,32]{3,2,1,0:T(4,128)(2,1)S(1)} collective-permute-done((bf16[2,2,4,32]{3,2,1,0:T(4,128)(2,1)S(1)}, bf16[2,2,4,32]{3,2,1,0:T(4,128)(2,1)S(1)}, u32[]{:S(2)}, u32[]{:S(2)}) %collective-permute-start.18) | collective-permute-done | bytes 1056 | tf_op jit(solution)/shard_map/ppermute | solution.py:395
  83.1 4.7 %collective-permute-done.19.second = bf16[2,2,4,32]{3,2,1,0:T(4,128)(2,1)S(1)} collective-permute-done((bf16[2,2,4,32]{3,2,1,0:T(4,128)(2,1)S(1)}, bf16[2,2,4,32]{3,2,1,0:T(4,128)(2,1)S(1)}, u32[]{:S(2)}, u32[]{:S(2)}) %collective-permute-start.19) | collective-permute-done | bytes 1056 | tf_op jit(solution)/shard_map/ppermute | solution.py:395
  87.8 0.6 shard_map.69
  88.4 1.9 %shard_map.70 = (bf16[10,64,256]{2,1,0:T(8,128)(2,1)S(1)}, bf16[10,64,256]{2,1,0:T(8,128)(2,1)S(1)}) custom-call(s32[4]{0:T(128)S(1)} %fusion.4.flags, s32[3,1]{1,0:T(4,128)S(1)} %copy.26.mask, bf16[8,256,256]{2,1,0:T(8,128)(2,1)S(1)} %get-tuple-element.55.cols, f32[64,256]{1,0:T(8,128)S(1)} %get-tuple-element.56.table, ...), custom_call_target="tpu_custom_call" | custom-call | flops 800000000 | bytes 4000000 | tf_op jit(solution)/shard_map/pallas_call | solution.py:309
  90.3 0.1 collective-permute-start.20
  90.4 4.1 %collective-permute-start.21 = (bf16[10,64,256]{2,1,0:T(8,128)(2,1)S(1)}, bf16[10,64,256]{2,1,0:T(8,128)(2,1)S(1)}, u32[]{:S(2)}, u32[]{:S(2)}) collective-permute-start(bf16[10,64,256]{2,1,0:T(8,128)(2,1)S(1)} %get-tuple-element.58), channel_id=1, source_target_pairs={{0,112},{1,113},{2,114},{3,115},{4,116},{5,117},{6,118},{7,119},{8... | collective-permute-start | bytes 983048 | tf_op jit(solution)/shard_map/ppermute | solution.py:395
  94.5 0.0 collective-permute-done.16.refs_0_.outer
  94.5 1.9 %shard_map.72 = (bf16[10,64,256]{2,1,0:T(8,128)(2,1)S(1)}, bf16[10,64,256]{2,1,0:T(8,128)(2,1)S(1)}) custom-call(s32[4]{0:T(128)S(1)} %fusion.4.flags, s32[3,1]{1,0:T(4,128)S(1)} %copy.26.mask, bf16[8,256,256]{2,1,0:T(8,128)(2,1)S(1)} %get-tuple-element.55.cols, f32[64,256]{1,0:T(8,128)S(1)} %get-tuple-element.56.table, ...), custom_call_target="tpu_custom_call" | custom-call | flops 800000000 | bytes 4000000 | tf_op jit(solution)/shard_map/pallas_call | solution.py:309
  96.4 0.1 collective-permute-start.22
  96.5 4.1 %collective-permute-start.23 = (bf16[10,64,256]{2,1,0:T(8,128)(2,1)S(1)}, bf16[10,64,256]{2,1,0:T(8,128)(2,1)S(1)}, u32[]{:S(2)}, u32[]{:S(2)}) collective-permute-start(bf16[10,64,256]{2,1,0:T(8,128)(2,1)S(1)} %get-tuple-element.62), channel_id=1, source_target_pairs={{0,112},{1,113},{2,114},{3,115},{4,116},{5,117},{6,118},{7,119},{8... | collective-permute-start | bytes 983048 | tf_op jit(solution)/shard_map/ppermute | solution.py:395
  100.6 2.4 %collective-permute-done.20.earlier.inner_earlier = bf16[10,64,256]{2,1,0:T(8,128)(2,1)S(1)} collective-permute-done((bf16[10,64,256]{2,1,0:T(8,128)(2,1)S(1)}, bf16[10,64,256]{2,1,0:T(8,128)(2,1)S(1)}, u32[]{:S(2)}, u32[]{:S(2)}) %collective-permute-start.20) | collective-permute-done | bytes 327712 | tf_op jit(solution)/shard_map/ppermute | solution.py:395
  103.1 2.2 %shard_map.71 = (bf16[8,64,256]{2,1,0:T(8,128)(2,1)S(1)}, bf16[6,64,256]{2,1,0:T(8,128)(2,1)S(1)}) custom-call(s32[4]{0:T(128)S(1)} %fusion.4.flags, s32[3,1]{1,0:T(4,128)S(1)} %copy.26.mask, bf16[192,576]{1,0:T(8,128)(2,1)S(1)} %get-tuple-element.37.wu, bf16[192,192]{1,0:T(8,128)(2,1)S(1)} %get-tuple-element.38.wm, ...), custom_call_target="tpu_custom_call" | custom-call | flops 600000000 | bytes 4000000 | tf_op jit(solution)/shard_map/pallas_call | solution.py:309
  105.3 3.4 %collective-permute-done.22.earlier = bf16[10,64,256]{2,1,0:T(8,128)(2,1)S(1)} collective-permute-done((bf16[10,64,256]{2,1,0:T(8,128)(2,1)S(1)}, bf16[10,64,256]{2,1,0:T(8,128)(2,1)S(1)}, u32[]{:S(2)}, u32[]{:S(2)}) %collective-permute-start.22) | collective-permute-done | bytes 327712 | tf_op jit(solution)/shard_map/ppermute | solution.py:395
  108.7 3.6 %shard_map.73 = bf16[16,64,256]{2,1,0:T(8,128)(2,1)} custom-call(s32[4]{0:T(128)S(1)} %fusion.4.flags, s32[3,1]{1,0:T(4,128)S(1)} %copy.26.mask, bf16[192,576]{1,0:T(8,128)(2,1)S(1)} %get-tuple-element.37.wu, bf16[192,192]{1,0:T(8,128)(2,1)S(1)} %get-tuple-element.38.wm, bf16[8,64,256]{2,1,0:T(8,128)(2,1)S(1)} %collective-permute-done.16.refs_0_.outer, ...), custom_call_target="tpu_custom_call" | custom-call | flops 900000000 | bytes 4000000 | tf_op jit(solution)/shard_map/pallas_call | solution.py:309
  (26 shorter events, 0.2 us)
Async XLA Ops:
  0.0 5.4 %copy-start.3 = (s32[3,4,1,2,32]{4,3,2,1,0:T(2,128)S(1)}, s32[3,4,1,2,32]{4,3,2,1,0:T(2,128)}, u32[]{:S(2)}) copy-start(s32[3,4,1,2,32]{4,3,2,1,0:T(2,128)} %param.8) | copy-start | bytes 9220
  1.1 4.3 %copy-start.2 = (s32[3,4,1,2,32]{4,3,2,1,0:T(2,128)S(1)}, s32[3,4,1,2,32]{4,3,2,1,0:T(2,128)}, u32[]{:S(2)}) copy-start(s32[3,4,1,2,32]{4,3,2,1,0:T(2,128)} %param.7) | copy-start | bytes 9220
  1.1 21.5 %collective-permute-start.2 = (bf16[8,64,256]{2,1,0:T(8,128)(2,1)S(1)}, bf16[8,64,256]{2,1,0:T(8,128)(2,1)S(1)}, u32[]{:S(2)}, u32[]{:S(2)}) collective-permute-start(bf16[8,64,256]{2,1,0:T(8,128)(2,1)S(1)} %get-tuple-element.66.refs_5_), channel_id=1, source_target_pairs={{1,66},{2,65},{3,68},{4,67},{5,70},{6,69},{7,72},{8,71},{9,74},{10... | collective-permute-start | bytes 786440 | tf_op jit(solution)/shard_map/ppermute | solution.py:395
  5.1 17.5 %collective-permute-start.3 = (bf16[8,64,256]{2,1,0:T(8,128)(2,1)S(1)}, bf16[8,64,256]{2,1,0:T(8,128)(2,1)S(1)}, u32[]{:S(2)}, u32[]{:S(2)}) collective-permute-start(bf16[8,64,256]{2,1,0:T(8,128)(2,1)S(1)} %get-tuple-element.66.refs_5_), channel_id=1, source_target_pairs={{0,64},{1,65},{2,66},{3,67},{4,68},{5,69},{6,70},{7,71},{8,72},{9,... | collective-permute-start | bytes 786440 | tf_op jit(solution)/shard_map/ppermute | solution.py:395
  6.5 6.1 %copy-start = (bf16[3,3,64,192]{3,2,1,0:T(8,128)(2,1)S(1)}, bf16[3,3,64,192]{3,2,1,0:T(8,128)(2,1)}, u32[]{:S(2)}) copy-start(bf16[3,3,64,192]{3,2,1,0:T(8,128)(2,1)} %uniting.1) | copy-start | bytes 663556
  6.5 6.1 %collective-permute-start = (bf16[3,64,256]{2,1,0:T(8,128)(2,1)S(1)}, bf16[3,64,256]{2,1,0:T(8,128)(2,1)S(1)}, u32[]{:S(2)}, u32[]{:S(2)}) collective-permute-start(bf16[3,64,256]{2,1,0:T(8,128)(2,1)S(1)} %pad_maximum_fusion), channel_id=1, source_target_pairs={{0,1},{1,0},{2,3},{3,2},{4,5},{5,4},{6,7},{7,6},{8,9},{9,8},{10,11... | collective-permute-start | bytes 294920 | tf_op jit(solution)/shard_map/ppermute | solution.py:395
  7.2 5.3 %copy-start.1 = (bf16[3,3,64,64]{3,2,1,0:T(8,128)(2,1)S(1)}, bf16[3,3,64,64]{3,2,1,0:T(8,128)(2,1)}, u32[]{:S(2)}) copy-start(bf16[3,3,64,64]{3,2,1,0:T(8,128)(2,1)} %mixing.1) | copy-start | bytes 221188
  7.4 9.4 %collective-permute-start.1 = (bf16[3,64,256]{2,1,0:T(8,128)(2,1)S(1)}, bf16[3,64,256]{2,1,0:T(8,128)(2,1)S(1)}, u32[]{:S(2)}, u32[]{:S(2)}) collective-permute-start(bf16[3,64,256]{2,1,0:T(8,128)(2,1)S(1)} %pad_maximum_fusion.1), channel_id=1, source_target_pairs={{1,2},{2,1},{3,4},{4,3},{5,6},{6,5},{7,8},{8,7},{9,10},{10,9},{11,... | collective-permute-start | bytes 294920 | tf_op jit(solution)/shard_map/ppermute | solution.py:395
  11.4 10.5 %collective-permute-start.4 = (bf16[8,64,256]{2,1,0:T(8,128)(2,1)S(1)}, bf16[8,64,256]{2,1,0:T(8,128)(2,1)S(1)}, u32[]{:S(2)}, u32[]{:S(2)}) collective-permute-start(bf16[8,64,256]{2,1,0:T(8,128)(2,1)S(1)} %get-tuple-element.65.refs_6_), channel_id=1, source_target_pairs={{0,64},{1,65},{2,66},{3,67},{4,68},{5,69},{6,70},{7,71},{8,72},{9,... | collective-permute-start | bytes 786440 | tf_op jit(solution)/shard_map/ppermute | solution.py:395
  11.8 0.7 copy-start.4
  21.9 1.5 %collective-permute-start.5 = (bf16[8,64,256]{2,1,0:T(8,128)(2,1)S(1)}, bf16[8,64,256]{2,1,0:T(8,128)(2,1)S(1)}, u32[]{:S(2)}, u32[]{:S(2)}) collective-permute-start(bf16[8,64,256]{2,1,0:T(8,128)(2,1)S(1)} %collective-permute-done.4.refs_2_), channel_id=1, source_target_pairs={{0,1},{1,0},{2,3},{3,2},{4,5},{5,4},{6,7},{7,6},{8,9},{9,8},{10,11... | collective-permute-start | bytes 786440 | tf_op jit(solution)/shard_map/ppermute | solution.py:395
  29.5 11.1 %collective-permute-start.9 = (bf16[8,64,256]{2,1,0:T(8,128)(2,1)S(1)}, bf16[8,64,256]{2,1,0:T(8,128)(2,1)S(1)}, u32[]{:S(2)}, u32[]{:S(2)}) collective-permute-start(bf16[8,64,256]{2,1,0:T(8,128)(2,1)S(1)} %get-tuple-element.48.refs_10_), channel_id=1, source_target_pairs={{0,32},{1,33},{2,34},{3,35},{4,36},{5,37},{6,38},{7,39},{8,40},{9,... | collective-permute-start | bytes 786440 | tf_op jit(solution)/shard_map/ppermute | solution.py:395
  33.4 12.2 %collective-permute-start.6 = (bf16[8,64,256]{2,1,0:T(8,128)(2,1)S(1)}, bf16[8,64,256]{2,1,0:T(8,128)(2,1)S(1)}, u32[]{:S(2)}, u32[]{:S(2)}) collective-permute-start(bf16[8,64,256]{2,1,0:T(8,128)(2,1)S(1)} %get-tuple-element.47.refs_9_), channel_id=1, source_target_pairs={{0,32},{1,33},{2,34},{3,35},{4,36},{5,37},{6,38},{7,39},{8,40},{9,... | collective-permute-start | bytes 786440 | tf_op jit(solution)/shard_map/ppermute | solution.py:395
  40.6 9.3 %collective-permute-start.12 = (bf16[8,64,256]{2,1,0:T(8,128)(2,1)S(1)}, bf16[8,64,256]{2,1,0:T(8,128)(2,1)S(1)}, u32[]{:S(2)}, u32[]{:S(2)}) collective-permute-start(bf16[8,64,256]{2,1,0:T(8,128)(2,1)S(1)} %collective-permute-done.9.refs_2_), channel_id=1, source_target_pairs={{0,64},{1,65},{2,66},{3,67},{4,68},{5,69},{6,70},{7,71},{8,72},{9,... | collective-permute-start | bytes 786440 | tf_op jit(solution)/shard_map/ppermute | solution.py:395
  45.7 7.8 %collective-permute-start.7 = (bf16[8,64,256]{2,1,0:T(8,128)(2,1)S(1)}, bf16[8,64,256]{2,1,0:T(8,128)(2,1)S(1)}, u32[]{:S(2)}, u32[]{:S(2)}) collective-permute-start(bf16[8,64,256]{2,1,0:T(8,128)(2,1)S(1)} %collective-permute-done.6.refs_1_), channel_id=1, source_target_pairs={{0,64},{1,65},{2,66},{3,67},{4,68},{5,69},{6,70},{7,71},{8,72},{9,... | collective-permute-start | bytes 786440 | tf_op jit(solution)/shard_map/ppermute | solution.py:395
  46.3 19.0 %collective-permute-start.10 = (bf16[8,64,256]{2,1,0:T(8,128)(2,1)S(1)}, bf16[8,64,256]{2,1,0:T(8,128)(2,1)S(1)}, u32[]{:S(2)}, u32[]{:S(2)}) collective-permute-start(bf16[8,64,256]{2,1,0:T(8,128)(2,1)S(1)} %collective-permute-done.9.refs_2_), channel_id=1, source_target_pairs={{0,1},{1,0},{2,3},{3,2},{4,5},{5,4},{6,7},{7,6},{8,9},{9,8},{10,11... | collective-permute-start | bytes 786440 | tf_op jit(solution)/shard_map/ppermute | solution.py:395
  46.4 19.0 %collective-permute-start.11 = (bf16[8,64,256]{2,1,0:T(8,128)(2,1)S(1)}, bf16[8,64,256]{2,1,0:T(8,128)(2,1)S(1)}, u32[]{:S(2)}, u32[]{:S(2)}) collective-permute-start(bf16[8,64,256]{2,1,0:T(8,128)(2,1)S(1)} %collective-permute-done.6.refs_1_), channel_id=1, source_target_pairs={{1,66},{2,65},{3,68},{4,67},{5,70},{6,69},{7,72},{8,71},{9,74},{10... | collective-permute-start | bytes 786440 | tf_op jit(solution)/shard_map/ppermute | solution.py:395
  49.9 15.4 %collective-permute-start.13 = (bf16[8,64,256]{2,1,0:T(8,128)(2,1)S(1)}, bf16[8,64,256]{2,1,0:T(8,128)(2,1)S(1)}, u32[]{:S(2)}, u32[]{:S(2)}) collective-permute-start(bf16[8,64,256]{2,1,0:T(8,128)(2,1)S(1)} %collective-permute-done.12.refs_6_), channel_id=1, source_target_pairs={{0,1},{1,0},{2,3},{3,2},{4,5},{5,4},{6,7},{7,6},{8,9},{9,8},{10,11... | collective-permute-start | bytes 786440 | tf_op jit(solution)/shard_map/ppermute | solution.py:395
  53.5 11.9 %collective-permute-start.8 = (bf16[8,64,256]{2,1,0:T(8,128)(2,1)S(1)}, bf16[8,64,256]{2,1,0:T(8,128)(2,1)S(1)}, u32[]{:S(2)}, u32[]{:S(2)}) collective-permute-start(bf16[8,64,256]{2,1,0:T(8,128)(2,1)S(1)} %collective-permute-done.7.refs_5_), channel_id=1, source_target_pairs={{1,66},{2,65},{3,68},{4,67},{5,70},{6,69},{7,72},{8,71},{9,74},{10... | collective-permute-start | bytes 786440 | tf_op jit(solution)/shard_map/ppermute | solution.py:395
  55.4 8.7 %collective-permute-start.14 = (bf16[2,64,256]{2,1,0:T(8,128)(2,1)S(1)}, bf16[2,64,256]{2,1,0:T(8,128)(2,1)S(1)}, u32[]{:S(2)}, u32[]{:S(2)}) collective-permute-start(bf16[2,64,256]{2,1,0:T(8,128)(2,1)S(1)} %get-tuple-element.49), channel_id=1, source_target_pairs={{1,2},{2,1},{3,4},{4,3},{5,6},{6,5},{7,8},{8,7},{9,10},{10,9},{11,... | collective-permute-start | bytes 196616 | tf_op jit(solution)/shard_map/ppermute | solution.py:395
  64.1 1.3 %collective-permute-start.15 = (bf16[2,64,256]{2,1,0:T(8,128)(2,1)S(1)}, bf16[2,64,256]{2,1,0:T(8,128)(2,1)S(1)}, u32[]{:S(2)}, u32[]{:S(2)}) collective-permute-start(bf16[2,64,256]{2,1,0:T(8,128)(2,1)S(1)} %get-tuple-element.50), channel_id=1, source_target_pairs={{0,1},{1,0},{2,3},{3,2},{4,5},{5,4},{6,7},{7,6},{8,9},{9,8},{10,11... | collective-permute-start | bytes 196616 | tf_op jit(solution)/shard_map/ppermute | solution.py:395
  72.1 16.3 %collective-permute-start.17 = (bf16[8,64,256]{2,1,0:T(8,128)(2,1)S(1)}, bf16[8,64,256]{2,1,0:T(8,128)(2,1)S(1)}, u32[]{:S(2)}, u32[]{:S(2)}) collective-permute-start(bf16[8,64,256]{2,1,0:T(8,128)(2,1)S(1)} %get-tuple-element.52.refs_1_.inner.refs_2_), channel_id=1, source_target_pairs={{0,1},{1,0},{2,3},{3,2},{4,5},{5,4},{6,7},{7,6},{8,9},{9,8},{10,11... | collective-permute-start | bytes 786440 | tf_op jit(solution)/shard_map/ppermute | solution.py:395
  72.3 22.2 %collective-permute-start.16 = (bf16[8,64,256]{2,1,0:T(8,128)(2,1)S(1)}, bf16[8,64,256]{2,1,0:T(8,128)(2,1)S(1)}, u32[]{:S(2)}, u32[]{:S(2)}) collective-permute-start(bf16[8,64,256]{2,1,0:T(8,128)(2,1)S(1)} %get-tuple-element.51.refs_0_.refs_1_.edge), channel_id=1, source_target_pairs={{1,2},{2,1},{3,4},{4,3},{5,6},{6,5},{7,8},{8,7},{9,10},{10,9},{11,... | collective-permute-start | bytes 786440 | tf_op jit(solution)/shard_map/ppermute | solution.py:395
  76.9 6.2 %collective-permute-start.18 = (bf16[2,2,4,32]{3,2,1,0:T(4,128)(2,1)S(1)}, bf16[2,2,4,32]{3,2,1,0:T(4,128)(2,1)S(1)}, u32[]{:S(2)}, u32[]{:S(2)}) collective-permute-start(bf16[2,2,4,32]{3,2,1,0:T(4,128)(2,1)S(1)} %get-tuple-element.53), channel_id=1, source_target_pairs={{0,112},{1,113},{2,114},{3,115},{4,116},{5,117},{6,118},{7,119},{8... | collective-permute-start | bytes 3080 | tf_op jit(solution)/shard_map/ppermute | solution.py:395
  80.8 7.0 %collective-permute-start.19 = (bf16[2,2,4,32]{3,2,1,0:T(4,128)(2,1)S(1)}, bf16[2,2,4,32]{3,2,1,0:T(4,128)(2,1)S(1)}, u32[]{:S(2)}, u32[]{:S(2)}) collective-permute-start(bf16[2,2,4,32]{3,2,1,0:T(4,128)(2,1)S(1)} %get-tuple-element.54), channel_id=1, source_target_pairs={{0,16},{1,17},{2,18},{3,19},{4,20},{5,21},{6,22},{7,23},{8,24},{9,... | collective-permute-start | bytes 3080 | tf_op jit(solution)/shard_map/ppermute | solution.py:395
  90.3 12.8 %collective-permute-start.20 = (bf16[10,64,256]{2,1,0:T(8,128)(2,1)S(1)}, bf16[10,64,256]{2,1,0:T(8,128)(2,1)S(1)}, u32[]{:S(2)}, u32[]{:S(2)}) collective-permute-start(bf16[10,64,256]{2,1,0:T(8,128)(2,1)S(1)} %get-tuple-element.57), channel_id=1, source_target_pairs={{0,16},{1,17},{2,18},{3,19},{4,20},{5,21},{6,22},{7,23},{8,24},{9,... | collective-permute-start | bytes 983048 | tf_op jit(solution)/shard_map/ppermute | solution.py:395
  90.4 12.7 %collective-permute-start.21 = (bf16[10,64,256]{2,1,0:T(8,128)(2,1)S(1)}, bf16[10,64,256]{2,1,0:T(8,128)(2,1)S(1)}, u32[]{:S(2)}, u32[]{:S(2)}) collective-permute-start(bf16[10,64,256]{2,1,0:T(8,128)(2,1)S(1)} %get-tuple-element.58), channel_id=1, source_target_pairs={{0,112},{1,113},{2,114},{3,115},{4,116},{5,117},{6,118},{7,119},{8... | collective-permute-start | bytes 983048 | tf_op jit(solution)/shard_map/ppermute | solution.py:395
  96.4 12.3 %collective-permute-start.22 = (bf16[10,64,256]{2,1,0:T(8,128)(2,1)S(1)}, bf16[10,64,256]{2,1,0:T(8,128)(2,1)S(1)}, u32[]{:S(2)}, u32[]{:S(2)}) collective-permute-start(bf16[10,64,256]{2,1,0:T(8,128)(2,1)S(1)} %get-tuple-element.61), channel_id=1, source_target_pairs={{0,16},{1,17},{2,18},{3,19},{4,20},{5,21},{6,22},{7,23},{8,24},{9,... | collective-permute-start | bytes 983048 | tf_op jit(solution)/shard_map/ppermute | solution.py:395
  96.5 12.2 %collective-permute-start.23 = (bf16[10,64,256]{2,1,0:T(8,128)(2,1)S(1)}, bf16[10,64,256]{2,1,0:T(8,128)(2,1)S(1)}, u32[]{:S(2)}, u32[]{:S(2)}) collective-permute-start(bf16[10,64,256]{2,1,0:T(8,128)(2,1)S(1)} %get-tuple-element.62), channel_id=1, source_target_pairs={{0,112},{1,113},{2,114},{3,115},{4,116},{5,117},{6,118},{7,119},{8... | collective-permute-start | bytes 983048 | tf_op jit(solution)/shard_map/ppermute | solution.py:395

commit v10 on v9

--- a/solution.py
+++ b/solution.py
@@ -168,11 +168,15 @@
         target[pl.ds(turn(turned, 8 * p, 24), 8)] = pieces[p][...]
 
 
-def level_kernel(sources, level, flags, mask, cols, table, wu, wm, *refs):
+def level_kernel(sources, level, split, flags, mask, cols, table, wu, wm, *refs):
     own_outer, own_edge, own_inner, own_near = refs[4 * sources : 4 * sources + 4]
-    outs = refs[4 * sources + 4 : 4 * sources + 8]
-    src, joined, act = refs[4 * sources + 8 : 4 * sources + 11]
-    passed = refs[4 * sources + 11 :]
+    if split:
+        out_edge, out_rim, joined, src, act = refs[4 * sources + 4 : 4 * sources + 9]
+        passed = refs[4 * sources + 9 :]
+    else:
+        out_edge, out_inner, out_rim, out_near = refs[4 * sources + 4 : 4 * sources + 8]
+        src, joined, act = refs[4 * sources + 8 : 4 * sources + 11]
+        passed = refs[4 * sources + 11 :]
     turned = flags[0]
     for i in range(sources):
         stack_rows(src.at[i], turned, refs[4 * i : 4 * i + 4])
@@ -193,12 +197,22 @@
     warp_into(flags, cols, table, source_of, passed, put_of)
     conv = Convolutions(flags, mask[level, 0], wu, wm, joined, act)
 
+    if split:
+
+        @pl.loop(0, 2)
+        def _(n):
+            for k in range(5):
+                conv.activate(8 * turned + 5 * n + k)
+
+        for k in range(HALF):
+            out_edge[k] = conv.finish(8 * turned + k)
+        out_rim[...] = out_edge[pl.ds(turn(turned, 0, 6), 2)]
+        return
+
     @pl.loop(0, 3)
     def _(n):
         for k in range(6):
             conv.activate(6 * n + k)
-
-    out_edge, out_inner, out_rim, out_near = outs
 
     @pl.loop(0, 2)
     def _(n):
@@ -208,6 +222,21 @@
             out_inner[y] = conv.finish(y + turn(turned, 8, 8))
 
     out_rim[...] = out_edge[pl.ds(turn(turned, 0, 6), 2)]
+    out_near[...] = out_inner[pl.ds(turn(turned, 6, 6), 2)]
+
+
+def inner_kernel(level, flags, mask, wu, wm, joined, out_inner, out_near, act):
+    turned = flags[0]
+    conv = Convolutions(flags, mask[level, 0], wu, wm, joined, act)
+    start = 8 - 8 * turned
+
+    @pl.loop(0, 2)
+    def _(n):
+        for k in range(5):
+            conv.activate(start + 5 * n + k)
+
+    for k in range(HALF):
+        out_inner[k] = conv.finish(start + k)
     out_near[...] = out_inner[pl.ds(turn(turned, 6, 6), 2)]
 
 
@@ -328,17 +357,32 @@
     return [pltpu.VMEM((20, 3 * CH, WIDTH), BF16), pltpu.VMEM((18, CH, WIDTH), BF16)]
 
 
-def run_level(level, flags, cols, table, wu, wm, sources, own, interpret=False):
+def run_level(level, flags, cols, table, wu, wm, sources, own, split=False, interpret=False):
     half = jax.ShapeDtypeStruct((HALF, CH, WIDTH), BF16)
     edge = jax.ShapeDtypeStruct((2, CH, WIDTH), BF16)
+    rows = jax.ShapeDtypeStruct((20, 3 * CH, WIDTH), BF16)
     operands = [*flags, cols, table, wu, wm] + [p for s in sources for p in s] + list(own)
     scratch = [pltpu.VMEM((len(sources), 32, CH, WIDTH), BF16)]
     return on_core(
-        functools.partial(level_kernel, len(sources), level),
-        (half, half, edge, edge),
-        scratch + band_buffers() + passed_buffers(),
-        3_000_000_000,
+        functools.partial(level_kernel, len(sources), level, split),
+        (half, edge, rows) if split else (half, half, edge, edge),
+        scratch + band_buffers()[split:] + passed_buffers(),
+        2_300_000_000 if split else 3_000_000_000,
         operands,
+        interpret,
+    )
+
+
+def run_inner(level, flags, wu, wm, joined, interpret=False):
+    return on_core(
+        functools.partial(inner_kernel, level),
+        (
+            jax.ShapeDtypeStruct((HALF, CH, WIDTH), BF16),
+            jax.ShapeDtypeStruct((2, CH, WIDTH), BF16),
+        ),
+        band_buffers()[1:],
+        700_000_000,
+        [*flags, wu, wm, joined],
         interpret,
     )
 
@@ -488,10 +532,19 @@
     )
     flags = (flags, update_mask)
     cols, table = make_columns(entries[0], entries[1])
-    edge, inner, rim, near = run_level(
-        2, flags, cols, table, wu, wm, [(h, e, i, n)], (own_outer, edge, inner, own_near)
-    )
-
+    edge, rim, joined = run_level(
+        2,
+        flags,
+        cols,
+        table,
+        wu,
+        wm,
+        [(h, e, i, n)],
+        (own_outer, edge, inner, own_near),
+        split=True,
+    )
+
+    inner, near = run_inner(2, flags, wu, wm, joined)
     own_outer = send(rim, row_to=off_chip)
     own_near = send(near, row_to=on_chip)
     e = send(edge, across)
@@ -506,7 +559,7 @@
     xn = send(xi, row_to=on_chip)
     cols, table = make_columns(entries[2], entries[3])
     next_cols, next_table = make_columns(for_ahead, for_back)
-    edge, inner, _, _ = run_level(
+    edge, _, joined = run_level(
         1,
         flags,
         cols,
@@ -515,8 +568,10 @@
         wm,
         [(h, e, i, n), (xh, xe, xi, xn)],
         (own_outer, edge, inner, own_near),
-    )
-
+        split=True,
+    )
+
+    inner, _ = run_inner(1, flags, wu, wm, joined)
     outer = send(edge, row_to=off_chip)
     near = send(inner, row_to=on_chip)
     halves = run_warp_half(False, flags, next_cols, next_table, (edge, inner, near))

time: 113 us -> 115 us (1.018)
  the two profiles are of different devices: /device:TPU:8 before, /device:TPU:7 now
where the time goes in v10:
time: 115 us; the launch traced here: 113 us
  starting transfers between devices  45.4 us (39%)
  waiting for transfers between devices  36.8 us (32%)
  Pallas kernels  26.8 us (23%)
  local copies, waits for them, and re-layouts  2.52 us (2%)
    ppermute x24, starting transfers between devices, send(): return lax.ppermute(x, ('tm', 'rows'), route)  45.4 us
    ppermute x24, waiting for transfers between devices, send(): return lax.ppermute(x, ('tm', 'rows'), route)  36.8 us
    pallas_call x8, Pallas kernels, on_core(): pl.pallas_call(kernel, out_shape=out_shape, in_specs=[pl.BlockSpec(memory...  25 us
  transfers between devices with their start and end apart: 24, of which 12 were waited for; matrix products, arithmetic and copies ran while one was open for 2% of the time, Pallas kernels for 7%

profile of v10, /device:TPU:7, one launch (start us, length us, event | category | flops | bytes accessed | tf_op | source)
XLA Modules:
  0.0 112.9 jit_solution(3188560130597945339)
XLA Ops:
  0.0 1.1 dynamic-slice_bitcast_fusion
  1.2 3.7 %collective-permute-start.2 = (bf16[8,64,256]{2,1,0:T(8,128)(2,1)S(1)}, bf16[8,64,256]{2,1,0:T(8,128)(2,1)S(1)}, u32[]{:S(2)}, u32[]{:S(2)}) collective-permute-start(bf16[8,64,256]{2,1,0:T(8,128)(2,1)S(1)} %get-tuple-element.70.refs_5_), channel_id=1, source_target_pairs={{1,66},{2,65},{3,68},{4,67},{5,70},{6,69},{7,72},{8,71},{9,74},{10... | collective-permute-start | bytes 786440 | tf_op jit(solution)/shard_map/ppermute | solution.py:439
  4.8 0.7 collective-permute-start.3
  5.5 0.7 fusion
  6.3 0.1 select_n.95
  6.4 0.9 dynamic-slice_bitcast_fusion.3
  7.3 0.1 collective-permute-start
  7.5 0.1 select_n.98
  7.6 5.3 %collective-permute-start.1 = (bf16[3,64,256]{2,1,0:T(8,128)(2,1)S(1)}, bf16[3,64,256]{2,1,0:T(8,128)(2,1)S(1)}, u32[]{:S(2)}, u32[]{:S(2)}) collective-permute-start(bf16[3,64,256]{2,1,0:T(8,128)(2,1)S(1)} %pad_maximum_fusion.1), channel_id=1, source_target_pairs={{1,2},{2,1},{3,4},{4,3},{5,6},{6,5},{7,8},{8,7},{9,10},{10,9},{11,... | collective-permute-start | bytes 294920 | tf_op jit(solution)/shard_map/ppermute | solution.py:439
  12.9 0.1 collective-permute-start.4
  13.1 0.1 copy.30.mask
  13.2 0.1 shard_map.64
  13.3 0.0 collective-permute-done.refs_7_
  13.3 4.1 %collective-permute-done.1.refs_4_ = bf16[3,64,256]{2,1,0:T(8,128)(2,1)S(1)} collective-permute-done((bf16[3,64,256]{2,1,0:T(8,128)(2,1)S(1)}, bf16[3,64,256]{2,1,0:T(8,128)(2,1)S(1)}, u32[]{:S(2)}, u32[]{:S(2)}) %collective-permute-start.1) | collective-permute-done | bytes 98336 | tf_op jit(solution)/shard_map/ppermute | solution.py:439
  17.4 0.1 select_n.100
  17.5 0.1 select_n.102
  17.6 2.9 %collective-permute-done.4.refs_2_ = bf16[8,64,256]{2,1,0:T(8,128)(2,1)S(1)} collective-permute-done((bf16[8,64,256]{2,1,0:T(8,128)(2,1)S(1)}, bf16[8,64,256]{2,1,0:T(8,128)(2,1)S(1)}, u32[]{:S(2)}, u32[]{:S(2)}) %collective-permute-start.4) | collective-permute-done | bytes 262176 | tf_op jit(solution)/shard_map/ppermute | solution.py:439
  20.5 0.2 collective-permute-start.5
  20.7 0.1 pad_maximum_fusion.2
  20.7 0.6 shard_map.66
  21.3 0.0 collective-permute-done.3.refs_1_
  21.4 0.7 collective-permute-done.5.refs_3_
  22.0 4.6 %shard_map.67 = (bf16[8,64,256]{2,1,0:T(8,128)(2,1)S(1)}, bf16[2,64,256]{2,1,0:T(8,128)(2,1)S(1)}, bf16[20,192,256]{2,1,0:T(8,128)(2,1)S(1)}) custom-call(s32[4]{0:T(128)S(1)} %fusion.4.flags, s32[3,1]{1,0:T(4,128)S(1)} %copy.30.mask, bf16[8,256,256]{2,1,0:T(8,128)(2,1)S(1)} %get-tuple-element.47.cols, f32[64,256]{1,0:T(8,128)S(1)} %get-tuple-element.48.table, ...), custom_call_target="tpu_custom_call" | custom-call | flops 2300000000 | bytes 4000000 | tf_op jit(solution)/shard_map/pallas_call | solution.py:338
  26.7 2.4 %shard_map.68 = (bf16[8,64,256]{2,1,0:T(8,128)(2,1)S(1)}, bf16[2,64,256]{2,1,0:T(8,128)(2,1)S(1)}) custom-call(s32[4]{0:T(128)S(1)} %fusion.4.flags, s32[3,1]{1,0:T(4,128)S(1)} %copy.30.mask, bf16[192,576]{1,0:T(8,128)(2,1)S(1)} %get-tuple-element.39.wu, bf16[192,192]{1,0:T(8,128)(2,1)S(1)} %get-tuple-element.40.wm, ...), custom_call_target="tpu_custom_call" | custom-call | flops 700000000 | bytes 4000000 | tf_op jit(solution)/shard_map/pallas_call | solution.py:338
  29.0 3.7 %collective-permute-start.9 = (bf16[8,64,256]{2,1,0:T(8,128)(2,1)S(1)}, bf16[8,64,256]{2,1,0:T(8,128)(2,1)S(1)}, u32[]{:S(2)}, u32[]{:S(2)}) collective-permute-start(bf16[8,64,256]{2,1,0:T(8,128)(2,1)S(1)} %get-tuple-element.51.refs_10_), channel_id=1, source_target_pairs={{0,32},{1,33},{2,34},{3,35},{4,36},{5,37},{6,38},{7,39},{8,40},{9,... | collective-permute-start | bytes 786440 | tf_op jit(solution)/shard_map/ppermute | solution.py:439
  32.7 0.1 collective-permute-start.6
  32.8 6.4 %collective-permute-done.9.refs_2_ = bf16[8,64,256]{2,1,0:T(8,128)(2,1)S(1)} collective-permute-done((bf16[8,64,256]{2,1,0:T(8,128)(2,1)S(1)}, bf16[8,64,256]{2,1,0:T(8,128)(2,1)S(1)}, u32[]{:S(2)}, u32[]{:S(2)}) %collective-permute-start.9) | collective-permute-done | bytes 262176 | tf_op jit(solution)/shard_map/ppermute | solution.py:439
  39.2 1.7 %collective-permute-start.12 = (bf16[8,64,256]{2,1,0:T(8,128)(2,1)S(1)}, bf16[8,64,256]{2,1,0:T(8,128)(2,1)S(1)}, u32[]{:S(2)}, u32[]{:S(2)}) collective-permute-start(bf16[8,64,256]{2,1,0:T(8,128)(2,1)S(1)} %collective-permute-done.9.refs_2_), channel_id=1, source_target_pairs={{0,64},{1,65},{2,66},{3,67},{4,68},{5,69},{6,70},{7,71},{8,72},{9,... | collective-permute-start | bytes 786440 | tf_op jit(solution)/shard_map/ppermute | solution.py:439
  41.0 3.9 %collective-permute-done.6.refs_1_ = bf16[8,64,256]{2,1,0:T(8,128)(2,1)S(1)} collective-permute-done((bf16[8,64,256]{2,1,0:T(8,128)(2,1)S(1)}, bf16[8,64,256]{2,1,0:T(8,128)(2,1)S(1)}, u32[]{:S(2)}, u32[]{:S(2)}) %collective-permute-start.6) | collective-permute-done | bytes 262176 | tf_op jit(solution)/shard_map/ppermute | solution.py:439
  44.9 1.7 %collective-permute-start.7 = (bf16[8,64,256]{2,1,0:T(8,128)(2,1)S(1)}, bf16[8,64,256]{2,1,0:T(8,128)(2,1)S(1)}, u32[]{:S(2)}, u32[]{:S(2)}) collective-permute-start(bf16[8,64,256]{2,1,0:T(8,128)(2,1)S(1)} %collective-permute-done.6.refs_1_), channel_id=1, source_target_pairs={{0,64},{1,65},{2,66},{3,67},{4,68},{5,69},{6,70},{7,71},{8,72},{9,... | collective-permute-start | bytes 786440 | tf_op jit(solution)/shard_map/ppermute | solution.py:439
  46.6 1.0 collective-permute-start.10
  47.6 4.1 %collective-permute-start.11 = (bf16[8,64,256]{2,1,0:T(8,128)(2,1)S(1)}, bf16[8,64,256]{2,1,0:T(8,128)(2,1)S(1)}, u32[]{:S(2)}, u32[]{:S(2)}) collective-permute-start(bf16[8,64,256]{2,1,0:T(8,128)(2,1)S(1)} %collective-permute-done.6.refs_1_), channel_id=1, source_target_pairs={{1,66},{2,65},{3,68},{4,67},{5,70},{6,69},{7,72},{8,71},{9,74},{10... | collective-permute-start | bytes 786440 | tf_op jit(solution)/shard_map/ppermute | solution.py:439
  51.7 0.0 collective-permute-done.12.refs_6_
  51.8 0.1 collective-permute-start.13
  51.9 0.7 collective-permute-done.7.refs_5_
  52.6 5.6 %collective-permute-start.8 = (bf16[8,64,256]{2,1,0:T(8,128)(2,1)S(1)}, bf16[8,64,256]{2,1,0:T(8,128)(2,1)S(1)}, u32[]{:S(2)}, u32[]{:S(2)}) collective-permute-start(bf16[8,64,256]{2,1,0:T(8,128)(2,1)S(1)} %collective-permute-done.7.refs_5_), channel_id=1, source_target_pairs={{1,66},{2,65},{3,68},{4,67},{5,70},{6,69},{7,72},{8,71},{9,74},{10... | collective-permute-start | bytes 786440 | tf_op jit(solution)/shard_map/ppermute | solution.py:439
  58.1 0.1 collective-permute-start.15
  58.2 1.2 %collective-permute-done.15.refs_11_ = bf16[2,64,256]{2,1,0:T(8,128)(2,1)S(1)} collective-permute-done((bf16[2,64,256]{2,1,0:T(8,128)(2,1)S(1)}, bf16[2,64,256]{2,1,0:T(8,128)(2,1)S(1)}, u32[]{:S(2)}, u32[]{:S(2)}) %collective-permute-start.15) | collective-permute-done | bytes 65568 | tf_op jit(solution)/shard_map/ppermute | solution.py:439
  59.5 3.7 %collective-permute-start.14 = (bf16[2,64,256]{2,1,0:T(8,128)(2,1)S(1)}, bf16[2,64,256]{2,1,0:T(8,128)(2,1)S(1)}, u32[]{:S(2)}, u32[]{:S(2)}) collective-permute-start(bf16[2,64,256]{2,1,0:T(8,128)(2,1)S(1)} %get-tuple-element.52), channel_id=1, source_target_pairs={{1,2},{2,1},{3,4},{4,3},{5,6},{6,5},{7,8},{8,7},{9,10},{10,9},{11,... | collective-permute-start | bytes 196616 | tf_op jit(solution)/shard_map/ppermute | solution.py:439
  63.2 0.6 shard_map.65
  63.8 4.0 %collective-permute-done.14.refs_8_ = bf16[2,64,256]{2,1,0:T(8,128)(2,1)S(1)} collective-permute-done((bf16[2,64,256]{2,1,0:T(8,128)(2,1)S(1)}, bf16[2,64,256]{2,1,0:T(8,128)(2,1)S(1)}, u32[]{:S(2)}, u32[]{:S(2)}) %collective-permute-start.14) | collective-permute-done | bytes 65568 | tf_op jit(solution)/shard_map/ppermute | solution.py:439
  67.7 0.0 collective-permute-done.10.refs_3_
  67.7 0.0 collective-permute-done.11.refs_4_
  67.7 0.0 collective-permute-done.13.refs_7_
  67.7 0.0 collective-permute-done.8.refs_0_
  67.8 5.3 %shard_map.69 = (bf16[8,64,256]{2,1,0:T(8,128)(2,1)S(1)}, bf16[2,64,256]{2,1,0:T(8,128)(2,1)}, bf16[20,192,256]{2,1,0:T(8,128)(2,1)S(1)}) custom-call(s32[4]{0:T(128)S(1)} %fusion.4.flags, s32[3,1]{1,0:T(4,128)S(1)} %copy.30.mask, bf16[8,256,256]{2,1,0:T(8,128)(2,1)S(1)} %get-tuple-element.43.cols, f32[64,256]{1,0:T(8,128)S(1)} %get-tuple-element.44.table, ...), custom_call_target="tpu_custom_call" | custom-call | flops 2300000000 | bytes 4000000 | tf_op jit(solution)/shard_map/pallas_call | solution.py:338
  73.1 3.0 %shard_map.70 = (bf16[8,64,256]{2,1,0:T(8,128)(2,1)S(1)}, bf16[2,64,256]{2,1,0:T(8,128)(2,1)}) custom-call(s32[4]{0:T(128)S(1)} %fusion.4.flags, s32[3,1]{1,0:T(4,128)S(1)} %copy.30.mask, bf16[192,576]{1,0:T(8,128)(2,1)S(1)} %get-tuple-element.39.wu, bf16[192,192]{1,0:T(8,128)(2,1)S(1)} %get-tuple-element.40.wm, ...), custom_call_target="tpu_custom_call" | custom-call | flops 700000000 | bytes 4000000 | tf_op jit(solution)/shard_map/pallas_call | solution.py:338
  76.1 3.7 %collective-permute-start.16 = (bf16[8,64,256]{2,1,0:T(8,128)(2,1)S(1)}, bf16[8,64,256]{2,1,0:T(8,128)(2,1)S(1)}, u32[]{:S(2)}, u32[]{:S(2)}) collective-permute-start(bf16[8,64,256]{2,1,0:T(8,128)(2,1)S(1)} %get-tuple-element.54.refs_0_.refs_1_.edge), channel_id=1, source_target_pairs={{1,2},{2,1},{3,4},{4,3},{5,6},{6,5},{7,8},{8,7},{9,10},{10,9},{11,... | collective-permute-start | bytes 786440 | tf_op jit(solution)/shard_map/ppermute | solution.py:439
  79.8 2.7 %collective-permute-start.18 = (bf16[2,2,4,32]{3,2,1,0:T(4,128)(2,1)S(1)}, bf16[2,2,4,32]{3,2,1,0:T(4,128)(2,1)S(1)}, u32[]{:S(2)}, u32[]{:S(2)}) collective-permute-start(bf16[2,2,4,32]{3,2,1,0:T(4,128)(2,1)S(1)} %get-tuple-element.57), channel_id=1, source_target_pairs={{0,112},{1,113},{2,114},{3,115},{4,116},{5,117},{6,118},{7,119},{8... | collective-permute-start | bytes 3080 | tf_op jit(solution)/shard_map/ppermute | solution.py:439
  82.4 0.0 collective-permute-start.19
  82.4 2.5 %collective-permute-done.18.first = bf16[2,2,4,32]{3,2,1,0:T(4,128)(2,1)S(1)} collective-permute-done((bf16[2,2,4,32]{3,2,1,0:T(4,128)(2,1)S(1)}, bf16[2,2,4,32]{3,2,1,0:T(4,128)(2,1)S(1)}, u32[]{:S(2)}, u32[]{:S(2)}) %collective-permute-start.18) | collective-permute-done | bytes 1056 | tf_op jit(solution)/shard_map/ppermute | solution.py:439
  84.9 3.2 %collective-permute-done.19.second = bf16[2,2,4,32]{3,2,1,0:T(4,128)(2,1)S(1)} collective-permute-done((bf16[2,2,4,32]{3,2,1,0:T(4,128)(2,1)S(1)}, bf16[2,2,4,32]{3,2,1,0:T(4,128)(2,1)S(1)}, u32[]{:S(2)}, u32[]{:S(2)}) %collective-permute-start.19) | collective-permute-done | bytes 1056 | tf_op jit(solution)/shard_map/ppermute | solution.py:439
  88.1 0.6 shard_map.71
  88.7 1.9 %shard_map.72 = (bf16[10,64,256]{2,1,0:T(8,128)(2,1)S(1)}, bf16[10,64,256]{2,1,0:T(8,128)(2,1)S(1)}) custom-call(s32[4]{0:T(128)S(1)} %fusion.4.flags, s32[3,1]{1,0:T(4,128)S(1)} %copy.30.mask, bf16[8,256,256]{2,1,0:T(8,128)(2,1)S(1)} %get-tuple-element.59.cols, f32[64,256]{1,0:T(8,128)S(1)} %get-tuple-element.60.table, ...), custom_call_target="tpu_custom_call" | custom-call | flops 800000000 | bytes 4000000 | tf_op jit(solution)/shard_map/pallas_call | solution.py:338
  90.6 0.1 collective-permute-start.20
  90.7 3.6 %collective-permute-start.21 = (bf16[10,64,256]{2,1,0:T(8,128)(2,1)S(1)}, bf16[10,64,256]{2,1,0:T(8,128)(2,1)S(1)}, u32[]{:S(2)}, u32[]{:S(2)}) collective-permute-start(bf16[10,64,256]{2,1,0:T(8,128)(2,1)S(1)} %get-tuple-element.62), channel_id=1, source_target_pairs={{0,112},{1,113},{2,114},{3,115},{4,116},{5,117},{6,118},{7,119},{8... | collective-permute-start | bytes 983048 | tf_op jit(solution)/shard_map/ppermute | solution.py:439
  94.3 1.9 %shard_map.74 = (bf16[10,64,256]{2,1,0:T(8,128)(2,1)S(1)}, bf16[10,64,256]{2,1,0:T(8,128)(2,1)S(1)}) custom-call(s32[4]{0:T(128)S(1)} %fusion.4.flags, s32[3,1]{1,0:T(4,128)S(1)} %copy.30.mask, bf16[8,256,256]{2,1,0:T(8,128)(2,1)S(1)} %get-tuple-element.59.cols, f32[64,256]{1,0:T(8,128)S(1)} %get-tuple-element.60.table, ...), custom_call_target="tpu_custom_call" | custom-call | flops 800000000 | bytes 4000000 | tf_op jit(solution)/shard_map/pallas_call | solution.py:338
  96.2 0.1 collective-permute-start.22
  96.3 3.6 %collective-permute-start.23 = (bf16[10,64,256]{2,1,0:T(8,128)(2,1)S(1)}, bf16[10,64,256]{2,1,0:T(8,128)(2,1)S(1)}, u32[]{:S(2)}, u32[]{:S(2)}) collective-permute-start(bf16[10,64,256]{2,1,0:T(8,128)(2,1)S(1)} %get-tuple-element.66), channel_id=1, source_target_pairs={{0,112},{1,113},{2,114},{3,115},{4,116},{5,117},{6,118},{7,119},{8... | collective-permute-start | bytes 983048 | tf_op jit(solution)/shard_map/ppermute | solution.py:439
  99.8 2.4 %collective-permute-done.20.earlier.inner_earlier = bf16[10,64,256]{2,1,0:T(8,128)(2,1)S(1)} collective-permute-done((bf16[10,64,256]{2,1,0:T(8,128)(2,1)S(1)}, bf16[10,64,256]{2,1,0:T(8,128)(2,1)S(1)}, u32[]{:S(2)}, u32[]{:S(2)}) %collective-permute-start.20) | collective-permute-done | bytes 327712 | tf_op jit(solution)/shard_map/ppermute | solution.py:439
  102.3 0.0 collective-permute-done.21.later.inner_later
  102.3 2.2 %shard_map.73 = (bf16[8,64,256]{2,1,0:T(8,128)(2,1)S(1)}, bf16[6,64,256]{2,1,0:T(8,128)(2,1)S(1)}) custom-call(s32[4]{0:T(128)S(1)} %fusion.4.flags, s32[3,1]{1,0:T(4,128)S(1)} %copy.30.mask, bf16[192,576]{1,0:T(8,128)(2,1)S(1)} %get-tuple-element.39.wu, bf16[192,192]{1,0:T(8,128)(2,1)S(1)} %get-tuple-element.40.wm, ...), custom_call_target="tpu_custom_call" | custom-call | flops 600000000 | bytes 4000000 | tf_op jit(solution)/shard_map/pallas_call | solution.py:338
  104.5 4.8 %collective-permute-done.22.earlier = bf16[10,64,256]{2,1,0:T(8,128)(2,1)S(1)} collective-permute-done((bf16[10,64,256]{2,1,0:T(8,128)(2,1)S(1)}, bf16[10,64,256]{2,1,0:T(8,128)(2,1)S(1)}, u32[]{:S(2)}, u32[]{:S(2)}) %collective-permute-start.22) | collective-permute-done | bytes 327712 | tf_op jit(solution)/shard_map/ppermute | solution.py:439
  109.3 3.6 %shard_map.75 = bf16[16,64,256]{2,1,0:T(8,128)(2,1)} custom-call(s32[4]{0:T(128)S(1)} %fusion.4.flags, s32[3,1]{1,0:T(4,128)S(1)} %copy.30.mask, bf16[192,576]{1,0:T(8,128)(2,1)S(1)} %get-tuple-element.39.wu, bf16[192,192]{1,0:T(8,128)(2,1)S(1)} %get-tuple-element.40.wm, bf16[8,64,256]{2,1,0:T(8,128)(2,1)S(1)} %collective-permute-done.16.refs_0_.outer, ...), custom_call_target="tpu_custom_call" | custom-call | flops 900000000 | bytes 4000000 | tf_op jit(solution)/shard_map/pallas_call | solution.py:338
  (24 shorter events, 0.2 us)
Async XLA Ops:
  0.0 13.1 %copy-start.2 = (s32[3,1]{0,1:T(1,128)S(1)}, s32[3,1]{0,1:T(1,128)}, u32[]{:S(2)}) copy-start(s32[3,1]{0,1:T(1,128)} %param.9) | copy-start | bytes 40
  0.0 13.2 %copy-start = (bf16[3,3,64,192]{3,2,1,0:T(8,128)(2,1)S(1)}, bf16[3,3,64,192]{3,2,1,0:T(8,128)(2,1)}, u32[]{:S(2)}) copy-start(bf16[3,3,64,192]{3,2,1,0:T(8,128)(2,1)} %uniting.1) | copy-start | bytes 663556
  0.0 13.2 %copy-start.1 = (bf16[3,3,64,64]{3,2,1,0:T(8,128)(2,1)S(1)}, bf16[3,3,64,64]{3,2,1,0:T(8,128)(2,1)}, u32[]{:S(2)}) copy-start(bf16[3,3,64,64]{3,2,1,0:T(8,128)(2,1)} %mixing.1) | copy-start | bytes 221188
  1.2 20.2 %collective-permute-start.2 = (bf16[8,64,256]{2,1,0:T(8,128)(2,1)S(1)}, bf16[8,64,256]{2,1,0:T(8,128)(2,1)S(1)}, u32[]{:S(2)}, u32[]{:S(2)}) collective-permute-start(bf16[8,64,256]{2,1,0:T(8,128)(2,1)S(1)} %get-tuple-element.70.refs_5_), channel_id=1, source_target_pairs={{1,66},{2,65},{3,68},{4,67},{5,70},{6,69},{7,72},{8,71},{9,74},{10... | collective-permute-start | bytes 786440 | tf_op jit(solution)/shard_map/ppermute | solution.py:439
  4.8 16.5 %collective-permute-start.3 = (bf16[8,64,256]{2,1,0:T(8,128)(2,1)S(1)}, bf16[8,64,256]{2,1,0:T(8,128)(2,1)S(1)}, u32[]{:S(2)}, u32[]{:S(2)}) collective-permute-start(bf16[8,64,256]{2,1,0:T(8,128)(2,1)S(1)} %get-tuple-element.70.refs_5_), channel_id=1, source_target_pairs={{0,64},{1,65},{2,66},{3,67},{4,68},{5,69},{6,70},{7,71},{8,72},{9,... | collective-permute-start | bytes 786440 | tf_op jit(solution)/shard_map/ppermute | solution.py:439
  7.3 6.0 %collective-permute-start = (bf16[3,64,256]{2,1,0:T(8,128)(2,1)S(1)}, bf16[3,64,256]{2,1,0:T(8,128)(2,1)S(1)}, u32[]{:S(2)}, u32[]{:S(2)}) collective-permute-start(bf16[3,64,256]{2,1,0:T(8,128)(2,1)S(1)} %pad_maximum_fusion), channel_id=1, source_target_pairs={{0,1},{1,0},{2,3},{3,2},{4,5},{5,4},{6,7},{7,6},{8,9},{9,8},{10,11... | collective-permute-start | bytes 294920 | tf_op jit(solution)/shard_map/ppermute | solution.py:439
  7.6 9.8 %collective-permute-start.1 = (bf16[3,64,256]{2,1,0:T(8,128)(2,1)S(1)}, bf16[3,64,256]{2,1,0:T(8,128)(2,1)S(1)}, u32[]{:S(2)}, u32[]{:S(2)}) collective-permute-start(bf16[3,64,256]{2,1,0:T(8,128)(2,1)S(1)} %pad_maximum_fusion.1), channel_id=1, source_target_pairs={{1,2},{2,1},{3,4},{4,3},{5,6},{6,5},{7,8},{8,7},{9,10},{10,9},{11,... | collective-permute-start | bytes 294920 | tf_op jit(solution)/shard_map/ppermute | solution.py:439
  12.9 7.6 %collective-permute-start.4 = (bf16[8,64,256]{2,1,0:T(8,128)(2,1)S(1)}, bf16[8,64,256]{2,1,0:T(8,128)(2,1)S(1)}, u32[]{:S(2)}, u32[]{:S(2)}) collective-permute-start(bf16[8,64,256]{2,1,0:T(8,128)(2,1)S(1)} %get-tuple-element.69.refs_6_), channel_id=1, source_target_pairs={{0,64},{1,65},{2,66},{3,67},{4,68},{5,69},{6,70},{7,71},{8,72},{9,... | collective-permute-start | bytes 786440 | tf_op jit(solution)/shard_map/ppermute | solution.py:439
  20.5 1.5 %collective-permute-start.5 = (bf16[8,64,256]{2,1,0:T(8,128)(2,1)S(1)}, bf16[8,64,256]{2,1,0:T(8,128)(2,1)S(1)}, u32[]{:S(2)}, u32[]{:S(2)}) collective-permute-start(bf16[8,64,256]{2,1,0:T(8,128)(2,1)S(1)} %collective-permute-done.4.refs_2_), channel_id=1, source_target_pairs={{0,1},{1,0},{2,3},{3,2},{4,5},{5,4},{6,7},{7,6},{8,9},{9,8},{10,11... | collective-permute-start | bytes 786440 | tf_op jit(solution)/shard_map/ppermute | solution.py:439
  29.0 10.2 %collective-permute-start.9 = (bf16[8,64,256]{2,1,0:T(8,128)(2,1)S(1)}, bf16[8,64,256]{2,1,0:T(8,128)(2,1)S(1)}, u32[]{:S(2)}, u32[]{:S(2)}) collective-permute-start(bf16[8,64,256]{2,1,0:T(8,128)(2,1)S(1)} %get-tuple-element.51.refs_10_), channel_id=1, source_target_pairs={{0,32},{1,33},{2,34},{3,35},{4,36},{5,37},{6,38},{7,39},{8,40},{9,... | collective-permute-start | bytes 786440 | tf_op jit(solution)/shard_map/ppermute | solution.py:439
  32.7 12.1 %collective-permute-start.6 = (bf16[8,64,256]{2,1,0:T(8,128)(2,1)S(1)}, bf16[8,64,256]{2,1,0:T(8,128)(2,1)S(1)}, u32[]{:S(2)}, u32[]{:S(2)}) collective-permute-start(bf16[8,64,256]{2,1,0:T(8,128)(2,1)S(1)} %get-tuple-element.49.refs_9_), channel_id=1, source_target_pairs={{0,32},{1,33},{2,34},{3,35},{4,36},{5,37},{6,38},{7,39},{8,40},{9,... | collective-permute-start | bytes 786440 | tf_op jit(solution)/shard_map/ppermute | solution.py:439
  39.2 12.5 %collective-permute-start.12 = (bf16[8,64,256]{2,1,0:T(8,128)(2,1)S(1)}, bf16[8,64,256]{2,1,0:T(8,128)(2,1)S(1)}, u32[]{:S(2)}, u32[]{:S(2)}) collective-permute-start(bf16[8,64,256]{2,1,0:T(8,128)(2,1)S(1)} %collective-permute-done.9.refs_2_), channel_id=1, source_target_pairs={{0,64},{1,65},{2,66},{3,67},{4,68},{5,69},{6,70},{7,71},{8,72},{9,... | collective-permute-start | bytes 786440 | tf_op jit(solution)/shard_map/ppermute | solution.py:439
  44.9 7.7 %collective-permute-start.7 = (bf16[8,64,256]{2,1,0:T(8,128)(2,1)S(1)}, bf16[8,64,256]{2,1,0:T(8,128)(2,1)S(1)}, u32[]{:S(2)}, u32[]{:S(2)}) collective-permute-start(bf16[8,64,256]{2,1,0:T(8,128)(2,1)S(1)} %collective-permute-done.6.refs_1_), channel_id=1, source_target_pairs={{0,64},{1,65},{2,66},{3,67},{4,68},{5,69},{6,70},{7,71},{8,72},{9,... | collective-permute-start | bytes 786440 | tf_op jit(solution)/shard_map/ppermute | solution.py:439
  46.6 21.1 %collective-permute-start.10 = (bf16[8,64,256]{2,1,0:T(8,128)(2,1)S(1)}, bf16[8,64,256]{2,1,0:T(8,128)(2,1)S(1)}, u32[]{:S(2)}, u32[]{:S(2)}) collective-permute-start(bf16[8,64,256]{2,1,0:T(8,128)(2,1)S(1)} %collective-permute-done.9.refs_2_), channel_id=1, source_target_pairs={{0,1},{1,0},{2,3},{3,2},{4,5},{5,4},{6,7},{7,6},{8,9},{9,8},{10,11... | collective-permute-start | bytes 786440 | tf_op jit(solution)/shard_map/ppermute | solution.py:439
  47.6 20.1 %collective-permute-start.11 = (bf16[8,64,256]{2,1,0:T(8,128)(2,1)S(1)}, bf16[8,64,256]{2,1,0:T(8,128)(2,1)S(1)}, u32[]{:S(2)}, u32[]{:S(2)}) collective-permute-start(bf16[8,64,256]{2,1,0:T(8,128)(2,1)S(1)} %collective-permute-done.6.refs_1_), channel_id=1, source_target_pairs={{1,66},{2,65},{3,68},{4,67},{5,70},{6,69},{7,72},{8,71},{9,74},{10... | collective-permute-start | bytes 786440 | tf_op jit(solution)/shard_map/ppermute | solution.py:439
  51.8 16.0 %collective-permute-start.13 = (bf16[8,64,256]{2,1,0:T(8,128)(2,1)S(1)}, bf16[8,64,256]{2,1,0:T(8,128)(2,1)S(1)}, u32[]{:S(2)}, u32[]{:S(2)}) collective-permute-start(bf16[8,64,256]{2,1,0:T(8,128)(2,1)S(1)} %collective-permute-done.12.refs_6_), channel_id=1, source_target_pairs={{0,1},{1,0},{2,3},{3,2},{4,5},{5,4},{6,7},{7,6},{8,9},{9,8},{10,11... | collective-permute-start | bytes 786440 | tf_op jit(solution)/shard_map/ppermute | solution.py:439
  52.6 15.2 %collective-permute-start.8 = (bf16[8,64,256]{2,1,0:T(8,128)(2,1)S(1)}, bf16[8,64,256]{2,1,0:T(8,128)(2,1)S(1)}, u32[]{:S(2)}, u32[]{:S(2)}) collective-permute-start(bf16[8,64,256]{2,1,0:T(8,128)(2,1)S(1)} %collective-permute-done.7.refs_5_), channel_id=1, source_target_pairs={{1,66},{2,65},{3,68},{4,67},{5,70},{6,69},{7,72},{8,71},{9,74},{10... | collective-permute-start | bytes 786440 | tf_op jit(solution)/shard_map/ppermute | solution.py:439
  58.1 1.3 %collective-permute-start.15 = (bf16[2,64,256]{2,1,0:T(8,128)(2,1)S(1)}, bf16[2,64,256]{2,1,0:T(8,128)(2,1)S(1)}, u32[]{:S(2)}, u32[]{:S(2)}) collective-permute-start(bf16[2,64,256]{2,1,0:T(8,128)(2,1)S(1)} %get-tuple-element.53), channel_id=1, source_target_pairs={{0,1},{1,0},{2,3},{3,2},{4,5},{5,4},{6,7},{7,6},{8,9},{9,8},{10,11... | collective-permute-start | bytes 196616 | tf_op jit(solution)/shard_map/ppermute | solution.py:439
  59.5 8.3 %collective-permute-start.14 = (bf16[2,64,256]{2,1,0:T(8,128)(2,1)S(1)}, bf16[2,64,256]{2,1,0:T(8,128)(2,1)S(1)}, u32[]{:S(2)}, u32[]{:S(2)}) collective-permute-start(bf16[2,64,256]{2,1,0:T(8,128)(2,1)S(1)} %get-tuple-element.52), channel_id=1, source_target_pairs={{1,2},{2,1},{3,4},{4,3},{5,6},{6,5},{7,8},{8,7},{9,10},{10,9},{11,... | collective-permute-start | bytes 196616 | tf_op jit(solution)/shard_map/ppermute | solution.py:439
  76.1 12.6 %collective-permute-start.17 = (bf16[8,64,256]{2,1,0:T(8,128)(2,1)S(1)}, bf16[8,64,256]{2,1,0:T(8,128)(2,1)S(1)}, u32[]{:S(2)}, u32[]{:S(2)}) collective-permute-start(bf16[8,64,256]{2,1,0:T(8,128)(2,1)S(1)} %get-tuple-element.56.refs_1_.inner.refs_2_), channel_id=1, source_target_pairs={{0,1},{1,0},{2,3},{3,2},{4,5},{5,4},{6,7},{7,6},{8,9},{9,8},{10,11... | collective-permute-start | bytes 786440 | tf_op jit(solution)/shard_map/ppermute | solution.py:439
  76.1 18.2 %collective-permute-start.16 = (bf16[8,64,256]{2,1,0:T(8,128)(2,1)S(1)}, bf16[8,64,256]{2,1,0:T(8,128)(2,1)S(1)}, u32[]{:S(2)}, u32[]{:S(2)}) collective-permute-start(bf16[8,64,256]{2,1,0:T(8,128)(2,1)S(1)} %get-tuple-element.54.refs_0_.refs_1_.edge), channel_id=1, source_target_pairs={{1,2},{2,1},{3,4},{4,3},{5,6},{6,5},{7,8},{8,7},{9,10},{10,9},{11,... | collective-permute-start | bytes 786440 | tf_op jit(solution)/shard_map/ppermute | solution.py:439
  79.8 5.1 %collective-permute-start.18 = (bf16[2,2,4,32]{3,2,1,0:T(4,128)(2,1)S(1)}, bf16[2,2,4,32]{3,2,1,0:T(4,128)(2,1)S(1)}, u32[]{:S(2)}, u32[]{:S(2)}) collective-permute-start(bf16[2,2,4,32]{3,2,1,0:T(4,128)(2,1)S(1)} %get-tuple-element.57), channel_id=1, source_target_pairs={{0,112},{1,113},{2,114},{3,115},{4,116},{5,117},{6,118},{7,119},{8... | collective-permute-start | bytes 3080 | tf_op jit(solution)/shard_map/ppermute | solution.py:439
  82.4 5.7 %collective-permute-start.19 = (bf16[2,2,4,32]{3,2,1,0:T(4,128)(2,1)S(1)}, bf16[2,2,4,32]{3,2,1,0:T(4,128)(2,1)S(1)}, u32[]{:S(2)}, u32[]{:S(2)}) collective-permute-start(bf16[2,2,4,32]{3,2,1,0:T(4,128)(2,1)S(1)} %get-tuple-element.58), channel_id=1, source_target_pairs={{0,16},{1,17},{2,18},{3,19},{4,20},{5,21},{6,22},{7,23},{8,24},{9,... | collective-permute-start | bytes 3080 | tf_op jit(solution)/shard_map/ppermute | solution.py:439
  90.6 11.6 %collective-permute-start.20 = (bf16[10,64,256]{2,1,0:T(8,128)(2,1)S(1)}, bf16[10,64,256]{2,1,0:T(8,128)(2,1)S(1)}, u32[]{:S(2)}, u32[]{:S(2)}) collective-permute-start(bf16[10,64,256]{2,1,0:T(8,128)(2,1)S(1)} %get-tuple-element.61), channel_id=1, source_target_pairs={{0,16},{1,17},{2,18},{3,19},{4,20},{5,21},{6,22},{7,23},{8,24},{9,... | collective-permute-start | bytes 983048 | tf_op jit(solution)/shard_map/ppermute | solution.py:439
  90.7 11.5 %collective-permute-start.21 = (bf16[10,64,256]{2,1,0:T(8,128)(2,1)S(1)}, bf16[10,64,256]{2,1,0:T(8,128)(2,1)S(1)}, u32[]{:S(2)}, u32[]{:S(2)}) collective-permute-start(bf16[10,64,256]{2,1,0:T(8,128)(2,1)S(1)} %get-tuple-element.62), channel_id=1, source_target_pairs={{0,112},{1,113},{2,114},{3,115},{4,116},{5,117},{6,118},{7,119},{8... | collective-permute-start | bytes 983048 | tf_op jit(solution)/shard_map/ppermute | solution.py:439
  96.2 13.1 %collective-permute-start.22 = (bf16[10,64,256]{2,1,0:T(8,128)(2,1)S(1)}, bf16[10,64,256]{2,1,0:T(8,128)(2,1)S(1)}, u32[]{:S(2)}, u32[]{:S(2)}) collective-permute-start(bf16[10,64,256]{2,1,0:T(8,128)(2,1)S(1)} %get-tuple-element.65), channel_id=1, source_target_pairs={{0,16},{1,17},{2,18},{3,19},{4,20},{5,21},{6,22},{7,23},{8,24},{9,... | collective-permute-start | bytes 983048 | tf_op jit(solution)/shard_map/ppermute | solution.py:439
  96.3 13.0 %collective-permute-start.23 = (bf16[10,64,256]{2,1,0:T(8,128)(2,1)S(1)}, bf16[10,64,256]{2,1,0:T(8,128)(2,1)S(1)}, u32[]{:S(2)}, u32[]{:S(2)}) collective-permute-start(bf16[10,64,256]{2,1,0:T(8,128)(2,1)S(1)} %get-tuple-element.66), channel_id=1, source_target_pairs={{0,112},{1,113},{2,114},{3,115},{4,116},{5,117},{6,118},{7,119},{8... | collective-permute-start | bytes 983048 | tf_op jit(solution)/shard_map/ppermute | solution.py:439

commit v11 on v10

--- a/solution.py
+++ b/solution.py
@@ -296,7 +296,6 @@
     outer,
     edge,
     inner,
-    near,
     inner_earlier,
     inner_later,
     inner_act,
@@ -311,26 +310,20 @@
     part = turned
     joined[pl.ds(turn(turned, 0, 18), 2), OWN] = outer[pl.ds(turn(turned, 6, 6), 2)]
     joined[pl.ds(turn(turned, 2, 12), 8), OWN] = edge[...]
-    joined[pl.ds(turn(turned, 10, 12), 8), OWN] = inner[...]
-    joined[pl.ds(turn(turned, 18, 18), 2), OWN] = near[pl.ds(turn(turned, 0, 6), 2)]
+    middle = pl.ds(10 - 2 * part, 2)
+    joined[middle, OWN] = inner[pl.ds(6 * part, 2)]
     joined[pl.ds(10 * part, 10), 0:CH] = earlier[...]
     joined[pl.ds(10 * part, 10), CH : 2 * CH] = later[...]
-    joined[pl.ds(10 - 10 * part, 10), 0:CH] = inner_earlier[...]
-    joined[pl.ds(10 - 10 * part, 10), CH : 2 * CH] = inner_later[...]
-    act[pl.ds(10 - 10 * part, 8)] = inner_act[...]
+    joined[middle, 0:CH] = inner_earlier[pl.ds(8 * part, 2)]
+    joined[middle, CH : 2 * CH] = inner_later[pl.ds(8 * part, 2)]
+    act[pl.ds(10 - 4 * part, 2)] = inner_act[pl.ds(6 * part, 2)]
     out[pl.ds(10 - 10 * part, 6)] = inner_rows[...]
     conv = Convolutions(flags, mask[0, 0], wu, wm, joined, act)
 
-    @pl.loop(0, 2)
-    def _(n):
-        for k in range(5):
-            conv.activate(8 * part + 5 * n + k)
-
-    @pl.loop(0, 2)
-    def _(n):
-        for k in range(5):
-            y = 6 * part + 5 * n + k
-            out[y] = conv.finish(y)
+    for k in range(10):
+        conv.activate(8 * part + k)
+    for k in range(10):
+        out[6 * part + k] = conv.finish(6 * part + k)
 
 
 def on_core(kernel, out_shape, scratch, cost, operands, interpret):
@@ -589,7 +582,6 @@
             outer,
             edge,
             inner,
-            near,
             inner_earlier,
             inner_later,
             inner_act,

time: 115 us -> 115 us (level)
  no operation moved by 1% of the time
where the time goes in v11:
time: 115 us; the launch traced here: 112 us
  starting transfers between devices  45.4 us (39%)
  waiting for transfers between devices  36.8 us (32%)
  Pallas kernels  26.3 us (23%)
  local copies, waits for them, and re-layouts  2.52 us (2%)
    ppermute x24, starting transfers between devices, send(): return lax.ppermute(x, ('tm', 'rows'), route)  45.4 us
    ppermute x24, waiting for transfers between devices, send(): return lax.ppermute(x, ('tm', 'rows'), route)  36.8 us
    pallas_call x8, Pallas kernels, on_core(): pl.pallas_call(kernel, out_shape=out_shape, in_specs=[pl.BlockSpec(memory...  24.4 us
  transfers between devices with their start and end apart: 24, of which 12 were waited for; matrix products, arithmetic and copies ran while one was open for 2% of the time, Pallas kernels for 7%

profile of v11, /device:TPU:7, one launch (start us, length us, event | category | flops | bytes accessed | tf_op | source)
XLA Modules:
  0.0 112.3 jit_solution(251801260526732988)
XLA Ops:
  0.0 1.1 dynamic-slice_bitcast_fusion
  1.2 3.7 %collective-permute-start.2 = (bf16[8,64,256]{2,1,0:T(8,128)(2,1)S(1)}, bf16[8,64,256]{2,1,0:T(8,128)(2,1)S(1)}, u32[]{:S(2)}, u32[]{:S(2)}) collective-permute-start(bf16[8,64,256]{2,1,0:T(8,128)(2,1)S(1)} %get-tuple-element.70.refs_5_), channel_id=1, source_target_pairs={{1,66},{2,65},{3,68},{4,67},{5,70},{6,69},{7,72},{8,71},{9,74},{10... | collective-permute-start | bytes 786440 | tf_op jit(solution)/shard_map/ppermute | solution.py:432
  4.8 0.7 collective-permute-start.3
  5.5 0.7 fusion
  6.3 0.1 select_n.95
  6.4 0.9 dynamic-slice_bitcast_fusion.3
  7.3 0.1 collective-permute-start
  7.5 0.1 select_n.98
  7.6 5.3 %collective-permute-start.1 = (bf16[3,64,256]{2,1,0:T(8,128)(2,1)S(1)}, bf16[3,64,256]{2,1,0:T(8,128)(2,1)S(1)}, u32[]{:S(2)}, u32[]{:S(2)}) collective-permute-start(bf16[3,64,256]{2,1,0:T(8,128)(2,1)S(1)} %pad_maximum_fusion.1), channel_id=1, source_target_pairs={{1,2},{2,1},{3,4},{4,3},{5,6},{6,5},{7,8},{8,7},{9,10},{10,9},{11,... | collective-permute-start | bytes 294920 | tf_op jit(solution)/shard_map/ppermute | solution.py:432
  12.9 0.1 collective-permute-start.4
  13.1 0.1 copy.30.mask
  13.2 0.1 shard_map.64
  13.3 0.0 collective-permute-done.refs_7_
  13.3 4.1 %collective-permute-done.1.refs_4_ = bf16[3,64,256]{2,1,0:T(8,128)(2,1)S(1)} collective-permute-done((bf16[3,64,256]{2,1,0:T(8,128)(2,1)S(1)}, bf16[3,64,256]{2,1,0:T(8,128)(2,1)S(1)}, u32[]{:S(2)}, u32[]{:S(2)}) %collective-permute-start.1) | collective-permute-done | bytes 98336 | tf_op jit(solution)/shard_map/ppermute | solution.py:432
  17.4 0.1 select_n.100
  17.5 0.1 select_n.102
  17.6 2.9 %collective-permute-done.4.refs_2_ = bf16[8,64,256]{2,1,0:T(8,128)(2,1)S(1)} collective-permute-done((bf16[8,64,256]{2,1,0:T(8,128)(2,1)S(1)}, bf16[8,64,256]{2,1,0:T(8,128)(2,1)S(1)}, u32[]{:S(2)}, u32[]{:S(2)}) %collective-permute-start.4) | collective-permute-done | bytes 262176 | tf_op jit(solution)/shard_map/ppermute | solution.py:432
  20.5 0.2 collective-permute-start.5
  20.7 0.1 pad_maximum_fusion.2
  20.7 0.6 shard_map.66
  21.3 0.0 collective-permute-done.3.refs_1_
  21.4 0.7 collective-permute-done.5.refs_3_
  22.0 4.6 %shard_map.67 = (bf16[8,64,256]{2,1,0:T(8,128)(2,1)S(1)}, bf16[2,64,256]{2,1,0:T(8,128)(2,1)S(1)}, bf16[20,192,256]{2,1,0:T(8,128)(2,1)S(1)}) custom-call(s32[4]{0:T(128)S(1)} %fusion.4.flags, s32[3,1]{1,0:T(4,128)S(1)} %copy.30.mask, bf16[8,256,256]{2,1,0:T(8,128)(2,1)S(1)} %get-tuple-element.47.cols, f32[64,256]{1,0:T(8,128)S(1)} %get-tuple-element.48.table, ...), custom_call_target="tpu_custom_call" | custom-call | flops 2300000000 | bytes 4000000 | tf_op jit(solution)/shard_map/pallas_call | solution.py:331
  26.7 2.4 %shard_map.68 = (bf16[8,64,256]{2,1,0:T(8,128)(2,1)S(1)}, bf16[2,64,256]{2,1,0:T(8,128)(2,1)S(1)}) custom-call(s32[4]{0:T(128)S(1)} %fusion.4.flags, s32[3,1]{1,0:T(4,128)S(1)} %copy.30.mask, bf16[192,576]{1,0:T(8,128)(2,1)S(1)} %get-tuple-element.39.wu, bf16[192,192]{1,0:T(8,128)(2,1)S(1)} %get-tuple-element.40.wm, ...), custom_call_target="tpu_custom_call" | custom-call | flops 700000000 | bytes 4000000 | tf_op jit(solution)/shard_map/pallas_call | solution.py:331
  29.0 3.7 %collective-permute-start.9 = (bf16[8,64,256]{2,1,0:T(8,128)(2,1)S(1)}, bf16[8,64,256]{2,1,0:T(8,128)(2,1)S(1)}, u32[]{:S(2)}, u32[]{:S(2)}) collective-permute-start(bf16[8,64,256]{2,1,0:T(8,128)(2,1)S(1)} %get-tuple-element.51.refs_10_), channel_id=1, source_target_pairs={{0,32},{1,33},{2,34},{3,35},{4,36},{5,37},{6,38},{7,39},{8,40},{9,... | collective-permute-start | bytes 786440 | tf_op jit(solution)/shard_map/ppermute | solution.py:432
  32.7 0.1 collective-permute-start.6
  32.8 6.4 %collective-permute-done.9.refs_2_ = bf16[8,64,256]{2,1,0:T(8,128)(2,1)S(1)} collective-permute-done((bf16[8,64,256]{2,1,0:T(8,128)(2,1)S(1)}, bf16[8,64,256]{2,1,0:T(8,128)(2,1)S(1)}, u32[]{:S(2)}, u32[]{:S(2)}) %collective-permute-start.9) | collective-permute-done | bytes 262176 | tf_op jit(solution)/shard_map/ppermute | solution.py:432
  39.2 1.7 %collective-permute-start.12 = (bf16[8,64,256]{2,1,0:T(8,128)(2,1)S(1)}, bf16[8,64,256]{2,1,0:T(8,128)(2,1)S(1)}, u32[]{:S(2)}, u32[]{:S(2)}) collective-permute-start(bf16[8,64,256]{2,1,0:T(8,128)(2,1)S(1)} %collective-permute-done.9.refs_2_), channel_id=1, source_target_pairs={{0,64},{1,65},{2,66},{3,67},{4,68},{5,69},{6,70},{7,71},{8,72},{9,... | collective-permute-start | bytes 786440 | tf_op jit(solution)/shard_map/ppermute | solution.py:432
  41.0 3.9 %collective-permute-done.6.refs_1_ = bf16[8,64,256]{2,1,0:T(8,128)(2,1)S(1)} collective-permute-done((bf16[8,64,256]{2,1,0:T(8,128)(2,1)S(1)}, bf16[8,64,256]{2,1,0:T(8,128)(2,1)S(1)}, u32[]{:S(2)}, u32[]{:S(2)}) %collective-permute-start.6) | collective-permute-done | bytes 262176 | tf_op jit(solution)/shard_map/ppermute | solution.py:432
  44.9 1.7 %collective-permute-start.7 = (bf16[8,64,256]{2,1,0:T(8,128)(2,1)S(1)}, bf16[8,64,256]{2,1,0:T(8,128)(2,1)S(1)}, u32[]{:S(2)}, u32[]{:S(2)}) collective-permute-start(bf16[8,64,256]{2,1,0:T(8,128)(2,1)S(1)} %collective-permute-done.6.refs_1_), channel_id=1, source_target_pairs={{0,64},{1,65},{2,66},{3,67},{4,68},{5,69},{6,70},{7,71},{8,72},{9,... | collective-permute-start | bytes 786440 | tf_op jit(solution)/shard_map/ppermute | solution.py:432
  46.6 1.0 collective-permute-start.10
  47.6 4.1 %collective-permute-start.11 = (bf16[8,64,256]{2,1,0:T(8,128)(2,1)S(1)}, bf16[8,64,256]{2,1,0:T(8,128)(2,1)S(1)}, u32[]{:S(2)}, u32[]{:S(2)}) collective-permute-start(bf16[8,64,256]{2,1,0:T(8,128)(2,1)S(1)} %collective-permute-done.6.refs_1_), channel_id=1, source_target_pairs={{1,66},{2,65},{3,68},{4,67},{5,70},{6,69},{7,72},{8,71},{9,74},{10... | collective-permute-start | bytes 786440 | tf_op jit(solution)/shard_map/ppermute | solution.py:432
  51.7 0.0 collective-permute-done.12.refs_6_
  51.8 0.1 collective-permute-start.13
  51.9 0.7 collective-permute-done.7.refs_5_
  52.6 5.6 %collective-permute-start.8 = (bf16[8,64,256]{2,1,0:T(8,128)(2,1)S(1)}, bf16[8,64,256]{2,1,0:T(8,128)(2,1)S(1)}, u32[]{:S(2)}, u32[]{:S(2)}) collective-permute-start(bf16[8,64,256]{2,1,0:T(8,128)(2,1)S(1)} %collective-permute-done.7.refs_5_), channel_id=1, source_target_pairs={{1,66},{2,65},{3,68},{4,67},{5,70},{6,69},{7,72},{8,71},{9,74},{10... | collective-permute-start | bytes 786440 | tf_op jit(solution)/shard_map/ppermute | solution.py:432
  58.1 0.1 collective-permute-start.15
  58.2 1.2 %collective-permute-done.15.refs_11_ = bf16[2,64,256]{2,1,0:T(8,128)(2,1)S(1)} collective-permute-done((bf16[2,64,256]{2,1,0:T(8,128)(2,1)S(1)}, bf16[2,64,256]{2,1,0:T(8,128)(2,1)S(1)}, u32[]{:S(2)}, u32[]{:S(2)}) %collective-permute-start.15) | collective-permute-done | bytes 65568 | tf_op jit(solution)/shard_map/ppermute | solution.py:432
  59.5 3.7 %collective-permute-start.14 = (bf16[2,64,256]{2,1,0:T(8,128)(2,1)S(1)}, bf16[2,64,256]{2,1,0:T(8,128)(2,1)S(1)}, u32[]{:S(2)}, u32[]{:S(2)}) collective-permute-start(bf16[2,64,256]{2,1,0:T(8,128)(2,1)S(1)} %get-tuple-element.52), channel_id=1, source_target_pairs={{1,2},{2,1},{3,4},{4,3},{5,6},{6,5},{7,8},{8,7},{9,10},{10,9},{11,... | collective-permute-start | bytes 196616 | tf_op jit(solution)/shard_map/ppermute | solution.py:432
  63.2 0.6 shard_map.65
  63.8 4.0 %collective-permute-done.14.refs_8_ = bf16[2,64,256]{2,1,0:T(8,128)(2,1)S(1)} collective-permute-done((bf16[2,64,256]{2,1,0:T(8,128)(2,1)S(1)}, bf16[2,64,256]{2,1,0:T(8,128)(2,1)S(1)}, u32[]{:S(2)}, u32[]{:S(2)}) %collective-permute-start.14) | collective-permute-done | bytes 65568 | tf_op jit(solution)/shard_map/ppermute | solution.py:432
  67.7 0.0 collective-permute-done.10.refs_3_
  67.7 0.0 collective-permute-done.11.refs_4_
  67.7 0.0 collective-permute-done.13.refs_7_
  67.7 0.0 collective-permute-done.8.refs_0_
  67.8 5.3 %shard_map.69 = (bf16[8,64,256]{2,1,0:T(8,128)(2,1)S(1)}, bf16[2,64,256]{2,1,0:T(8,128)(2,1)}, bf16[20,192,256]{2,1,0:T(8,128)(2,1)S(1)}) custom-call(s32[4]{0:T(128)S(1)} %fusion.4.flags, s32[3,1]{1,0:T(4,128)S(1)} %copy.30.mask, bf16[8,256,256]{2,1,0:T(8,128)(2,1)S(1)} %get-tuple-element.43.cols, f32[64,256]{1,0:T(8,128)S(1)} %get-tuple-element.44.table, ...), custom_call_target="tpu_custom_call" | custom-call | flops 2300000000 | bytes 4000000 | tf_op jit(solution)/shard_map/pallas_call | solution.py:331
  73.1 3.0 %shard_map.70 = (bf16[8,64,256]{2,1,0:T(8,128)(2,1)S(1)}, bf16[2,64,256]{2,1,0:T(8,128)(2,1)}) custom-call(s32[4]{0:T(128)S(1)} %fusion.4.flags, s32[3,1]{1,0:T(4,128)S(1)} %copy.30.mask, bf16[192,576]{1,0:T(8,128)(2,1)S(1)} %get-tuple-element.39.wu, bf16[192,192]{1,0:T(8,128)(2,1)S(1)} %get-tuple-element.40.wm, ...), custom_call_target="tpu_custom_call" | custom-call | flops 700000000 | bytes 4000000 | tf_op jit(solution)/shard_map/pallas_call | solution.py:331
  76.1 3.7 %collective-permute-start.16 = (bf16[8,64,256]{2,1,0:T(8,128)(2,1)S(1)}, bf16[8,64,256]{2,1,0:T(8,128)(2,1)S(1)}, u32[]{:S(2)}, u32[]{:S(2)}) collective-permute-start(bf16[8,64,256]{2,1,0:T(8,128)(2,1)S(1)} %get-tuple-element.54.refs_0_.refs_1_.edge), channel_id=1, source_target_pairs={{1,2},{2,1},{3,4},{4,3},{5,6},{6,5},{7,8},{8,7},{9,10},{10,9},{11,... | collective-permute-start | bytes 786440 | tf_op jit(solution)/shard_map/ppermute | solution.py:432
  79.8 2.7 %collective-permute-start.17 = (bf16[2,2,4,32]{3,2,1,0:T(4,128)(2,1)S(1)}, bf16[2,2,4,32]{3,2,1,0:T(4,128)(2,1)S(1)}, u32[]{:S(2)}, u32[]{:S(2)}) collective-permute-start(bf16[2,2,4,32]{3,2,1,0:T(4,128)(2,1)S(1)} %get-tuple-element.57), channel_id=1, source_target_pairs={{0,112},{1,113},{2,114},{3,115},{4,116},{5,117},{6,118},{7,119},{8... | collective-permute-start | bytes 3080 | tf_op jit(solution)/shard_map/ppermute | solution.py:432
  82.4 0.0 collective-permute-start.18
  82.4 2.5 %collective-permute-done.17.first = bf16[2,2,4,32]{3,2,1,0:T(4,128)(2,1)S(1)} collective-permute-done((bf16[2,2,4,32]{3,2,1,0:T(4,128)(2,1)S(1)}, bf16[2,2,4,32]{3,2,1,0:T(4,128)(2,1)S(1)}, u32[]{:S(2)}, u32[]{:S(2)}) %collective-permute-start.17) | collective-permute-done | bytes 1056 | tf_op jit(solution)/shard_map/ppermute | solution.py:432
  84.9 3.2 %collective-permute-done.18.second = bf16[2,2,4,32]{3,2,1,0:T(4,128)(2,1)S(1)} collective-permute-done((bf16[2,2,4,32]{3,2,1,0:T(4,128)(2,1)S(1)}, bf16[2,2,4,32]{3,2,1,0:T(4,128)(2,1)S(1)}, u32[]{:S(2)}, u32[]{:S(2)}) %collective-permute-start.18) | collective-permute-done | bytes 1056 | tf_op jit(solution)/shard_map/ppermute | solution.py:432
  88.1 0.6 shard_map.71
  88.7 1.9 %shard_map.72 = (bf16[10,64,256]{2,1,0:T(8,128)(2,1)S(1)}, bf16[10,64,256]{2,1,0:T(8,128)(2,1)S(1)}) custom-call(s32[4]{0:T(128)S(1)} %fusion.4.flags, s32[3,1]{1,0:T(4,128)S(1)} %copy.30.mask, bf16[8,256,256]{2,1,0:T(8,128)(2,1)S(1)} %get-tuple-element.59.cols, f32[64,256]{1,0:T(8,128)S(1)} %get-tuple-element.60.table, ...), custom_call_target="tpu_custom_call" | custom-call | flops 800000000 | bytes 4000000 | tf_op jit(solution)/shard_map/pallas_call | solution.py:331
  90.6 0.1 collective-permute-start.20
  90.7 3.6 %collective-permute-start.21 = (bf16[10,64,256]{2,1,0:T(8,128)(2,1)S(1)}, bf16[10,64,256]{2,1,0:T(8,128)(2,1)S(1)}, u32[]{:S(2)}, u32[]{:S(2)}) collective-permute-start(bf16[10,64,256]{2,1,0:T(8,128)(2,1)S(1)} %get-tuple-element.62), channel_id=1, source_target_pairs={{0,112},{1,113},{2,114},{3,115},{4,116},{5,117},{6,118},{7,119},{8... | collective-permute-start | bytes 983048 | tf_op jit(solution)/shard_map/ppermute | solution.py:432
  94.3 1.9 %shard_map.74 = (bf16[10,64,256]{2,1,0:T(8,128)(2,1)S(1)}, bf16[10,64,256]{2,1,0:T(8,128)(2,1)S(1)}) custom-call(s32[4]{0:T(128)S(1)} %fusion.4.flags, s32[3,1]{1,0:T(4,128)S(1)} %copy.30.mask, bf16[8,256,256]{2,1,0:T(8,128)(2,1)S(1)} %get-tuple-element.59.cols, f32[64,256]{1,0:T(8,128)S(1)} %get-tuple-element.60.table, ...), custom_call_target="tpu_custom_call" | custom-call | flops 800000000 | bytes 4000000 | tf_op jit(solution)/shard_map/pallas_call | solution.py:331
  96.2 0.1 collective-permute-start.22
  96.3 3.6 %collective-permute-start.23 = (bf16[10,64,256]{2,1,0:T(8,128)(2,1)S(1)}, bf16[10,64,256]{2,1,0:T(8,128)(2,1)S(1)}, u32[]{:S(2)}, u32[]{:S(2)}) collective-permute-start(bf16[10,64,256]{2,1,0:T(8,128)(2,1)S(1)} %get-tuple-element.66), channel_id=1, source_target_pairs={{0,112},{1,113},{2,114},{3,115},{4,116},{5,117},{6,118},{7,119},{8... | collective-permute-start | bytes 983048 | tf_op jit(solution)/shard_map/ppermute | solution.py:432
  99.8 2.4 %collective-permute-done.20.earlier.inner_earlier = bf16[10,64,256]{2,1,0:T(8,128)(2,1)S(1)} collective-permute-done((bf16[10,64,256]{2,1,0:T(8,128)(2,1)S(1)}, bf16[10,64,256]{2,1,0:T(8,128)(2,1)S(1)}, u32[]{:S(2)}, u32[]{:S(2)}) %collective-permute-start.20) | collective-permute-done | bytes 327712 | tf_op jit(solution)/shard_map/ppermute | solution.py:432
  102.3 0.0 collective-permute-done.21.later.inner_later
  102.3 2.2 %shard_map.73 = (bf16[8,64,256]{2,1,0:T(8,128)(2,1)S(1)}, bf16[6,64,256]{2,1,0:T(8,128)(2,1)S(1)}) custom-call(s32[4]{0:T(128)S(1)} %fusion.4.flags, s32[3,1]{1,0:T(4,128)S(1)} %copy.30.mask, bf16[192,576]{1,0:T(8,128)(2,1)S(1)} %get-tuple-element.39.wu, bf16[192,192]{1,0:T(8,128)(2,1)S(1)} %get-tuple-element.40.wm, ...), custom_call_target="tpu_custom_call" | custom-call | flops 600000000 | bytes 4000000 | tf_op jit(solution)/shard_map/pallas_call | solution.py:331
  104.5 4.8 %collective-permute-done.22.earlier = bf16[10,64,256]{2,1,0:T(8,128)(2,1)S(1)} collective-permute-done((bf16[10,64,256]{2,1,0:T(8,128)(2,1)S(1)}, bf16[10,64,256]{2,1,0:T(8,128)(2,1)S(1)}, u32[]{:S(2)}, u32[]{:S(2)}) %collective-permute-start.22) | collective-permute-done | bytes 327712 | tf_op jit(solution)/shard_map/ppermute | solution.py:432
  109.3 3.1 %shard_map.75 = bf16[16,64,256]{2,1,0:T(8,128)(2,1)} custom-call(s32[4]{0:T(128)S(1)} %fusion.4.flags, s32[3,1]{1,0:T(4,128)S(1)} %copy.30.mask, bf16[192,576]{1,0:T(8,128)(2,1)S(1)} %get-tuple-element.39.wu, bf16[192,192]{1,0:T(8,128)(2,1)S(1)} %get-tuple-element.40.wm, bf16[8,64,256]{2,1,0:T(8,128)(2,1)S(1)} %collective-permute-done.16.refs_0_.outer, ...), custom_call_target="tpu_custom_call" | custom-call | flops 900000000 | bytes 4000000 | tf_op jit(solution)/shard_map/pallas_call | solution.py:331
  (24 shorter events, 0.2 us)
Async XLA Ops:
  0.0 13.1 %copy-start.2 = (s32[3,1]{0,1:T(1,128)S(1)}, s32[3,1]{0,1:T(1,128)}, u32[]{:S(2)}) copy-start(s32[3,1]{0,1:T(1,128)} %param.9) | copy-start | bytes 40
  0.0 13.2 %copy-start = (bf16[3,3,64,192]{3,2,1,0:T(8,128)(2,1)S(1)}, bf16[3,3,64,192]{3,2,1,0:T(8,128)(2,1)}, u32[]{:S(2)}) copy-start(bf16[3,3,64,192]{3,2,1,0:T(8,128)(2,1)} %uniting.1) | copy-start | bytes 663556
  0.0 13.2 %copy-start.1 = (bf16[3,3,64,64]{3,2,1,0:T(8,128)(2,1)S(1)}, bf16[3,3,64,64]{3,2,1,0:T(8,128)(2,1)}, u32[]{:S(2)}) copy-start(bf16[3,3,64,64]{3,2,1,0:T(8,128)(2,1)} %mixing.1) | copy-start | bytes 221188
  1.2 20.2 %collective-permute-start.2 = (bf16[8,64,256]{2,1,0:T(8,128)(2,1)S(1)}, bf16[8,64,256]{2,1,0:T(8,128)(2,1)S(1)}, u32[]{:S(2)}, u32[]{:S(2)}) collective-permute-start(bf16[8,64,256]{2,1,0:T(8,128)(2,1)S(1)} %get-tuple-element.70.refs_5_), channel_id=1, source_target_pairs={{1,66},{2,65},{3,68},{4,67},{5,70},{6,69},{7,72},{8,71},{9,74},{10... | collective-permute-start | bytes 786440 | tf_op jit(solution)/shard_map/ppermute | solution.py:432
  4.8 16.5 %collective-permute-start.3 = (bf16[8,64,256]{2,1,0:T(8,128)(2,1)S(1)}, bf16[8,64,256]{2,1,0:T(8,128)(2,1)S(1)}, u32[]{:S(2)}, u32[]{:S(2)}) collective-permute-start(bf16[8,64,256]{2,1,0:T(8,128)(2,1)S(1)} %get-tuple-element.70.refs_5_), channel_id=1, source_target_pairs={{0,64},{1,65},{2,66},{3,67},{4,68},{5,69},{6,70},{7,71},{8,72},{9,... | collective-permute-start | bytes 786440 | tf_op jit(solution)/shard_map/ppermute | solution.py:432
  7.3 6.0 %collective-permute-start = (bf16[3,64,256]{2,1,0:T(8,128)(2,1)S(1)}, bf16[3,64,256]{2,1,0:T(8,128)(2,1)S(1)}, u32[]{:S(2)}, u32[]{:S(2)}) collective-permute-start(bf16[3,64,256]{2,1,0:T(8,128)(2,1)S(1)} %pad_maximum_fusion), channel_id=1, source_target_pairs={{0,1},{1,0},{2,3},{3,2},{4,5},{5,4},{6,7},{7,6},{8,9},{9,8},{10,11... | collective-permute-start | bytes 294920 | tf_op jit(solution)/shard_map/ppermute | solution.py:432
  7.6 9.8 %collective-permute-start.1 = (bf16[3,64,256]{2,1,0:T(8,128)(2,1)S(1)}, bf16[3,64,256]{2,1,0:T(8,128)(2,1)S(1)}, u32[]{:S(2)}, u32[]{:S(2)}) collective-permute-start(bf16[3,64,256]{2,1,0:T(8,128)(2,1)S(1)} %pad_maximum_fusion.1), channel_id=1, source_target_pairs={{1,2},{2,1},{3,4},{4,3},{5,6},{6,5},{7,8},{8,7},{9,10},{10,9},{11,... | collective-permute-start | bytes 294920 | tf_op jit(solution)/shard_map/ppermute | solution.py:432
  12.9 7.6 %collective-permute-start.4 = (bf16[8,64,256]{2,1,0:T(8,128)(2,1)S(1)}, bf16[8,64,256]{2,1,0:T(8,128)(2,1)S(1)}, u32[]{:S(2)}, u32[]{:S(2)}) collective-permute-start(bf16[8,64,256]{2,1,0:T(8,128)(2,1)S(1)} %get-tuple-element.69.refs_6_), channel_id=1, source_target_pairs={{0,64},{1,65},{2,66},{3,67},{4,68},{5,69},{6,70},{7,71},{8,72},{9,... | collective-permute-start | bytes 786440 | tf_op jit(solution)/shard_map/ppermute | solution.py:432
  20.5 1.5 %collective-permute-start.5 = (bf16[8,64,256]{2,1,0:T(8,128)(2,1)S(1)}, bf16[8,64,256]{2,1,0:T(8,128)(2,1)S(1)}, u32[]{:S(2)}, u32[]{:S(2)}) collective-permute-start(bf16[8,64,256]{2,1,0:T(8,128)(2,1)S(1)} %collective-permute-done.4.refs_2_), channel_id=1, source_target_pairs={{0,1},{1,0},{2,3},{3,2},{4,5},{5,4},{6,7},{7,6},{8,9},{9,8},{10,11... | collective-permute-start | bytes 786440 | tf_op jit(solution)/shard_map/ppermute | solution.py:432
  29.0 10.2 %collective-permute-start.9 = (bf16[8,64,256]{2,1,0:T(8,128)(2,1)S(1)}, bf16[8,64,256]{2,1,0:T(8,128)(2,1)S(1)}, u32[]{:S(2)}, u32[]{:S(2)}) collective-permute-start(bf16[8,64,256]{2,1,0:T(8,128)(2,1)S(1)} %get-tuple-element.51.refs_10_), channel_id=1, source_target_pairs={{0,32},{1,33},{2,34},{3,35},{4,36},{5,37},{6,38},{7,39},{8,40},{9,... | collective-permute-start | bytes 786440 | tf_op jit(solution)/shard_map/ppermute | solution.py:432
  32.7 12.1 %collective-permute-start.6 = (bf16[8,64,256]{2,1,0:T(8,128)(2,1)S(1)}, bf16[8,64,256]{2,1,0:T(8,128)(2,1)S(1)}, u32[]{:S(2)}, u32[]{:S(2)}) collective-permute-start(bf16[8,64,256]{2,1,0:T(8,128)(2,1)S(1)} %get-tuple-element.49.refs_9_), channel_id=1, source_target_pairs={{0,32},{1,33},{2,34},{3,35},{4,36},{5,37},{6,38},{7,39},{8,40},{9,... | collective-permute-start | bytes 786440 | tf_op jit(solution)/shard_map/ppermute | solution.py:432
  39.2 12.5 %collective-permute-start.12 = (bf16[8,64,256]{2,1,0:T(8,128)(2,1)S(1)}, bf16[8,64,256]{2,1,0:T(8,128)(2,1)S(1)}, u32[]{:S(2)}, u32[]{:S(2)}) collective-permute-start(bf16[8,64,256]{2,1,0:T(8,128)(2,1)S(1)} %collective-permute-done.9.refs_2_), channel_id=1, source_target_pairs={{0,64},{1,65},{2,66},{3,67},{4,68},{5,69},{6,70},{7,71},{8,72},{9,... | collective-permute-start | bytes 786440 | tf_op jit(solution)/shard_map/ppermute | solution.py:432
  44.9 7.7 %collective-permute-start.7 = (bf16[8,64,256]{2,1,0:T(8,128)(2,1)S(1)}, bf16[8,64,256]{2,1,0:T(8,128)(2,1)S(1)}, u32[]{:S(2)}, u32[]{:S(2)}) collective-permute-start(bf16[8,64,256]{2,1,0:T(8,128)(2,1)S(1)} %collective-permute-done.6.refs_1_), channel_id=1, source_target_pairs={{0,64},{1,65},{2,66},{3,67},{4,68},{5,69},{6,70},{7,71},{8,72},{9,... | collective-permute-start | bytes 786440 | tf_op jit(solution)/shard_map/ppermute | solution.py:432
  46.6 21.1 %collective-permute-start.10 = (bf16[8,64,256]{2,1,0:T(8,128)(2,1)S(1)}, bf16[8,64,256]{2,1,0:T(8,128)(2,1)S(1)}, u32[]{:S(2)}, u32[]{:S(2)}) collective-permute-start(bf16[8,64,256]{2,1,0:T(8,128)(2,1)S(1)} %collective-permute-done.9.refs_2_), channel_id=1, source_target_pairs={{0,1},{1,0},{2,3},{3,2},{4,5},{5,4},{6,7},{7,6},{8,9},{9,8},{10,11... | collective-permute-start | bytes 786440 | tf_op jit(solution)/shard_map/ppermute | solution.py:432
  47.6 20.1 %collective-permute-start.11 = (bf16[8,64,256]{2,1,0:T(8,128)(2,1)S(1)}, bf16[8,64,256]{2,1,0:T(8,128)(2,1)S(1)}, u32[]{:S(2)}, u32[]{:S(2)}) collective-permute-start(bf16[8,64,256]{2,1,0:T(8,128)(2,1)S(1)} %collective-permute-done.6.refs_1_), channel_id=1, source_target_pairs={{1,66},{2,65},{3,68},{4,67},{5,70},{6,69},{7,72},{8,71},{9,74},{10... | collective-permute-start | bytes 786440 | tf_op jit(solution)/shard_map/ppermute | solution.py:432
  51.8 16.0 %collective-permute-start.13 = (bf16[8,64,256]{2,1,0:T(8,128)(2,1)S(1)}, bf16[8,64,256]{2,1,0:T(8,128)(2,1)S(1)}, u32[]{:S(2)}, u32[]{:S(2)}) collective-permute-start(bf16[8,64,256]{2,1,0:T(8,128)(2,1)S(1)} %collective-permute-done.12.refs_6_), channel_id=1, source_target_pairs={{0,1},{1,0},{2,3},{3,2},{4,5},{5,4},{6,7},{7,6},{8,9},{9,8},{10,11... | collective-permute-start | bytes 786440 | tf_op jit(solution)/shard_map/ppermute | solution.py:432
  52.6 15.2 %collective-permute-start.8 = (bf16[8,64,256]{2,1,0:T(8,128)(2,1)S(1)}, bf16[8,64,256]{2,1,0:T(8,128)(2,1)S(1)}, u32[]{:S(2)}, u32[]{:S(2)}) collective-permute-start(bf16[8,64,256]{2,1,0:T(8,128)(2,1)S(1)} %collective-permute-done.7.refs_5_), channel_id=1, source_target_pairs={{1,66},{2,65},{3,68},{4,67},{5,70},{6,69},{7,72},{8,71},{9,74},{10... | collective-permute-start | bytes 786440 | tf_op jit(solution)/shard_map/ppermute | solution.py:432
  58.1 1.3 %collective-permute-start.15 = (bf16[2,64,256]{2,1,0:T(8,128)(2,1)S(1)}, bf16[2,64,256]{2,1,0:T(8,128)(2,1)S(1)}, u32[]{:S(2)}, u32[]{:S(2)}) collective-permute-start(bf16[2,64,256]{2,1,0:T(8,128)(2,1)S(1)} %get-tuple-element.53), channel_id=1, source_target_pairs={{0,1},{1,0},{2,3},{3,2},{4,5},{5,4},{6,7},{7,6},{8,9},{9,8},{10,11... | collective-permute-start | bytes 196616 | tf_op jit(solution)/shard_map/ppermute | solution.py:432
  59.5 8.3 %collective-permute-start.14 = (bf16[2,64,256]{2,1,0:T(8,128)(2,1)S(1)}, bf16[2,64,256]{2,1,0:T(8,128)(2,1)S(1)}, u32[]{:S(2)}, u32[]{:S(2)}) collective-permute-start(bf16[2,64,256]{2,1,0:T(8,128)(2,1)S(1)} %get-tuple-element.52), channel_id=1, source_target_pairs={{1,2},{2,1},{3,4},{4,3},{5,6},{6,5},{7,8},{8,7},{9,10},{10,9},{11,... | collective-permute-start | bytes 196616 | tf_op jit(solution)/shard_map/ppermute | solution.py:432
  76.1 12.6 %collective-permute-start.19 = (bf16[8,64,256]{2,1,0:T(8,128)(2,1)S(1)}, bf16[8,64,256]{2,1,0:T(8,128)(2,1)S(1)}, u32[]{:S(2)}, u32[]{:S(2)}) collective-permute-start(bf16[8,64,256]{2,1,0:T(8,128)(2,1)S(1)} %get-tuple-element.56.refs_1_.inner.refs_2_), channel_id=1, source_target_pairs={{0,1},{1,0},{2,3},{3,2},{4,5},{5,4},{6,7},{7,6},{8,9},{9,8},{10,11... | collective-permute-start | bytes 786440 | tf_op jit(solution)/shard_map/ppermute | solution.py:432
  76.1 18.2 %collective-permute-start.16 = (bf16[8,64,256]{2,1,0:T(8,128)(2,1)S(1)}, bf16[8,64,256]{2,1,0:T(8,128)(2,1)S(1)}, u32[]{:S(2)}, u32[]{:S(2)}) collective-permute-start(bf16[8,64,256]{2,1,0:T(8,128)(2,1)S(1)} %get-tuple-element.54.refs_0_.refs_1_.edge), channel_id=1, source_target_pairs={{1,2},{2,1},{3,4},{4,3},{5,6},{6,5},{7,8},{8,7},{9,10},{10,9},{11,... | collective-permute-start | bytes 786440 | tf_op jit(solution)/shard_map/ppermute | solution.py:432
  79.8 5.1 %collective-permute-start.17 = (bf16[2,2,4,32]{3,2,1,0:T(4,128)(2,1)S(1)}, bf16[2,2,4,32]{3,2,1,0:T(4,128)(2,1)S(1)}, u32[]{:S(2)}, u32[]{:S(2)}) collective-permute-start(bf16[2,2,4,32]{3,2,1,0:T(4,128)(2,1)S(1)} %get-tuple-element.57), channel_id=1, source_target_pairs={{0,112},{1,113},{2,114},{3,115},{4,116},{5,117},{6,118},{7,119},{8... | collective-permute-start | bytes 3080 | tf_op jit(solution)/shard_map/ppermute | solution.py:432
  82.4 5.7 %collective-permute-start.18 = (bf16[2,2,4,32]{3,2,1,0:T(4,128)(2,1)S(1)}, bf16[2,2,4,32]{3,2,1,0:T(4,128)(2,1)S(1)}, u32[]{:S(2)}, u32[]{:S(2)}) collective-permute-start(bf16[2,2,4,32]{3,2,1,0:T(4,128)(2,1)S(1)} %get-tuple-element.58), channel_id=1, source_target_pairs={{0,16},{1,17},{2,18},{3,19},{4,20},{5,21},{6,22},{7,23},{8,24},{9,... | collective-permute-start | bytes 3080 | tf_op jit(solution)/shard_map/ppermute | solution.py:432
  90.6 11.6 %collective-permute-start.20 = (bf16[10,64,256]{2,1,0:T(8,128)(2,1)S(1)}, bf16[10,64,256]{2,1,0:T(8,128)(2,1)S(1)}, u32[]{:S(2)}, u32[]{:S(2)}) collective-permute-start(bf16[10,64,256]{2,1,0:T(8,128)(2,1)S(1)} %get-tuple-element.61), channel_id=1, source_target_pairs={{0,16},{1,17},{2,18},{3,19},{4,20},{5,21},{6,22},{7,23},{8,24},{9,... | collective-permute-start | bytes 983048 | tf_op jit(solution)/shard_map/ppermute | solution.py:432
  90.7 11.5 %collective-permute-start.21 = (bf16[10,64,256]{2,1,0:T(8,128)(2,1)S(1)}, bf16[10,64,256]{2,1,0:T(8,128)(2,1)S(1)}, u32[]{:S(2)}, u32[]{:S(2)}) collective-permute-start(bf16[10,64,256]{2,1,0:T(8,128)(2,1)S(1)} %get-tuple-element.62), channel_id=1, source_target_pairs={{0,112},{1,113},{2,114},{3,115},{4,116},{5,117},{6,118},{7,119},{8... | collective-permute-start | bytes 983048 | tf_op jit(solution)/shard_map/ppermute | solution.py:432
  96.2 13.1 %collective-permute-start.22 = (bf16[10,64,256]{2,1,0:T(8,128)(2,1)S(1)}, bf16[10,64,256]{2,1,0:T(8,128)(2,1)S(1)}, u32[]{:S(2)}, u32[]{:S(2)}) collective-permute-start(bf16[10,64,256]{2,1,0:T(8,128)(2,1)S(1)} %get-tuple-element.65), channel_id=1, source_target_pairs={{0,16},{1,17},{2,18},{3,19},{4,20},{5,21},{6,22},{7,23},{8,24},{9,... | collective-permute-start | bytes 983048 | tf_op jit(solution)/shard_map/ppermute | solution.py:432
  96.3 13.0 %collective-permute-start.23 = (bf16[10,64,256]{2,1,0:T(8,128)(2,1)S(1)}, bf16[10,64,256]{2,1,0:T(8,128)(2,1)S(1)}, u32[]{:S(2)}, u32[]{:S(2)}) collective-permute-start(bf16[10,64,256]{2,1,0:T(8,128)(2,1)S(1)} %get-tuple-element.66), channel_id=1, source_target_pairs={{0,112},{1,113},{2,114},{3,115},{4,116},{5,117},{6,118},{7,119},{8... | collective-permute-start | bytes 983048 | tf_op jit(solution)/shard_map/ppermute | solution.py:432
